TPU v7x, 256 devices: a whole 4x4x8 slice. The times are simulated.
256 devices in a mesh: ctx: 16 (over z, core), dp: 16 (over y, x).
Axes of the slice: x: 4, y: 4, z: 8, core: 2. Of those that a mesh axis runs over, the one named last changes fastest.
Arguments:
- queries: bfloat16 [16, 2048, 4096], P('dp', 'ctx'), may hold values from -48 to 48
- grad_out: bfloat16 [16, 2048, 4096], P('dp', 'ctx'), may hold values from -48 to 48
- neighbour_keys: bfloat16 [64, 128, 4096], P('dp', None, 'ctx'), may hold values from -6 to 6
- neighbour_values: bfloat16 [64, 128, 4096], P('dp', None, 'ctx'), may hold values from -6 to 6
- distinct_ids: int32 [16, 16], replicated, may hold values from 0 to 63, as said below
- group_refs: int32 [16, 32, 2], replicated, may hold values from 0 to 15, as said below
Outputs:
- grad_queries: bfloat16 [16, 2048, 4096], P('dp', 'ctx')
- grad_keys: bfloat16 [64, 128, 4096], P('dp', None, 'ctx')
- grad_values: bfloat16 [64, 128, 4096], P('dp', None, 'ctx')
Inputs may be any that keep to these rules, and one draw needn't show every extreme that they name: `distinct_ids`: each row lists 16 different neighbours. Neighbour n is owned by data replica n // 4. No owner holds more than 2 of one row's neighbours, and one owner, the same for every row, holds exactly 2 in every row. `group_refs`: every position of a replica's row of distinct_ids occurs in that replica's entries.
All inputs are finite; a program needn't handle non-finite values.
Results may differ from a plain program's by a relative error of at most 0.0075.
Values may be sent and summed in bfloat16 or wider, within the bound.
No kernel may reach another device: no remote copies, remote signals or barrier semaphores. Data moves between devices by JAX's collectives and lax.ppermute only.
A program may use at most 128 MiB of HBM per device.

v0:
```python
import math

import jax
import jax.numpy as jnp
from jax import lax
from jax.sharding import PartitionSpec as P

DH = 128
GROUP = 64


def shift_blocks(token_rows, head_count):
    padding = jnp.zeros((GROUP - 1, token_rows.shape[1]), token_rows.dtype)
    joined = jnp.concatenate([token_rows[GROUP - 1 :], padding], axis=0)
    return joined.reshape(-1, GROUP, head_count, DH).transpose(0, 2, 1, 3)


def owner_tables(distinct_ids, owned_count, capacity, replicas):
    owners = distinct_ids // owned_count
    local_index = distinct_ids % owned_count
    marked = (owners[:, :, None] == jnp.arange(replicas)[None, None, :]).astype(jnp.int32)
    ranking = jnp.sum(jnp.cumsum(marked, axis=1) * marked, axis=2) - 1
    return (local_index, owners * capacity + ranking)


def on_device(queries, grad_out, neighbour_keys, neighbour_values, distinct_ids, group_refs):
    replicas = lax.axis_size("dp")
    my_replica = lax.axis_index("dp")
    owned_count = neighbour_keys.shape[0]
    capacity = owned_count // 2
    neighbour_tokens = neighbour_keys.shape[1]
    head_width = neighbour_keys.shape[2]
    head_count = head_width // DH
    distinct = distinct_ids.shape[1]
    score_scale = 1.0 / math.sqrt(DH)
    query_heads, grad_heads = (
        lax.all_to_all(queries, "ctx", split_axis=2, concat_axis=1, tiled=True),
        lax.all_to_all(grad_out, "ctx", split_axis=2, concat_axis=1, tiled=True),
    )
    query_heads = query_heads[0]
    grad_heads = grad_heads[0]
    token_count = query_heads.shape[0]
    group_total = token_count // GROUP
    local_index, position = owner_tables(distinct_ids, owned_count, capacity, replicas)
    own_list = lax.dynamic_index_in_dim(distinct_ids, my_replica, 0, keepdims=False)
    own_slots = lax.dynamic_index_in_dim(group_refs, my_replica, 0, keepdims=False).reshape(-1)
    own_position = lax.dynamic_index_in_dim(position, my_replica, 0, keepdims=False)
    slot_range = my_replica * capacity + jnp.arange(capacity)
    matches = (position[:, :, None] == slot_range[None, None, :]).astype(jnp.int32)
    send_rows = jnp.sum(matches * local_index[:, :, None], axis=1).reshape(-1)
    send_valid = jnp.sum(matches, axis=1).reshape(-1)
    pool_keys, pool_values = (
        lax.all_gather(neighbour_keys, "dp", axis=0, tiled=True),
        lax.all_gather(neighbour_values, "dp", axis=0, tiled=True),
    )
    distinct_keys = jnp.take(pool_keys, own_list, axis=0)
    distinct_values = jnp.take(pool_values, own_list, axis=0)
    pair_count = group_refs.shape[2]
    slot_keys = (
        jnp.take(distinct_keys, own_slots, axis=0)
        .reshape(group_total, pair_count * neighbour_tokens, head_count, DH)
        .transpose(0, 2, 1, 3)
    )
    slot_values = (
        jnp.take(distinct_values, own_slots, axis=0)
        .reshape(group_total, pair_count * neighbour_tokens, head_count, DH)
        .transpose(0, 2, 1, 3)
    )
    query_blocks = shift_blocks(query_heads, head_count)
    grad_blocks = shift_blocks(grad_heads, head_count)
    scores = (
        jnp.einsum("chqd,chkd->chqk", query_blocks, slot_keys, preferred_element_type=jnp.float32)
        * score_scale
    )
    row_max = jnp.max(scores, axis=-1, keepdims=True)
    totals = row_max + jnp.log(jnp.sum(jnp.exp(scores - row_max), axis=-1, keepdims=True))
    attention = jnp.exp(scores - totals)
    grad_attention = jnp.einsum(
        "chqd,chkd->chqk", grad_blocks, slot_values, preferred_element_type=jnp.float32
    )
    row_dots = jnp.sum(attention * grad_attention, axis=-1, keepdims=True)
    grad_low = (attention * (grad_attention - row_dots)).astype(jnp.bfloat16)
    attention_low = attention.astype(jnp.bfloat16)
    grad_query_blocks = (
        jnp.einsum("chqk,chkd->cqhd", grad_low, slot_keys, preferred_element_type=jnp.float32)
        * score_scale
    )
    key_slots = (
        jnp.einsum("chqk,chqd->ckhd", grad_low, query_blocks, preferred_element_type=jnp.float32)
        * score_scale
    )
    value_slots = jnp.einsum(
        "chqk,chqd->ckhd", attention_low, grad_blocks, preferred_element_type=jnp.float32
    )
    flat_query = grad_query_blocks.reshape(token_count, head_width)
    grad_tokens = jnp.concatenate(
        [jnp.zeros((GROUP - 1, head_width), jnp.float32), flat_query[: token_count - GROUP + 1]],
        axis=0,
    ).astype(jnp.bfloat16)
    grad_queries = lax.all_to_all(grad_tokens[None], "ctx", split_axis=1, concat_axis=2, tiled=True)
    slot_count = own_slots.shape[0]
    selector = (own_slots[None, :] == jnp.arange(distinct)[:, None]).astype(jnp.float32)
    key_terms = jnp.dot(
        selector, key_slots.reshape(slot_count, -1), precision=lax.Precision.HIGHEST
    ).astype(jnp.bfloat16)
    value_terms = jnp.dot(
        selector, value_slots.reshape(slot_count, -1), precision=lax.Precision.HIGHEST
    ).astype(jnp.bfloat16)
    located = (own_position[None, :] == jnp.arange(replicas * capacity)[:, None]).astype(jnp.int32)
    back_rows = jnp.sum(located * jnp.arange(distinct)[None, :], axis=1)
    back_valid = jnp.sum(located, axis=1)[:, None] > 0
    empty_rows = jnp.zeros((replicas * capacity, key_terms.shape[1]), jnp.bfloat16)
    keys_send = jnp.where(back_valid, jnp.take(key_terms, back_rows, axis=0), empty_rows).reshape(
        replicas, capacity, neighbour_tokens, head_width
    )
    values_send = jnp.where(
        back_valid, jnp.take(value_terms, back_rows, axis=0), empty_rows
    ).reshape(replicas, capacity, neighbour_tokens, head_width)
    keys_in, values_in = (
        lax.all_to_all(keys_send, "dp", split_axis=0, concat_axis=0, tiled=True),
        lax.all_to_all(values_send, "dp", split_axis=0, concat_axis=0, tiled=True),
    )
    owner_select = (
        (send_rows[None, :] == jnp.arange(owned_count)[:, None]) & (send_valid[None, :] > 0)
    ).astype(jnp.bfloat16)
    grad_keys = jnp.dot(
        owner_select, keys_in.reshape(replicas * capacity, -1), preferred_element_type=jnp.float32
    )
    grad_values = jnp.dot(
        owner_select, values_in.reshape(replicas * capacity, -1), preferred_element_type=jnp.float32
    )
    grad_keys = grad_keys.astype(jnp.bfloat16).reshape(owned_count, neighbour_tokens, head_width)
    grad_values = grad_values.astype(jnp.bfloat16).reshape(
        owned_count, neighbour_tokens, head_width
    )
    return (grad_queries, grad_keys, grad_values)


def solution(mesh):
    return jax.shard_map(
        on_device,
        mesh=mesh,
        in_specs=(
            P("dp", "ctx", None),
            P("dp", "ctx", None),
            P("dp", None, "ctx"),
            P("dp", None, "ctx"),
            P(),
            P(),
        ),
        out_specs=(P("dp", "ctx", None), P("dp", None, "ctx"), P("dp", None, "ctx")),
        check_vma=False,
    )
```

profile of v0, /device:TPU:8, one launch (start us, length us, event | category | flops | bytes accessed | tf_op | source)
XLA Modules:
  0.0 377.9 jit_solution(5333341220551715197)
XLA Ops:
  8.7 5.0 %copy.81 = bf16[1,128,4096]{1,0,2:T(2,128)(2,1)S(1)} copy(bf16[1,128,4096]{2,1,0:T(8,128)(2,1)} %param.12) | data formatting | bytes 2097152 | tf_op args[0]
  14.2 22.4 %reduce.2 = bf16[4096,128]{1,0:T(8,128)(2,1)S(1)} reduce(bf16[4096,1,128]{2,1,0:T(2,128)(2,1)S(1)} %bitcast.105, bf16[]{:T(256)} %broadcast.124), dimensions={1}, to_apply=%bitcast.70.reduce_sub_computation | reduce | bytes 2097154
  37.7 8.6 %all-to-all-start = ((bf16[16,2,16384]{2,1,0:T(2,128)(2,1)}), bf16[16,2,16384]{2,1,0:T(2,128)(2,1)S(1)}, u32[]{:S(2)}, u32[]{:S(2)}) async-start(bf16[16,2,16384]{2,1,0:T(2,128)(2,1)} %reshape.183), calls=%async_computation | async-start | bytes 2097152 | tf_op jit(solution)/shard_map/all_to_all | solution.py:37
  46.3 5.1 %copy.84 = bf16[1,128,4096]{1,0,2:T(2,128)(2,1)S(1)} copy(bf16[1,128,4096]{2,1,0:T(8,128)(2,1)} %param.13) | data formatting | bytes 2097152 | tf_op args[1]
  51.4 23.4 %reduce.3 = bf16[4096,128]{1,0:T(8,128)(2,1)} reduce(bf16[4096,1,128]{2,1,0:T(2,128)(2,1)S(1)} %bitcast.108, bf16[]{:T(256)} %broadcast.124), dimensions={1}, to_apply=%bitcast.68.reduce_sub_computation | reduce | bytes 2097154
  77.1 7.6 %all-to-all-start.1 = ((bf16[16,2,16384]{2,1,0:T(2,128)(2,1)}), bf16[16,2,16384]{2,1,0:T(2,128)(2,1)}, u32[]{:S(2)}, u32[]{:S(2)}) async-start(bf16[16,2,16384]{2,1,0:T(2,128)(2,1)} %reshape.181), calls=%async_computation.1 | async-start | bytes 2097152 | tf_op jit(solution)/shard_map/all_to_all | solution.py:38
  88.1 23.2 %all-to-all-done.1 = bf16[16,2,16384]{2,1,0:T(2,128)(2,1)} async-done(((bf16[16,2,16384]{2,1,0:T(2,128)(2,1)}), bf16[16,2,16384]{2,1,0:T(2,128)(2,1)}, u32[]{:S(2)}, u32[]{:S(2)}) %all-to-all-start.1) | async-done | bytes 1048608 | tf_op jit(solution)/shard_map/all_to_all | solution.py:38
  111.4 4.3 %reshape.182 = bf16[4096,1,128]{2,1,0:T(2,128)(2,1)S(1)} reshape(bf16[16,2,16384]{2,1,0:T(2,128)(2,1)} %all-to-all-done.1) | data formatting | bytes 2097152
  119.8 3.9 %gather_fusion = bf16[16,128,256]{2,1,0:T(8,128)(2,1)} fusion(bf16[64,128,256]{2,1,0:T(8,128)(2,1)} %all-gather.3.cloned.1.call-done, s32[1024]{0:T(1024)S(1)} %pad_clamp_fusion.2), kind=kCustom, calls=%fused_computation.clone | custom fusion | bytes 2097216 | tf_op jit(solution)/shard_map/jit(_take)/gather | solution.py:56
  123.7 4.9 %all-gather.5.cloned.1.call-done = bf16[64,128,256]{2,1,0:T(8,128)(2,1)} async-done(((bf16[4,128,256]{2,1,0:T(8,128)(2,1)}), bf16[64,128,256]{2,1,0:T(8,128)(2,1)}) %all-gather.5.cloned.1.call-update) | async-done | bytes 4194320 | tf_op jit(solution)/shard_map/all_gather | solution.py:54
  128.6 3.8 gather_fusion.2
  139.8 6.0 %broadcast_select_fusion.1 = (bf16[64,128,256]{2,1,0:T(8,128)(2,1)}, bf16[64,128,256]{2,1,0:T(8,128)(2,1)}) fusion(bf16[64,128,256]{2,1,0:T(8,128)(2,1)} %gather_fusion.1, pred[64]{0:T(512)(128)(4,1)S(1)} %compare_and_fusion.1, bf16[64,128,256]{2,1,0:T(8,128)(2,1)} %gather_fusion.3), kind=kLoop, calls=%fused_computation.23 | loop fusion | flops 4194304 | bytes 16777280 | tf_op jit(solution)/shard_map/jit(_take)/select_n | solution.py:60
  145.7 6.9 %reshape.101 = bf16[32,256,2,128]{3,2,1,0:T(2,128)(2,1)} reshape(bf16[64,128,256]{2,1,0:T(8,128)(2,1)} %get-tuple-element.28) | data formatting | bytes 8388608 | tf_op jit(solution)/shard_map/reshape | solution.py:61
  152.6 6.9 %reshape.104 = bf16[32,256,2,128]{3,2,1,0:T(2,128)(2,1)} reshape(bf16[64,128,256]{2,1,0:T(8,128)(2,1)} %get-tuple-element.29) | data formatting | bytes 8388608 | tf_op jit(solution)/shard_map/reshape | solution.py:66
  159.6 3.9 %multiply_reduce_fusion.1 = (f32[32,2,64]{2,1,0:T(2,128)S(1)}, f32[32,2,64,256]{3,2,1,0:T(8,128)S(1)}) fusion(bf16[32,256,2,128]{3,2,1,0:T(2,128)(2,1)} %reshape.101, bf16[32,64,2,128]{3,2,1,0:T(2,128)(2,1)S(1)} %reshape.102), kind=kOutput, calls=%fused_computation.26 | convolution fusion | flops 270528512 | bytes 9453568 | tf_op jit(solution)/shard_map/chqd,chkd->chqk/dot_general | solution.py:72
  164.9 4.1 %convolution_bitcast_fusion = f32[32,256,2,128]{1,3,2,0:T(8,128)} fusion(f32[32,2,64,256]{3,2,1,0:T(8,128)S(1)} %get-tuple-element.33, f32[32,2,64]{2,1,0:T(2,128)S(1)} %bitcast.119, bf16[32,64,2,128]{3,2,1,0:T(2,128)(2,1)S(1)} %copy-done.4), kind=kOutput, calls=%fused_computation.27 | convolution fusion | flops 271581184 | bytes 13647872 | tf_op jit(solution)/shard_map/chqk,chqd->ckhd/dot_general | solution.py:92
  174.6 4.5 %multiply_bitcast_fusion = f32[32,256,2,128]{1,3,2,0:T(8,128)} fusion(bf16[32,2,64,256]{3,2,1,0:T(8,128)(2,1)S(1)} %multiply_convert_fusion, bf16[32,64,2,128]{3,2,1,0:T(2,128)(2,1)S(1)} %reshape.102), kind=kOutput, calls=%fused_computation.10 | convolution fusion | flops 270532608 | bytes 11534336 | tf_op jit(solution)/shard_map/chqk,chqd->ckhd/dot_general | solution.py:89
  180.7 11.7 %copy.159 = bf16[1,2048,256]{2,0,1:T(2,128)(2,1)S(1)} copy(bf16[1,2048,256]{2,1,0:T(8,128)(2,1)S(1)} %pad_bitcast_fusion) | data formatting | bytes 2097152 | tf_op jit(solution)/shard_map/broadcast_in_dim | solution.py:100
  192.5 10.6 %reduce.4 = bf16[2048,256]{1,0:T(8,128)(2,1)S(1)} reduce(bf16[2048,1,256]{2,1,0:T(2,128)(2,1)S(1)} %bitcast.106, bf16[]{:T(256)} %broadcast.124), dimensions={1}, to_apply=%bitcast.93.reduce_sub_computation | reduce | bytes 2097154
  204.2 15.6 %all-to-all-start.2 = ((bf16[16,2,16384]{2,1,0:T(2,128)(2,1)}), bf16[16,2,16384]{2,1,0:T(2,128)(2,1)S(1)}, u32[]{:S(2)}, u32[]{:S(2)}) async-start(bf16[16,2,16384]{2,1,0:T(2,128)(2,1)} %reshape.185), calls=%async_computation.2 | async-start | bytes 2097152 | tf_op jit(solution)/shard_map/all_to_all | solution.py:100
  219.8 13.1 %copy.100 = f32[32,256,2,128]{3,2,1,0:T(2,128)} copy(f32[32,256,2,128]{1,3,2,0:T(8,128)} %convolution_bitcast_fusion) | data formatting | bytes 16777216 | tf_op jit(solution)/shard_map/chqk,chqd->ckhd/transpose | solution.py:92
  233.0 11.5 %reshape.110 = f32[64,32768]{1,0:T(8,128)} reshape(f32[32,256,2,128]{3,2,1,0:T(2,128)} %copy.100) | data formatting | bytes 16777216 | tf_op jit(solution)/shard_map/reshape | solution.py:107
  244.5 6.2 %convolution_convert_fusion = bf16[16,32768]{1,0:T(8,128)(2,1)S(1)} fusion(f32[64,32768]{1,0:T(8,128)} %reshape.110, s32[64]{0:T(128)S(1)} %reshape.100), kind=kOutput, calls=%fused_computation.6 | convolution fusion | flops 403178496 | bytes 9437440 | tf_op jit(solution)/shard_map/dot_general | solution.py:106
  250.7 13.1 %copy.99 = f32[32,256,2,128]{3,2,1,0:T(2,128)} copy(f32[32,256,2,128]{1,3,2,0:T(8,128)} %multiply_bitcast_fusion) | data formatting | bytes 16777216 | tf_op jit(solution)/shard_map/mul | solution.py:89
  263.8 11.5 %reshape.106 = f32[64,32768]{1,0:T(8,128)} reshape(f32[32,256,2,128]{3,2,1,0:T(2,128)} %copy.99) | data formatting | bytes 16777216 | tf_op jit(solution)/shard_map/reshape | solution.py:104
  275.3 6.2 %convolution_convert_fusion.1 = bf16[16,32768]{1,0:T(8,128)(2,1)S(1)} fusion(f32[64,32768]{1,0:T(8,128)} %reshape.106, s32[64]{0:T(128)S(1)} %reshape.100), kind=kOutput, calls=%fused_computation.7 | convolution fusion | flops 403178496 | bytes 9437440 | tf_op jit(solution)/shard_map/dot_general | solution.py:103
  281.5 3.3 gather_fusion.5
  284.8 3.2 gather_fusion.4
  292.6 5.8 %all-to-all-start.3 = ((bf16[16,2,128,256]{3,2,1,0:T(8,128)(2,1)}), bf16[16,2,128,256]{3,2,1,0:T(8,128)(2,1)}, u32[]{:S(2)}, u32[]{:S(2)}) async-start(bf16[16,2,128,256]{3,2,1,0:T(8,128)(2,1)} %bitcast.103), calls=%async_computation.3 | async-start | bytes 4194304 | tf_op jit(solution)/shard_map/all_to_all | solution.py:120
  300.1 30.8 %all-to-all-done.3 = bf16[16,2,128,256]{3,2,1,0:T(8,128)(2,1)} async-done(((bf16[16,2,128,256]{3,2,1,0:T(8,128)(2,1)}), bf16[16,2,128,256]{3,2,1,0:T(8,128)(2,1)}, u32[]{:S(2)}, u32[]{:S(2)}) %all-to-all-start.3) | async-done | bytes 2097184 | tf_op jit(solution)/shard_map/all_to_all | solution.py:120
  330.9 6.4 %all-to-all-start.4 = ((bf16[16,2,128,256]{3,2,1,0:T(8,128)(2,1)}), bf16[16,2,128,256]{3,2,1,0:T(8,128)(2,1)}, u32[]{:S(2)}, u32[]{:S(2)}) async-start(bf16[16,2,128,256]{3,2,1,0:T(8,128)(2,1)} %bitcast.102), calls=%async_computation.4 | async-start | bytes 4194304 | tf_op jit(solution)/shard_map/all_to_all | solution.py:121
  345.2 21.7 %all-to-all-done.4 = bf16[16,2,128,256]{3,2,1,0:T(8,128)(2,1)} async-done(((bf16[16,2,128,256]{3,2,1,0:T(8,128)(2,1)}), bf16[16,2,128,256]{3,2,1,0:T(8,128)(2,1)}, u32[]{:S(2)}, u32[]{:S(2)}) %all-to-all-start.4) | async-done | bytes 2097184 | tf_op jit(solution)/shard_map/all_to_all | solution.py:121
  (85 shorter events, 48.0 us)
Async XLA Ops:
  7.2 77.5 %copy-start = (s32[16,32,2]{1,2,0:T(2,128)S(1)}, s32[16,32,2]{1,2,0:T(2,128)}, u32[]{:S(2)}) copy-start(s32[16,32,2]{1,2,0:T(2,128)} %param.17) | copy-start | bytes 12292
  7.2 112.6 %all-gather.3.cloned.1.call-start = ((), (), s32[]{:S(2)}) async-start(), calls=%async_computation.5 | async-start | bytes 4456448 | tf_op jit(solution)/shard_map/all_gather | solution.py:53
  7.9 120.7 %all-gather.5.cloned.1.call-start = ((), (), s32[]{:S(2)}) async-start(), calls=%async_computation.6 | async-start | bytes 4456448 | tf_op jit(solution)/shard_map/all_gather | solution.py:54
  37.7 39.4 %all-to-all-start = ((bf16[16,2,16384]{2,1,0:T(2,128)(2,1)}), bf16[16,2,16384]{2,1,0:T(2,128)(2,1)S(1)}, u32[]{:S(2)}, u32[]{:S(2)}) async-start(bf16[16,2,16384]{2,1,0:T(2,128)(2,1)} %reshape.183), calls=%async_computation | async-start | bytes 2097152 | tf_op jit(solution)/shard_map/all_to_all | solution.py:37
  46.3 30.7 %copy-start.5 = (s32[16,16]{1,0:T(8,128)S(1)}, s32[16,16]{1,0:T(8,128)}, u32[]{:S(2)}) copy-start(s32[16,16]{1,0:T(8,128)} %param.16) | copy-start | bytes 3076
  77.1 34.2 %all-to-all-start.1 = ((bf16[16,2,16384]{2,1,0:T(2,128)(2,1)}), bf16[16,2,16384]{2,1,0:T(2,128)(2,1)}, u32[]{:S(2)}, u32[]{:S(2)}) async-start(bf16[16,2,16384]{2,1,0:T(2,128)(2,1)} %reshape.181), calls=%async_computation.1 | async-start | bytes 2097152 | tf_op jit(solution)/shard_map/all_to_all | solution.py:38
  163.4 1.5 copy-start.4
  164.9 4.1 %copy-start.3 = (bf16[32,256,2,128]{3,2,1,0:T(2,128)(2,1)S(1)}, bf16[32,256,2,128]{3,2,1,0:T(2,128)(2,1)}, u32[]{:S(2)}) copy-start(bf16[32,256,2,128]{3,2,1,0:T(2,128)(2,1)} %reshape.104) | copy-start | bytes 12582916
  171.6 2.2 copy-start.2
  204.2 88.4 %all-to-all-start.2 = ((bf16[16,2,16384]{2,1,0:T(2,128)(2,1)}), bf16[16,2,16384]{2,1,0:T(2,128)(2,1)S(1)}, u32[]{:S(2)}, u32[]{:S(2)}) async-start(bf16[16,2,16384]{2,1,0:T(2,128)(2,1)} %reshape.185), calls=%async_computation.2 | async-start | bytes 2097152 | tf_op jit(solution)/shard_map/all_to_all | solution.py:100
  292.6 38.4 %all-to-all-start.3 = ((bf16[16,2,128,256]{3,2,1,0:T(8,128)(2,1)}), bf16[16,2,128,256]{3,2,1,0:T(8,128)(2,1)}, u32[]{:S(2)}, u32[]{:S(2)}) async-start(bf16[16,2,128,256]{3,2,1,0:T(8,128)(2,1)} %bitcast.103), calls=%async_computation.3 | async-start | bytes 4194304 | tf_op jit(solution)/shard_map/all_to_all | solution.py:120
  330.9 36.0 %all-to-all-start.4 = ((bf16[16,2,128,256]{3,2,1,0:T(8,128)(2,1)}), bf16[16,2,128,256]{3,2,1,0:T(8,128)(2,1)}, u32[]{:S(2)}, u32[]{:S(2)}) async-start(bf16[16,2,128,256]{3,2,1,0:T(8,128)(2,1)} %bitcast.102), calls=%async_computation.4 | async-start | bytes 4194304 | tf_op jit(solution)/shard_map/all_to_all | solution.py:121
  344.1 26.7 %copy-start.1 = (s32[16,32,2]{1,2,0:T(2,128)S(1)}, s32[16,32,2]{1,2,0:T(2,128)}, u32[]{:S(2)}) copy-start(s32[16,32,2]{1,2,0:T(2,128)} %param.17) | copy-start | bytes 12292
Sparse Core Ops, SparseCore 0:
  10.4 59.3 all-gather.2
  72.3 56.2 all-gather.4
where the time goes:
time: 385 us; the launch traced here: 378 us
  local copies, waits for them, and re-layouts  137 us (36%)
  waiting for transfers between devices  82 us (21%)
  other arithmetic  70.6 us (18%)
  starting transfers between devices  44 us (11%)
  matrix products  29.1 us (8%)
  between operations  14.7 us (4%)
    unnamed x3, other arithmetic  56.4 us
    unnamed x33, local copies, waits for them, and re-layouts  35.9 us
    all_to_all x1, waiting for transfers between devices, on_device(): lax.all_to_all(keys_send, 'dp', split_axis=0, concat_axis=0, tiled=True)  30.8 us
    all_to_all x1, waiting for transfers between devices, on_device(): lax.all_to_all(grad_out, 'ctx', split_axis=2, concat_axis=1, tiled=True)  23.2 us
    all_to_all x1, waiting for transfers between devices, on_device(): lax.all_to_all(values_send, 'dp', split_axis=0, concat_axis=0, tiled=True)  21.7 us
    all_to_all x1, starting transfers between devices, on_device(): lax.all_to_all(grad_tokens[None], 'ctx', split_axis=1, concat_axis=2, til...  15.6 us
    transpose x1, local copies, waits for them, and re-layouts, on_device(): jnp.einsum('chqk,chqd->ckhd', attention_low, grad_blocks, preferred_eleme...  13.1 us
    mul x1, local copies, waits for them, and re-layouts, on_device(): jnp.einsum('chqk,chqd->ckhd', grad_low, query_blocks, preferred_element_t...  13.1 us
  transfers between devices with their start and end apart: 7, of which 4 were waited for; matrix products, arithmetic and copies ran while one was open for 42% of the time, Pallas kernels for 0%

commit v1 on v0

v1 whole, which is shorter than its diff:
```python
import functools
import math

import jax
import jax.numpy as jnp
from jax import lax
from jax.experimental import pallas as pl
from jax.experimental.pallas import tpu as pltpu
from jax.sharding import PartitionSpec as P

DH = 128
GROUP = 64
BF16 = jnp.bfloat16
F32 = jnp.float32
HBM = pl.BlockSpec(memory_space=pl.ANY)
VMEM = pl.BlockSpec(memory_space=pltpu.VMEM)
SMEM = pl.BlockSpec(memory_space=pltpu.SMEM)


def owner_tables(distinct_ids, owned_count, capacity, replicas):
    owners = distinct_ids // owned_count
    local_index = distinct_ids % owned_count
    marked = (owners[:, :, None] == jnp.arange(replicas)[None, None, :]).astype(jnp.int32)
    ranking = jnp.sum(jnp.cumsum(marked, axis=1) * marked, axis=2) - 1
    return (owners, local_index, ranking)


def pack_heads_body(parts, width, q_ref, g_ref, out_ref, sems):
    copies = []
    for j in range(parts):
        for i, ref in enumerate((q_ref, g_ref)):
            copy = pltpu.make_async_copy(
                ref.at[:, pl.ds(j * width, width)], out_ref.at[j, i], sems.at[j, i]
            )
            copy.start()
            copies.append(copy)
    for copy in copies:
        copy.wait()


def pack_heads(queries, grad_out, parts):
    tokens, features = queries.shape
    width = features // parts
    return pl.pallas_call(
        functools.partial(pack_heads_body, parts, width),
        out_shape=jax.ShapeDtypeStruct((parts, 2, tokens, width), BF16),
        in_specs=[HBM, HBM],
        out_specs=HBM,
        scratch_shapes=[pltpu.SemaphoreType.DMA((parts, 2))],
    )(queries, grad_out)


def join_heads_body(parts, width, in_ref, out_ref, sems):
    copies = []
    for j in range(parts):
        copy = pltpu.make_async_copy(
            in_ref.at[j], out_ref.at[:, pl.ds(j * width, width)], sems.at[j]
        )
        copy.start()
        copies.append(copy)
    for copy in copies:
        copy.wait()


def join_heads(blocks):
    parts, tokens, width = blocks.shape
    return pl.pallas_call(
        functools.partial(join_heads_body, parts, width),
        out_shape=jax.ShapeDtypeStruct((tokens, parts * width), BF16),
        in_specs=[HBM],
        out_specs=HBM,
        scratch_shapes=[pltpu.SemaphoreType.DMA((parts,))],
    )(blocks)


def matmul(a, b, contract):
    return lax.dot_general(a, b, ((contract[:1], contract[1:]), ((), ())), preferred_element_type=F32)


def block_diagonal(rows):
    zero = jnp.zeros((rows.shape[0], DH), BF16)
    return jnp.concatenate(
        [
            jnp.concatenate([rows[:, :DH], zero], axis=1),
            jnp.concatenate([zero, rows[:, DH:]], axis=1),
        ],
        axis=0,
    )


def attend_body(
    groups, distinct, unroll, refs_ref, rows_ref, tokens_ref, pool_ref, gq_ref, send_ref,
    keys, values, key_sum, value_sum, query_last, grad_last, held, sems,
):
    scale = 1.0 / math.sqrt(DH)
    owned = pool_ref.shape[0] // (tokens_ref.shape[0] * 2)
    copies = []
    for j in range(distinct):
        for i, ref in enumerate((keys, values)):
            copies.append(
                pltpu.make_async_copy(pool_ref.at[rows_ref[0, j] + i * owned], ref.at[j], sems.at[j, i])
            )
    for copy in copies:
        copy.start()
    key_sum[...] = jnp.zeros_like(key_sum)
    value_sum[...] = jnp.zeros_like(value_sum)
    send_ref[...] = jnp.zeros_like(send_ref)
    width = gq_ref.shape[2]
    row = lax.broadcasted_iota(jnp.int32, (GROUP, width), 0)

    def rolled(kind, block):
        part = tokens_ref[block // 2, kind, pl.ds((block % 2) * GROUP, GROUP), :]
        return pltpu.roll(part.astype(F32), 1, 0)

    held[...] = jnp.zeros_like(held)
    query_last[...] = rolled(0, 0)
    grad_last[...] = rolled(1, 0)
    for copy in copies:
        copy.wait()

    def shifted(kind, group, last):
        following = rolled(kind, jnp.minimum(group + 1, groups - 1))
        following = jnp.where(group + 1 < groups, following, 0.0)
        block = jnp.where(row == 0, last[...], following)
        last[...] = following
        return block_diagonal(block.astype(BF16))

    def step(group):
        query = shifted(0, group, query_last)
        grad = shifted(1, group, grad_last)
        pair = (refs_ref[0, 2 * group], refs_ref[0, 2 * group + 1])
        block_keys = [keys[j] for j in pair]
        scores = [matmul(k, query, (1, 1)) for k in block_keys]
        grads = [matmul(values[j], grad, (1, 1)) for j in pair]
        top = jnp.maximum(*[jnp.max(s, axis=0, keepdims=True) for s in scores])
        weights = [jnp.exp((s - top) * scale) for s in scores]
        total = sum(jnp.sum(w, axis=0, keepdims=True) for w in weights)
        inverse = 1.0 / total
        weights = [w * inverse for w in weights]
        dots = sum(jnp.sum(w * g, axis=0, keepdims=True) for w, g in zip(weights, grads))
        grad_low = [(w * (g - dots)).astype(BF16) for w, g in zip(weights, grads)]
        weights_low = [w.astype(BF16) for w in weights]
        for j, w, g in zip(pair, weights_low, grad_low):
            value_sum[j] += matmul(w, grad, (1, 0))
            key_sum[j] += matmul(g, query, (1, 0))
        both = sum(matmul(g, k, (0, 0)) for g, k in zip(grad_low, block_keys)) * scale
        back = jnp.concatenate([both[:GROUP, :DH], both[GROUP:, DH:]], axis=1)
        back = pltpu.roll(back, GROUP - 1, 0)
        gq_ref[group // 2, pl.ds((group % 2) * GROUP, GROUP), :] = jnp.where(
            row == GROUP - 1, back, held[...]
        ).astype(BF16)
        held[...] = back

    def steps(index, carry):
        for u in range(unroll):
            step(index * unroll + u)
        return carry

    lax.fori_loop(0, groups // unroll, steps, 0)
    for j in range(distinct):
        send_ref[rows_ref[1, j]] = (key_sum[j] * scale).astype(BF16)
        send_ref[rows_ref[1, j] + rows_ref[2, 0]] = value_sum[j].astype(BF16)


def attend(slots, rows, tokens, pool, groups, distinct, send_rows):
    parts, _, part_tokens, width = tokens.shape
    nbr = pool.shape[1]
    return pl.pallas_call(
        functools.partial(attend_body, groups, distinct, 2),
        out_shape=(
            jax.ShapeDtypeStruct((parts, part_tokens, width), BF16),
            jax.ShapeDtypeStruct((send_rows, nbr, width), BF16),
        ),
        in_specs=[SMEM, SMEM, VMEM, HBM],
        out_specs=(VMEM, VMEM),
        scratch_shapes=[
            pltpu.VMEM((distinct, nbr, width), BF16),
            pltpu.VMEM((distinct, nbr, width), BF16),
            pltpu.VMEM((distinct, nbr, width), F32),
            pltpu.VMEM((distinct, nbr, width), F32),
            pltpu.VMEM((GROUP, width), F32),
            pltpu.VMEM((GROUP, width), F32),
            pltpu.VMEM((GROUP, width), F32),
            pltpu.SemaphoreType.DMA((distinct, 2)),
        ],
        compiler_params=pltpu.CompilerParams(vmem_limit_bytes=48 * 1024 * 1024),
    )(slots, rows, tokens, pool)


def collect_body(senders, capacity, local_ref, valid_ref, in_ref, keys_ref, values_ref, sums):
    sums[...] = jnp.zeros_like(sums)

    def step(r, carry):
        for k in range(capacity):
            slot = r * capacity + k

            @pl.when(valid_ref[0, slot] > 0)
            def _():
                n = local_ref[0, slot]
                sums[0, n] += in_ref[r, k].astype(F32)
                sums[1, n] += in_ref[r, capacity + k].astype(F32)

        return carry

    lax.fori_loop(0, senders, step, 0)
    keys_ref[...] = sums[0].astype(BF16)
    values_ref[...] = sums[1].astype(BF16)


def collect(local, valid, arrived, owned):
    senders, twice, nbr, width = arrived.shape
    out = jax.ShapeDtypeStruct((owned, nbr, width), BF16)
    return pl.pallas_call(
        functools.partial(collect_body, senders, twice // 2),
        out_shape=(out, out),
        in_specs=[SMEM, SMEM, VMEM],
        out_specs=(VMEM, VMEM),
        scratch_shapes=[pltpu.VMEM((2, owned, nbr, width), F32)],
        compiler_params=pltpu.CompilerParams(vmem_limit_bytes=32 * 1024 * 1024),
    )(local[None], valid[None], arrived)


def on_device(queries, grad_out, neighbour_keys, neighbour_values, distinct_ids, group_refs):
    replicas = lax.axis_size("dp")
    parts = lax.axis_size("ctx")
    me = lax.axis_index("dp")
    owned, nbr, width = neighbour_keys.shape
    capacity = owned // 2
    distinct = distinct_ids.shape[1]
    groups = group_refs.shape[1]
    owners, local_index, ranking = owner_tables(distinct_ids, owned, capacity, replicas)
    pick = lambda table: lax.dynamic_index_in_dim(table, me, 0, keepdims=False)
    slots = pick(group_refs).reshape(1, -1)
    pool_row = pick(owners) * 2 * owned + pick(local_index)
    send_row = pick(owners) * 2 * capacity + pick(ranking)
    rows = jnp.stack([pool_row, send_row, jnp.full_like(send_row, capacity)])
    matches = (
        (owners[:, :, None] == me)
        & (ranking[:, :, None] == jnp.arange(capacity)[None, None, :])
    ).astype(jnp.int32)
    arrive_local = jnp.sum(matches * local_index[:, :, None], axis=1).reshape(-1)
    arrive_valid = jnp.sum(matches, axis=1).reshape(-1)

    pool = lax.all_gather(
        jnp.concatenate([neighbour_keys, neighbour_values], axis=0), "dp", axis=0, tiled=True
    )
    packed = pack_heads(queries[0], grad_out[0], parts)
    tokens = lax.all_to_all(packed, "ctx", split_axis=0, concat_axis=0, tiled=True)
    back, send = attend(slots, rows, tokens, pool, groups, distinct, replicas * 2 * capacity)
    back = lax.all_to_all(back, "ctx", split_axis=0, concat_axis=0, tiled=True)
    arrived = lax.all_to_all(
        send.reshape(replicas, 2 * capacity, nbr, width), "dp", split_axis=0, concat_axis=0, tiled=True
    )
    grad_keys, grad_values = collect(arrive_local, arrive_valid, arrived, owned)
    return (join_heads(back)[None], grad_keys, grad_values)


def solution(mesh):
    return jax.shard_map(
        on_device,
        mesh=mesh,
        in_specs=(
            P("dp", "ctx", None),
            P("dp", "ctx", None),
            P("dp", None, "ctx"),
            P("dp", None, "ctx"),
            P(),
            P(),
        ),
        out_specs=(P("dp", "ctx", None), P("dp", None, "ctx"), P("dp", None, "ctx")),
        check_vma=False,
    )
```

time: 385 us -> 268 us (0.70)
  local copies, waits for them, and re-layouts: 137 us -> 0.79 us
  Pallas kernels: 0 us -> 121 us
  other arithmetic: 70.6 us -> 2.57 us
  blocking collectives: 0 us -> 31.9 us
  matrix products: 29.1 us -> 0 us
  starting transfers between devices: 44 us -> 16 us
    pallas_call x0 -> x4, Pallas kernels: none -> 121 us  [the longest x1 64.9 us: pack_heads(): pl.pallas_call(functools.partial(pack_heads_body, parts, width), out_shap...]
    unnamed x3 -> x0, other arithmetic: 56.4 us -> none
    reshape x7 -> x1, local copies, waits for them, and re-layouts: 38.4 us -> 0.11 us  [on_device(): slots = pick(group_refs).reshape(1, -1)]
    unnamed x33 -> x4, local copies, waits for them, and re-layouts: 35.9 us -> 0.02 us
    all_to_all x0 -> x1, blocking collectives: none -> 31.9 us  [on_device(): back = lax.all_to_all(back, 'ctx', split_axis=0, concat_axis=0, tiled=True)]
    dot_general x9 -> x0, matrix products: 29.1 us -> none  [the longest x1 6.21 us: on_device(): jnp.dot(selector, value_slots.reshape(slot_count, -1), precision=lax.Prec...]
    all_to_all x5 -> x2, starting transfers between devices: 43.9 us -> 16 us  [the longest x1 8.58 us: on_device(): lax.all_to_all(packed, 'ctx', split_axis=0, concat_axis=0, tiled=True)]
    gather x6 -> x0, local copies, waits for them, and re-layouts: 19.7 us -> none  [the longest x1 3.86 us: on_device(): distinct_keys = jnp.take(pool_keys, own_list, axis=0)]
  transfers between devices with their start and end apart: 7 -> 3, of which waited for: 4 -> 2; matrix products, arithmetic and copies ran while one was open for 42% -> 1% of each run, Pallas kernels for 0% -> 37%
where the time goes in v1:
time: 268 us; the launch traced here: 265 us
  Pallas kernels  121 us (45%)
  waiting for transfers between devices  78.2 us (29%)
  blocking collectives  31.9 us (12%)
  starting transfers between devices  16 us (6%)
  between operations  14.1 us (5%)
    pallas_call x1, Pallas kernels, pack_heads(): pl.pallas_call(functools.partial(pack_heads_body, parts, width), out_shap...  64.9 us
    all_to_all x1, waiting for transfers between devices, on_device(): lax.all_to_all(packed, 'ctx', split_axis=0, concat_axis=0, tiled=True)  48.2 us
    pallas_call x1, Pallas kernels, join_heads(): pl.pallas_call(functools.partial(join_heads_body, parts, width), out_shap...  33 us
    all_to_all x1, blocking collectives, on_device(): back = lax.all_to_all(back, 'ctx', split_axis=0, concat_axis=0, tiled=True)  31.9 us
    all_to_all x1, waiting for transfers between devices, on_device(): lax.all_to_all(send.reshape(replicas, 2 * capacity, nbr, width), 'dp', sp...  30 us
    pallas_call x1, Pallas kernels, attend(): pl.pallas_call(functools.partial(attend_body, groups, distinct, 2), out_s...  19.2 us
    all_to_all x1, starting transfers between devices, on_device(): lax.all_to_all(packed, 'ctx', split_axis=0, concat_axis=0, tiled=True)  8.58 us
    all_to_all x1, starting transfers between devices, on_device(): lax.all_to_all(send.reshape(replicas, 2 * capacity, nbr, width), 'dp', sp...  7.39 us
  transfers between devices with their start and end apart: 3, of which 2 were waited for; matrix products, arithmetic and copies ran while one was open for 1% of the time, Pallas kernels for 37%

profile of v1, /device:TPU:8, one launch (start us, length us, event | category | flops | bytes accessed | tf_op | source)
XLA Modules:
  0.0 264.5 jit_solution(4531747526018567216)
XLA Ops:
  7.2 0.0 copy-start
  7.2 0.0 all-gather.2.cloned.1.call-start
  7.2 1.9 pad_maximum_fusion
  9.1 0.0 all-gather.2.cloned.1.call-update
  9.1 0.0 copy-start.1
  9.1 64.9 %shard_map.85 = bf16[16,2,128,256]{3,2,1,0:T(8,128)(2,1)} custom-call(bf16[128,4096]{1,0:T(8,128)(2,1)} %bitcast.7, bf16[128,4096]{1,0:T(8,128)(2,1)} %bitcast.8), custom_call_target="tpu_custom_call" | custom-call | tf_op jit(solution)/shard_map/pallas_call | solution.py:44
  74.1 8.6 %all-to-all-start = ((bf16[16,2,128,256]{3,2,1,0:T(8,128)(2,1)}), bf16[16,2,128,256]{3,2,1,0:T(8,128)(2,1)S(1)}, u32[]{:S(2)}, u32[]{:S(2)}) async-start(bf16[16,2,128,256]{3,2,1,0:T(8,128)(2,1)} %shard_map.85), calls=%async_computation | async-start | bytes 4194304 | tf_op jit(solution)/shard_map/all_to_all | solution.py:248
  82.7 0.1 pad.4.clone
  82.7 0.0 copy-done.1
  82.7 0.1 copy.17
  82.8 0.5 fusion.7
  83.3 0.1 copy.18
  83.3 0.0 copy-done
  83.3 0.1 copy.16
  83.4 0.1 reshape.20.refs_ref
  83.6 0.1 add_add_fusion.rows_ref
  83.7 48.2 %all-to-all-done.tokens_ref = bf16[16,2,128,256]{3,2,1,0:T(8,128)(2,1)S(1)} async-done(((bf16[16,2,128,256]{3,2,1,0:T(8,128)(2,1)}), bf16[16,2,128,256]{3,2,1,0:T(8,128)(2,1)S(1)}, u32[]{:S(2)}, u32[]{:S(2)}) %all-to-all-start) | async-done | bytes 2097184 | tf_op jit(solution)/shard_map/all_to_all | solution.py:248
  131.8 0.0 all-gather.2.cloned.1.call-done.pool_ref
  131.8 19.2 %shard_map.86 = (bf16[16,128,256]{2,1,0:T(8,128)(2,1)S(1)}, bf16[64,128,256]{2,1,0:T(8,128)(2,1)}) custom-call(s32[1,64]{1,0:T(1,128)S(1)} %reshape.20.refs_ref, s32[3,16]{1,0:T(4,128)S(1)} %add_add_fusion.rows_ref, bf16[16,2,128,256]{3,2,1,0:T(8,128)(2,1)S(1)} %all-to-all-done.tokens_ref, bf16[128,128,256]{2,1,0:T(8,128)(2,1)} %all-gather.2.cloned.1.call-done.pool_ref), custom_call_target="tpu_custom_call" | custom-call | tf_op jit(solution)/shard_map/pallas_call | solution.py:168
  151.1 31.9 %all_to_all.15.in_ref = bf16[16,128,256]{2,1,0:T(8,128)(2,1)} all-to-all(bf16[16,128,256]{2,1,0:T(8,128)(2,1)S(1)} %get-tuple-element.7), channel_id=1, replica_groups=mesh['ctx'=16,'dp'=16] {'ctx'}, dimensions={0} | all-to-all | bytes 2097152 | tf_op jit(solution)/shard_map/all_to_all | solution.py:250
  183.0 7.4 %all-to-all-start.2 = ((bf16[16,4,128,256]{3,2,1,0:T(8,128)(2,1)}), bf16[16,4,128,256]{3,2,1,0:T(8,128)(2,1)}, u32[]{:S(2)}, u32[]{:S(2)}) async-start(bf16[16,4,128,256]{3,2,1,0:T(8,128)(2,1)} %bitcast.5), calls=%async_computation.2 | async-start | bytes 8388608 | tf_op jit(solution)/shard_map/all_to_all | solution.py:251
  190.4 0.1 convert_reduce_fusion
  190.5 0.1 copy.20
  190.6 0.1 broadcast_in_dim_reshape.7.valid_ref
  190.7 0.1 copy.19
  190.8 0.1 broadcast_in_dim_reshape.6.local_ref
  190.9 33.0 %shard_map.87 = bf16[128,4096]{1,0:T(8,128)(2,1)} custom-call(bf16[16,128,256]{2,1,0:T(8,128)(2,1)} %all_to_all.15.in_ref), custom_call_target="tpu_custom_call" | custom-call | tf_op jit(solution)/shard_map/pallas_call | solution.py:67
  223.9 30.0 %all-to-all-done.2.in_ref = bf16[16,4,128,256]{3,2,1,0:T(8,128)(2,1)} async-done(((bf16[16,4,128,256]{3,2,1,0:T(8,128)(2,1)}), bf16[16,4,128,256]{3,2,1,0:T(8,128)(2,1)}, u32[]{:S(2)}, u32[]{:S(2)}) %all-to-all-start.2) | async-done | bytes 4194336 | tf_op jit(solution)/shard_map/all_to_all | solution.py:251
  253.9 3.8 %shard_map.88 = (bf16[4,128,256]{2,1,0:T(8,128)(2,1)}, bf16[4,128,256]{2,1,0:T(8,128)(2,1)}) custom-call(s32[1,32]{1,0:T(1,128)S(1)} %broadcast_in_dim_reshape.6.local_ref, s32[1,32]{1,0:T(1,128)S(1)} %broadcast_in_dim_reshape.7.valid_ref, bf16[16,4,128,256]{3,2,1,0:T(8,128)(2,1)} %all-to-all-done.2.in_ref), custom_call_target="tpu_custom_call" | custom-call | tf_op jit(solution)/shard_map/pallas_call | solution.py:213
  (4 shorter events, 0.0 us)
Async XLA Ops:
  7.2 76.2 %copy-start = (s32[16,32,2]{1,2,0:T(2,128)S(1)}, s32[16,32,2]{1,2,0:T(2,128)}, u32[]{:S(2)}) copy-start(s32[16,32,2]{1,2,0:T(2,128)} %param.11) | copy-start | bytes 12292
  7.2 124.6 %all-gather.2.cloned.1.call-start = ((), (), s32[]{:S(2)}) async-start(), calls=%async_computation.3 | async-start | bytes 8912896 | tf_op jit(solution)/shard_map/all_gather | solution.py:244
  9.1 73.6 %copy-start.1 = (s32[16,16]{1,0:T(8,128)S(1)}, s32[16,16]{1,0:T(8,128)}, u32[]{:S(2)}) copy-start(s32[16,16]{1,0:T(8,128)} %param.10) | copy-start | bytes 3076
  74.1 57.8 %all-to-all-start = ((bf16[16,2,128,256]{3,2,1,0:T(8,128)(2,1)}), bf16[16,2,128,256]{3,2,1,0:T(8,128)(2,1)S(1)}, u32[]{:S(2)}, u32[]{:S(2)}) async-start(bf16[16,2,128,256]{3,2,1,0:T(8,128)(2,1)} %shard_map.85), calls=%async_computation | async-start | bytes 4194304 | tf_op jit(solution)/shard_map/all_to_all | solution.py:248
  183.0 70.9 %all-to-all-start.2 = ((bf16[16,4,128,256]{3,2,1,0:T(8,128)(2,1)}), bf16[16,4,128,256]{3,2,1,0:T(8,128)(2,1)}, u32[]{:S(2)}, u32[]{:S(2)}) async-start(bf16[16,4,128,256]{3,2,1,0:T(8,128)(2,1)} %bitcast.5), calls=%async_computation.2 | async-start | bytes 8388608 | tf_op jit(solution)/shard_map/all_to_all | solution.py:251
Sparse Core Ops, SparseCore 0:
  11.0 78.5 all-gather.1

commit v2 on v1

--- a/solution.py
+++ b/solution.py
@@ -25,51 +25,42 @@
     return (owners, local_index, ranking)
 
 
-def pack_heads_body(parts, width, q_ref, g_ref, out_ref, sems):
-    copies = []
-    for j in range(parts):
-        for i, ref in enumerate((q_ref, g_ref)):
-            copy = pltpu.make_async_copy(
-                ref.at[:, pl.ds(j * width, width)], out_ref.at[j, i], sems.at[j, i]
-            )
-            copy.start()
-            copies.append(copy)
-    for copy in copies:
-        copy.wait()
+def pack_heads_body(width, q_ref, g_ref, out_ref):
+    for j in range(out_ref.shape[0]):
+        out_ref[j, 0] = q_ref[:, j * width : (j + 1) * width]
+        out_ref[j, 1] = g_ref[:, j * width : (j + 1) * width]
 
 
 def pack_heads(queries, grad_out, parts):
     tokens, features = queries.shape
     width = features // parts
-    return pl.pallas_call(
-        functools.partial(pack_heads_body, parts, width),
+    steps = 4
+    per_step = parts // steps
+    block = pl.BlockSpec((tokens, per_step * width), lambda i: (0, i))
+    return pl.pallas_call(
+        functools.partial(pack_heads_body, width),
+        grid=(steps,),
         out_shape=jax.ShapeDtypeStruct((parts, 2, tokens, width), BF16),
-        in_specs=[HBM, HBM],
-        out_specs=HBM,
-        scratch_shapes=[pltpu.SemaphoreType.DMA((parts, 2))],
+        in_specs=[block, block],
+        out_specs=pl.BlockSpec((per_step, 2, tokens, width), lambda i: (i, 0, 0, 0)),
     )(queries, grad_out)
 
 
-def join_heads_body(parts, width, in_ref, out_ref, sems):
-    copies = []
-    for j in range(parts):
-        copy = pltpu.make_async_copy(
-            in_ref.at[j], out_ref.at[:, pl.ds(j * width, width)], sems.at[j]
-        )
-        copy.start()
-        copies.append(copy)
-    for copy in copies:
-        copy.wait()
+def join_heads_body(width, in_ref, out_ref):
+    for j in range(in_ref.shape[0]):
+        out_ref[:, j * width : (j + 1) * width] = in_ref[j]
 
 
 def join_heads(blocks):
     parts, tokens, width = blocks.shape
-    return pl.pallas_call(
-        functools.partial(join_heads_body, parts, width),
+    steps = 4
+    per_step = parts // steps
+    return pl.pallas_call(
+        functools.partial(join_heads_body, width),
+        grid=(steps,),
         out_shape=jax.ShapeDtypeStruct((tokens, parts * width), BF16),
-        in_specs=[HBM],
-        out_specs=HBM,
-        scratch_shapes=[pltpu.SemaphoreType.DMA((parts,))],
+        in_specs=[pl.BlockSpec((per_step, tokens, width), lambda i: (i, 0, 0))],
+        out_specs=pl.BlockSpec((tokens, per_step * width), lambda i: (0, i)),
     )(blocks)
 
 

time: 268 us -> 227 us (0.85)
  Pallas kernels: 121 us -> 30.2 us
  waiting for transfers between devices: 78.2 us -> 127 us
    pallas_call x2, Pallas kernels: 97.9 us -> 7.17 us  [the longest x1 3.79 us: pack_heads(): pl.pallas_call(functools.partial(pack_heads_body, width), grid=(steps,),...]
    all_to_all x1, waiting for transfers between devices: 30 us -> 59.6 us  [on_device(): lax.all_to_all(send.reshape(replicas, 2 * capacity, nbr, width), 'dp', sp...]
    all_gather x1, waiting for transfers between devices: 0.01 us -> 19 us  [on_device(): lax.all_gather(jnp.concatenate([neighbour_keys, neighbour_values], axis=0...]
  transfers between devices with their start and end apart: 3 -> 3, of which waited for: 2 -> 3; matrix products, arithmetic and copies ran while one was open for 1% -> 1% of each run, Pallas kernels for 37% -> 3%
where the time goes in v2:
time: 227 us; the launch traced here: 223 us
  waiting for transfers between devices  127 us (56%)
  blocking collectives  34.3 us (15%)
  Pallas kernels  30.2 us (13%)
  starting transfers between devices  14.4 us (6%)
  between operations  14.1 us (6%)
  other arithmetic  2.57 us (1%)
    all_to_all x1, waiting for transfers between devices, on_device(): lax.all_to_all(send.reshape(replicas, 2 * capacity, nbr, width), 'dp', sp...  59.6 us
    all_to_all x1, waiting for transfers between devices, on_device(): lax.all_to_all(packed, 'ctx', split_axis=0, concat_axis=0, tiled=True)  48.2 us
    all_to_all x1, blocking collectives, on_device(): back = lax.all_to_all(back, 'ctx', split_axis=0, concat_axis=0, tiled=True)  34.3 us
    pallas_call x1, Pallas kernels, attend(): pl.pallas_call(functools.partial(attend_body, groups, distinct, 2), out_s...  19.2 us
    all_gather x1, waiting for transfers between devices, on_device(): lax.all_gather(jnp.concatenate([neighbour_keys, neighbour_values], axis=0...  19 us
    all_to_all x1, starting transfers between devices, on_device(): lax.all_to_all(packed, 'ctx', split_axis=0, concat_axis=0, tiled=True)  8.57 us
    all_to_all x1, starting transfers between devices, on_device(): lax.all_to_all(send.reshape(replicas, 2 * capacity, nbr, width), 'dp', sp...  5.76 us
  transfers between devices with their start and end apart: 3, of which 3 were waited for; matrix products, arithmetic and copies ran while one was open for 1% of the time, Pallas kernels for 3%

profile of v2, /device:TPU:8, one launch (start us, length us, event | category | flops | bytes accessed | tf_op | source)
XLA Modules:
  0.0 223.1 jit_solution(8885064382683289999)
XLA Ops:
  7.2 0.0 copy-start
  7.2 0.0 all-gather.2.cloned.1.call-start
  7.2 1.9 pad_maximum_fusion
  9.1 0.0 all-gather.2.cloned.1.call-update
  9.1 0.0 copy-start.1
  9.1 3.8 %shard_map.85 = bf16[16,2,128,256]{3,2,1,0:T(8,128)(2,1)} custom-call(bf16[128,4096]{1,0:T(8,128)(2,1)} %bitcast.7, bf16[128,4096]{1,0:T(8,128)(2,1)} %bitcast.8), custom_call_target="tpu_custom_call" | custom-call | tf_op jit(solution)/shard_map/pallas_call | solution.py:40
  12.9 8.6 %all-to-all-start = ((bf16[16,2,128,256]{3,2,1,0:T(8,128)(2,1)}), bf16[16,2,128,256]{3,2,1,0:T(8,128)(2,1)S(1)}, u32[]{:S(2)}, u32[]{:S(2)}) async-start(bf16[16,2,128,256]{3,2,1,0:T(8,128)(2,1)} %shard_map.85), calls=%async_computation | async-start | bytes 4194304 | tf_op jit(solution)/shard_map/all_to_all | solution.py:239
  21.5 0.1 pad.4.clone
  21.6 0.0 copy-done.1
  21.6 0.1 copy.17
  21.7 0.5 fusion.7
  22.1 0.1 copy.18
  22.2 0.0 copy-done
  22.2 0.1 copy.16
  22.3 0.1 reshape.20.refs_ref
  22.4 0.1 add_add_fusion.rows_ref
  22.5 48.2 %all-to-all-done.tokens_ref = bf16[16,2,128,256]{3,2,1,0:T(8,128)(2,1)S(1)} async-done(((bf16[16,2,128,256]{3,2,1,0:T(8,128)(2,1)}), bf16[16,2,128,256]{3,2,1,0:T(8,128)(2,1)S(1)}, u32[]{:S(2)}, u32[]{:S(2)}) %all-to-all-start) | async-done | bytes 2097184 | tf_op jit(solution)/shard_map/all_to_all | solution.py:239
  70.7 19.0 %all-gather.2.cloned.1.call-done.pool_ref = bf16[128,128,256]{2,1,0:T(8,128)(2,1)} async-done(((bf16[8,128,256]{2,1,0:T(8,128)(2,1)}), bf16[128,128,256]{2,1,0:T(8,128)(2,1)}) %all-gather.2.cloned.1.call-update) | async-done | bytes 8388624 | tf_op jit(solution)/shard_map/all_gather | solution.py:235
  89.6 19.2 %shard_map.86 = (bf16[16,128,256]{2,1,0:T(8,128)(2,1)S(1)}, bf16[64,128,256]{2,1,0:T(8,128)(2,1)}) custom-call(s32[1,64]{1,0:T(1,128)S(1)} %reshape.20.refs_ref, s32[3,16]{1,0:T(4,128)S(1)} %add_add_fusion.rows_ref, bf16[16,2,128,256]{3,2,1,0:T(8,128)(2,1)S(1)} %all-to-all-done.tokens_ref, bf16[128,128,256]{2,1,0:T(8,128)(2,1)} %all-gather.2.cloned.1.call-done.pool_ref), custom_call_target="tpu_custom_call" | custom-call | tf_op jit(solution)/shard_map/pallas_call | solution.py:159
  108.9 34.3 %all_to_all.15.in_ref = bf16[16,128,256]{2,1,0:T(8,128)(2,1)} all-to-all(bf16[16,128,256]{2,1,0:T(8,128)(2,1)S(1)} %get-tuple-element.7), channel_id=1, replica_groups=mesh['ctx'=16,'dp'=16] {'ctx'}, dimensions={0} | all-to-all | bytes 2097152 | tf_op jit(solution)/shard_map/all_to_all | solution.py:241
  143.2 5.8 %all-to-all-start.2 = ((bf16[16,4,128,256]{3,2,1,0:T(8,128)(2,1)}), bf16[16,4,128,256]{3,2,1,0:T(8,128)(2,1)}, u32[]{:S(2)}, u32[]{:S(2)}) async-start(bf16[16,4,128,256]{3,2,1,0:T(8,128)(2,1)} %bitcast.5), calls=%async_computation.2 | async-start | bytes 8388608 | tf_op jit(solution)/shard_map/all_to_all | solution.py:242
  148.9 0.1 convert_reduce_fusion
  149.1 0.1 copy.20
  149.2 0.1 broadcast_in_dim_reshape.7.valid_ref
  149.2 0.1 copy.19
  149.3 0.1 broadcast_in_dim_reshape.6.local_ref
  149.4 3.4 %shard_map.87 = bf16[128,4096]{1,0:T(8,128)(2,1)} custom-call(bf16[16,128,256]{2,1,0:T(8,128)(2,1)} %all_to_all.15.in_ref), custom_call_target="tpu_custom_call" | custom-call | tf_op jit(solution)/shard_map/pallas_call | solution.py:58
  152.8 59.6 %all-to-all-done.2.in_ref = bf16[16,4,128,256]{3,2,1,0:T(8,128)(2,1)} async-done(((bf16[16,4,128,256]{3,2,1,0:T(8,128)(2,1)}), bf16[16,4,128,256]{3,2,1,0:T(8,128)(2,1)}, u32[]{:S(2)}, u32[]{:S(2)}) %all-to-all-start.2) | async-done | bytes 4194336 | tf_op jit(solution)/shard_map/all_to_all | solution.py:242
  212.4 3.8 %shard_map.88 = (bf16[4,128,256]{2,1,0:T(8,128)(2,1)}, bf16[4,128,256]{2,1,0:T(8,128)(2,1)}) custom-call(s32[1,32]{1,0:T(1,128)S(1)} %broadcast_in_dim_reshape.6.local_ref, s32[1,32]{1,0:T(1,128)S(1)} %broadcast_in_dim_reshape.7.valid_ref, bf16[16,4,128,256]{3,2,1,0:T(8,128)(2,1)} %all-to-all-done.2.in_ref), custom_call_target="tpu_custom_call" | custom-call | tf_op jit(solution)/shard_map/pallas_call | solution.py:204
  (4 shorter events, 0.0 us)
Async XLA Ops:
  7.2 15.0 %copy-start = (s32[16,32,2]{1,2,0:T(2,128)S(1)}, s32[16,32,2]{1,2,0:T(2,128)}, u32[]{:S(2)}) copy-start(s32[16,32,2]{1,2,0:T(2,128)} %param.11) | copy-start | bytes 12292
  7.2 82.5 %all-gather.2.cloned.1.call-start = ((), (), s32[]{:S(2)}) async-start(), calls=%async_computation.3 | async-start | bytes 8912896 | tf_op jit(solution)/shard_map/all_gather | solution.py:235
  9.1 12.5 %copy-start.1 = (s32[16,16]{1,0:T(8,128)S(1)}, s32[16,16]{1,0:T(8,128)}, u32[]{:S(2)}) copy-start(s32[16,16]{1,0:T(8,128)} %param.10) | copy-start | bytes 3076
  12.9 57.8 %all-to-all-start = ((bf16[16,2,128,256]{3,2,1,0:T(8,128)(2,1)}), bf16[16,2,128,256]{3,2,1,0:T(8,128)(2,1)S(1)}, u32[]{:S(2)}, u32[]{:S(2)}) async-start(bf16[16,2,128,256]{3,2,1,0:T(8,128)(2,1)} %shard_map.85), calls=%async_computation | async-start | bytes 4194304 | tf_op jit(solution)/shard_map/all_to_all | solution.py:239
  143.2 69.2 %all-to-all-start.2 = ((bf16[16,4,128,256]{3,2,1,0:T(8,128)(2,1)}), bf16[16,4,128,256]{3,2,1,0:T(8,128)(2,1)}, u32[]{:S(2)}, u32[]{:S(2)}) async-start(bf16[16,4,128,256]{3,2,1,0:T(8,128)(2,1)} %bitcast.5), calls=%async_computation.2 | async-start | bytes 8388608 | tf_op jit(solution)/shard_map/all_to_all | solution.py:242
Sparse Core Ops, SparseCore 0:
  11.0 78.5 all-gather.1

commit v3 on v1

v3 whole, which is shorter than its diff:
```python
import functools
import math

import jax
import jax.numpy as jnp
from jax import lax
from jax.experimental import pallas as pl
from jax.experimental.pallas import tpu as pltpu
from jax.sharding import PartitionSpec as P

DH = 128
GROUP = 64
BF16 = jnp.bfloat16
F32 = jnp.float32
HBM = pl.BlockSpec(memory_space=pltpu.MemorySpace.HBM)
VMEM = pl.BlockSpec(memory_space=pltpu.VMEM)
SMEM = pl.BlockSpec(memory_space=pltpu.SMEM)
SELECT_VMEM = 10 * 1024 * 1024
SPREAD_VMEM = 8 * 1024 * 1024
ATTEND_VMEM = 20 * 1024 * 1024
COLLECT_VMEM = 8 * 1024 * 1024


SIDE = 4


def place(n, owned):
    owner = lax.div(n, owned)
    return (lax.div(owner, SIDE), lax.rem(owner, SIDE), lax.rem(n, owned))


def shift(value, axis, amount):
    pairs = []
    for y in range(SIDE):
        for x in range(SIDE):
            to = (y, (x + amount) % SIDE) if axis == "x" else ((y + amount) % SIDE, x)
            pairs.append((y * SIDE + x, to[0] * SIDE + to[1]))
    return lax.ppermute(value, "dp", pairs)


DISTANCES = (2, 1, 3)


def gather_lines(lines):
    parts = [[own, None, None, None] for own, _ in lines]
    for distance in DISTANCES:
        for part, (own, axis) in zip(parts, lines):
            part[distance] = shift(own, axis, -distance)
    return parts


def exchange_lines(lines):
    parts = [list(chunks) for chunks, _, _ in lines]
    for distance in DISTANCES:
        for part, (chunks, axis, sign) in zip(parts, lines):
            part[distance] = shift(chunks[distance], axis, sign * distance)
    return parts


def chunk_shapes(most, nbr, width, own_type=BF16):
    return tuple(
        jax.ShapeDtypeStruct((most, nbr, width), own_type if k == 0 else BF16) for k in range(SIDE)
    )


def pack_heads_body(parts, width, q_ref, g_ref, out_ref, sems):
    copies = []
    for i, ref in enumerate((q_ref, g_ref)):
        for j in range(parts):
            copies.append(
                pltpu.make_async_copy(
                    ref.at[:, pl.ds(j * width, width)], out_ref.at[j, i], sems.at[i, j]
                )
            )
    for copy in copies:
        copy.start()
    for copy in copies:
        copy.wait()


def pack_heads(queries, grad_out, parts):
    tokens, features = queries.shape
    width = features // parts
    return pl.pallas_call(
        functools.partial(pack_heads_body, parts, width),
        out_shape=jax.ShapeDtypeStruct((parts, 2, tokens, width), BF16),
        in_specs=[HBM, HBM],
        out_specs=VMEM,
        scratch_shapes=[pltpu.SemaphoreType.DMA((2, parts))],
    )(queries, grad_out)


def join_heads_body(parts, width, in_ref, out_ref, sems):
    copies = [
        pltpu.make_async_copy(in_ref.at[j], out_ref.at[:, pl.ds(j * width, width)], sems.at[j])
        for j in range(parts)
    ]
    for copy in copies:
        copy.start()
    for copy in copies:
        copy.wait()


def join_heads(blocks):
    parts, tokens, width = blocks.shape
    return pl.pallas_call(
        functools.partial(join_heads_body, parts, width),
        out_shape=jax.ShapeDtypeStruct((tokens, parts * width), BF16),
        in_specs=[VMEM],
        out_specs=HBM,
        scratch_shapes=[pltpu.SemaphoreType.DMA((parts,))],
    )(blocks)


def matmul(a, b, contract):
    return lax.dot_general(a, b, ((contract[:1], contract[1:]), ((), ())), preferred_element_type=F32)


def block_diagonal(rows):
    zero = jnp.zeros((rows.shape[0], DH), BF16)
    return jnp.concatenate(
        [
            jnp.concatenate([rows[:, :DH], zero], axis=1),
            jnp.concatenate([zero, rows[:, DH:]], axis=1),
        ],
        axis=0,
    )


def tables_body(owned, most, ids_ref, take_ref, add_ref):
    me = lax.axis_index("dp")
    mine = (lax.div(me, SIDE), lax.rem(me, SIDE))
    distinct = ids_ref.shape[1]
    for across in range(2):
        for n in range(SIDE * most):
            take_ref[across, n] = 0
        for n in range(SIDE * owned * SIDE):
            add_ref[across, n] = -1
        for k in range(SIDE):
            other = lax.rem(mine[across] + k, SIDE)
            replica = other * SIDE + mine[1] if across == 0 else mine[0] * SIDE + other

            def step(j, count):
                where = place(ids_ref[replica, j], owned)
                found = where[across] == mine[across]

                @pl.when(found)
                def _():
                    distance = lax.rem(where[1 - across] - mine[1 - across] + SIDE, SIDE)
                    row = distance * owned + where[2]
                    take_ref[across, k * most + count] = row
                    add_ref[across, row * SIDE + k] = count

                return count + found.astype(jnp.int32)

            lax.fori_loop(0, distinct, step, jnp.int32(0))


def tables(ids, owned, most):
    return pl.pallas_call(
        functools.partial(tables_body, owned, most),
        out_shape=(
            jax.ShapeDtypeStruct((2, SIDE * most), jnp.int32),
            jax.ShapeDtypeStruct((2, SIDE * owned * SIDE), jnp.int32),
        ),
        in_specs=[SMEM],
        out_specs=(SMEM, SMEM),
    )(ids)


def select_body(take_ref, *refs):
    lines, kept, sems = refs[16:18], refs[18:20], refs[20]
    copies = []
    for across in range(2):
        parts = refs[4 * across : 4 * across + 4]
        line = lines[across]
        owned = parts[0].shape[0]
        for k, part in enumerate(parts):
            for n in range(owned):
                line[k * owned + n] = part[n]
        own, *sent = refs[8 + 4 * across : 12 + 4 * across]
        most = own.shape[0]

        def pick(n, carry):
            kept[across][n] = line[take_ref[across, n]]
            for k, out in enumerate(sent):
                out[n] = line[take_ref[across, (k + 1) * most + n]]
            return carry

        lax.fori_loop(0, most, pick, 0, unroll=2)
        copies.append(pltpu.make_async_copy(kept[across], own, sems.at[across]))
        copies[-1].start()
    for copy in copies:
        copy.wait()


def select(take, keys, values, most):
    owned, nbr, width = keys[0].shape
    line = pltpu.VMEM((SIDE * owned, nbr, width), BF16)
    kept = pltpu.VMEM((most, nbr, width), BF16)
    shapes = chunk_shapes(most, nbr, width)
    out = pl.pallas_call(
        select_body,
        out_shape=((pltpu.HBM(shapes[0].shape, BF16),) + shapes[1:]) * 2,
        in_specs=[SMEM] + [VMEM] * 8,
        out_specs=((HBM,) + (VMEM,) * 3) * 2,
        scratch_shapes=[line, line, kept, kept, pltpu.SemaphoreType.DMA((2,))],
        compiler_params=pltpu.CompilerParams(vmem_limit_bytes=SELECT_VMEM),
    )(take, *keys, *values)
    return (out[:4], out[4:])


def spread_body(add_ref, *refs):
    for across in range(2):
        chunks = refs[4 * across : 4 * across + 4]
        outs = refs[8 + 4 * across : 12 + 4 * across]
        most, owned = chunks[0].shape[0], outs[0].shape[0]

        def add(n, carry):
            for distance, out in enumerate(outs):
                value = jnp.zeros(out.shape[1:], F32)
                for k, chunk in enumerate(chunks):
                    index = add_ref[across, (distance * owned + n) * SIDE + k]
                    term = chunk[jnp.clip(index, 0, most - 1)].astype(F32)
                    value += jnp.where(index >= 0, term, 0.0)
                out[n] = value.astype(out.dtype)
            return carry

        lax.fori_loop(0, owned, add, 0)


def spread(add, keys, values, owned):
    _, nbr, width = keys[0].shape
    out = pl.pallas_call(
        spread_body,
        out_shape=chunk_shapes(owned, nbr, width, F32) * 2,
        in_specs=[SMEM] + [VMEM] * 8,
        out_specs=(VMEM,) * 8,
        compiler_params=pltpu.CompilerParams(vmem_limit_bytes=SPREAD_VMEM),
    )(add, *keys, *values)
    return (out[:4], out[4:])


def attend_body(
    groups, distinct, owned, most, unroll, ids_ref, refs_ref, tokens_ref, *refs
):
    key_parts, value_parts = refs[:4], refs[4:8]
    gq_out, key_out, value_out = refs[8], refs[9:13], refs[13:17]
    (keys, values, key_sum, value_sum, gq_ref, key_send, value_send, query_last, grad_last, held,
     key_rows, value_rows, counts, in_sems, out_sems, gq_sem) = refs[17:]
    scale = 1.0 / math.sqrt(DH)
    copies = [
        pltpu.make_async_copy(part, pool.at[pl.ds(k * most, most)], in_sems.at[i, k])
        for i, (parts, pool) in enumerate(((key_parts, keys), (value_parts, values)))
        for k, part in enumerate(parts)
    ]
    for copy in copies:
        copy.start()

    def clear(j, carry):
        key_sum[j] = jnp.zeros(key_sum.shape[1:], F32)
        value_sum[j] = jnp.zeros(value_sum.shape[1:], F32)
        return carry

    lax.fori_loop(0, distinct, clear, 0)
    width = gq_ref.shape[2]
    row = lax.broadcasted_iota(jnp.int32, (GROUP, width), 0)
    me = lax.axis_index("dp")
    mine = (me // SIDE, me % SIDE)
    for i in range(2 * SIDE):
        counts[i] = 0

    def rank(j, carry):
        where = place(ids_ref[me, j], owned)
        for i, table in enumerate((key_rows, value_rows)):
            distance = (mine[i] - where[i] + SIDE) % SIDE
            count = counts[i * SIDE + distance]
            table[j] = distance * most + count
            counts[i * SIDE + distance] = count + 1
        return carry

    lax.fori_loop(0, distinct, rank, 0)

    def rolled(kind, block):
        part = tokens_ref[block // 2, kind, pl.ds((block % 2) * GROUP, GROUP), :]
        return pltpu.roll(part.astype(F32), 1, 0)

    held[...] = jnp.zeros_like(held)
    query_last[...] = rolled(0, 0)
    grad_last[...] = rolled(1, 0)
    for copy in copies:
        copy.wait()

    def shifted(kind, group, last):
        following = rolled(kind, jnp.minimum(group + 1, groups - 1))
        following = jnp.where(group + 1 < groups, following, 0.0)
        block = jnp.where(row == 0, last[...], following)
        last[...] = following
        return block_diagonal(block.astype(BF16))

    def step(group):
        query = shifted(0, group, query_last)
        grad = shifted(1, group, grad_last)
        pair = (refs_ref[me, 2 * group], refs_ref[me, 2 * group + 1])
        block_keys = [keys[key_rows[j]] for j in pair]
        scores = [matmul(k, query, (1, 1)) for k in block_keys]
        grads = [matmul(values[value_rows[j]], grad, (1, 1)) for j in pair]
        top = jnp.maximum(*[jnp.max(s, axis=0, keepdims=True) for s in scores])
        weights = [jnp.exp((s - top) * scale) for s in scores]
        total = sum(jnp.sum(w, axis=0, keepdims=True) for w in weights)
        inverse = 1.0 / total
        weights = [w * inverse for w in weights]
        dots = sum(jnp.sum(w * g, axis=0, keepdims=True) for w, g in zip(weights, grads))
        grad_low = [(w * (g - dots)).astype(BF16) for w, g in zip(weights, grads)]
        weights_low = [w.astype(BF16) for w in weights]
        for j, w, g in zip(pair, weights_low, grad_low):
            value_sum[j] += matmul(w, grad, (1, 0))
            key_sum[j] += matmul(g, query, (1, 0))
        both = sum(matmul(g, k, (0, 0)) for g, k in zip(grad_low, block_keys)) * scale
        back = jnp.concatenate([both[:GROUP, :DH], both[GROUP:, DH:]], axis=1)
        back = pltpu.roll(back, GROUP - 1, 0)
        gq_ref[group // 2, pl.ds((group % 2) * GROUP, GROUP), :] = jnp.where(
            row == GROUP - 1, back, held[...]
        ).astype(BF16)
        held[...] = back

    def steps(index, carry):
        for u in range(unroll):
            step(index * unroll + u)
        return carry

    lax.fori_loop(0, groups // unroll, steps, 0)

    copies = [pltpu.make_async_copy(gq_ref, gq_out, gq_sem)]
    copies[0].start()

    def give(j, carry):
        key_send[key_rows[j]] = (key_sum[j] * scale).astype(BF16)
        value_send[value_rows[j]] = value_sum[j].astype(BF16)
        return carry

    lax.fori_loop(0, distinct, give, 0, unroll=2)
    for i, (send, parts) in enumerate(((key_send, key_out), (value_send, value_out))):
        for k, part in enumerate(parts):
            copy = pltpu.make_async_copy(send.at[pl.ds(k * most, most)], part, out_sems.at[i, k])
            copy.start()
            copies.append(copy)
    for copy in copies:
        copy.wait()


def attend(ids, refs, tokens, keys, values, owned, most):
    parts, _, part_tokens, width = tokens.shape
    nbr = keys[0].shape[1]
    distinct = ids.shape[1]
    groups = refs.shape[1]
    flat = refs.reshape(refs.shape[0], -1)
    pool = pltpu.VMEM((SIDE * most, nbr, width), BF16)
    total = pltpu.VMEM((distinct, nbr, width), F32)
    rows = pltpu.VMEM((GROUP, width), F32)
    table = pltpu.SMEM((distinct,), jnp.int32)
    shapes = (jax.ShapeDtypeStruct((parts, part_tokens, width), BF16),) + chunk_shapes(
        most, nbr, width
    ) * 2
    constrain = lambda value: pltpu.with_memory_space_constraint(value, pltpu.MemorySpace.HBM)
    keys, values = jax.tree.map(constrain, (list(keys), list(values)))
    out = pl.pallas_call(
        functools.partial(attend_body, groups, distinct, owned, most, 2),
        out_shape=tuple(pltpu.HBM(shape.shape, shape.dtype) for shape in shapes),
        in_specs=[SMEM, SMEM, VMEM] + [HBM] * 8,
        out_specs=(HBM,) * 9,
        scratch_shapes=[pool, pool, total, total, pltpu.VMEM((parts, part_tokens, width), BF16),
                        pool, pool, rows, rows, rows, table, table,
                        pltpu.SMEM((2 * SIDE,), jnp.int32),
                        pltpu.SemaphoreType.DMA((2, SIDE)), pltpu.SemaphoreType.DMA((2, SIDE)),
                        pltpu.SemaphoreType.DMA],
        compiler_params=pltpu.CompilerParams(vmem_limit_bytes=ATTEND_VMEM),
    )(ids, flat, tokens, *keys, *values)
    return (out[0], out[1:5], out[5:])


def collect_body(*refs):
    for i, out in enumerate(refs[8:]):
        own, *others = refs[4 * i : 4 * i + 4]
        for n in range(own.shape[0]):
            value = own[n]
            for other in others:
                value += other[n].astype(F32)
            out[n] = value.astype(BF16)


def collect(keys, values):
    out = jax.ShapeDtypeStruct(keys[0].shape, BF16)
    return pl.pallas_call(
        collect_body,
        out_shape=(out, out),
        in_specs=[VMEM] * 8,
        out_specs=(VMEM, VMEM),
        compiler_params=pltpu.CompilerParams(vmem_limit_bytes=COLLECT_VMEM),
    )(*keys, *values)


def on_device(queries, grad_out, neighbour_keys, neighbour_values, distinct_ids, group_refs):
    parts = lax.axis_size("ctx")
    owned = neighbour_keys.shape[0]
    most = SIDE * (owned // 2)
    take, add = tables(distinct_ids, owned, most)
    lines = gather_lines(((neighbour_keys, "x"), (neighbour_values, "y")))
    packed = pack_heads(queries[0], grad_out[0], parts)
    tokens = lax.all_to_all(packed, "ctx", split_axis=0, concat_axis=0, tiled=True)
    keys, values = select(take, *lines, most)
    keys, values = exchange_lines(((keys, "y", 1), (values, "x", 1)))
    back, keys, values = attend(distinct_ids, group_refs, tokens, keys, values, owned, most)
    keys, values = exchange_lines(((keys, "y", -1), (values, "x", -1)))
    back = lax.all_to_all(back, "ctx", split_axis=0, concat_axis=0, tiled=True)
    keys, values = spread(add, keys, values, owned)
    keys, values = exchange_lines(((keys, "x", 1), (values, "y", 1)))
    grad_queries = join_heads(back)[None]
    grad_queries, keys, values = lax.optimization_barrier((grad_queries, keys, values))
    grad_keys, grad_values = collect(keys, values)
    return (grad_queries, grad_keys, grad_values)


def solution(mesh):
    return jax.shard_map(
        on_device,
        mesh=mesh,
        in_specs=(
            P("dp", "ctx", None),
            P("dp", "ctx", None),
            P("dp", None, "ctx"),
            P("dp", None, "ctx"),
            P(),
            P(),
        ),
        out_specs=(P("dp", "ctx", None), P("dp", None, "ctx"), P("dp", None, "ctx")),
        check_vma=False,
    )
```

time: 268 us -> 161 us (0.60); the launches traced: 265 us -> 160 us
  Pallas kernels: 121 us -> 37.5 us
  blocking collectives: 31.9 us -> 0 us
  starting transfers between devices: 16 us -> 46.6 us
  between operations: 14.1 us -> 0.87 us
  waiting for transfers between devices: 78.2 us -> 74.6 us
    ppermute x0 -> x24, waiting for transfers between devices: none -> 74.6 us  [shift(): return lax.ppermute(value, 'dp', pairs)]
    pallas_call x1, Pallas kernels: 64.9 us -> 3.18 us  [pack_heads(): pl.pallas_call(functools.partial(pack_heads_body, parts, width), out_shap...]
    all_to_all x1, waiting for transfers between devices: 48.2 us -> 0.01 us  [on_device(): lax.all_to_all(packed, 'ctx', split_axis=0, concat_axis=0, tiled=True)]
    all_to_all x1 -> x0, blocking collectives: 31.9 us -> none  [on_device(): back = lax.all_to_all(back, 'ctx', split_axis=0, concat_axis=0, tiled=True)]
    ppermute x0 -> x24, starting transfers between devices: none -> 30.8 us  [shift(): return lax.ppermute(value, 'dp', pairs)]
    pallas_call x1, Pallas kernels: 33 us -> 2.31 us  [join_heads(): pl.pallas_call(functools.partial(join_heads_body, parts, width), out_shap...]
    all_to_all x1, waiting for transfers between devices: 30 us -> 0.01 us  [on_device(): back = lax.all_to_all(back, 'ctx', split_axis=0, concat_axis=0, tiled=True)]
    pallas_call x2 -> x5, Pallas kernels: 23.1 us -> 32 us  [the longest x1 20.2 us: attend(): pl.pallas_call(functools.partial(attend_body, groups, distinct, owned, mo...]
  transfers between devices with their start and end apart: 3 -> 26, of which waited for: 2 -> 13; matrix products, arithmetic and copies ran while one was open for 1% -> 0% of each run, Pallas kernels for 37% -> 8%
where the time goes in v3:
time: 161 us; the launch traced here: 160 us
  waiting for transfers between devices  74.6 us (46%)
  starting transfers between devices  46.6 us (29%)
  Pallas kernels  37.5 us (23%)
    ppermute x24, waiting for transfers between devices, shift(): return lax.ppermute(value, 'dp', pairs)  74.6 us
    ppermute x24, starting transfers between devices, shift(): return lax.ppermute(value, 'dp', pairs)  30.8 us
    pallas_call x1, Pallas kernels, attend(): pl.pallas_call(functools.partial(attend_body, groups, distinct, owned, mo...  20.2 us
    all_to_all x1, starting transfers between devices, on_device(): lax.all_to_all(packed, 'ctx', split_axis=0, concat_axis=0, tiled=True)  8.71 us
    all_to_all x1, starting transfers between devices, on_device(): back = lax.all_to_all(back, 'ctx', split_axis=0, concat_axis=0, tiled=True)  7.13 us
    pallas_call x1, Pallas kernels, tables(): pl.pallas_call(functools.partial(tables_body, owned, most), out_shape=(ja...  3.94 us
    pallas_call x1, Pallas kernels, select(): pl.pallas_call(select_body, out_shape=((pltpu.HBM(shapes[0].shape, BF16),...  3.9 us
  transfers between devices with their start and end apart: 26, of which 13 were waited for; matrix products, arithmetic and copies ran while one was open for 0% of the time, Pallas kernels for 8%

profile of v3, /device:TPU:8, one launch (start us, length us, event | category | flops | bytes accessed | tf_op | source)
XLA Modules:
  0.0 160.5 jit_solution(12581584714850034669)
XLA Ops:
  0.6 3.2 %shard_map.85 = bf16[16,2,128,256]{3,2,1,0:T(8,128)(2,1)} custom-call(bf16[128,4096]{1,0:T(8,128)(2,1)} %bitcast.5, bf16[128,4096]{1,0:T(8,128)(2,1)} %bitcast.6), custom_call_target="tpu_custom_call" | custom-call | tf_op jit(solution)/shard_map/pallas_call | solution.py:84
  3.9 8.7 %all-to-all-start = ((bf16[16,2,128,256]{3,2,1,0:T(8,128)(2,1)}), bf16[16,2,128,256]{3,2,1,0:T(8,128)(2,1)S(1)}, u32[]{:S(2)}, u32[]{:S(2)}) async-start(bf16[16,2,128,256]{3,2,1,0:T(8,128)(2,1)} %shard_map.85), calls=%async_computation | async-start | bytes 4194304 | tf_op jit(solution)/shard_map/all_to_all | solution.py:410
  12.6 3.1 %collective-permute-start.1 = (bf16[4,128,256]{2,1,0:T(8,128)(2,1)S(1)}, bf16[4,128,256]{2,1,0:T(8,128)(2,1)S(1)}, u32[]{:S(2)}, u32[]{:S(2)}) collective-permute-start(bf16[4,128,256]{2,1,0:T(8,128)(2,1)S(1)} %copy-done.2), channel_id=1, source_target_pairs={{0,2},{1,3},{2,0},{3,1},{4,6},{5,7},{6,4},{7,5},{8,10},{9,11},{10,... | collective-permute-start | bytes 786440 | tf_op jit(solution)/shard_map/ppermute | solution.py:38
  15.7 1.1 collective-permute-start
  17.7 2.3 %collective-permute-start.4 = (bf16[4,128,256]{2,1,0:T(8,128)(2,1)S(1)}, bf16[4,128,256]{2,1,0:T(8,128)(2,1)}, u32[]{:S(2)}, u32[]{:S(2)}) collective-permute-start(bf16[4,128,256]{2,1,0:T(8,128)(2,1)S(1)} %copy-done.3), channel_id=1, source_target_pairs={{0,8},{1,9},{2,10},{3,11},{4,12},{5,13},{6,14},{7,15},{8,0},{9,1},... | collective-permute-start | bytes 786440 | tf_op jit(solution)/shard_map/ppermute | solution.py:38
  20.0 1.3 collective-permute-start.3
  21.4 2.0 %collective-permute-done.1.refs_2_ = bf16[4,128,256]{2,1,0:T(8,128)(2,1)S(1)} collective-permute-done((bf16[4,128,256]{2,1,0:T(8,128)(2,1)S(1)}, bf16[4,128,256]{2,1,0:T(8,128)(2,1)S(1)}, u32[]{:S(2)}, u32[]{:S(2)}) %collective-permute-start.1) | collective-permute-done | bytes 262176 | tf_op jit(solution)/shard_map/ppermute | solution.py:38
  23.3 1.6 collective-permute-start.5
  24.9 3.9 %shard_map.86 = (s32[2,32]{1,0:T(2,128)}, s32[2,64]{1,0:T(2,128)}) custom-call(s32[16,16]{1,0:T(8,128)} %ids_ref.3), custom_call_target="tpu_custom_call" | custom-call | tf_op jit(solution)/shard_map/pallas_call | solution.py:160
  28.9 3.9 %collective-permute-done.3.refs_5_ = bf16[4,128,256]{2,1,0:T(8,128)(2,1)} collective-permute-done((bf16[4,128,256]{2,1,0:T(8,128)(2,1)S(1)}, bf16[4,128,256]{2,1,0:T(8,128)(2,1)}, u32[]{:S(2)}, u32[]{:S(2)}) %collective-permute-start.3) | collective-permute-done | bytes 262176 | tf_op jit(solution)/shard_map/ppermute | solution.py:38
  33.6 3.9 %shard_map.87 = (bf16[8,128,256]{2,1,0:T(8,128)(2,1)}, bf16[8,128,256]{2,1,0:T(8,128)(2,1)S(1)}, bf16[8,128,256]{2,1,0:T(8,128)(2,1)}, bf16[8,128,256]{2,1,0:T(8...) custom-call(s32[2,32]{1,0:T(2,128)S(1)} %copy-done.6, ...), custom_call_target="tpu_custom_call" | custom-call | tf_op jit(solution)/shard_map/pallas_call | solution.py:202
  37.5 1.5 collective-permute-start.6
  39.0 1.3 collective-permute-start.7
  40.3 2.0 %collective-permute-start.8 = (bf16[8,128,256]{2,1,0:T(8,128)(2,1)}, bf16[8,128,256]{2,1,0:T(8,128)(2,1)}, u32[]{:S(2)}, u32[]{:S(2)}) collective-permute-start(bf16[8,128,256]{2,1,0:T(8,128)(2,1)} %get-tuple-element.45), channel_id=1, source_target_pairs={{0,12},{1,13},{2,14},{3,15},{4,0},{5,1},{6,2},{7,3},{8,4},{9,5},{1... | collective-permute-start | bytes 1572872 | tf_op jit(solution)/shard_map/ppermute | solution.py:38
  43.0 3.2 %collective-permute-start.10 = (bf16[8,128,256]{2,1,0:T(8,128)(2,1)}, bf16[8,128,256]{2,1,0:T(8,128)(2,1)}, u32[]{:S(2)}, u32[]{:S(2)}) collective-permute-start(bf16[8,128,256]{2,1,0:T(8,128)(2,1)} %get-tuple-element.48), channel_id=1, source_target_pairs={{0,2},{1,3},{2,0},{3,1},{4,6},{5,7},{6,4},{7,5},{8,10},{9,11},{10,... | collective-permute-start | bytes 1572872 | tf_op jit(solution)/shard_map/ppermute | solution.py:38
  46.2 6.2 %collective-permute-done.6.refs_1_ = bf16[8,128,256]{2,1,0:T(8,128)(2,1)S(1)} collective-permute-done((bf16[8,128,256]{2,1,0:T(8,128)(2,1)S(1)}, bf16[8,128,256]{2,1,0:T(8,128)(2,1)S(1)}, u32[]{:S(2)}, u32[]{:S(2)}) %collective-permute-start.6) | collective-permute-done | bytes 524320 | tf_op jit(solution)/shard_map/ppermute | solution.py:38
  52.4 2.4 %collective-permute-start.11 = (bf16[8,128,256]{2,1,0:T(8,128)(2,1)}, bf16[8,128,256]{2,1,0:T(8,128)(2,1)}, u32[]{:S(2)}, u32[]{:S(2)}) collective-permute-start(bf16[8,128,256]{2,1,0:T(8,128)(2,1)} %get-tuple-element.49), channel_id=1, source_target_pairs={{0,3},{1,0},{2,1},{3,2},{4,7},{5,4},{6,5},{7,6},{8,11},{9,8},{10,9... | collective-permute-start | bytes 1572872 | tf_op jit(solution)/shard_map/ppermute | solution.py:38
  55.6 9.4 %collective-permute-done.8.refs_3_ = bf16[8,128,256]{2,1,0:T(8,128)(2,1)} collective-permute-done((bf16[8,128,256]{2,1,0:T(8,128)(2,1)}, bf16[8,128,256]{2,1,0:T(8,128)(2,1)}, u32[]{:S(2)}, u32[]{:S(2)}) %collective-permute-start.8) | collective-permute-done | bytes 524320 | tf_op jit(solution)/shard_map/ppermute | solution.py:38
  65.0 3.8 %collective-permute-done.10.refs_6_ = bf16[8,128,256]{2,1,0:T(8,128)(2,1)} collective-permute-done((bf16[8,128,256]{2,1,0:T(8,128)(2,1)}, bf16[8,128,256]{2,1,0:T(8,128)(2,1)}, u32[]{:S(2)}, u32[]{:S(2)}) %collective-permute-start.10) | collective-permute-done | bytes 524320 | tf_op jit(solution)/shard_map/ppermute | solution.py:38
  68.7 20.2 %shard_map.88 = (bf16[16,128,256]{2,1,0:T(8,128)(2,1)}, bf16[8,128,256]{2,1,0:T(8,128)(2,1)}, bf16[8,128,256]{2,1,0:T(8,128)(2,1)}, bf16[8,128,256]{2,1,0:T(8,12...) custom-call(s32[16,16]{1,0:T(8,128)S(1)} %copy-done.4, ...), custom_call_target="tpu_custom_call" | custom-call | tf_op jit(solution)/shard_map/pallas_call | solution.py:367
  89.0 7.1 %all-to-all-start.1 = ((bf16[16,128,256]{2,1,0:T(8,128)(2,1)}), bf16[16,128,256]{2,1,0:T(8,128)(2,1)}, u32[]{:S(2)}, u32[]{:S(2)}) async-start(bf16[16,128,256]{2,1,0:T(8,128)(2,1)} %get-tuple-element.50), calls=%async_computation.1 | async-start | bytes 2097152 | tf_op jit(solution)/shard_map/all_to_all | solution.py:415
  97.5 1.4 collective-permute-start.14
  98.9 3.1 %collective-permute-start.15 = (bf16[8,128,256]{2,1,0:T(8,128)(2,1)}, bf16[8,128,256]{2,1,0:T(8,128)(2,1)S(1)}, u32[]{:S(2)}, u32[]{:S(2)}) collective-permute-start(bf16[8,128,256]{2,1,0:T(8,128)(2,1)} %get-tuple-element.57), channel_id=1, source_target_pairs={{0,3},{1,0},{2,1},{3,2},{4,7},{5,4},{6,5},{7,6},{8,11},{9,8},{10,9... | collective-permute-start | bytes 1572872 | tf_op jit(solution)/shard_map/ppermute | solution.py:38
  102.0 19.8 %collective-permute-done.12.refs_1_ = bf16[8,128,256]{2,1,0:T(8,128)(2,1)S(1)} collective-permute-done((bf16[8,128,256]{2,1,0:T(8,128)(2,1)}, bf16[8,128,256]{2,1,0:T(8,128)(2,1)S(1)}, u32[]{:S(2)}, u32[]{:S(2)}) %collective-permute-start.12) | collective-permute-done | bytes 524320 | tf_op jit(solution)/shard_map/ppermute | solution.py:38
  122.1 1.5 collective-permute-done.14.refs_3_
  124.3 12.1 %collective-permute-done.17.refs_7_ = bf16[8,128,256]{2,1,0:T(8,128)(2,1)S(1)} collective-permute-done((bf16[8,128,256]{2,1,0:T(8,128)(2,1)S(1)}, bf16[8,128,256]{2,1,0:T(8,128)(2,1)S(1)}, u32[]{:S(2)}, u32[]{:S(2)}) %collective-permute-start.17) | collective-permute-done | bytes 524320 | tf_op jit(solution)/shard_map/ppermute | solution.py:38
  136.4 3.0 %shard_map.90 = (f32[4,128,256]{2,1,0:T(8,128)S(1)}, bf16[4,128,256]{2,1,0:T(8,128)(2,1)S(1)}, bf16[4,128,256]{2,1,0:T(8,128)(2,1)}, bf16[4,128,256]{2,1,0:T(8,1...) custom-call(s32[2,64]{1,0:T(2,128)S(1)} %copy-done.5, ...), custom_call_target="tpu_custom_call" | custom-call | tf_op jit(solution)/shard_map/pallas_call | solution.py:234
  139.4 2.9 %collective-permute-start.19 = (bf16[4,128,256]{2,1,0:T(8,128)(2,1)}, bf16[4,128,256]{2,1,0:T(8,128)(2,1)S(1)}, u32[]{:S(2)}, u32[]{:S(2)}) collective-permute-start(bf16[4,128,256]{2,1,0:T(8,128)(2,1)} %get-tuple-element.62), channel_id=1, source_target_pairs={{0,2},{1,3},{2,0},{3,1},{4,6},{5,7},{6,4},{7,5},{8,10},{9,11},{10,... | collective-permute-start | bytes 786440 | tf_op jit(solution)/shard_map/ppermute | solution.py:38
  142.7 10.5 %collective-permute-done.18.refs_1_ = bf16[4,128,256]{2,1,0:T(8,128)(2,1)S(1)} collective-permute-done((bf16[4,128,256]{2,1,0:T(8,128)(2,1)S(1)}, bf16[4,128,256]{2,1,0:T(8,128)(2,1)S(1)}, u32[]{:S(2)}, u32[]{:S(2)}) %collective-permute-start.18) | collective-permute-done | bytes 262176 | tf_op jit(solution)/shard_map/ppermute | solution.py:38
  153.1 2.3 %shard_map.89 = bf16[128,4096]{1,0:T(8,128)(2,1)} custom-call(bf16[16,128,256]{2,1,0:T(8,128)(2,1)} %all-to-all-done.1.in_ref), custom_call_target="tpu_custom_call" | custom-call | tf_op jit(solution)/shard_map/pallas_call | solution.py:106
  155.5 4.0 %collective-permute-done.23.refs_7_ = bf16[4,128,256]{2,1,0:T(8,128)(2,1)S(1)} collective-permute-done((bf16[4,128,256]{2,1,0:T(8,128)(2,1)S(1)}, bf16[4,128,256]{2,1,0:T(8,128)(2,1)S(1)}, u32[]{:S(2)}, u32[]{:S(2)}) %collective-permute-start.23) | collective-permute-done | bytes 262176 | tf_op jit(solution)/shard_map/ppermute | solution.py:38
  159.5 1.0 shard_map.91
  (53 shorter events, 5.9 us)
Async XLA Ops:
  3.8 50.9 %copy-start.9 = (s32[16,32,2]{1,2,0:T(2,128)S(1)}, s32[16,32,2]{1,2,0:T(2,128)}, u32[]{:S(2)}) copy-start(s32[16,32,2]{1,2,0:T(2,128)} %param.11) | copy-start | bytes 12292
  3.9 64.9 %all-to-all-start = ((bf16[16,2,128,256]{3,2,1,0:T(8,128)(2,1)}), bf16[16,2,128,256]{3,2,1,0:T(8,128)(2,1)S(1)}, u32[]{:S(2)}, u32[]{:S(2)}) async-start(bf16[16,2,128,256]{3,2,1,0:T(8,128)(2,1)} %shard_map.85), calls=%async_computation | async-start | bytes 4194304 | tf_op jit(solution)/shard_map/all_to_all | solution.py:410
  12.6 56.2 %copy-start.4 = (s32[16,16]{1,0:T(8,128)S(1)}, s32[16,16]{1,0:T(8,128)}, u32[]{:S(2)}) copy-start(s32[16,16]{1,0:T(8,128)} %ids_ref.3) | copy-start | bytes 3076
  12.6 10.7 %collective-permute-start.1 = (bf16[4,128,256]{2,1,0:T(8,128)(2,1)S(1)}, bf16[4,128,256]{2,1,0:T(8,128)(2,1)S(1)}, u32[]{:S(2)}, u32[]{:S(2)}) collective-permute-start(bf16[4,128,256]{2,1,0:T(8,128)(2,1)S(1)} %copy-done.2), channel_id=1, source_target_pairs={{0,2},{1,3},{2,0},{3,1},{4,6},{5,7},{6,4},{7,5},{8,10},{9,11},{10,... | collective-permute-start | bytes 786440 | tf_op jit(solution)/shard_map/ppermute | solution.py:38
  15.7 13.2 %collective-permute-start = (bf16[4,128,256]{2,1,0:T(8,128)(2,1)S(1)}, bf16[4,128,256]{2,1,0:T(8,128)(2,1)S(1)}, u32[]{:S(2)}, u32[]{:S(2)}) collective-permute-start(bf16[4,128,256]{2,1,0:T(8,128)(2,1)S(1)} %copy-done.2), channel_id=1, source_target_pairs={{0,3},{1,0},{2,1},{3,2},{4,7},{5,4},{6,5},{7,6},{8,11},{9,8},{10,9... | collective-permute-start | bytes 786440 | tf_op jit(solution)/shard_map/ppermute | solution.py:38
  16.9 12.0 %collective-permute-start.2 = (bf16[4,128,256]{2,1,0:T(8,128)(2,1)S(1)}, bf16[4,128,256]{2,1,0:T(8,128)(2,1)S(1)}, u32[]{:S(2)}, u32[]{:S(2)}) collective-permute-start(bf16[4,128,256]{2,1,0:T(8,128)(2,1)S(1)} %copy-done.2), channel_id=1, source_target_pairs={{0,1},{1,2},{2,3},{3,0},{4,5},{5,6},{6,7},{7,4},{8,9},{9,10},{10,1... | collective-permute-start | bytes 786440 | tf_op jit(solution)/shard_map/ppermute | solution.py:38
  17.7 11.1 %collective-permute-start.4 = (bf16[4,128,256]{2,1,0:T(8,128)(2,1)S(1)}, bf16[4,128,256]{2,1,0:T(8,128)(2,1)}, u32[]{:S(2)}, u32[]{:S(2)}) collective-permute-start(bf16[4,128,256]{2,1,0:T(8,128)(2,1)S(1)} %copy-done.3), channel_id=1, source_target_pairs={{0,8},{1,9},{2,10},{3,11},{4,12},{5,13},{6,14},{7,15},{8,0},{9,1},... | collective-permute-start | bytes 786440 | tf_op jit(solution)/shard_map/ppermute | solution.py:38
  20.0 12.7 %collective-permute-start.3 = (bf16[4,128,256]{2,1,0:T(8,128)(2,1)S(1)}, bf16[4,128,256]{2,1,0:T(8,128)(2,1)}, u32[]{:S(2)}, u32[]{:S(2)}) collective-permute-start(bf16[4,128,256]{2,1,0:T(8,128)(2,1)S(1)} %copy-done.3), channel_id=1, source_target_pairs={{0,12},{1,13},{2,14},{3,15},{4,0},{5,1},{6,2},{7,3},{8,4},{9,5},{1... | collective-permute-start | bytes 786440 | tf_op jit(solution)/shard_map/ppermute | solution.py:38
  23.3 9.5 %collective-permute-start.5 = (bf16[4,128,256]{2,1,0:T(8,128)(2,1)S(1)}, bf16[4,128,256]{2,1,0:T(8,128)(2,1)}, u32[]{:S(2)}, u32[]{:S(2)}) collective-permute-start(bf16[4,128,256]{2,1,0:T(8,128)(2,1)S(1)} %copy-done.3), channel_id=1, source_target_pairs={{0,4},{1,5},{2,6},{3,7},{4,8},{5,9},{6,10},{7,11},{8,12},{9,13},{1... | collective-permute-start | bytes 786440 | tf_op jit(solution)/shard_map/ppermute | solution.py:38
  37.5 14.9 %collective-permute-start.6 = (bf16[8,128,256]{2,1,0:T(8,128)(2,1)S(1)}, bf16[8,128,256]{2,1,0:T(8,128)(2,1)S(1)}, u32[]{:S(2)}, u32[]{:S(2)}) collective-permute-start(bf16[8,128,256]{2,1,0:T(8,128)(2,1)S(1)} %get-tuple-element.43), channel_id=1, source_target_pairs={{0,4},{1,5},{2,6},{3,7},{4,8},{5,9},{6,10},{7,11},{8,12},{9,13},{1... | collective-permute-start | bytes 1572872 | tf_op jit(solution)/shard_map/ppermute | solution.py:38
  39.0 16.6 %collective-permute-start.7 = (bf16[8,128,256]{2,1,0:T(8,128)(2,1)}, bf16[8,128,256]{2,1,0:T(8,128)(2,1)S(1)}, u32[]{:S(2)}, u32[]{:S(2)}) collective-permute-start(bf16[8,128,256]{2,1,0:T(8,128)(2,1)} %get-tuple-element.44), channel_id=1, source_target_pairs={{0,8},{1,9},{2,10},{3,11},{4,12},{5,13},{6,14},{7,15},{8,0},{9,1},... | collective-permute-start | bytes 1572872 | tf_op jit(solution)/shard_map/ppermute | solution.py:38
  40.3 24.6 %collective-permute-start.8 = (bf16[8,128,256]{2,1,0:T(8,128)(2,1)}, bf16[8,128,256]{2,1,0:T(8,128)(2,1)}, u32[]{:S(2)}, u32[]{:S(2)}) collective-permute-start(bf16[8,128,256]{2,1,0:T(8,128)(2,1)} %get-tuple-element.45), channel_id=1, source_target_pairs={{0,12},{1,13},{2,14},{3,15},{4,0},{5,1},{6,2},{7,3},{8,4},{9,5},{1... | collective-permute-start | bytes 1572872 | tf_op jit(solution)/shard_map/ppermute | solution.py:38
  42.4 22.6 %collective-permute-start.9 = (bf16[8,128,256]{2,1,0:T(8,128)(2,1)}, bf16[8,128,256]{2,1,0:T(8,128)(2,1)}, u32[]{:S(2)}, u32[]{:S(2)}) collective-permute-start(bf16[8,128,256]{2,1,0:T(8,128)(2,1)} %get-tuple-element.47), channel_id=1, source_target_pairs={{0,1},{1,2},{2,3},{3,0},{4,5},{5,6},{6,7},{7,4},{8,9},{9,10},{10,1... | collective-permute-start | bytes 1572872 | tf_op jit(solution)/shard_map/ppermute | solution.py:38
  43.0 25.8 %collective-permute-start.10 = (bf16[8,128,256]{2,1,0:T(8,128)(2,1)}, bf16[8,128,256]{2,1,0:T(8,128)(2,1)}, u32[]{:S(2)}, u32[]{:S(2)}) collective-permute-start(bf16[8,128,256]{2,1,0:T(8,128)(2,1)} %get-tuple-element.48), channel_id=1, source_target_pairs={{0,2},{1,3},{2,0},{3,1},{4,6},{5,7},{6,4},{7,5},{8,10},{9,11},{10,... | collective-permute-start | bytes 1572872 | tf_op jit(solution)/shard_map/ppermute | solution.py:38
  52.4 16.4 %collective-permute-start.11 = (bf16[8,128,256]{2,1,0:T(8,128)(2,1)}, bf16[8,128,256]{2,1,0:T(8,128)(2,1)}, u32[]{:S(2)}, u32[]{:S(2)}) collective-permute-start(bf16[8,128,256]{2,1,0:T(8,128)(2,1)} %get-tuple-element.49), channel_id=1, source_target_pairs={{0,3},{1,0},{2,1},{3,2},{4,7},{5,4},{6,5},{7,6},{8,11},{9,8},{10,9... | collective-permute-start | bytes 1572872 | tf_op jit(solution)/shard_map/ppermute | solution.py:38
  89.0 32.8 %copy-start.10 = (bf16[8,128,256]{2,1,0:T(8,128)(2,1)S(1)}, bf16[8,128,256]{2,1,0:T(8,128)(2,1)}, u32[]{:S(2)}) copy-start(bf16[8,128,256]{2,1,0:T(8,128)(2,1)} %get-tuple-element.59) | copy-start | bytes 1572868
  89.0 47.4 %copy-start = (bf16[8,128,256]{2,1,0:T(8,128)(2,1)S(1)}, bf16[8,128,256]{2,1,0:T(8,128)(2,1)}, u32[]{:S(2)}) copy-start(bf16[8,128,256]{2,1,0:T(8,128)(2,1)} %get-tuple-element.52.refs_0_) | copy-start | bytes 1572868
  89.0 47.4 %copy-start.1 = (bf16[8,128,256]{2,1,0:T(8,128)(2,1)S(1)}, bf16[8,128,256]{2,1,0:T(8,128)(2,1)}, u32[]{:S(2)}) copy-start(bf16[8,128,256]{2,1,0:T(8,128)(2,1)} %get-tuple-element.56.refs_4_) | copy-start | bytes 1572868
  89.0 47.4 %copy-start.5 = (s32[2,64]{1,0:T(2,128)S(1)}, s32[2,64]{1,0:T(2,128)}, u32[]{:S(2)}) copy-start(s32[2,64]{1,0:T(2,128)} %get-tuple-element.51.add_ref) | copy-start | bytes 1540
  89.0 64.1 %all-to-all-start.1 = ((bf16[16,128,256]{2,1,0:T(8,128)(2,1)}), bf16[16,128,256]{2,1,0:T(8,128)(2,1)}, u32[]{:S(2)}, u32[]{:S(2)}) async-start(bf16[16,128,256]{2,1,0:T(8,128)(2,1)} %get-tuple-element.50), calls=%async_computation.1 | async-start | bytes 2097152 | tf_op jit(solution)/shard_map/all_to_all | solution.py:415
  96.2 25.6 %collective-permute-start.12 = (bf16[8,128,256]{2,1,0:T(8,128)(2,1)}, bf16[8,128,256]{2,1,0:T(8,128)(2,1)S(1)}, u32[]{:S(2)}, u32[]{:S(2)}) collective-permute-start(bf16[8,128,256]{2,1,0:T(8,128)(2,1)} %get-tuple-element.53), channel_id=1, source_target_pairs={{0,12},{1,13},{2,14},{3,15},{4,0},{5,1},{6,2},{7,3},{8,4},{9,5},{1... | collective-permute-start | bytes 1572872 | tf_op jit(solution)/shard_map/ppermute | solution.py:38
  96.7 25.4 %collective-permute-start.13 = (bf16[8,128,256]{2,1,0:T(8,128)(2,1)}, bf16[8,128,256]{2,1,0:T(8,128)(2,1)S(1)}, u32[]{:S(2)}, u32[]{:S(2)}) collective-permute-start(bf16[8,128,256]{2,1,0:T(8,128)(2,1)} %get-tuple-element.54), channel_id=1, source_target_pairs={{0,8},{1,9},{2,10},{3,11},{4,12},{5,13},{6,14},{7,15},{8,0},{9,1},... | collective-permute-start | bytes 1572872 | tf_op jit(solution)/shard_map/ppermute | solution.py:38
  97.5 26.2 %collective-permute-start.14 = (bf16[8,128,256]{2,1,0:T(8,128)(2,1)}, bf16[8,128,256]{2,1,0:T(8,128)(2,1)S(1)}, u32[]{:S(2)}, u32[]{:S(2)}) collective-permute-start(bf16[8,128,256]{2,1,0:T(8,128)(2,1)} %get-tuple-element.55), channel_id=1, source_target_pairs={{0,4},{1,5},{2,6},{3,7},{4,8},{5,9},{6,10},{7,11},{8,12},{9,13},{1... | collective-permute-start | bytes 1572872 | tf_op jit(solution)/shard_map/ppermute | solution.py:38
  98.9 25.4 %collective-permute-start.15 = (bf16[8,128,256]{2,1,0:T(8,128)(2,1)}, bf16[8,128,256]{2,1,0:T(8,128)(2,1)S(1)}, u32[]{:S(2)}, u32[]{:S(2)}) collective-permute-start(bf16[8,128,256]{2,1,0:T(8,128)(2,1)} %get-tuple-element.57), channel_id=1, source_target_pairs={{0,3},{1,0},{2,1},{3,2},{4,7},{5,4},{6,5},{7,6},{8,11},{9,8},{10,9... | collective-permute-start | bytes 1572872 | tf_op jit(solution)/shard_map/ppermute | solution.py:38
  102.0 22.3 %collective-permute-start.16 = (bf16[8,128,256]{2,1,0:T(8,128)(2,1)S(1)}, bf16[8,128,256]{2,1,0:T(8,128)(2,1)S(1)}, u32[]{:S(2)}, u32[]{:S(2)}) collective-permute-start(bf16[8,128,256]{2,1,0:T(8,128)(2,1)S(1)} %copy-done.11), channel_id=1, source_target_pairs={{0,2},{1,3},{2,0},{3,1},{4,6},{5,7},{6,4},{7,5},{8,10},{9,11},{10,... | collective-permute-start | bytes 1572872 | tf_op jit(solution)/shard_map/ppermute | solution.py:38
  121.8 14.6 %collective-permute-start.17 = (bf16[8,128,256]{2,1,0:T(8,128)(2,1)S(1)}, bf16[8,128,256]{2,1,0:T(8,128)(2,1)S(1)}, u32[]{:S(2)}, u32[]{:S(2)}) collective-permute-start(bf16[8,128,256]{2,1,0:T(8,128)(2,1)S(1)} %copy-done.10), channel_id=1, source_target_pairs={{0,1},{1,2},{2,3},{3,0},{4,5},{5,6},{6,7},{7,4},{8,9},{9,10},{10,1... | collective-permute-start | bytes 1572872 | tf_op jit(solution)/shard_map/ppermute | solution.py:38
  139.4 13.7 %collective-permute-start.18 = (bf16[4,128,256]{2,1,0:T(8,128)(2,1)S(1)}, bf16[4,128,256]{2,1,0:T(8,128)(2,1)S(1)}, u32[]{:S(2)}, u32[]{:S(2)}) collective-permute-start(bf16[4,128,256]{2,1,0:T(8,128)(2,1)S(1)} %get-tuple-element.61), channel_id=1, source_target_pairs={{0,1},{1,2},{2,3},{3,0},{4,5},{5,6},{6,7},{7,4},{8,9},{9,10},{10,1... | collective-permute-start | bytes 786440 | tf_op jit(solution)/shard_map/ppermute | solution.py:38
  139.4 16.0 %collective-permute-start.19 = (bf16[4,128,256]{2,1,0:T(8,128)(2,1)}, bf16[4,128,256]{2,1,0:T(8,128)(2,1)S(1)}, u32[]{:S(2)}, u32[]{:S(2)}) collective-permute-start(bf16[4,128,256]{2,1,0:T(8,128)(2,1)} %get-tuple-element.62), channel_id=1, source_target_pairs={{0,2},{1,3},{2,0},{3,1},{4,6},{5,7},{6,4},{7,5},{8,10},{9,11},{10,... | collective-permute-start | bytes 786440 | tf_op jit(solution)/shard_map/ppermute | solution.py:38
  142.3 13.1 %collective-permute-start.20 = (bf16[4,128,256]{2,1,0:T(8,128)(2,1)}, bf16[4,128,256]{2,1,0:T(8,128)(2,1)S(1)}, u32[]{:S(2)}, u32[]{:S(2)}) collective-permute-start(bf16[4,128,256]{2,1,0:T(8,128)(2,1)} %get-tuple-element.63), channel_id=1, source_target_pairs={{0,3},{1,0},{2,1},{3,2},{4,7},{5,4},{6,5},{7,6},{8,11},{9,8},{10,9... | collective-permute-start | bytes 786440 | tf_op jit(solution)/shard_map/ppermute | solution.py:38
  142.7 12.8 %collective-permute-start.21 = (bf16[4,128,256]{2,1,0:T(8,128)(2,1)S(1)}, bf16[4,128,256]{2,1,0:T(8,128)(2,1)S(1)}, u32[]{:S(2)}, u32[]{:S(2)}) collective-permute-start(bf16[4,128,256]{2,1,0:T(8,128)(2,1)S(1)} %get-tuple-element.65), channel_id=1, source_target_pairs={{0,4},{1,5},{2,6},{3,7},{4,8},{5,9},{6,10},{7,11},{8,12},{9,13},{1... | collective-permute-start | bytes 786440 | tf_op jit(solution)/shard_map/ppermute | solution.py:38
  142.7 12.8 %collective-permute-start.22 = (bf16[4,128,256]{2,1,0:T(8,128)(2,1)S(1)}, bf16[4,128,256]{2,1,0:T(8,128)(2,1)S(1)}, u32[]{:S(2)}, u32[]{:S(2)}) collective-permute-start(bf16[4,128,256]{2,1,0:T(8,128)(2,1)S(1)} %get-tuple-element.66), channel_id=1, source_target_pairs={{0,8},{1,9},{2,10},{3,11},{4,12},{5,13},{6,14},{7,15},{8,0},{9,1},... | collective-permute-start | bytes 786440 | tf_op jit(solution)/shard_map/ppermute | solution.py:38
  153.1 6.4 %collective-permute-start.23 = (bf16[4,128,256]{2,1,0:T(8,128)(2,1)S(1)}, bf16[4,128,256]{2,1,0:T(8,128)(2,1)S(1)}, u32[]{:S(2)}, u32[]{:S(2)}) collective-permute-start(bf16[4,128,256]{2,1,0:T(8,128)(2,1)S(1)} %get-tuple-element.67), channel_id=1, source_target_pairs={{0,12},{1,13},{2,14},{3,15},{4,0},{5,1},{6,2},{7,3},{8,4},{9,5},{1... | collective-permute-start | bytes 786440 | tf_op jit(solution)/shard_map/ppermute | solution.py:38
  (6 other events, 65.9 us)

commit v4 on v3

--- a/solution.py
+++ b/solution.py
@@ -247,7 +247,7 @@
     key_parts, value_parts = refs[:4], refs[4:8]
     gq_out, key_out, value_out = refs[8], refs[9:13], refs[13:17]
     (keys, values, key_sum, value_sum, gq_ref, key_send, value_send, query_last, grad_last, held,
-     key_rows, value_rows, counts, in_sems, out_sems, gq_sem) = refs[17:]
+     key_rows, value_rows, key_back, value_back, counts, in_sems, out_sems, gq_sem) = refs[17:]
     scale = 1.0 / math.sqrt(DH)
     copies = [
         pltpu.make_async_copy(part, pool.at[pl.ds(k * most, most)], in_sems.at[i, k])
@@ -269,13 +269,19 @@
     mine = (me // SIDE, me % SIDE)
     for i in range(2 * SIDE):
         counts[i] = 0
+    for n in range(SIDE * most):
+        key_back[n] = -1
+        value_back[n] = -1
 
     def rank(j, carry):
         where = place(ids_ref[me, j], owned)
-        for i, table in enumerate((key_rows, value_rows)):
+        for i, (table, back_rows) in enumerate(
+            ((key_rows, key_back), (value_rows, value_back))
+        ):
             distance = (mine[i] - where[i] + SIDE) % SIDE
             count = counts[i * SIDE + distance]
             table[j] = distance * most + count
+            back_rows[distance * most + count] = j
             counts[i * SIDE + distance] = count + 1
         return carry
 
@@ -298,51 +304,64 @@
         last[...] = following
         return block_diagonal(block.astype(BF16))
 
-    def step(group):
-        query = shifted(0, group, query_last)
-        grad = shifted(1, group, grad_last)
-        pair = (refs_ref[me, 2 * group], refs_ref[me, 2 * group + 1])
-        block_keys = [keys[key_rows[j]] for j in pair]
-        scores = [matmul(k, query, (1, 1)) for k in block_keys]
-        grads = [matmul(values[value_rows[j]], grad, (1, 1)) for j in pair]
-        top = jnp.maximum(*[jnp.max(s, axis=0, keepdims=True) for s in scores])
-        weights = [jnp.exp((s - top) * scale) for s in scores]
-        total = sum(jnp.sum(w, axis=0, keepdims=True) for w in weights)
-        inverse = 1.0 / total
-        weights = [w * inverse for w in weights]
-        dots = sum(jnp.sum(w * g, axis=0, keepdims=True) for w, g in zip(weights, grads))
-        grad_low = [(w * (g - dots)).astype(BF16) for w, g in zip(weights, grads)]
-        weights_low = [w.astype(BF16) for w in weights]
-        for j, w, g in zip(pair, weights_low, grad_low):
-            value_sum[j] += matmul(w, grad, (1, 0))
-            key_sum[j] += matmul(g, query, (1, 0))
-        both = sum(matmul(g, k, (0, 0)) for g, k in zip(grad_low, block_keys)) * scale
-        back = jnp.concatenate([both[:GROUP, :DH], both[GROUP:, DH:]], axis=1)
-        back = pltpu.roll(back, GROUP - 1, 0)
-        gq_ref[group // 2, pl.ds((group % 2) * GROUP, GROUP), :] = jnp.where(
-            row == GROUP - 1, back, held[...]
-        ).astype(BF16)
-        held[...] = back
-
     def steps(index, carry):
-        for u in range(unroll):
-            step(index * unroll + u)
+        batch = [index * unroll + u for u in range(unroll)]
+        state = []
+        for group in batch:
+            query = shifted(0, group, query_last)
+            grad = shifted(1, group, grad_last)
+            pair = (refs_ref[me, 2 * group], refs_ref[me, 2 * group + 1])
+            block_keys = [keys[key_rows[j]] for j in pair]
+            scores = [matmul(k, query, (1, 1)) for k in block_keys]
+            grads = [matmul(values[value_rows[j]], grad, (1, 1)) for j in pair]
+            state.append((group, query, grad, pair, block_keys, scores, grads))
+        lows = []
+        for group, query, grad, pair, block_keys, scores, grads in state:
+            top = jnp.maximum(*[jnp.max(s, axis=0, keepdims=True) for s in scores])
+            weights = [jnp.exp2((s - top) * (scale * math.log2(math.e))) for s in scores]
+            total = sum(jnp.sum(w, axis=0, keepdims=True) for w in weights)
+            inverse = 1.0 / total
+            weights = [w * inverse for w in weights]
+            dots = sum(jnp.sum(w * g, axis=0, keepdims=True) for w, g in zip(weights, grads))
+            grad_low = [(w * (g - dots)).astype(BF16) for w, g in zip(weights, grads)]
+            lows.append(([w.astype(BF16) for w in weights], grad_low))
+        for (group, query, grad, pair, block_keys, _, _), (weights_low, grad_low) in zip(state, lows):
+            terms = [(matmul(w, grad, (1, 0)), matmul(g, query, (1, 0))) for w, g in zip(weights_low, grad_low)]
+            both = sum(matmul(g, k, (0, 0)) for g, k in zip(grad_low, block_keys)) * scale
+            back = jnp.concatenate([both[:GROUP, :DH], both[GROUP:, DH:]], axis=1)
+            back = pltpu.roll(back, GROUP - 1, 0)
+            for j, (value_term, key_term) in zip(pair, terms):
+                value_sum[j] += value_term
+                key_sum[j] += key_term
+            gq_ref[group // 2, pl.ds((group % 2) * GROUP, GROUP), :] = jnp.where(
+                row == GROUP - 1, back, held[...]
+            ).astype(BF16)
+            held[...] = back
         return carry
 
     lax.fori_loop(0, groups // unroll, steps, 0)
-
     copies = [pltpu.make_async_copy(gq_ref, gq_out, gq_sem)]
     copies[0].start()
-
-    def give(j, carry):
-        key_send[key_rows[j]] = (key_sum[j] * scale).astype(BF16)
-        value_send[value_rows[j]] = value_sum[j].astype(BF16)
-        return carry
-
-    lax.fori_loop(0, distinct, give, 0, unroll=2)
-    for i, (send, parts) in enumerate(((key_send, key_out), (value_send, value_out))):
-        for k, part in enumerate(parts):
-            copy = pltpu.make_async_copy(send.at[pl.ds(k * most, most)], part, out_sems.at[i, k])
+    for k in (2, 1, 3, 0):
+        for i, (send, total, back_rows, out, factor) in enumerate(
+            ((key_send, key_sum, key_back, key_out, scale),
+             (value_send, value_sum, value_back, value_out, 1.0))
+        ):
+
+            def give(n, carry):
+                slot = k * most + n
+                j = back_rows[slot]
+
+                @pl.when(j >= 0)
+                def _():
+                    send[slot] = (total[jnp.maximum(j, 0)] * factor).astype(BF16)
+
+                return carry
+
+            lax.fori_loop(0, most, give, 0)
+            copy = pltpu.make_async_copy(
+                send.at[pl.ds(k * most, most)], out[k], out_sems.at[i, k]
+            )
             copy.start()
             copies.append(copy)
     for copy in copies:
@@ -359,18 +378,19 @@
     total = pltpu.VMEM((distinct, nbr, width), F32)
     rows = pltpu.VMEM((GROUP, width), F32)
     table = pltpu.SMEM((distinct,), jnp.int32)
+    reverse = pltpu.SMEM((SIDE * most,), jnp.int32)
     shapes = (jax.ShapeDtypeStruct((parts, part_tokens, width), BF16),) + chunk_shapes(
         most, nbr, width
     ) * 2
     constrain = lambda value: pltpu.with_memory_space_constraint(value, pltpu.MemorySpace.HBM)
     keys, values = jax.tree.map(constrain, (list(keys), list(values)))
     out = pl.pallas_call(
-        functools.partial(attend_body, groups, distinct, owned, most, 2),
+        functools.partial(attend_body, groups, distinct, owned, most, 8),
         out_shape=tuple(pltpu.HBM(shape.shape, shape.dtype) for shape in shapes),
         in_specs=[SMEM, SMEM, VMEM] + [HBM] * 8,
         out_specs=(HBM,) * 9,
         scratch_shapes=[pool, pool, total, total, pltpu.VMEM((parts, part_tokens, width), BF16),
-                        pool, pool, rows, rows, rows, table, table,
+                        pool, pool, rows, rows, rows, table, table, reverse, reverse,
                         pltpu.SMEM((2 * SIDE,), jnp.int32),
                         pltpu.SemaphoreType.DMA((2, SIDE)), pltpu.SemaphoreType.DMA((2, SIDE)),
                         pltpu.SemaphoreType.DMA],

time: 161 us -> 148 us (0.919)
  Pallas kernels: 37.5 us -> 29.3 us
  waiting for transfers between devices: 74.6 us -> 69.4 us
    pallas_call x1, Pallas kernels: 20.2 us -> 12 us  [attend(): pl.pallas_call(functools.partial(attend_body, groups, distinct, owned, mo...]
    ppermute x24, waiting for transfers between devices: 74.6 us -> 69.4 us  [shift(): return lax.ppermute(value, 'dp', pairs)]
  transfers between devices with their start and end apart: 26 -> 26, of which waited for: 13 -> 13; matrix products, arithmetic and copies ran while one was open for 0% -> 0% of each run, Pallas kernels for 8% -> 9%
where the time goes in v4:
time: 148 us; the launch traced here: 147 us
  waiting for transfers between devices  69.4 us (47%)
  starting transfers between devices  46.8 us (32%)
  Pallas kernels  29.3 us (20%)
    ppermute x24, waiting for transfers between devices, shift(): return lax.ppermute(value, 'dp', pairs)  69.4 us
    ppermute x24, starting transfers between devices, shift(): return lax.ppermute(value, 'dp', pairs)  31 us
    pallas_call x1, Pallas kernels, attend(): pl.pallas_call(functools.partial(attend_body, groups, distinct, owned, mo...  12 us
    all_to_all x1, starting transfers between devices, on_device(): lax.all_to_all(packed, 'ctx', split_axis=0, concat_axis=0, tiled=True)  8.71 us
    all_to_all x1, starting transfers between devices, on_device(): back = lax.all_to_all(back, 'ctx', split_axis=0, concat_axis=0, tiled=True)  7.13 us
    pallas_call x1, Pallas kernels, tables(): pl.pallas_call(functools.partial(tables_body, owned, most), out_shape=(ja...  3.94 us
    pallas_call x1, Pallas kernels, select(): pl.pallas_call(select_body, out_shape=((pltpu.HBM(shapes[0].shape, BF16),...  3.9 us
    pallas_call x1, Pallas kernels, pack_heads(): pl.pallas_call(functools.partial(pack_heads_body, parts, width), out_shap...  3.18 us
  transfers between devices with their start and end apart: 26, of which 13 were waited for; matrix products, arithmetic and copies ran while one was open for 0% of the time, Pallas kernels for 9%

profile of v4, /device:TPU:8, one launch (start us, length us, event | category | flops | bytes accessed | tf_op | source)
XLA Modules:
  0.0 147.3 jit_solution(10224295903261240994)
XLA Ops:
  0.6 3.2 %shard_map.85 = bf16[16,2,128,256]{3,2,1,0:T(8,128)(2,1)} custom-call(bf16[128,4096]{1,0:T(8,128)(2,1)} %bitcast.5, bf16[128,4096]{1,0:T(8,128)(2,1)} %bitcast.6), custom_call_target="tpu_custom_call" | custom-call | tf_op jit(solution)/shard_map/pallas_call | solution.py:84
  3.9 8.7 %all-to-all-start = ((bf16[16,2,128,256]{3,2,1,0:T(8,128)(2,1)}), bf16[16,2,128,256]{3,2,1,0:T(8,128)(2,1)S(1)}, u32[]{:S(2)}, u32[]{:S(2)}) async-start(bf16[16,2,128,256]{3,2,1,0:T(8,128)(2,1)} %shard_map.85), calls=%async_computation | async-start | bytes 4194304 | tf_op jit(solution)/shard_map/all_to_all | solution.py:430
  12.6 3.1 %collective-permute-start.1 = (bf16[4,128,256]{2,1,0:T(8,128)(2,1)S(1)}, bf16[4,128,256]{2,1,0:T(8,128)(2,1)S(1)}, u32[]{:S(2)}, u32[]{:S(2)}) collective-permute-start(bf16[4,128,256]{2,1,0:T(8,128)(2,1)S(1)} %copy-done.2), channel_id=1, source_target_pairs={{0,2},{1,3},{2,0},{3,1},{4,6},{5,7},{6,4},{7,5},{8,10},{9,11},{10,... | collective-permute-start | bytes 786440 | tf_op jit(solution)/shard_map/ppermute | solution.py:38
  15.7 1.1 collective-permute-start
  17.7 2.3 %collective-permute-start.4 = (bf16[4,128,256]{2,1,0:T(8,128)(2,1)S(1)}, bf16[4,128,256]{2,1,0:T(8,128)(2,1)}, u32[]{:S(2)}, u32[]{:S(2)}) collective-permute-start(bf16[4,128,256]{2,1,0:T(8,128)(2,1)S(1)} %copy-done.3), channel_id=1, source_target_pairs={{0,8},{1,9},{2,10},{3,11},{4,12},{5,13},{6,14},{7,15},{8,0},{9,1},... | collective-permute-start | bytes 786440 | tf_op jit(solution)/shard_map/ppermute | solution.py:38
  20.0 1.3 collective-permute-start.3
  21.4 2.0 %collective-permute-done.1.refs_2_ = bf16[4,128,256]{2,1,0:T(8,128)(2,1)S(1)} collective-permute-done((bf16[4,128,256]{2,1,0:T(8,128)(2,1)S(1)}, bf16[4,128,256]{2,1,0:T(8,128)(2,1)S(1)}, u32[]{:S(2)}, u32[]{:S(2)}) %collective-permute-start.1) | collective-permute-done | bytes 262176 | tf_op jit(solution)/shard_map/ppermute | solution.py:38
  23.3 1.6 %collective-permute-start.5 = (bf16[4,128,256]{2,1,0:T(8,128)(2,1)S(1)}, bf16[4,128,256]{2,1,0:T(8,128)(2,1)}, u32[]{:S(2)}, u32[]{:S(2)}) collective-permute-start(bf16[4,128,256]{2,1,0:T(8,128)(2,1)S(1)} %copy-done.3), channel_id=1, source_target_pairs={{0,4},{1,5},{2,6},{3,7},{4,8},{5,9},{6,10},{7,11},{8,12},{9,13},{1... | collective-permute-start | bytes 786440 | tf_op jit(solution)/shard_map/ppermute | solution.py:38
  24.9 3.9 %shard_map.86 = (s32[2,32]{1,0:T(2,128)}, s32[2,64]{1,0:T(2,128)}) custom-call(s32[16,16]{1,0:T(8,128)} %ids_ref.3), custom_call_target="tpu_custom_call" | custom-call | tf_op jit(solution)/shard_map/pallas_call | solution.py:160
  28.9 3.9 %collective-permute-done.3.refs_5_ = bf16[4,128,256]{2,1,0:T(8,128)(2,1)} collective-permute-done((bf16[4,128,256]{2,1,0:T(8,128)(2,1)S(1)}, bf16[4,128,256]{2,1,0:T(8,128)(2,1)}, u32[]{:S(2)}, u32[]{:S(2)}) %collective-permute-start.3) | collective-permute-done | bytes 262176 | tf_op jit(solution)/shard_map/ppermute | solution.py:38
  33.6 3.9 %shard_map.87 = (bf16[8,128,256]{2,1,0:T(8,128)(2,1)}, bf16[8,128,256]{2,1,0:T(8,128)(2,1)S(1)}, bf16[8,128,256]{2,1,0:T(8,128)(2,1)}, bf16[8,128,256]{2,1,0:T(8...) custom-call(s32[2,32]{1,0:T(2,128)S(1)} %copy-done.6, ...), custom_call_target="tpu_custom_call" | custom-call | tf_op jit(solution)/shard_map/pallas_call | solution.py:202
  37.5 1.5 %collective-permute-start.6 = (bf16[8,128,256]{2,1,0:T(8,128)(2,1)S(1)}, bf16[8,128,256]{2,1,0:T(8,128)(2,1)S(1)}, u32[]{:S(2)}, u32[]{:S(2)}) collective-permute-start(bf16[8,128,256]{2,1,0:T(8,128)(2,1)S(1)} %get-tuple-element.43), channel_id=1, source_target_pairs={{0,4},{1,5},{2,6},{3,7},{4,8},{5,9},{6,10},{7,11},{8,12},{9,13},{1... | collective-permute-start | bytes 1572872 | tf_op jit(solution)/shard_map/ppermute | solution.py:38
  39.0 1.3 collective-permute-start.7
  40.3 2.0 %collective-permute-start.8 = (bf16[8,128,256]{2,1,0:T(8,128)(2,1)}, bf16[8,128,256]{2,1,0:T(8,128)(2,1)}, u32[]{:S(2)}, u32[]{:S(2)}) collective-permute-start(bf16[8,128,256]{2,1,0:T(8,128)(2,1)} %get-tuple-element.45), channel_id=1, source_target_pairs={{0,12},{1,13},{2,14},{3,15},{4,0},{5,1},{6,2},{7,3},{8,4},{9,5},{1... | collective-permute-start | bytes 1572872 | tf_op jit(solution)/shard_map/ppermute | solution.py:38
  43.0 3.2 %collective-permute-start.10 = (bf16[8,128,256]{2,1,0:T(8,128)(2,1)}, bf16[8,128,256]{2,1,0:T(8,128)(2,1)}, u32[]{:S(2)}, u32[]{:S(2)}) collective-permute-start(bf16[8,128,256]{2,1,0:T(8,128)(2,1)} %get-tuple-element.48), channel_id=1, source_target_pairs={{0,2},{1,3},{2,0},{3,1},{4,6},{5,7},{6,4},{7,5},{8,10},{9,11},{10,... | collective-permute-start | bytes 1572872 | tf_op jit(solution)/shard_map/ppermute | solution.py:38
  46.2 6.2 %collective-permute-done.6.refs_1_ = bf16[8,128,256]{2,1,0:T(8,128)(2,1)S(1)} collective-permute-done((bf16[8,128,256]{2,1,0:T(8,128)(2,1)S(1)}, bf16[8,128,256]{2,1,0:T(8,128)(2,1)S(1)}, u32[]{:S(2)}, u32[]{:S(2)}) %collective-permute-start.6) | collective-permute-done | bytes 524320 | tf_op jit(solution)/shard_map/ppermute | solution.py:38
  52.4 2.4 %collective-permute-start.11 = (bf16[8,128,256]{2,1,0:T(8,128)(2,1)}, bf16[8,128,256]{2,1,0:T(8,128)(2,1)}, u32[]{:S(2)}, u32[]{:S(2)}) collective-permute-start(bf16[8,128,256]{2,1,0:T(8,128)(2,1)} %get-tuple-element.49), channel_id=1, source_target_pairs={{0,3},{1,0},{2,1},{3,2},{4,7},{5,4},{6,5},{7,6},{8,11},{9,8},{10,9... | collective-permute-start | bytes 1572872 | tf_op jit(solution)/shard_map/ppermute | solution.py:38
  55.6 9.4 %collective-permute-done.8.refs_3_ = bf16[8,128,256]{2,1,0:T(8,128)(2,1)} collective-permute-done((bf16[8,128,256]{2,1,0:T(8,128)(2,1)}, bf16[8,128,256]{2,1,0:T(8,128)(2,1)}, u32[]{:S(2)}, u32[]{:S(2)}) %collective-permute-start.8) | collective-permute-done | bytes 524320 | tf_op jit(solution)/shard_map/ppermute | solution.py:38
  65.0 3.8 %collective-permute-done.10.refs_6_ = bf16[8,128,256]{2,1,0:T(8,128)(2,1)} collective-permute-done((bf16[8,128,256]{2,1,0:T(8,128)(2,1)}, bf16[8,128,256]{2,1,0:T(8,128)(2,1)}, u32[]{:S(2)}, u32[]{:S(2)}) %collective-permute-start.10) | collective-permute-done | bytes 524320 | tf_op jit(solution)/shard_map/ppermute | solution.py:38
  68.7 12.0 %shard_map.88 = (bf16[16,128,256]{2,1,0:T(8,128)(2,1)}, bf16[8,128,256]{2,1,0:T(8,128)(2,1)}, bf16[8,128,256]{2,1,0:T(8,128)(2,1)}, bf16[8,128,256]{2,1,0:T(8,12...) custom-call(s32[16,16]{1,0:T(8,128)S(1)} %copy-done.4, ...), custom_call_target="tpu_custom_call" | custom-call | tf_op jit(solution)/shard_map/pallas_call | solution.py:387
  80.8 7.1 %all-to-all-start.1 = ((bf16[16,128,256]{2,1,0:T(8,128)(2,1)}), bf16[16,128,256]{2,1,0:T(8,128)(2,1)}, u32[]{:S(2)}, u32[]{:S(2)}) async-start(bf16[16,128,256]{2,1,0:T(8,128)(2,1)} %get-tuple-element.50), calls=%async_computation.1 | async-start | bytes 2097152 | tf_op jit(solution)/shard_map/all_to_all | solution.py:435
  89.5 1.4 collective-permute-start.14
  90.9 3.1 %collective-permute-start.15 = (bf16[8,128,256]{2,1,0:T(8,128)(2,1)}, bf16[8,128,256]{2,1,0:T(8,128)(2,1)S(1)}, u32[]{:S(2)}, u32[]{:S(2)}) collective-permute-start(bf16[8,128,256]{2,1,0:T(8,128)(2,1)} %get-tuple-element.57), channel_id=1, source_target_pairs={{0,3},{1,0},{2,1},{3,2},{4,7},{5,4},{6,5},{7,6},{8,11},{9,8},{10,9... | collective-permute-start | bytes 1572872 | tf_op jit(solution)/shard_map/ppermute | solution.py:38
  94.0 19.6 %collective-permute-done.12.refs_1_ = bf16[8,128,256]{2,1,0:T(8,128)(2,1)S(1)} collective-permute-done((bf16[8,128,256]{2,1,0:T(8,128)(2,1)}, bf16[8,128,256]{2,1,0:T(8,128)(2,1)S(1)}, u32[]{:S(2)}, u32[]{:S(2)}) %collective-permute-start.12) | collective-permute-done | bytes 524320 | tf_op jit(solution)/shard_map/ppermute | solution.py:38
  113.9 1.5 %collective-permute-done.14.refs_3_ = bf16[8,128,256]{2,1,0:T(8,128)(2,1)S(1)} collective-permute-done((bf16[8,128,256]{2,1,0:T(8,128)(2,1)}, bf16[8,128,256]{2,1,0:T(8,128)(2,1)S(1)}, u32[]{:S(2)}, u32[]{:S(2)}) %collective-permute-start.14) | collective-permute-done | bytes 524320 | tf_op jit(solution)/shard_map/ppermute | solution.py:38
  116.1 10.4 %collective-permute-done.17.refs_7_ = bf16[8,128,256]{2,1,0:T(8,128)(2,1)S(1)} collective-permute-done((bf16[8,128,256]{2,1,0:T(8,128)(2,1)S(1)}, bf16[8,128,256]{2,1,0:T(8,128)(2,1)S(1)}, u32[]{:S(2)}, u32[]{:S(2)}) %collective-permute-start.17) | collective-permute-done | bytes 524320 | tf_op jit(solution)/shard_map/ppermute | solution.py:38
  126.6 3.0 %shard_map.90 = (f32[4,128,256]{2,1,0:T(8,128)S(1)}, bf16[4,128,256]{2,1,0:T(8,128)(2,1)S(1)}, bf16[4,128,256]{2,1,0:T(8,128)(2,1)}, bf16[4,128,256]{2,1,0:T(8,1...) custom-call(s32[2,64]{1,0:T(2,128)S(1)} %copy-done.5, ...), custom_call_target="tpu_custom_call" | custom-call | tf_op jit(solution)/shard_map/pallas_call | solution.py:234
  129.5 2.9 %collective-permute-start.19 = (bf16[4,128,256]{2,1,0:T(8,128)(2,1)}, bf16[4,128,256]{2,1,0:T(8,128)(2,1)S(1)}, u32[]{:S(2)}, u32[]{:S(2)}) collective-permute-start(bf16[4,128,256]{2,1,0:T(8,128)(2,1)} %get-tuple-element.62), channel_id=1, source_target_pairs={{0,2},{1,3},{2,0},{3,1},{4,6},{5,7},{6,4},{7,5},{8,10},{9,11},{10,... | collective-permute-start | bytes 786440 | tf_op jit(solution)/shard_map/ppermute | solution.py:38
  132.8 7.1 %collective-permute-done.18.refs_1_ = bf16[4,128,256]{2,1,0:T(8,128)(2,1)S(1)} collective-permute-done((bf16[4,128,256]{2,1,0:T(8,128)(2,1)S(1)}, bf16[4,128,256]{2,1,0:T(8,128)(2,1)S(1)}, u32[]{:S(2)}, u32[]{:S(2)}) %collective-permute-start.18) | collective-permute-done | bytes 262176 | tf_op jit(solution)/shard_map/ppermute | solution.py:38
  139.9 2.3 %shard_map.89 = bf16[128,4096]{1,0:T(8,128)(2,1)} custom-call(bf16[16,128,256]{2,1,0:T(8,128)(2,1)} %all-to-all-done.1.in_ref), custom_call_target="tpu_custom_call" | custom-call | tf_op jit(solution)/shard_map/pallas_call | solution.py:106
  142.3 4.0 %collective-permute-done.23.refs_7_ = bf16[4,128,256]{2,1,0:T(8,128)(2,1)S(1)} collective-permute-done((bf16[4,128,256]{2,1,0:T(8,128)(2,1)S(1)}, bf16[4,128,256]{2,1,0:T(8,128)(2,1)S(1)}, u32[]{:S(2)}, u32[]{:S(2)}) %collective-permute-start.23) | collective-permute-done | bytes 262176 | tf_op jit(solution)/shard_map/ppermute | solution.py:38
  146.3 1.0 shard_map.91
  (53 shorter events, 6.1 us)
Async XLA Ops:
  3.8 50.9 %copy-start.9 = (s32[16,32,2]{1,2,0:T(2,128)S(1)}, s32[16,32,2]{1,2,0:T(2,128)}, u32[]{:S(2)}) copy-start(s32[16,32,2]{1,2,0:T(2,128)} %param.11) | copy-start | bytes 12292
  3.9 64.9 %all-to-all-start = ((bf16[16,2,128,256]{3,2,1,0:T(8,128)(2,1)}), bf16[16,2,128,256]{3,2,1,0:T(8,128)(2,1)S(1)}, u32[]{:S(2)}, u32[]{:S(2)}) async-start(bf16[16,2,128,256]{3,2,1,0:T(8,128)(2,1)} %shard_map.85), calls=%async_computation | async-start | bytes 4194304 | tf_op jit(solution)/shard_map/all_to_all | solution.py:430
  12.6 56.2 %copy-start.4 = (s32[16,16]{1,0:T(8,128)S(1)}, s32[16,16]{1,0:T(8,128)}, u32[]{:S(2)}) copy-start(s32[16,16]{1,0:T(8,128)} %ids_ref.3) | copy-start | bytes 3076
  12.6 10.7 %collective-permute-start.1 = (bf16[4,128,256]{2,1,0:T(8,128)(2,1)S(1)}, bf16[4,128,256]{2,1,0:T(8,128)(2,1)S(1)}, u32[]{:S(2)}, u32[]{:S(2)}) collective-permute-start(bf16[4,128,256]{2,1,0:T(8,128)(2,1)S(1)} %copy-done.2), channel_id=1, source_target_pairs={{0,2},{1,3},{2,0},{3,1},{4,6},{5,7},{6,4},{7,5},{8,10},{9,11},{10,... | collective-permute-start | bytes 786440 | tf_op jit(solution)/shard_map/ppermute | solution.py:38
  15.7 13.2 %collective-permute-start = (bf16[4,128,256]{2,1,0:T(8,128)(2,1)S(1)}, bf16[4,128,256]{2,1,0:T(8,128)(2,1)S(1)}, u32[]{:S(2)}, u32[]{:S(2)}) collective-permute-start(bf16[4,128,256]{2,1,0:T(8,128)(2,1)S(1)} %copy-done.2), channel_id=1, source_target_pairs={{0,3},{1,0},{2,1},{3,2},{4,7},{5,4},{6,5},{7,6},{8,11},{9,8},{10,9... | collective-permute-start | bytes 786440 | tf_op jit(solution)/shard_map/ppermute | solution.py:38
  16.9 12.0 %collective-permute-start.2 = (bf16[4,128,256]{2,1,0:T(8,128)(2,1)S(1)}, bf16[4,128,256]{2,1,0:T(8,128)(2,1)S(1)}, u32[]{:S(2)}, u32[]{:S(2)}) collective-permute-start(bf16[4,128,256]{2,1,0:T(8,128)(2,1)S(1)} %copy-done.2), channel_id=1, source_target_pairs={{0,1},{1,2},{2,3},{3,0},{4,5},{5,6},{6,7},{7,4},{8,9},{9,10},{10,1... | collective-permute-start | bytes 786440 | tf_op jit(solution)/shard_map/ppermute | solution.py:38
  17.7 11.1 %collective-permute-start.4 = (bf16[4,128,256]{2,1,0:T(8,128)(2,1)S(1)}, bf16[4,128,256]{2,1,0:T(8,128)(2,1)}, u32[]{:S(2)}, u32[]{:S(2)}) collective-permute-start(bf16[4,128,256]{2,1,0:T(8,128)(2,1)S(1)} %copy-done.3), channel_id=1, source_target_pairs={{0,8},{1,9},{2,10},{3,11},{4,12},{5,13},{6,14},{7,15},{8,0},{9,1},... | collective-permute-start | bytes 786440 | tf_op jit(solution)/shard_map/ppermute | solution.py:38
  20.0 12.7 %collective-permute-start.3 = (bf16[4,128,256]{2,1,0:T(8,128)(2,1)S(1)}, bf16[4,128,256]{2,1,0:T(8,128)(2,1)}, u32[]{:S(2)}, u32[]{:S(2)}) collective-permute-start(bf16[4,128,256]{2,1,0:T(8,128)(2,1)S(1)} %copy-done.3), channel_id=1, source_target_pairs={{0,12},{1,13},{2,14},{3,15},{4,0},{5,1},{6,2},{7,3},{8,4},{9,5},{1... | collective-permute-start | bytes 786440 | tf_op jit(solution)/shard_map/ppermute | solution.py:38
  23.3 9.5 %collective-permute-start.5 = (bf16[4,128,256]{2,1,0:T(8,128)(2,1)S(1)}, bf16[4,128,256]{2,1,0:T(8,128)(2,1)}, u32[]{:S(2)}, u32[]{:S(2)}) collective-permute-start(bf16[4,128,256]{2,1,0:T(8,128)(2,1)S(1)} %copy-done.3), channel_id=1, source_target_pairs={{0,4},{1,5},{2,6},{3,7},{4,8},{5,9},{6,10},{7,11},{8,12},{9,13},{1... | collective-permute-start | bytes 786440 | tf_op jit(solution)/shard_map/ppermute | solution.py:38
  37.5 14.9 %collective-permute-start.6 = (bf16[8,128,256]{2,1,0:T(8,128)(2,1)S(1)}, bf16[8,128,256]{2,1,0:T(8,128)(2,1)S(1)}, u32[]{:S(2)}, u32[]{:S(2)}) collective-permute-start(bf16[8,128,256]{2,1,0:T(8,128)(2,1)S(1)} %get-tuple-element.43), channel_id=1, source_target_pairs={{0,4},{1,5},{2,6},{3,7},{4,8},{5,9},{6,10},{7,11},{8,12},{9,13},{1... | collective-permute-start | bytes 1572872 | tf_op jit(solution)/shard_map/ppermute | solution.py:38
  39.0 16.6 %collective-permute-start.7 = (bf16[8,128,256]{2,1,0:T(8,128)(2,1)}, bf16[8,128,256]{2,1,0:T(8,128)(2,1)S(1)}, u32[]{:S(2)}, u32[]{:S(2)}) collective-permute-start(bf16[8,128,256]{2,1,0:T(8,128)(2,1)} %get-tuple-element.44), channel_id=1, source_target_pairs={{0,8},{1,9},{2,10},{3,11},{4,12},{5,13},{6,14},{7,15},{8,0},{9,1},... | collective-permute-start | bytes 1572872 | tf_op jit(solution)/shard_map/ppermute | solution.py:38
  40.3 24.6 %collective-permute-start.8 = (bf16[8,128,256]{2,1,0:T(8,128)(2,1)}, bf16[8,128,256]{2,1,0:T(8,128)(2,1)}, u32[]{:S(2)}, u32[]{:S(2)}) collective-permute-start(bf16[8,128,256]{2,1,0:T(8,128)(2,1)} %get-tuple-element.45), channel_id=1, source_target_pairs={{0,12},{1,13},{2,14},{3,15},{4,0},{5,1},{6,2},{7,3},{8,4},{9,5},{1... | collective-permute-start | bytes 1572872 | tf_op jit(solution)/shard_map/ppermute | solution.py:38
  42.4 22.6 %collective-permute-start.9 = (bf16[8,128,256]{2,1,0:T(8,128)(2,1)}, bf16[8,128,256]{2,1,0:T(8,128)(2,1)}, u32[]{:S(2)}, u32[]{:S(2)}) collective-permute-start(bf16[8,128,256]{2,1,0:T(8,128)(2,1)} %get-tuple-element.47), channel_id=1, source_target_pairs={{0,1},{1,2},{2,3},{3,0},{4,5},{5,6},{6,7},{7,4},{8,9},{9,10},{10,1... | collective-permute-start | bytes 1572872 | tf_op jit(solution)/shard_map/ppermute | solution.py:38
  43.0 25.8 %collective-permute-start.10 = (bf16[8,128,256]{2,1,0:T(8,128)(2,1)}, bf16[8,128,256]{2,1,0:T(8,128)(2,1)}, u32[]{:S(2)}, u32[]{:S(2)}) collective-permute-start(bf16[8,128,256]{2,1,0:T(8,128)(2,1)} %get-tuple-element.48), channel_id=1, source_target_pairs={{0,2},{1,3},{2,0},{3,1},{4,6},{5,7},{6,4},{7,5},{8,10},{9,11},{10,... | collective-permute-start | bytes 1572872 | tf_op jit(solution)/shard_map/ppermute | solution.py:38
  52.4 16.4 %collective-permute-start.11 = (bf16[8,128,256]{2,1,0:T(8,128)(2,1)}, bf16[8,128,256]{2,1,0:T(8,128)(2,1)}, u32[]{:S(2)}, u32[]{:S(2)}) collective-permute-start(bf16[8,128,256]{2,1,0:T(8,128)(2,1)} %get-tuple-element.49), channel_id=1, source_target_pairs={{0,3},{1,0},{2,1},{3,2},{4,7},{5,4},{6,5},{7,6},{8,11},{9,8},{10,9... | collective-permute-start | bytes 1572872 | tf_op jit(solution)/shard_map/ppermute | solution.py:38
  80.8 32.8 %copy-start.10 = (bf16[8,128,256]{2,1,0:T(8,128)(2,1)S(1)}, bf16[8,128,256]{2,1,0:T(8,128)(2,1)}, u32[]{:S(2)}) copy-start(bf16[8,128,256]{2,1,0:T(8,128)(2,1)} %get-tuple-element.59) | copy-start | bytes 1572868
  80.8 45.8 %copy-start = (bf16[8,128,256]{2,1,0:T(8,128)(2,1)S(1)}, bf16[8,128,256]{2,1,0:T(8,128)(2,1)}, u32[]{:S(2)}) copy-start(bf16[8,128,256]{2,1,0:T(8,128)(2,1)} %get-tuple-element.52.refs_0_) | copy-start | bytes 1572868
  80.8 45.8 %copy-start.1 = (bf16[8,128,256]{2,1,0:T(8,128)(2,1)S(1)}, bf16[8,128,256]{2,1,0:T(8,128)(2,1)}, u32[]{:S(2)}) copy-start(bf16[8,128,256]{2,1,0:T(8,128)(2,1)} %get-tuple-element.56.refs_4_) | copy-start | bytes 1572868
  80.8 45.8 %copy-start.5 = (s32[2,64]{1,0:T(2,128)S(1)}, s32[2,64]{1,0:T(2,128)}, u32[]{:S(2)}) copy-start(s32[2,64]{1,0:T(2,128)} %get-tuple-element.51.add_ref) | copy-start | bytes 1540
  80.8 59.1 %all-to-all-start.1 = ((bf16[16,128,256]{2,1,0:T(8,128)(2,1)}), bf16[16,128,256]{2,1,0:T(8,128)(2,1)}, u32[]{:S(2)}, u32[]{:S(2)}) async-start(bf16[16,128,256]{2,1,0:T(8,128)(2,1)} %get-tuple-element.50), calls=%async_computation.1 | async-start | bytes 2097152 | tf_op jit(solution)/shard_map/all_to_all | solution.py:435
  88.0 25.6 %collective-permute-start.12 = (bf16[8,128,256]{2,1,0:T(8,128)(2,1)}, bf16[8,128,256]{2,1,0:T(8,128)(2,1)S(1)}, u32[]{:S(2)}, u32[]{:S(2)}) collective-permute-start(bf16[8,128,256]{2,1,0:T(8,128)(2,1)} %get-tuple-element.53), channel_id=1, source_target_pairs={{0,12},{1,13},{2,14},{3,15},{4,0},{5,1},{6,2},{7,3},{8,4},{9,5},{1... | collective-permute-start | bytes 1572872 | tf_op jit(solution)/shard_map/ppermute | solution.py:38
  88.6 25.3 %collective-permute-start.13 = (bf16[8,128,256]{2,1,0:T(8,128)(2,1)}, bf16[8,128,256]{2,1,0:T(8,128)(2,1)S(1)}, u32[]{:S(2)}, u32[]{:S(2)}) collective-permute-start(bf16[8,128,256]{2,1,0:T(8,128)(2,1)} %get-tuple-element.54), channel_id=1, source_target_pairs={{0,8},{1,9},{2,10},{3,11},{4,12},{5,13},{6,14},{7,15},{8,0},{9,1},... | collective-permute-start | bytes 1572872 | tf_op jit(solution)/shard_map/ppermute | solution.py:38
  89.5 26.0 %collective-permute-start.14 = (bf16[8,128,256]{2,1,0:T(8,128)(2,1)}, bf16[8,128,256]{2,1,0:T(8,128)(2,1)S(1)}, u32[]{:S(2)}, u32[]{:S(2)}) collective-permute-start(bf16[8,128,256]{2,1,0:T(8,128)(2,1)} %get-tuple-element.55), channel_id=1, source_target_pairs={{0,4},{1,5},{2,6},{3,7},{4,8},{5,9},{6,10},{7,11},{8,12},{9,13},{1... | collective-permute-start | bytes 1572872 | tf_op jit(solution)/shard_map/ppermute | solution.py:38
  90.9 25.2 %collective-permute-start.15 = (bf16[8,128,256]{2,1,0:T(8,128)(2,1)}, bf16[8,128,256]{2,1,0:T(8,128)(2,1)S(1)}, u32[]{:S(2)}, u32[]{:S(2)}) collective-permute-start(bf16[8,128,256]{2,1,0:T(8,128)(2,1)} %get-tuple-element.57), channel_id=1, source_target_pairs={{0,3},{1,0},{2,1},{3,2},{4,7},{5,4},{6,5},{7,6},{8,11},{9,8},{10,9... | collective-permute-start | bytes 1572872 | tf_op jit(solution)/shard_map/ppermute | solution.py:38
  94.0 22.2 %collective-permute-start.16 = (bf16[8,128,256]{2,1,0:T(8,128)(2,1)S(1)}, bf16[8,128,256]{2,1,0:T(8,128)(2,1)S(1)}, u32[]{:S(2)}, u32[]{:S(2)}) collective-permute-start(bf16[8,128,256]{2,1,0:T(8,128)(2,1)S(1)} %copy-done.11), channel_id=1, source_target_pairs={{0,2},{1,3},{2,0},{3,1},{4,6},{5,7},{6,4},{7,5},{8,10},{9,11},{10,... | collective-permute-start | bytes 1572872 | tf_op jit(solution)/shard_map/ppermute | solution.py:38
  113.6 13.0 %collective-permute-start.17 = (bf16[8,128,256]{2,1,0:T(8,128)(2,1)S(1)}, bf16[8,128,256]{2,1,0:T(8,128)(2,1)S(1)}, u32[]{:S(2)}, u32[]{:S(2)}) collective-permute-start(bf16[8,128,256]{2,1,0:T(8,128)(2,1)S(1)} %copy-done.10), channel_id=1, source_target_pairs={{0,1},{1,2},{2,3},{3,0},{4,5},{5,6},{6,7},{7,4},{8,9},{9,10},{10,1... | collective-permute-start | bytes 1572872 | tf_op jit(solution)/shard_map/ppermute | solution.py:38
  129.5 10.4 %collective-permute-start.18 = (bf16[4,128,256]{2,1,0:T(8,128)(2,1)S(1)}, bf16[4,128,256]{2,1,0:T(8,128)(2,1)S(1)}, u32[]{:S(2)}, u32[]{:S(2)}) collective-permute-start(bf16[4,128,256]{2,1,0:T(8,128)(2,1)S(1)} %get-tuple-element.61), channel_id=1, source_target_pairs={{0,1},{1,2},{2,3},{3,0},{4,5},{5,6},{6,7},{7,4},{8,9},{9,10},{10,1... | collective-permute-start | bytes 786440 | tf_op jit(solution)/shard_map/ppermute | solution.py:38
  129.5 12.7 %collective-permute-start.19 = (bf16[4,128,256]{2,1,0:T(8,128)(2,1)}, bf16[4,128,256]{2,1,0:T(8,128)(2,1)S(1)}, u32[]{:S(2)}, u32[]{:S(2)}) collective-permute-start(bf16[4,128,256]{2,1,0:T(8,128)(2,1)} %get-tuple-element.62), channel_id=1, source_target_pairs={{0,2},{1,3},{2,0},{3,1},{4,6},{5,7},{6,4},{7,5},{8,10},{9,11},{10,... | collective-permute-start | bytes 786440 | tf_op jit(solution)/shard_map/ppermute | solution.py:38
  132.5 9.8 %collective-permute-start.20 = (bf16[4,128,256]{2,1,0:T(8,128)(2,1)}, bf16[4,128,256]{2,1,0:T(8,128)(2,1)S(1)}, u32[]{:S(2)}, u32[]{:S(2)}) collective-permute-start(bf16[4,128,256]{2,1,0:T(8,128)(2,1)} %get-tuple-element.63), channel_id=1, source_target_pairs={{0,3},{1,0},{2,1},{3,2},{4,7},{5,4},{6,5},{7,6},{8,11},{9,8},{10,9... | collective-permute-start | bytes 786440 | tf_op jit(solution)/shard_map/ppermute | solution.py:38
  132.8 9.5 %collective-permute-start.21 = (bf16[4,128,256]{2,1,0:T(8,128)(2,1)S(1)}, bf16[4,128,256]{2,1,0:T(8,128)(2,1)S(1)}, u32[]{:S(2)}, u32[]{:S(2)}) collective-permute-start(bf16[4,128,256]{2,1,0:T(8,128)(2,1)S(1)} %get-tuple-element.65), channel_id=1, source_target_pairs={{0,4},{1,5},{2,6},{3,7},{4,8},{5,9},{6,10},{7,11},{8,12},{9,13},{1... | collective-permute-start | bytes 786440 | tf_op jit(solution)/shard_map/ppermute | solution.py:38
  132.8 9.5 %collective-permute-start.22 = (bf16[4,128,256]{2,1,0:T(8,128)(2,1)S(1)}, bf16[4,128,256]{2,1,0:T(8,128)(2,1)S(1)}, u32[]{:S(2)}, u32[]{:S(2)}) collective-permute-start(bf16[4,128,256]{2,1,0:T(8,128)(2,1)S(1)} %get-tuple-element.66), channel_id=1, source_target_pairs={{0,8},{1,9},{2,10},{3,11},{4,12},{5,13},{6,14},{7,15},{8,0},{9,1},... | collective-permute-start | bytes 786440 | tf_op jit(solution)/shard_map/ppermute | solution.py:38
  139.9 6.4 %collective-permute-start.23 = (bf16[4,128,256]{2,1,0:T(8,128)(2,1)S(1)}, bf16[4,128,256]{2,1,0:T(8,128)(2,1)S(1)}, u32[]{:S(2)}, u32[]{:S(2)}) collective-permute-start(bf16[4,128,256]{2,1,0:T(8,128)(2,1)S(1)} %get-tuple-element.67), channel_id=1, source_target_pairs={{0,12},{1,13},{2,14},{3,15},{4,0},{5,1},{6,2},{7,3},{8,4},{9,5},{1... | collective-permute-start | bytes 786440 | tf_op jit(solution)/shard_map/ppermute | solution.py:38
  (6 other events, 66.0 us)

commit v5 on v4

--- a/solution.py
+++ b/solution.py
@@ -38,23 +38,20 @@
     return lax.ppermute(value, "dp", pairs)
 
 
-DISTANCES = (2, 1, 3)
-
-
-def gather_lines(lines):
-    parts = [[own, None, None, None] for own, _ in lines]
-    for distance in DISTANCES:
-        for part, (own, axis) in zip(parts, lines):
-            part[distance] = shift(own, axis, -distance)
-    return parts
-
-
 def exchange_lines(lines):
     parts = [list(chunks) for chunks, _, _ in lines]
-    for distance in DISTANCES:
-        for part, (chunks, axis, sign) in zip(parts, lines):
-            part[distance] = shift(chunks[distance], axis, sign * distance)
+    for n, distances in ((0, (2, 1, 3)), (1, (1, 3, 2))):
+        chunks, axis, sign = lines[n]
+        for distance in distances:
+            value = chunks[distance]
+            if n == 1 and distance == 2:
+                value, parts[n][1] = lax.optimization_barrier((value, parts[n][1]))
+            parts[n][distance] = shift(value, axis, sign * distance)
     return parts
+
+
+def gather_lines(keys, values):
+    return exchange_lines((((keys,) * SIDE, "x", -1), ((values,) * SIDE, "y", -1)))
 
 
 def chunk_shapes(most, nbr, width, own_type=BF16):
@@ -425,7 +422,7 @@
     owned = neighbour_keys.shape[0]
     most = SIDE * (owned // 2)
     take, add = tables(distinct_ids, owned, most)
-    lines = gather_lines(((neighbour_keys, "x"), (neighbour_values, "y")))
+    lines = gather_lines(neighbour_keys, neighbour_values)
     packed = pack_heads(queries[0], grad_out[0], parts)
     tokens = lax.all_to_all(packed, "ctx", split_axis=0, concat_axis=0, tiled=True)
     keys, values = select(take, *lines, most)

time: 148 us -> 139 us (0.939)
  waiting for transfers between devices: 69.4 us -> 51.5 us
  starting transfers between devices: 46.8 us -> 55.5 us
    ppermute x24, waiting for transfers between devices: 69.4 us -> 51.5 us  [shift(): return lax.ppermute(value, 'dp', pairs)]
    ppermute x24, starting transfers between devices: 31 us -> 40.2 us  [shift(): return lax.ppermute(value, 'dp', pairs)]
  transfers between devices with their start and end apart: 26 -> 26, of which waited for: 13 -> 14; matrix products, arithmetic and copies ran while one was open for 0% -> 0% of each run, Pallas kernels for 9% -> 9%
where the time goes in v5:
time: 139 us; the launch traced here: 138 us
  starting transfers between devices  55.5 us (40%)
  waiting for transfers between devices  51.5 us (37%)
  Pallas kernels  29.3 us (21%)
    ppermute x24, waiting for transfers between devices, shift(): return lax.ppermute(value, 'dp', pairs)  51.5 us
    ppermute x24, starting transfers between devices, shift(): return lax.ppermute(value, 'dp', pairs)  40.2 us
    pallas_call x1, Pallas kernels, attend(): pl.pallas_call(functools.partial(attend_body, groups, distinct, owned, mo...  12 us
    all_to_all x1, starting transfers between devices, on_device(): lax.all_to_all(packed, 'ctx', split_axis=0, concat_axis=0, tiled=True)  8.71 us
    all_to_all x1, starting transfers between devices, on_device(): back = lax.all_to_all(back, 'ctx', split_axis=0, concat_axis=0, tiled=True)  6.6 us
    pallas_call x1, Pallas kernels, tables(): pl.pallas_call(functools.partial(tables_body, owned, most), out_shape=(ja...  3.94 us
    pallas_call x1, Pallas kernels, select(): pl.pallas_call(select_body, out_shape=((pltpu.HBM(shapes[0].shape, BF16),...  3.9 us
    pallas_call x1, Pallas kernels, pack_heads(): pl.pallas_call(functools.partial(pack_heads_body, parts, width), out_shap...  3.18 us
  transfers between devices with their start and end apart: 26, of which 14 were waited for; matrix products, arithmetic and copies ran while one was open for 0% of the time, Pallas kernels for 9%

profile of v5, /device:TPU:8, one launch (start us, length us, event | category | flops | bytes accessed | tf_op | source)
XLA Modules:
  0.0 138.1 jit_solution(6140111611777443006)
XLA Ops:
  0.6 3.2 %shard_map.85 = bf16[16,2,128,256]{3,2,1,0:T(8,128)(2,1)} custom-call(bf16[128,4096]{1,0:T(8,128)(2,1)} %bitcast.5, bf16[128,4096]{1,0:T(8,128)(2,1)} %bitcast.6), custom_call_target="tpu_custom_call" | custom-call | tf_op jit(solution)/shard_map/pallas_call | solution.py:81
  3.9 8.7 %all-to-all-start = ((bf16[16,2,128,256]{3,2,1,0:T(8,128)(2,1)}), bf16[16,2,128,256]{3,2,1,0:T(8,128)(2,1)S(1)}, u32[]{:S(2)}, u32[]{:S(2)}) async-start(bf16[16,2,128,256]{3,2,1,0:T(8,128)(2,1)} %shard_map.85), calls=%async_computation | async-start | bytes 4194304 | tf_op jit(solution)/shard_map/all_to_all | solution.py:427
  13.1 3.0 %collective-permute-start.1 = (bf16[4,128,256]{2,1,0:T(8,128)(2,1)S(1)}, bf16[4,128,256]{2,1,0:T(8,128)(2,1)S(1)}, u32[]{:S(2)}, u32[]{:S(2)}) collective-permute-start(bf16[4,128,256]{2,1,0:T(8,128)(2,1)S(1)} %copy-done.2), channel_id=1, source_target_pairs={{0,2},{1,3},{2,0},{3,1},{4,6},{5,7},{6,4},{7,5},{8,10},{9,11},{10,... | collective-permute-start | bytes 786440 | tf_op jit(solution)/shard_map/ppermute | solution.py:38
  18.2 1.6 %collective-permute-start.5 = (bf16[4,128,256]{2,1,0:T(8,128)(2,1)S(1)}, bf16[4,128,256]{2,1,0:T(8,128)(2,1)}, u32[]{:S(2)}, u32[]{:S(2)}) collective-permute-start(bf16[4,128,256]{2,1,0:T(8,128)(2,1)S(1)} %copy-done.3), channel_id=1, source_target_pairs={{0,4},{1,5},{2,6},{3,7},{4,8},{5,9},{6,10},{7,11},{8,12},{9,13},{1... | collective-permute-start | bytes 786440 | tf_op jit(solution)/shard_map/ppermute | solution.py:38
  19.8 1.6 %collective-permute-done.3.refs_5_ = bf16[4,128,256]{2,1,0:T(8,128)(2,1)S(1)} collective-permute-done((bf16[4,128,256]{2,1,0:T(8,128)(2,1)S(1)}, bf16[4,128,256]{2,1,0:T(8,128)(2,1)S(1)}, u32[]{:S(2)}, u32[]{:S(2)}) %collective-permute-start.3) | collective-permute-done | bytes 262176 | tf_op jit(solution)/shard_map/ppermute | solution.py:38
  21.3 3.5 %collective-permute-start.4 = (bf16[4,128,256]{2,1,0:T(8,128)(2,1)S(1)}, bf16[4,128,256]{2,1,0:T(8,128)(2,1)}, u32[]{:S(2)}, u32[]{:S(2)}) collective-permute-start(bf16[4,128,256]{2,1,0:T(8,128)(2,1)S(1)} %copy-done.3), channel_id=1, source_target_pairs={{0,8},{1,9},{2,10},{3,11},{4,12},{5,13},{6,14},{7,15},{8,0},{9,1},... | collective-permute-start | bytes 786440 | tf_op jit(solution)/shard_map/ppermute | solution.py:38
  24.8 3.9 %shard_map.86 = (s32[2,32]{1,0:T(2,128)}, s32[2,64]{1,0:T(2,128)}) custom-call(s32[16,16]{1,0:T(8,128)} %ids_ref.3), custom_call_target="tpu_custom_call" | custom-call | tf_op jit(solution)/shard_map/pallas_call | solution.py:157
  28.8 2.2 %collective-permute-done.4.refs_6_ = bf16[4,128,256]{2,1,0:T(8,128)(2,1)} collective-permute-done((bf16[4,128,256]{2,1,0:T(8,128)(2,1)S(1)}, bf16[4,128,256]{2,1,0:T(8,128)(2,1)}, u32[]{:S(2)}, u32[]{:S(2)}) %collective-permute-start.4) | collective-permute-done | bytes 262176 | tf_op jit(solution)/shard_map/ppermute | solution.py:38
  31.7 3.9 %shard_map.87 = (bf16[8,128,256]{2,1,0:T(8,128)(2,1)}, bf16[8,128,256]{2,1,0:T(8,128)(2,1)}, bf16[8,128,256]{2,1,0:T(8,128)(2,1)}, bf16[8,128,256]{2,1,0:T(8,128...) custom-call(s32[2,32]{1,0:T(2,128)S(1)} %copy-done.6, ...), custom_call_target="tpu_custom_call" | custom-call | tf_op jit(solution)/shard_map/pallas_call | solution.py:199
  35.6 1.6 %collective-permute-start.9 = (bf16[8,128,256]{2,1,0:T(8,128)(2,1)S(1)}, bf16[8,128,256]{2,1,0:T(8,128)(2,1)S(1)}, u32[]{:S(2)}, u32[]{:S(2)}) collective-permute-start(bf16[8,128,256]{2,1,0:T(8,128)(2,1)S(1)} %get-tuple-element.58), channel_id=1, source_target_pairs={{0,1},{1,2},{2,3},{3,0},{4,5},{5,6},{6,7},{7,4},{8,9},{9,10},{10,1... | collective-permute-start | bytes 1572872 | tf_op jit(solution)/shard_map/ppermute | solution.py:38
  37.2 2.2 %collective-permute-start.6 = (bf16[8,128,256]{2,1,0:T(8,128)(2,1)}, bf16[8,128,256]{2,1,0:T(8,128)(2,1)S(1)}, u32[]{:S(2)}, u32[]{:S(2)}) collective-permute-start(bf16[8,128,256]{2,1,0:T(8,128)(2,1)} %get-tuple-element.53), channel_id=1, source_target_pairs={{0,4},{1,5},{2,6},{3,7},{4,8},{5,9},{6,10},{7,11},{8,12},{9,13},{1... | collective-permute-start | bytes 1572872 | tf_op jit(solution)/shard_map/ppermute | solution.py:38
  39.4 3.6 %collective-permute-start.7 = (bf16[8,128,256]{2,1,0:T(8,128)(2,1)}, bf16[8,128,256]{2,1,0:T(8,128)(2,1)}, u32[]{:S(2)}, u32[]{:S(2)}) collective-permute-start(bf16[8,128,256]{2,1,0:T(8,128)(2,1)} %get-tuple-element.54), channel_id=1, source_target_pairs={{0,8},{1,9},{2,10},{3,11},{4,12},{5,13},{6,14},{7,15},{8,0},{9,1},... | collective-permute-start | bytes 1572872 | tf_op jit(solution)/shard_map/ppermute | solution.py:38
  43.1 2.6 %collective-permute-start.11 = (bf16[8,128,256]{2,1,0:T(8,128)(2,1)}, bf16[8,128,256]{2,1,0:T(8,128)(2,1)}, u32[]{:S(2)}, u32[]{:S(2)}) collective-permute-start(bf16[8,128,256]{2,1,0:T(8,128)(2,1)} %get-tuple-element.61), channel_id=1, source_target_pairs={{0,3},{1,0},{2,1},{3,2},{4,7},{5,4},{6,5},{7,6},{8,11},{9,8},{10,9... | collective-permute-start | bytes 1572872 | tf_op jit(solution)/shard_map/ppermute | solution.py:38
  45.6 4.1 %collective-permute-done.9.refs_5_ = bf16[8,128,256]{2,1,0:T(8,128)(2,1)S(1)} collective-permute-done((bf16[8,128,256]{2,1,0:T(8,128)(2,1)S(1)}, bf16[8,128,256]{2,1,0:T(8,128)(2,1)S(1)}, u32[]{:S(2)}, u32[]{:S(2)}) %collective-permute-start.9) | collective-permute-done | bytes 524320 | tf_op jit(solution)/shard_map/ppermute | solution.py:38
  49.8 1.8 %collective-permute-start.10 = (bf16[8,128,256]{2,1,0:T(8,128)(2,1)}, bf16[8,128,256]{2,1,0:T(8,128)(2,1)}, u32[]{:S(2)}, u32[]{:S(2)}) collective-permute-start(bf16[8,128,256]{2,1,0:T(8,128)(2,1)} %get-tuple-element.60), channel_id=1, source_target_pairs={{0,2},{1,3},{2,0},{3,1},{4,6},{5,7},{6,4},{7,5},{8,10},{9,11},{10,... | collective-permute-start | bytes 1572872 | tf_op jit(solution)/shard_map/ppermute | solution.py:38
  51.7 9.6 %collective-permute-done.6.refs_1_ = bf16[8,128,256]{2,1,0:T(8,128)(2,1)S(1)} collective-permute-done((bf16[8,128,256]{2,1,0:T(8,128)(2,1)}, bf16[8,128,256]{2,1,0:T(8,128)(2,1)S(1)}, u32[]{:S(2)}, u32[]{:S(2)}) %collective-permute-start.6) | collective-permute-done | bytes 524320 | tf_op jit(solution)/shard_map/ppermute | solution.py:38
  61.3 3.6 %collective-permute-done.8.refs_3_ = bf16[8,128,256]{2,1,0:T(8,128)(2,1)} collective-permute-done((bf16[8,128,256]{2,1,0:T(8,128)(2,1)}, bf16[8,128,256]{2,1,0:T(8,128)(2,1)}, u32[]{:S(2)}, u32[]{:S(2)}) %collective-permute-start.8) | collective-permute-done | bytes 524320 | tf_op jit(solution)/shard_map/ppermute | solution.py:38
  65.4 12.0 %shard_map.88 = (bf16[16,128,256]{2,1,0:T(8,128)(2,1)}, bf16[8,128,256]{2,1,0:T(8,128)(2,1)}, bf16[8,128,256]{2,1,0:T(8,128)(2,1)}, bf16[8,128,256]{2,1,0:T(8,12...) custom-call(s32[16,16]{1,0:T(8,128)S(1)} %copy-done.4, ...), custom_call_target="tpu_custom_call" | custom-call | tf_op jit(solution)/shard_map/pallas_call | solution.py:384
  77.5 6.6 %all-to-all-start.1 = ((bf16[16,128,256]{2,1,0:T(8,128)(2,1)}), bf16[16,128,256]{2,1,0:T(8,128)(2,1)}, u32[]{:S(2)}, u32[]{:S(2)}) async-start(bf16[16,128,256]{2,1,0:T(8,128)(2,1)} %get-tuple-element.62), calls=%async_computation.1 | async-start | bytes 2097152 | tf_op jit(solution)/shard_map/all_to_all | solution.py:432
  84.1 3.9 %collective-permute-start.15 = (bf16[8,128,256]{2,1,0:T(8,128)(2,1)}, bf16[8,128,256]{2,1,0:T(8,128)(2,1)S(1)}, u32[]{:S(2)}, u32[]{:S(2)}) collective-permute-start(bf16[8,128,256]{2,1,0:T(8,128)(2,1)} %get-tuple-element.70), channel_id=1, source_target_pairs={{0,3},{1,0},{2,1},{3,2},{4,7},{5,4},{6,5},{7,6},{8,11},{9,8},{10,9... | collective-permute-start | bytes 1572872 | tf_op jit(solution)/shard_map/ppermute | solution.py:38
  88.0 2.1 %collective-permute-start.12 = (bf16[8,128,256]{2,1,0:T(8,128)(2,1)}, bf16[8,128,256]{2,1,0:T(8,128)(2,1)S(1)}, u32[]{:S(2)}, u32[]{:S(2)}) collective-permute-start(bf16[8,128,256]{2,1,0:T(8,128)(2,1)} %get-tuple-element.65), channel_id=1, source_target_pairs={{0,12},{1,13},{2,14},{3,15},{4,0},{5,1},{6,2},{7,3},{8,4},{9,5},{1... | collective-permute-start | bytes 1572872 | tf_op jit(solution)/shard_map/ppermute | solution.py:38
  91.9 7.9 %collective-permute-done.15.refs_5_ = bf16[8,128,256]{2,1,0:T(8,128)(2,1)S(1)} collective-permute-done((bf16[8,128,256]{2,1,0:T(8,128)(2,1)}, bf16[8,128,256]{2,1,0:T(8,128)(2,1)S(1)}, u32[]{:S(2)}, u32[]{:S(2)}) %collective-permute-start.15) | collective-permute-done | bytes 524320 | tf_op jit(solution)/shard_map/ppermute | solution.py:38
  99.8 2.1 %collective-permute-start.16 = (bf16[8,128,256]{2,1,0:T(8,128)(2,1)S(1)}, bf16[8,128,256]{2,1,0:T(8,128)(2,1)S(1)}, u32[]{:S(2)}, u32[]{:S(2)}) collective-permute-start(bf16[8,128,256]{2,1,0:T(8,128)(2,1)S(1)} %copy-done.10), channel_id=1, source_target_pairs={{0,2},{1,3},{2,0},{3,1},{4,6},{5,7},{6,4},{7,5},{8,10},{9,11},{10,... | collective-permute-start | bytes 1572872 | tf_op jit(solution)/shard_map/ppermute | solution.py:38
  102.8 11.5 %collective-permute-done.13.refs_2_ = bf16[8,128,256]{2,1,0:T(8,128)(2,1)S(1)} collective-permute-done((bf16[8,128,256]{2,1,0:T(8,128)(2,1)}, bf16[8,128,256]{2,1,0:T(8,128)(2,1)S(1)}, u32[]{:S(2)}, u32[]{:S(2)}) %collective-permute-start.13) | collective-permute-done | bytes 524320 | tf_op jit(solution)/shard_map/ppermute | solution.py:38
  114.9 2.2 %collective-permute-done.17.refs_7_ = bf16[8,128,256]{2,1,0:T(8,128)(2,1)S(1)} collective-permute-done((bf16[8,128,256]{2,1,0:T(8,128)(2,1)S(1)}, bf16[8,128,256]{2,1,0:T(8,128)(2,1)S(1)}, u32[]{:S(2)}, u32[]{:S(2)}) %collective-permute-start.17) | collective-permute-done | bytes 524320 | tf_op jit(solution)/shard_map/ppermute | solution.py:38
  117.2 3.0 %shard_map.90 = (f32[4,128,256]{2,1,0:T(8,128)S(1)}, bf16[4,128,256]{2,1,0:T(8,128)(2,1)}, bf16[4,128,256]{2,1,0:T(8,128)(2,1)}, bf16[4,128,256]{2,1,0:T(8,128)(...) custom-call(s32[2,64]{1,0:T(2,128)S(1)} %copy-done.5, ...), custom_call_target="tpu_custom_call" | custom-call | tf_op jit(solution)/shard_map/pallas_call | solution.py:231
  120.1 2.3 %collective-permute-start.21 = (bf16[4,128,256]{2,1,0:T(8,128)(2,1)S(1)}, bf16[4,128,256]{2,1,0:T(8,128)(2,1)S(1)}, u32[]{:S(2)}, u32[]{:S(2)}) collective-permute-start(bf16[4,128,256]{2,1,0:T(8,128)(2,1)S(1)} %get-tuple-element.80), channel_id=1, source_target_pairs={{0,4},{1,5},{2,6},{3,7},{4,8},{5,9},{6,10},{7,11},{8,12},{9,13},{1... | collective-permute-start | bytes 786440 | tf_op jit(solution)/shard_map/ppermute | solution.py:38
  122.5 1.8 %collective-permute-start.19 = (bf16[4,128,256]{2,1,0:T(8,128)(2,1)}, bf16[4,128,256]{2,1,0:T(8,128)(2,1)S(1)}, u32[]{:S(2)}, u32[]{:S(2)}) collective-permute-start(bf16[4,128,256]{2,1,0:T(8,128)(2,1)} %get-tuple-element.76), channel_id=1, source_target_pairs={{0,2},{1,3},{2,0},{3,1},{4,6},{5,7},{6,4},{7,5},{8,10},{9,11},{10,... | collective-permute-start | bytes 786440 | tf_op jit(solution)/shard_map/ppermute | solution.py:38
  126.5 2.3 %collective-permute-start.22 = (bf16[4,128,256]{2,1,0:T(8,128)(2,1)S(1)}, bf16[4,128,256]{2,1,0:T(8,128)(2,1)S(1)}, u32[]{:S(2)}, u32[]{:S(2)}) collective-permute-start(bf16[4,128,256]{2,1,0:T(8,128)(2,1)S(1)} %get-tuple-element.82), channel_id=1, source_target_pairs={{0,8},{1,9},{2,10},{3,11},{4,12},{5,13},{6,14},{7,15},{8,0},{9,1},... | collective-permute-start | bytes 786440 | tf_op jit(solution)/shard_map/ppermute | solution.py:38
  128.8 2.3 %shard_map.89 = bf16[128,4096]{1,0:T(8,128)(2,1)} custom-call(bf16[16,128,256]{2,1,0:T(8,128)(2,1)} %all-to-all-done.1.in_ref), custom_call_target="tpu_custom_call" | custom-call | tf_op jit(solution)/shard_map/pallas_call | solution.py:103
  131.1 4.0 %collective-permute-done.18.refs_1_ = bf16[4,128,256]{2,1,0:T(8,128)(2,1)S(1)} collective-permute-done((bf16[4,128,256]{2,1,0:T(8,128)(2,1)}, bf16[4,128,256]{2,1,0:T(8,128)(2,1)S(1)}, u32[]{:S(2)}, u32[]{:S(2)}) %collective-permute-start.18) | collective-permute-done | bytes 262176 | tf_op jit(solution)/shard_map/ppermute | solution.py:38
  135.1 2.0 %collective-permute-done.23.refs_7_ = bf16[4,128,256]{2,1,0:T(8,128)(2,1)S(1)} collective-permute-done((bf16[4,128,256]{2,1,0:T(8,128)(2,1)S(1)}, bf16[4,128,256]{2,1,0:T(8,128)(2,1)S(1)}, u32[]{:S(2)}, u32[]{:S(2)}) %collective-permute-start.23) | collective-permute-done | bytes 262176 | tf_op jit(solution)/shard_map/ppermute | solution.py:38
  (53 shorter events, 10.5 us)
Async XLA Ops:
  3.8 47.8 %copy-start.9 = (s32[16,32,2]{1,2,0:T(2,128)S(1)}, s32[16,32,2]{1,2,0:T(2,128)}, u32[]{:S(2)}) copy-start(s32[16,32,2]{1,2,0:T(2,128)} %param.11) | copy-start | bytes 12292
  3.9 61.5 %all-to-all-start = ((bf16[16,2,128,256]{3,2,1,0:T(8,128)(2,1)}), bf16[16,2,128,256]{3,2,1,0:T(8,128)(2,1)S(1)}, u32[]{:S(2)}, u32[]{:S(2)}) async-start(bf16[16,2,128,256]{3,2,1,0:T(8,128)(2,1)} %shard_map.85), calls=%async_computation | async-start | bytes 4194304 | tf_op jit(solution)/shard_map/all_to_all | solution.py:427
  12.6 52.8 %copy-start.4 = (s32[16,16]{1,0:T(8,128)S(1)}, s32[16,16]{1,0:T(8,128)}, u32[]{:S(2)}) copy-start(s32[16,16]{1,0:T(8,128)} %ids_ref.3) | copy-start | bytes 3076
  12.6 8.7 %collective-permute-start.3 = (bf16[4,128,256]{2,1,0:T(8,128)(2,1)S(1)}, bf16[4,128,256]{2,1,0:T(8,128)(2,1)S(1)}, u32[]{:S(2)}, u32[]{:S(2)}) collective-permute-start(bf16[4,128,256]{2,1,0:T(8,128)(2,1)S(1)} %copy-done.3), channel_id=1, source_target_pairs={{0,12},{1,13},{2,14},{3,15},{4,0},{5,1},{6,2},{7,3},{8,4},{9,5},{1... | collective-permute-start | bytes 786440 | tf_op jit(solution)/shard_map/ppermute | solution.py:38
  13.1 15.6 %collective-permute-start.1 = (bf16[4,128,256]{2,1,0:T(8,128)(2,1)S(1)}, bf16[4,128,256]{2,1,0:T(8,128)(2,1)S(1)}, u32[]{:S(2)}, u32[]{:S(2)}) collective-permute-start(bf16[4,128,256]{2,1,0:T(8,128)(2,1)S(1)} %copy-done.2), channel_id=1, source_target_pairs={{0,2},{1,3},{2,0},{3,1},{4,6},{5,7},{6,4},{7,5},{8,10},{9,11},{10,... | collective-permute-start | bytes 786440 | tf_op jit(solution)/shard_map/ppermute | solution.py:38
  16.2 12.6 %collective-permute-start = (bf16[4,128,256]{2,1,0:T(8,128)(2,1)S(1)}, bf16[4,128,256]{2,1,0:T(8,128)(2,1)S(1)}, u32[]{:S(2)}, u32[]{:S(2)}) collective-permute-start(bf16[4,128,256]{2,1,0:T(8,128)(2,1)S(1)} %copy-done.2), channel_id=1, source_target_pairs={{0,3},{1,0},{2,1},{3,2},{4,7},{5,4},{6,5},{7,6},{8,11},{9,8},{10,9... | collective-permute-start | bytes 786440 | tf_op jit(solution)/shard_map/ppermute | solution.py:38
  17.3 11.5 %collective-permute-start.2 = (bf16[4,128,256]{2,1,0:T(8,128)(2,1)S(1)}, bf16[4,128,256]{2,1,0:T(8,128)(2,1)}, u32[]{:S(2)}, u32[]{:S(2)}) collective-permute-start(bf16[4,128,256]{2,1,0:T(8,128)(2,1)S(1)} %copy-done.2), channel_id=1, source_target_pairs={{0,1},{1,2},{2,3},{3,0},{4,5},{5,6},{6,7},{7,4},{8,9},{9,10},{10,1... | collective-permute-start | bytes 786440 | tf_op jit(solution)/shard_map/ppermute | solution.py:38
  18.2 10.6 %collective-permute-start.5 = (bf16[4,128,256]{2,1,0:T(8,128)(2,1)S(1)}, bf16[4,128,256]{2,1,0:T(8,128)(2,1)}, u32[]{:S(2)}, u32[]{:S(2)}) collective-permute-start(bf16[4,128,256]{2,1,0:T(8,128)(2,1)S(1)} %copy-done.3), channel_id=1, source_target_pairs={{0,4},{1,5},{2,6},{3,7},{4,8},{5,9},{6,10},{7,11},{8,12},{9,13},{1... | collective-permute-start | bytes 786440 | tf_op jit(solution)/shard_map/ppermute | solution.py:38
  21.3 9.7 %collective-permute-start.4 = (bf16[4,128,256]{2,1,0:T(8,128)(2,1)S(1)}, bf16[4,128,256]{2,1,0:T(8,128)(2,1)}, u32[]{:S(2)}, u32[]{:S(2)}) collective-permute-start(bf16[4,128,256]{2,1,0:T(8,128)(2,1)S(1)} %copy-done.3), channel_id=1, source_target_pairs={{0,8},{1,9},{2,10},{3,11},{4,12},{5,13},{6,14},{7,15},{8,0},{9,1},... | collective-permute-start | bytes 786440 | tf_op jit(solution)/shard_map/ppermute | solution.py:38
  35.6 14.2 %collective-permute-start.9 = (bf16[8,128,256]{2,1,0:T(8,128)(2,1)S(1)}, bf16[8,128,256]{2,1,0:T(8,128)(2,1)S(1)}, u32[]{:S(2)}, u32[]{:S(2)}) collective-permute-start(bf16[8,128,256]{2,1,0:T(8,128)(2,1)S(1)} %get-tuple-element.58), channel_id=1, source_target_pairs={{0,1},{1,2},{2,3},{3,0},{4,5},{5,6},{6,7},{7,4},{8,9},{9,10},{10,1... | collective-permute-start | bytes 1572872 | tf_op jit(solution)/shard_map/ppermute | solution.py:38
  37.2 24.1 %collective-permute-start.6 = (bf16[8,128,256]{2,1,0:T(8,128)(2,1)}, bf16[8,128,256]{2,1,0:T(8,128)(2,1)S(1)}, u32[]{:S(2)}, u32[]{:S(2)}) collective-permute-start(bf16[8,128,256]{2,1,0:T(8,128)(2,1)} %get-tuple-element.53), channel_id=1, source_target_pairs={{0,4},{1,5},{2,6},{3,7},{4,8},{5,9},{6,10},{7,11},{8,12},{9,13},{1... | collective-permute-start | bytes 1572872 | tf_op jit(solution)/shard_map/ppermute | solution.py:38
  39.4 21.9 %collective-permute-start.7 = (bf16[8,128,256]{2,1,0:T(8,128)(2,1)}, bf16[8,128,256]{2,1,0:T(8,128)(2,1)}, u32[]{:S(2)}, u32[]{:S(2)}) collective-permute-start(bf16[8,128,256]{2,1,0:T(8,128)(2,1)} %get-tuple-element.54), channel_id=1, source_target_pairs={{0,8},{1,9},{2,10},{3,11},{4,12},{5,13},{6,14},{7,15},{8,0},{9,1},... | collective-permute-start | bytes 1572872 | tf_op jit(solution)/shard_map/ppermute | solution.py:38
  43.0 21.9 %collective-permute-start.8 = (bf16[8,128,256]{2,1,0:T(8,128)(2,1)}, bf16[8,128,256]{2,1,0:T(8,128)(2,1)}, u32[]{:S(2)}, u32[]{:S(2)}) collective-permute-start(bf16[8,128,256]{2,1,0:T(8,128)(2,1)} %get-tuple-element.55), channel_id=1, source_target_pairs={{0,12},{1,13},{2,14},{3,15},{4,0},{5,1},{6,2},{7,3},{8,4},{9,5},{1... | collective-permute-start | bytes 1572872 | tf_op jit(solution)/shard_map/ppermute | solution.py:38
  43.1 22.3 %collective-permute-start.11 = (bf16[8,128,256]{2,1,0:T(8,128)(2,1)}, bf16[8,128,256]{2,1,0:T(8,128)(2,1)}, u32[]{:S(2)}, u32[]{:S(2)}) collective-permute-start(bf16[8,128,256]{2,1,0:T(8,128)(2,1)} %get-tuple-element.61), channel_id=1, source_target_pairs={{0,3},{1,0},{2,1},{3,2},{4,7},{5,4},{6,5},{7,6},{8,11},{9,8},{10,9... | collective-permute-start | bytes 1572872 | tf_op jit(solution)/shard_map/ppermute | solution.py:38
  49.8 15.6 %collective-permute-start.10 = (bf16[8,128,256]{2,1,0:T(8,128)(2,1)}, bf16[8,128,256]{2,1,0:T(8,128)(2,1)}, u32[]{:S(2)}, u32[]{:S(2)}) collective-permute-start(bf16[8,128,256]{2,1,0:T(8,128)(2,1)} %get-tuple-element.60), channel_id=1, source_target_pairs={{0,2},{1,3},{2,0},{3,1},{4,6},{5,7},{6,4},{7,5},{8,10},{9,11},{10,... | collective-permute-start | bytes 1572872 | tf_op jit(solution)/shard_map/ppermute | solution.py:38
  77.4 22.3 %copy-start.10 = (bf16[8,128,256]{2,1,0:T(8,128)(2,1)S(1)}, bf16[8,128,256]{2,1,0:T(8,128)(2,1)}, u32[]{:S(2)}) copy-start(bf16[8,128,256]{2,1,0:T(8,128)(2,1)} %get-tuple-element.72) | copy-start | bytes 1572868
  77.4 39.7 %copy-start = (bf16[8,128,256]{2,1,0:T(8,128)(2,1)S(1)}, bf16[8,128,256]{2,1,0:T(8,128)(2,1)}, u32[]{:S(2)}) copy-start(bf16[8,128,256]{2,1,0:T(8,128)(2,1)} %get-tuple-element.64.refs_0_) | copy-start | bytes 1572868
  77.5 39.7 %copy-start.1 = (bf16[8,128,256]{2,1,0:T(8,128)(2,1)S(1)}, bf16[8,128,256]{2,1,0:T(8,128)(2,1)}, u32[]{:S(2)}) copy-start(bf16[8,128,256]{2,1,0:T(8,128)(2,1)} %get-tuple-element.68.refs_4_) | copy-start | bytes 1572868
  77.5 39.7 %copy-start.5 = (s32[2,64]{1,0:T(2,128)S(1)}, s32[2,64]{1,0:T(2,128)}, u32[]{:S(2)}) copy-start(s32[2,64]{1,0:T(2,128)} %get-tuple-element.63.add_ref) | copy-start | bytes 1540
  77.5 51.3 %all-to-all-start.1 = ((bf16[16,128,256]{2,1,0:T(8,128)(2,1)}), bf16[16,128,256]{2,1,0:T(8,128)(2,1)}, u32[]{:S(2)}, u32[]{:S(2)}) async-start(bf16[16,128,256]{2,1,0:T(8,128)(2,1)} %get-tuple-element.62), calls=%async_computation.1 | async-start | bytes 2097152 | tf_op jit(solution)/shard_map/all_to_all | solution.py:432
  84.1 15.7 %collective-permute-start.15 = (bf16[8,128,256]{2,1,0:T(8,128)(2,1)}, bf16[8,128,256]{2,1,0:T(8,128)(2,1)S(1)}, u32[]{:S(2)}, u32[]{:S(2)}) collective-permute-start(bf16[8,128,256]{2,1,0:T(8,128)(2,1)} %get-tuple-element.70), channel_id=1, source_target_pairs={{0,3},{1,0},{2,1},{3,2},{4,7},{5,4},{6,5},{7,6},{8,11},{9,8},{10,9... | collective-permute-start | bytes 1572872 | tf_op jit(solution)/shard_map/ppermute | solution.py:38
  88.0 14.8 %collective-permute-start.12 = (bf16[8,128,256]{2,1,0:T(8,128)(2,1)}, bf16[8,128,256]{2,1,0:T(8,128)(2,1)S(1)}, u32[]{:S(2)}, u32[]{:S(2)}) collective-permute-start(bf16[8,128,256]{2,1,0:T(8,128)(2,1)} %get-tuple-element.65), channel_id=1, source_target_pairs={{0,12},{1,13},{2,14},{3,15},{4,0},{5,1},{6,2},{7,3},{8,4},{9,5},{1... | collective-permute-start | bytes 1572872 | tf_op jit(solution)/shard_map/ppermute | solution.py:38
  90.1 24.1 %collective-permute-start.13 = (bf16[8,128,256]{2,1,0:T(8,128)(2,1)}, bf16[8,128,256]{2,1,0:T(8,128)(2,1)S(1)}, u32[]{:S(2)}, u32[]{:S(2)}) collective-permute-start(bf16[8,128,256]{2,1,0:T(8,128)(2,1)} %get-tuple-element.66), channel_id=1, source_target_pairs={{0,8},{1,9},{2,10},{3,11},{4,12},{5,13},{6,14},{7,15},{8,0},{9,1},... | collective-permute-start | bytes 1572872 | tf_op jit(solution)/shard_map/ppermute | solution.py:38
  91.2 23.7 %collective-permute-start.14 = (bf16[8,128,256]{2,1,0:T(8,128)(2,1)}, bf16[8,128,256]{2,1,0:T(8,128)(2,1)S(1)}, u32[]{:S(2)}, u32[]{:S(2)}) collective-permute-start(bf16[8,128,256]{2,1,0:T(8,128)(2,1)} %get-tuple-element.67), channel_id=1, source_target_pairs={{0,4},{1,5},{2,6},{3,7},{4,8},{5,9},{6,10},{7,11},{8,12},{9,13},{1... | collective-permute-start | bytes 1572872 | tf_op jit(solution)/shard_map/ppermute | solution.py:38
  91.9 25.3 %collective-permute-start.17 = (bf16[8,128,256]{2,1,0:T(8,128)(2,1)S(1)}, bf16[8,128,256]{2,1,0:T(8,128)(2,1)S(1)}, u32[]{:S(2)}, u32[]{:S(2)}) collective-permute-start(bf16[8,128,256]{2,1,0:T(8,128)(2,1)S(1)} %copy-done.11), channel_id=1, source_target_pairs={{0,1},{1,2},{2,3},{3,0},{4,5},{5,6},{6,7},{7,4},{8,9},{9,10},{10,1... | collective-permute-start | bytes 1572872 | tf_op jit(solution)/shard_map/ppermute | solution.py:38
  99.8 17.4 %collective-permute-start.16 = (bf16[8,128,256]{2,1,0:T(8,128)(2,1)S(1)}, bf16[8,128,256]{2,1,0:T(8,128)(2,1)S(1)}, u32[]{:S(2)}, u32[]{:S(2)}) collective-permute-start(bf16[8,128,256]{2,1,0:T(8,128)(2,1)S(1)} %copy-done.10), channel_id=1, source_target_pairs={{0,2},{1,3},{2,0},{3,1},{4,6},{5,7},{6,4},{7,5},{8,10},{9,11},{10,... | collective-permute-start | bytes 1572872 | tf_op jit(solution)/shard_map/ppermute | solution.py:38
  120.1 6.4 %collective-permute-start.21 = (bf16[4,128,256]{2,1,0:T(8,128)(2,1)S(1)}, bf16[4,128,256]{2,1,0:T(8,128)(2,1)S(1)}, u32[]{:S(2)}, u32[]{:S(2)}) collective-permute-start(bf16[4,128,256]{2,1,0:T(8,128)(2,1)S(1)} %get-tuple-element.80), channel_id=1, source_target_pairs={{0,4},{1,5},{2,6},{3,7},{4,8},{5,9},{6,10},{7,11},{8,12},{9,13},{1... | collective-permute-start | bytes 786440 | tf_op jit(solution)/shard_map/ppermute | solution.py:38
  122.5 12.6 %collective-permute-start.18 = (bf16[4,128,256]{2,1,0:T(8,128)(2,1)}, bf16[4,128,256]{2,1,0:T(8,128)(2,1)S(1)}, u32[]{:S(2)}, u32[]{:S(2)}) collective-permute-start(bf16[4,128,256]{2,1,0:T(8,128)(2,1)} %get-tuple-element.75), channel_id=1, source_target_pairs={{0,1},{1,2},{2,3},{3,0},{4,5},{5,6},{6,7},{7,4},{8,9},{9,10},{10,1... | collective-permute-start | bytes 786440 | tf_op jit(solution)/shard_map/ppermute | solution.py:38
  122.5 12.6 %collective-permute-start.19 = (bf16[4,128,256]{2,1,0:T(8,128)(2,1)}, bf16[4,128,256]{2,1,0:T(8,128)(2,1)S(1)}, u32[]{:S(2)}, u32[]{:S(2)}) collective-permute-start(bf16[4,128,256]{2,1,0:T(8,128)(2,1)} %get-tuple-element.76), channel_id=1, source_target_pairs={{0,2},{1,3},{2,0},{3,1},{4,6},{5,7},{6,4},{7,5},{8,10},{9,11},{10,... | collective-permute-start | bytes 786440 | tf_op jit(solution)/shard_map/ppermute | solution.py:38
  124.2 10.9 %collective-permute-start.20 = (bf16[4,128,256]{2,1,0:T(8,128)(2,1)S(1)}, bf16[4,128,256]{2,1,0:T(8,128)(2,1)S(1)}, u32[]{:S(2)}, u32[]{:S(2)}) collective-permute-start(bf16[4,128,256]{2,1,0:T(8,128)(2,1)S(1)} %get-tuple-element.77), channel_id=1, source_target_pairs={{0,3},{1,0},{2,1},{3,2},{4,7},{5,4},{6,5},{7,6},{8,11},{9,8},{10,9... | collective-permute-start | bytes 786440 | tf_op jit(solution)/shard_map/ppermute | solution.py:38
  125.7 11.4 %collective-permute-start.23 = (bf16[4,128,256]{2,1,0:T(8,128)(2,1)S(1)}, bf16[4,128,256]{2,1,0:T(8,128)(2,1)S(1)}, u32[]{:S(2)}, u32[]{:S(2)}) collective-permute-start(bf16[4,128,256]{2,1,0:T(8,128)(2,1)S(1)} %get-tuple-element.83), channel_id=1, source_target_pairs={{0,12},{1,13},{2,14},{3,15},{4,0},{5,1},{6,2},{7,3},{8,4},{9,5},{1... | collective-permute-start | bytes 786440 | tf_op jit(solution)/shard_map/ppermute | solution.py:38
  126.5 10.6 %collective-permute-start.22 = (bf16[4,128,256]{2,1,0:T(8,128)(2,1)S(1)}, bf16[4,128,256]{2,1,0:T(8,128)(2,1)S(1)}, u32[]{:S(2)}, u32[]{:S(2)}) collective-permute-start(bf16[4,128,256]{2,1,0:T(8,128)(2,1)S(1)} %get-tuple-element.82), channel_id=1, source_target_pairs={{0,8},{1,9},{2,10},{3,11},{4,12},{5,13},{6,14},{7,15},{8,0},{9,1},... | collective-permute-start | bytes 786440 | tf_op jit(solution)/shard_map/ppermute | solution.py:38
  (6 other events, 52.8 us)

commit v6 on v5

--- a/solution.py
+++ b/solution.py
@@ -60,30 +60,39 @@
     )
 
 
-def pack_heads_body(parts, width, q_ref, g_ref, out_ref, sems):
-    copies = []
-    for i, ref in enumerate((q_ref, g_ref)):
-        for j in range(parts):
-            copies.append(
-                pltpu.make_async_copy(
-                    ref.at[:, pl.ds(j * width, width)], out_ref.at[j, i], sems.at[i, j]
-                )
+def pack_heads_body(parts, width, q_ref, g_ref, out_ref, held, in_sems, out_sems):
+    arrivals = []
+    for j in range(parts):
+        for i, ref in enumerate((q_ref, g_ref)):
+            copy = pltpu.make_async_copy(
+                ref.at[:, pl.ds(j * width, width)], held.at[j, i], in_sems.at[j, i]
             )
-    for copy in copies:
-        copy.start()
-    for copy in copies:
+            copy.start()
+            arrivals.append(copy)
+    departures = []
+    for j in range(parts):
+        for copy in arrivals[2 * j : 2 * j + 2]:
+            copy.wait()
+        departures.append(pltpu.make_async_copy(held.at[j], out_ref.at[j], out_sems.at[j]))
+        departures[-1].start()
+    for copy in departures:
         copy.wait()
 
 
 def pack_heads(queries, grad_out, parts):
     tokens, features = queries.shape
     width = features // parts
+    shape = (parts, 2, tokens, width)
     return pl.pallas_call(
         functools.partial(pack_heads_body, parts, width),
-        out_shape=jax.ShapeDtypeStruct((parts, 2, tokens, width), BF16),
+        out_shape=pltpu.HBM(shape, BF16),
         in_specs=[HBM, HBM],
-        out_specs=VMEM,
-        scratch_shapes=[pltpu.SemaphoreType.DMA((2, parts))],
+        out_specs=HBM,
+        scratch_shapes=[
+            pltpu.VMEM(shape, BF16),
+            pltpu.SemaphoreType.DMA((parts, 2)),
+            pltpu.SemaphoreType.DMA((parts,)),
+        ],
     )(queries, grad_out)
 
 
@@ -146,7 +155,7 @@
                     distance = lax.rem(where[1 - across] - mine[1 - across] + SIDE, SIDE)
                     row = distance * owned + where[2]
                     take_ref[across, k * most + count] = row
-                    add_ref[across, row * SIDE + k] = count
+                    add_ref[across, row * SIDE + k] = count + (other if across == 0 else k) * most
 
                 return count + found.astype(jnp.int32)
 
@@ -207,18 +216,27 @@
     return (out[:4], out[4:])
 
 
-def spread_body(add_ref, *refs):
-    for across in range(2):
-        chunks = refs[4 * across : 4 * across + 4]
-        outs = refs[8 + 4 * across : 12 + 4 * across]
-        most, owned = chunks[0].shape[0], outs[0].shape[0]
+def spread_body(add_ref, key_ref, *refs):
+    value_refs, key_outs, value_outs, (pool, sems) = refs[:4], refs[4:8], refs[8:12], refs[12:]
+    most = value_refs[0].shape[0]
+    copies = [
+        pltpu.make_async_copy(ref, pool.at[pl.ds(k * most, most)], sems.at[k])
+        for k, ref in enumerate(value_refs)
+    ]
+    for copy in copies:
+        copy.start()
+    for across, terms, outs in ((0, key_ref, key_outs), (1, pool, value_outs)):
+        owned = outs[0].shape[0]
+        if across == 1:
+            for copy in copies:
+                copy.wait()
 
         def add(n, carry):
             for distance, out in enumerate(outs):
                 value = jnp.zeros(out.shape[1:], F32)
-                for k, chunk in enumerate(chunks):
+                for k in range(SIDE):
                     index = add_ref[across, (distance * owned + n) * SIDE + k]
-                    term = chunk[jnp.clip(index, 0, most - 1)].astype(F32)
+                    term = terms[jnp.maximum(index, 0)].astype(F32)
                     value += jnp.where(index >= 0, term, 0.0)
                 out[n] = value.astype(out.dtype)
             return carry
@@ -226,15 +244,20 @@
         lax.fori_loop(0, owned, add, 0)
 
 
+def in_hbm(values):
+    return [pltpu.with_memory_space_constraint(v, pltpu.MemorySpace.HBM) for v in values]
+
+
 def spread(add, keys, values, owned):
-    _, nbr, width = keys[0].shape
+    rows, nbr, width = keys.shape
     out = pl.pallas_call(
         spread_body,
         out_shape=chunk_shapes(owned, nbr, width, F32) * 2,
-        in_specs=[SMEM] + [VMEM] * 8,
+        in_specs=[SMEM, VMEM] + [HBM] * 4,
         out_specs=(VMEM,) * 8,
+        scratch_shapes=[pltpu.VMEM((rows, nbr, width), BF16), pltpu.SemaphoreType.DMA((SIDE,))],
         compiler_params=pltpu.CompilerParams(vmem_limit_bytes=SPREAD_VMEM),
-    )(add, *keys, *values)
+    )(add, keys, *in_hbm(values))
     return (out[:4], out[4:])
 
 
@@ -242,9 +265,10 @@
     groups, distinct, owned, most, unroll, ids_ref, refs_ref, tokens_ref, *refs
 ):
     key_parts, value_parts = refs[:4], refs[4:8]
-    gq_out, key_out, value_out = refs[8], refs[9:13], refs[13:17]
+    gq_out, key_all, value_out = refs[8], refs[9], refs[10:14]
+    key_out = [key_all.at[pl.ds(k * most, most)] for k in range(SIDE)]
     (keys, values, key_sum, value_sum, gq_ref, key_send, value_send, query_last, grad_last, held,
-     key_rows, value_rows, key_back, value_back, counts, in_sems, out_sems, gq_sem) = refs[17:]
+     key_rows, value_rows, key_back, value_back, counts, in_sems, out_sems, gq_sem) = refs[14:]
     scale = 1.0 / math.sqrt(DH)
     copies = [
         pltpu.make_async_copy(part, pool.at[pl.ds(k * most, most)], in_sems.at[i, k])
@@ -278,7 +302,7 @@
             distance = (mine[i] - where[i] + SIDE) % SIDE
             count = counts[i * SIDE + distance]
             table[j] = distance * most + count
-            back_rows[distance * most + count] = j
+            back_rows[(where[0] if i == 0 else distance) * most + count] = j
             counts[i * SIDE + distance] = count + 1
         return carry
 
@@ -376,24 +400,23 @@
     rows = pltpu.VMEM((GROUP, width), F32)
     table = pltpu.SMEM((distinct,), jnp.int32)
     reverse = pltpu.SMEM((SIDE * most,), jnp.int32)
-    shapes = (jax.ShapeDtypeStruct((parts, part_tokens, width), BF16),) + chunk_shapes(
-        most, nbr, width
-    ) * 2
-    constrain = lambda value: pltpu.with_memory_space_constraint(value, pltpu.MemorySpace.HBM)
-    keys, values = jax.tree.map(constrain, (list(keys), list(values)))
+    shapes = (
+        jax.ShapeDtypeStruct((parts, part_tokens, width), BF16),
+        jax.ShapeDtypeStruct((SIDE * most, nbr, width), BF16),
+    ) + chunk_shapes(most, nbr, width)
     out = pl.pallas_call(
         functools.partial(attend_body, groups, distinct, owned, most, 8),
         out_shape=tuple(pltpu.HBM(shape.shape, shape.dtype) for shape in shapes),
         in_specs=[SMEM, SMEM, VMEM] + [HBM] * 8,
-        out_specs=(HBM,) * 9,
+        out_specs=(HBM,) * 6,
         scratch_shapes=[pool, pool, total, total, pltpu.VMEM((parts, part_tokens, width), BF16),
                         pool, pool, rows, rows, rows, table, table, reverse, reverse,
                         pltpu.SMEM((2 * SIDE,), jnp.int32),
                         pltpu.SemaphoreType.DMA((2, SIDE)), pltpu.SemaphoreType.DMA((2, SIDE)),
                         pltpu.SemaphoreType.DMA],
         compiler_params=pltpu.CompilerParams(vmem_limit_bytes=ATTEND_VMEM),
-    )(ids, flat, tokens, *keys, *values)
-    return (out[0], out[1:5], out[5:])
+    )(ids, flat, tokens, *in_hbm(keys), *in_hbm(values))
+    return (out[0], out[1], out[2:])
 
 
 def collect_body(*refs):
@@ -428,7 +451,12 @@
     keys, values = select(take, *lines, most)
     keys, values = exchange_lines(((keys, "y", 1), (values, "x", 1)))
     back, keys, values = attend(distinct_ids, group_refs, tokens, keys, values, owned, most)
-    keys, values = exchange_lines(((keys, "y", -1), (values, "x", -1)))
+    keys = lax.all_to_all(
+        keys, "dp", split_axis=0, concat_axis=0, tiled=True,
+        axis_index_groups=[[y * SIDE + x for y in range(SIDE)] for x in range(SIDE)],
+    )
+    values = (values[0],) + tuple(shift(values[k], "x", -k) for k in range(1, SIDE))
+    back, keys, values = lax.optimization_barrier((back, keys, values))
     back = lax.all_to_all(back, "ctx", split_axis=0, concat_axis=0, tiled=True)
     keys, values = spread(add, keys, values, owned)
     keys, values = exchange_lines(((keys, "x", 1), (values, "y", 1)))

time: 139 us -> 149 us (1.072)
  the two profiles are of different devices: /device:TPU:8 before, /device:TPU:1 now
where the time goes in v6:
time: 149 us
  waiting for transfers between devices  67.1 us (45%)
  starting transfers between devices  50.3 us (34%)
  Pallas kernels  29.7 us (20%)
    ppermute x21, waiting for transfers between devices, shift(): return lax.ppermute(value, 'dp', pairs)  53.8 us
    ppermute x21, starting transfers between devices, shift(): return lax.ppermute(value, 'dp', pairs)  28.4 us
    all_to_all x1, waiting for transfers between devices, on_device(): back = lax.all_to_all(back, 'ctx', split_axis=0, concat_axis=0, tiled=True)  13.3 us
    pallas_call x1, Pallas kernels, attend(): pl.pallas_call(functools.partial(attend_body, groups, distinct, owned, mo...  12 us
    all_to_all x1, starting transfers between devices, on_device(): lax.all_to_all(packed, 'ctx', split_axis=0, concat_axis=0, tiled=True)  10.1 us
    all_to_all x1, starting transfers between devices, on_device(): back = lax.all_to_all(back, 'ctx', split_axis=0, concat_axis=0, tiled=True)  7.06 us
    all_to_all x1, starting transfers between devices, on_device(): lax.all_to_all(keys, 'dp', split_axis=0, concat_axis=0, tiled=True, axis_...  4.71 us
    pallas_call x1, Pallas kernels, tables(): pl.pallas_call(functools.partial(tables_body, owned, most), out_shape=(ja...  3.94 us
  transfers between devices with their start and end apart: 24, of which 12 were waited for; matrix products, arithmetic and copies ran while one was open for 0% of the time, Pallas kernels for 9%

profile of v6, /device:TPU:1, one launch (start us, length us, event | category | flops | bytes accessed | tf_op | source)
XLA Modules:
  0.0 148.8 jit_solution(4343104266680484493)
XLA Ops:
  0.6 2.7 %shard_map.85 = bf16[16,2,128,256]{3,2,1,0:T(8,128)(2,1)} custom-call(bf16[128,4096]{1,0:T(8,128)(2,1)} %bitcast.5, bf16[128,4096]{1,0:T(8,128)(2,1)} %bitcast.6), custom_call_target="tpu_custom_call" | custom-call | tf_op jit(solution)/shard_map/pallas_call | solution.py:86
  3.4 10.1 %all-to-all-start = ((bf16[16,2,128,256]{3,2,1,0:T(8,128)(2,1)}), bf16[16,2,128,256]{3,2,1,0:T(8,128)(2,1)S(1)}, u32[]{:S(2)}, u32[]{:S(2)}) async-start(bf16[16,2,128,256]{3,2,1,0:T(8,128)(2,1)} %shard_map.85), calls=%async_computation | async-start | bytes 4194304 | tf_op jit(solution)/shard_map/all_to_all | solution.py:450
  13.6 2.8 %collective-permute-start.3 = (bf16[4,128,256]{2,1,0:T(8,128)(2,1)S(1)}, bf16[4,128,256]{2,1,0:T(8,128)(2,1)S(1)}, u32[]{:S(2)}, u32[]{:S(2)}) collective-permute-start(bf16[4,128,256]{2,1,0:T(8,128)(2,1)S(1)} %copy-done.1), channel_id=1, source_target_pairs={{0,12},{1,13},{2,14},{3,15},{4,0},{5,1},{6,2},{7,3},{8,4},{9,5},{1... | collective-permute-start | bytes 786440 | tf_op jit(solution)/shard_map/ppermute | solution.py:38
  16.4 2.7 %collective-permute-start.1 = (bf16[4,128,256]{2,1,0:T(8,128)(2,1)S(1)}, bf16[4,128,256]{2,1,0:T(8,128)(2,1)S(1)}, u32[]{:S(2)}, u32[]{:S(2)}) collective-permute-start(bf16[4,128,256]{2,1,0:T(8,128)(2,1)S(1)} %copy-done), channel_id=1, source_target_pairs={{0,2},{1,3},{2,0},{3,1},{4,6},{5,7},{6,4},{7,5},{8,10},{9,11},{10,... | collective-permute-start | bytes 786440 | tf_op jit(solution)/shard_map/ppermute | solution.py:38
  20.6 1.4 collective-permute-done.3.refs_5_
  22.0 2.4 %collective-permute-start.4 = (bf16[4,128,256]{2,1,0:T(8,128)(2,1)S(1)}, bf16[4,128,256]{2,1,0:T(8,128)(2,1)}, u32[]{:S(2)}, u32[]{:S(2)}) collective-permute-start(bf16[4,128,256]{2,1,0:T(8,128)(2,1)S(1)} %copy-done.1), channel_id=1, source_target_pairs={{0,8},{1,9},{2,10},{3,11},{4,12},{5,13},{6,14},{7,15},{8,0},{9,1},... | collective-permute-start | bytes 786440 | tf_op jit(solution)/shard_map/ppermute | solution.py:38
  24.4 3.9 %shard_map.86 = (s32[2,32]{1,0:T(2,128)}, s32[2,64]{1,0:T(2,128)}) custom-call(s32[16,16]{1,0:T(8,128)} %ids_ref.3), custom_call_target="tpu_custom_call" | custom-call | tf_op jit(solution)/shard_map/pallas_call | solution.py:166
  28.4 2.9 %collective-permute-done.refs_1_ = bf16[4,128,256]{2,1,0:T(8,128)(2,1)S(1)} collective-permute-done((bf16[4,128,256]{2,1,0:T(8,128)(2,1)S(1)}, bf16[4,128,256]{2,1,0:T(8,128)(2,1)S(1)}, u32[]{:S(2)}, u32[]{:S(2)}) %collective-permute-start) | collective-permute-done | bytes 262176 | tf_op jit(solution)/shard_map/ppermute | solution.py:38
  31.8 1.3 collective-permute-done.4.refs_6_
  33.8 3.9 %shard_map.87 = (bf16[8,128,256]{2,1,0:T(8,128)(2,1)}, bf16[8,128,256]{2,1,0:T(8,128)(2,1)}, bf16[8,128,256]{2,1,0:T(8,128)(2,1)}, bf16[8,128,256]{2,1,0:T(8,128...) custom-call(s32[2,32]{1,0:T(2,128)S(1)} %copy-done.4, ...), custom_call_target="tpu_custom_call" | custom-call | tf_op jit(solution)/shard_map/pallas_call | solution.py:208
  38.1 2.9 %collective-permute-start.7 = (bf16[8,128,256]{2,1,0:T(8,128)(2,1)}, bf16[8,128,256]{2,1,0:T(8,128)(2,1)}, u32[]{:S(2)}, u32[]{:S(2)}) collective-permute-start(bf16[8,128,256]{2,1,0:T(8,128)(2,1)} %get-tuple-element.55), channel_id=1, source_target_pairs={{0,8},{1,9},{2,10},{3,11},{4,12},{5,13},{6,14},{7,15},{8,0},{9,1},... | collective-permute-start | bytes 1572872 | tf_op jit(solution)/shard_map/ppermute | solution.py:38
  41.1 1.3 collective-permute-start.8
  42.4 1.8 %collective-permute-start.11 = (bf16[8,128,256]{2,1,0:T(8,128)(2,1)}, bf16[8,128,256]{2,1,0:T(8,128)(2,1)}, u32[]{:S(2)}, u32[]{:S(2)}) collective-permute-start(bf16[8,128,256]{2,1,0:T(8,128)(2,1)} %get-tuple-element.62), channel_id=1, source_target_pairs={{0,3},{1,0},{2,1},{3,2},{4,7},{5,4},{6,5},{7,6},{8,11},{9,8},{10,9... | collective-permute-start | bytes 1572872 | tf_op jit(solution)/shard_map/ppermute | solution.py:38
  44.1 5.2 %collective-permute-done.9.refs_5_ = bf16[8,128,256]{2,1,0:T(8,128)(2,1)S(1)} collective-permute-done((bf16[8,128,256]{2,1,0:T(8,128)(2,1)S(1)}, bf16[8,128,256]{2,1,0:T(8,128)(2,1)S(1)}, u32[]{:S(2)}, u32[]{:S(2)}) %collective-permute-start.9) | collective-permute-done | bytes 524320 | tf_op jit(solution)/shard_map/ppermute | solution.py:38
  49.3 1.5 %collective-permute-start.10 = (bf16[8,128,256]{2,1,0:T(8,128)(2,1)}, bf16[8,128,256]{2,1,0:T(8,128)(2,1)}, u32[]{:S(2)}, u32[]{:S(2)}) collective-permute-start(bf16[8,128,256]{2,1,0:T(8,128)(2,1)} %get-tuple-element.61), channel_id=1, source_target_pairs={{0,2},{1,3},{2,0},{3,1},{4,6},{5,7},{6,4},{7,5},{8,10},{9,11},{10,... | collective-permute-start | bytes 1572872 | tf_op jit(solution)/shard_map/ppermute | solution.py:38
  51.0 11.5 %collective-permute-done.7.refs_2_ = bf16[8,128,256]{2,1,0:T(8,128)(2,1)} collective-permute-done((bf16[8,128,256]{2,1,0:T(8,128)(2,1)}, bf16[8,128,256]{2,1,0:T(8,128)(2,1)}, u32[]{:S(2)}, u32[]{:S(2)}) %collective-permute-start.7) | collective-permute-done | bytes 524320 | tf_op jit(solution)/shard_map/ppermute | solution.py:38
  62.5 1.8 %collective-permute-done.8.refs_3_ = bf16[8,128,256]{2,1,0:T(8,128)(2,1)} collective-permute-done((bf16[8,128,256]{2,1,0:T(8,128)(2,1)}, bf16[8,128,256]{2,1,0:T(8,128)(2,1)}, u32[]{:S(2)}, u32[]{:S(2)}) %collective-permute-start.8) | collective-permute-done | bytes 524320 | tf_op jit(solution)/shard_map/ppermute | solution.py:38
  64.3 12.0 %shard_map.88 = (bf16[16,128,256]{2,1,0:T(8,128)(2,1)}, bf16[32,128,256]{2,1,0:T(8,128)(2,1)}, bf16[8,128,256]{2,1,0:T(8,128)(2,1)}, bf16[8,128,256]{2,1,0:T(8,1...) custom-call(s32[16,16]{1,0:T(8,128)S(1)} %copy-done.2, s32[16,64]{1,0:T(8,128)S(1)} %copy.11.refs_ref, ...), custom_call_target="tpu_custom_call" | custom-call | tf_op jit(solution)/shard_map/pallas_call | solution.py:407
  76.4 4.7 %all-to-all-start.1 = ((bf16[32,128,256]{2,1,0:T(8,128)(2,1)}), bf16[32,128,256]{2,1,0:T(8,128)(2,1)S(1)}, u32[]{:S(2)}, u32[]{:S(2)}) async-start(bf16[32,128,256]{2,1,0:T(8,128)(2,1)} %get-tuple-element.64), calls=%async_computation.1 | async-start | bytes 4194304 | tf_op jit(solution)/shard_map/all_to_all | solution.py:454
  81.1 2.4 %collective-permute-start.12 = (bf16[8,128,256]{2,1,0:T(8,128)(2,1)}, bf16[8,128,256]{2,1,0:T(8,128)(2,1)S(1)}, u32[]{:S(2)}, u32[]{:S(2)}) collective-permute-start(bf16[8,128,256]{2,1,0:T(8,128)(2,1)} %get-tuple-element.66), channel_id=1, source_target_pairs={{0,3},{1,0},{2,1},{3,2},{4,7},{5,4},{6,5},{7,6},{8,11},{9,8},{10,9... | collective-permute-start | bytes 1572872 | tf_op jit(solution)/shard_map/ppermute | solution.py:38
  84.9 6.6 %collective-permute-done.12.refs_1_ = bf16[8,128,256]{2,1,0:T(8,128)(2,1)S(1)} collective-permute-done((bf16[8,128,256]{2,1,0:T(8,128)(2,1)}, bf16[8,128,256]{2,1,0:T(8,128)(2,1)S(1)}, u32[]{:S(2)}, u32[]{:S(2)}) %collective-permute-start.12) | collective-permute-done | bytes 524320 | tf_op jit(solution)/shard_map/ppermute | solution.py:38
  91.4 3.2 %collective-permute-done.13.refs_2_ = bf16[8,128,256]{2,1,0:T(8,128)(2,1)S(1)} collective-permute-done((bf16[8,128,256]{2,1,0:T(8,128)(2,1)}, bf16[8,128,256]{2,1,0:T(8,128)(2,1)S(1)}, u32[]{:S(2)}, u32[]{:S(2)}) %collective-permute-start.13) | collective-permute-done | bytes 524320 | tf_op jit(solution)/shard_map/ppermute | solution.py:38
  94.6 15.7 %collective-permute-done.14.refs_3_ = bf16[8,128,256]{2,1,0:T(8,128)(2,1)} collective-permute-done((bf16[8,128,256]{2,1,0:T(8,128)(2,1)}, bf16[8,128,256]{2,1,0:T(8,128)(2,1)}, u32[]{:S(2)}, u32[]{:S(2)}) %collective-permute-start.14) | collective-permute-done | bytes 524320 | tf_op jit(solution)/shard_map/ppermute | solution.py:38
  110.3 7.1 %all-to-all-start.2 = ((bf16[16,128,256]{2,1,0:T(8,128)(2,1)}), bf16[16,128,256]{2,1,0:T(8,128)(2,1)}, u32[]{:S(2)}, u32[]{:S(2)}) async-start(bf16[16,128,256]{2,1,0:T(8,128)(2,1)} %get-tuple-element.69), calls=%async_computation.2 | async-start | bytes 2097152 | tf_op jit(solution)/shard_map/all_to_all | solution.py:460
  117.4 3.8 %shard_map.90 = (f32[4,128,256]{2,1,0:T(8,128)S(1)}, bf16[4,128,256]{2,1,0:T(8,128)(2,1)}, bf16[4,128,256]{2,1,0:T(8,128)(2,1)}, bf16[4,128,256]{2,1,0:T(8,128)(...) custom-call(s32[2,64]{1,0:T(2,128)S(1)} %copy-done.3, ...), custom_call_target="tpu_custom_call" | custom-call | tf_op jit(solution)/shard_map/pallas_call | solution.py:253
  121.3 1.5 %collective-permute-start.18 = (bf16[4,128,256]{2,1,0:T(8,128)(2,1)S(1)}, bf16[4,128,256]{2,1,0:T(8,128)(2,1)S(1)}, u32[]{:S(2)}, u32[]{:S(2)}) collective-permute-start(bf16[4,128,256]{2,1,0:T(8,128)(2,1)S(1)} %get-tuple-element.82), channel_id=1, source_target_pairs={{0,4},{1,5},{2,6},{3,7},{4,8},{5,9},{6,10},{7,11},{8,12},{9,13},{1... | collective-permute-start | bytes 786440 | tf_op jit(solution)/shard_map/ppermute | solution.py:38
  122.8 1.5 %collective-permute-start.16 = (bf16[4,128,256]{2,1,0:T(8,128)(2,1)}, bf16[4,128,256]{2,1,0:T(8,128)(2,1)S(1)}, u32[]{:S(2)}, u32[]{:S(2)}) collective-permute-start(bf16[4,128,256]{2,1,0:T(8,128)(2,1)} %get-tuple-element.78), channel_id=1, source_target_pairs={{0,2},{1,3},{2,0},{3,1},{4,6},{5,7},{6,4},{7,5},{8,10},{9,11},{10,... | collective-permute-start | bytes 786440 | tf_op jit(solution)/shard_map/ppermute | solution.py:38
  125.5 1.3 collective-permute-start.20
  126.8 3.6 %collective-permute-done.18.refs_5_ = bf16[4,128,256]{2,1,0:T(8,128)(2,1)S(1)} collective-permute-done((bf16[4,128,256]{2,1,0:T(8,128)(2,1)S(1)}, bf16[4,128,256]{2,1,0:T(8,128)(2,1)S(1)}, u32[]{:S(2)}, u32[]{:S(2)}) %collective-permute-start.18) | collective-permute-done | bytes 262176 | tf_op jit(solution)/shard_map/ppermute | solution.py:38
  130.4 1.7 %collective-permute-start.19 = (bf16[4,128,256]{2,1,0:T(8,128)(2,1)S(1)}, bf16[4,128,256]{2,1,0:T(8,128)(2,1)S(1)}, u32[]{:S(2)}, u32[]{:S(2)}) collective-permute-start(bf16[4,128,256]{2,1,0:T(8,128)(2,1)S(1)} %get-tuple-element.84), channel_id=1, source_target_pairs={{0,8},{1,9},{2,10},{3,11},{4,12},{5,13},{6,14},{7,15},{8,0},{9,1},... | collective-permute-start | bytes 786440 | tf_op jit(solution)/shard_map/ppermute | solution.py:38
  132.2 13.3 %all-to-all-done.2.in_ref = bf16[16,128,256]{2,1,0:T(8,128)(2,1)} async-done(((bf16[16,128,256]{2,1,0:T(8,128)(2,1)}), bf16[16,128,256]{2,1,0:T(8,128)(2,1)}, u32[]{:S(2)}, u32[]{:S(2)}) %all-to-all-start.2) | async-done | bytes 1048608 | tf_op jit(solution)/shard_map/all_to_all | solution.py:460
  145.4 2.3 %shard_map.89 = bf16[128,4096]{1,0:T(8,128)(2,1)} custom-call(bf16[16,128,256]{2,1,0:T(8,128)(2,1)} %all-to-all-done.2.in_ref), custom_call_target="tpu_custom_call" | custom-call | tf_op jit(solution)/shard_map/pallas_call | solution.py:112
  (45 shorter events, 6.9 us)
Async XLA Ops:
  3.4 13.0 %copy-start = (bf16[4,128,256]{2,1,0:T(8,128)(2,1)S(1)}, bf16[4,128,256]{2,1,0:T(8,128)(2,1)}, u32[]{:S(2)}) copy-start(bf16[4,128,256]{2,1,0:T(8,128)(2,1)} %refs_0_.1) | copy-start | bytes 786436
  3.4 47.5 %copy-start.9 = (s32[16,32,2]{1,2,0:T(2,128)S(1)}, s32[16,32,2]{1,2,0:T(2,128)}, u32[]{:S(2)}) copy-start(s32[16,32,2]{1,2,0:T(2,128)} %param.11) | copy-start | bytes 12292
  3.4 60.9 %all-to-all-start = ((bf16[16,2,128,256]{3,2,1,0:T(8,128)(2,1)}), bf16[16,2,128,256]{3,2,1,0:T(8,128)(2,1)S(1)}, u32[]{:S(2)}, u32[]{:S(2)}) async-start(bf16[16,2,128,256]{3,2,1,0:T(8,128)(2,1)} %shard_map.85), calls=%async_computation | async-start | bytes 4194304 | tf_op jit(solution)/shard_map/all_to_all | solution.py:450
  13.5 50.8 %copy-start.2 = (s32[16,16]{1,0:T(8,128)S(1)}, s32[16,16]{1,0:T(8,128)}, u32[]{:S(2)}) copy-start(s32[16,16]{1,0:T(8,128)} %ids_ref.3) | copy-start | bytes 3076
  13.6 8.5 %collective-permute-start.3 = (bf16[4,128,256]{2,1,0:T(8,128)(2,1)S(1)}, bf16[4,128,256]{2,1,0:T(8,128)(2,1)S(1)}, u32[]{:S(2)}, u32[]{:S(2)}) collective-permute-start(bf16[4,128,256]{2,1,0:T(8,128)(2,1)S(1)} %copy-done.1), channel_id=1, source_target_pairs={{0,12},{1,13},{2,14},{3,15},{4,0},{5,1},{6,2},{7,3},{8,4},{9,5},{1... | collective-permute-start | bytes 786440 | tf_op jit(solution)/shard_map/ppermute | solution.py:38
  16.4 12.0 %collective-permute-start.1 = (bf16[4,128,256]{2,1,0:T(8,128)(2,1)S(1)}, bf16[4,128,256]{2,1,0:T(8,128)(2,1)S(1)}, u32[]{:S(2)}, u32[]{:S(2)}) collective-permute-start(bf16[4,128,256]{2,1,0:T(8,128)(2,1)S(1)} %copy-done), channel_id=1, source_target_pairs={{0,2},{1,3},{2,0},{3,1},{4,6},{5,7},{6,4},{7,5},{8,10},{9,11},{10,... | collective-permute-start | bytes 786440 | tf_op jit(solution)/shard_map/ppermute | solution.py:38
  19.1 12.1 %collective-permute-start = (bf16[4,128,256]{2,1,0:T(8,128)(2,1)S(1)}, bf16[4,128,256]{2,1,0:T(8,128)(2,1)S(1)}, u32[]{:S(2)}, u32[]{:S(2)}) collective-permute-start(bf16[4,128,256]{2,1,0:T(8,128)(2,1)S(1)} %copy-done), channel_id=1, source_target_pairs={{0,3},{1,0},{2,1},{3,2},{4,7},{5,4},{6,5},{7,6},{8,11},{9,8},{10,9... | collective-permute-start | bytes 786440 | tf_op jit(solution)/shard_map/ppermute | solution.py:38
  20.0 11.8 %collective-permute-start.2 = (bf16[4,128,256]{2,1,0:T(8,128)(2,1)S(1)}, bf16[4,128,256]{2,1,0:T(8,128)(2,1)}, u32[]{:S(2)}, u32[]{:S(2)}) collective-permute-start(bf16[4,128,256]{2,1,0:T(8,128)(2,1)S(1)} %copy-done), channel_id=1, source_target_pairs={{0,1},{1,2},{2,3},{3,0},{4,5},{5,6},{6,7},{7,4},{8,9},{9,10},{10,1... | collective-permute-start | bytes 786440 | tf_op jit(solution)/shard_map/ppermute | solution.py:38
  20.6 11.2 %collective-permute-start.5 = (bf16[4,128,256]{2,1,0:T(8,128)(2,1)S(1)}, bf16[4,128,256]{2,1,0:T(8,128)(2,1)}, u32[]{:S(2)}, u32[]{:S(2)}) collective-permute-start(bf16[4,128,256]{2,1,0:T(8,128)(2,1)S(1)} %copy-done.1), channel_id=1, source_target_pairs={{0,4},{1,5},{2,6},{3,7},{4,8},{5,9},{6,10},{7,11},{8,12},{9,13},{1... | collective-permute-start | bytes 786440 | tf_op jit(solution)/shard_map/ppermute | solution.py:38
  22.0 11.1 %collective-permute-start.4 = (bf16[4,128,256]{2,1,0:T(8,128)(2,1)S(1)}, bf16[4,128,256]{2,1,0:T(8,128)(2,1)}, u32[]{:S(2)}, u32[]{:S(2)}) collective-permute-start(bf16[4,128,256]{2,1,0:T(8,128)(2,1)S(1)} %copy-done.1), channel_id=1, source_target_pairs={{0,8},{1,9},{2,10},{3,11},{4,12},{5,13},{6,14},{7,15},{8,0},{9,1},... | collective-permute-start | bytes 786440 | tf_op jit(solution)/shard_map/ppermute | solution.py:38
  37.7 11.6 %collective-permute-start.9 = (bf16[8,128,256]{2,1,0:T(8,128)(2,1)S(1)}, bf16[8,128,256]{2,1,0:T(8,128)(2,1)S(1)}, u32[]{:S(2)}, u32[]{:S(2)}) collective-permute-start(bf16[8,128,256]{2,1,0:T(8,128)(2,1)S(1)} %get-tuple-element.59), channel_id=1, source_target_pairs={{0,1},{1,2},{2,3},{3,0},{4,5},{5,6},{6,7},{7,4},{8,9},{9,10},{10,1... | collective-permute-start | bytes 1572872 | tf_op jit(solution)/shard_map/ppermute | solution.py:38
  38.1 12.9 %collective-permute-start.6 = (bf16[8,128,256]{2,1,0:T(8,128)(2,1)}, bf16[8,128,256]{2,1,0:T(8,128)(2,1)S(1)}, u32[]{:S(2)}, u32[]{:S(2)}) collective-permute-start(bf16[8,128,256]{2,1,0:T(8,128)(2,1)} %get-tuple-element.54), channel_id=1, source_target_pairs={{0,4},{1,5},{2,6},{3,7},{4,8},{5,9},{6,10},{7,11},{8,12},{9,13},{1... | collective-permute-start | bytes 1572872 | tf_op jit(solution)/shard_map/ppermute | solution.py:38
  38.1 24.4 %collective-permute-start.7 = (bf16[8,128,256]{2,1,0:T(8,128)(2,1)}, bf16[8,128,256]{2,1,0:T(8,128)(2,1)}, u32[]{:S(2)}, u32[]{:S(2)}) collective-permute-start(bf16[8,128,256]{2,1,0:T(8,128)(2,1)} %get-tuple-element.55), channel_id=1, source_target_pairs={{0,8},{1,9},{2,10},{3,11},{4,12},{5,13},{6,14},{7,15},{8,0},{9,1},... | collective-permute-start | bytes 1572872 | tf_op jit(solution)/shard_map/ppermute | solution.py:38
  41.1 23.2 %collective-permute-start.8 = (bf16[8,128,256]{2,1,0:T(8,128)(2,1)}, bf16[8,128,256]{2,1,0:T(8,128)(2,1)}, u32[]{:S(2)}, u32[]{:S(2)}) collective-permute-start(bf16[8,128,256]{2,1,0:T(8,128)(2,1)} %get-tuple-element.56), channel_id=1, source_target_pairs={{0,12},{1,13},{2,14},{3,15},{4,0},{5,1},{6,2},{7,3},{8,4},{9,5},{1... | collective-permute-start | bytes 1572872 | tf_op jit(solution)/shard_map/ppermute | solution.py:38
  42.4 21.9 %collective-permute-start.11 = (bf16[8,128,256]{2,1,0:T(8,128)(2,1)}, bf16[8,128,256]{2,1,0:T(8,128)(2,1)}, u32[]{:S(2)}, u32[]{:S(2)}) collective-permute-start(bf16[8,128,256]{2,1,0:T(8,128)(2,1)} %get-tuple-element.62), channel_id=1, source_target_pairs={{0,3},{1,0},{2,1},{3,2},{4,7},{5,4},{6,5},{7,6},{8,11},{9,8},{10,9... | collective-permute-start | bytes 1572872 | tf_op jit(solution)/shard_map/ppermute | solution.py:38
  49.3 15.0 %copy-start.5 = (bf16[8,128,256]{2,1,0:T(8,128)(2,1)}, bf16[8,128,256]{2,1,0:T(8,128)(2,1)S(1)}, u32[]{:S(2)}) copy-start(bf16[8,128,256]{2,1,0:T(8,128)(2,1)S(1)} %collective-permute-done.9.refs_5_) | copy-start | bytes 1572868
  49.3 15.0 %collective-permute-start.10 = (bf16[8,128,256]{2,1,0:T(8,128)(2,1)}, bf16[8,128,256]{2,1,0:T(8,128)(2,1)}, u32[]{:S(2)}, u32[]{:S(2)}) collective-permute-start(bf16[8,128,256]{2,1,0:T(8,128)(2,1)} %get-tuple-element.61), channel_id=1, source_target_pairs={{0,2},{1,3},{2,0},{3,1},{4,6},{5,7},{6,4},{7,5},{8,10},{9,11},{10,... | collective-permute-start | bytes 1572872 | tf_op jit(solution)/shard_map/ppermute | solution.py:38
  51.0 13.3 %copy-start.6 = (bf16[8,128,256]{2,1,0:T(8,128)(2,1)}, bf16[8,128,256]{2,1,0:T(8,128)(2,1)S(1)}, u32[]{:S(2)}) copy-start(bf16[8,128,256]{2,1,0:T(8,128)(2,1)S(1)} %collective-permute-done.6.refs_1_) | copy-start | bytes 1572868
  76.4 34.0 %all-to-all-start.1 = ((bf16[32,128,256]{2,1,0:T(8,128)(2,1)}), bf16[32,128,256]{2,1,0:T(8,128)(2,1)S(1)}, u32[]{:S(2)}, u32[]{:S(2)}) async-start(bf16[32,128,256]{2,1,0:T(8,128)(2,1)} %get-tuple-element.64), calls=%async_computation.1 | async-start | bytes 4194304 | tf_op jit(solution)/shard_map/all_to_all | solution.py:454
  81.1 36.4 %copy-start.3 = (s32[2,64]{1,0:T(2,128)S(1)}, s32[2,64]{1,0:T(2,128)}, u32[]{:S(2)}) copy-start(s32[2,64]{1,0:T(2,128)} %get-tuple-element.70.add_ref) | copy-start | bytes 1540
  81.1 10.4 %collective-permute-start.12 = (bf16[8,128,256]{2,1,0:T(8,128)(2,1)}, bf16[8,128,256]{2,1,0:T(8,128)(2,1)S(1)}, u32[]{:S(2)}, u32[]{:S(2)}) collective-permute-start(bf16[8,128,256]{2,1,0:T(8,128)(2,1)} %get-tuple-element.66), channel_id=1, source_target_pairs={{0,3},{1,0},{2,1},{3,2},{4,7},{5,4},{6,5},{7,6},{8,11},{9,8},{10,9... | collective-permute-start | bytes 1572872 | tf_op jit(solution)/shard_map/ppermute | solution.py:38
  83.4 11.2 %collective-permute-start.13 = (bf16[8,128,256]{2,1,0:T(8,128)(2,1)}, bf16[8,128,256]{2,1,0:T(8,128)(2,1)S(1)}, u32[]{:S(2)}, u32[]{:S(2)}) collective-permute-start(bf16[8,128,256]{2,1,0:T(8,128)(2,1)} %get-tuple-element.67), channel_id=1, source_target_pairs={{0,2},{1,3},{2,0},{3,1},{4,6},{5,7},{6,4},{7,5},{8,10},{9,11},{10,... | collective-permute-start | bytes 1572872 | tf_op jit(solution)/shard_map/ppermute | solution.py:38
  84.1 26.2 %collective-permute-start.14 = (bf16[8,128,256]{2,1,0:T(8,128)(2,1)}, bf16[8,128,256]{2,1,0:T(8,128)(2,1)}, u32[]{:S(2)}, u32[]{:S(2)}) collective-permute-start(bf16[8,128,256]{2,1,0:T(8,128)(2,1)} %get-tuple-element.68), channel_id=1, source_target_pairs={{0,1},{1,2},{2,3},{3,0},{4,5},{5,6},{6,7},{7,4},{8,9},{9,10},{10,1... | collective-permute-start | bytes 1572872 | tf_op jit(solution)/shard_map/ppermute | solution.py:38
  91.4 26.0 %copy-start.7 = (bf16[8,128,256]{2,1,0:T(8,128)(2,1)}, bf16[8,128,256]{2,1,0:T(8,128)(2,1)S(1)}, u32[]{:S(2)}) copy-start(bf16[8,128,256]{2,1,0:T(8,128)(2,1)S(1)} %collective-permute-done.12.refs_1_) | copy-start | bytes 1572868
  94.6 22.8 %copy-start.8 = (bf16[8,128,256]{2,1,0:T(8,128)(2,1)}, bf16[8,128,256]{2,1,0:T(8,128)(2,1)S(1)}, u32[]{:S(2)}) copy-start(bf16[8,128,256]{2,1,0:T(8,128)(2,1)S(1)} %collective-permute-done.13.refs_2_) | copy-start | bytes 1572868
  110.3 35.1 %all-to-all-start.2 = ((bf16[16,128,256]{2,1,0:T(8,128)(2,1)}), bf16[16,128,256]{2,1,0:T(8,128)(2,1)}, u32[]{:S(2)}, u32[]{:S(2)}) async-start(bf16[16,128,256]{2,1,0:T(8,128)(2,1)} %get-tuple-element.69), calls=%async_computation.2 | async-start | bytes 2097152 | tf_op jit(solution)/shard_map/all_to_all | solution.py:460
  121.3 9.2 %collective-permute-start.18 = (bf16[4,128,256]{2,1,0:T(8,128)(2,1)S(1)}, bf16[4,128,256]{2,1,0:T(8,128)(2,1)S(1)}, u32[]{:S(2)}, u32[]{:S(2)}) collective-permute-start(bf16[4,128,256]{2,1,0:T(8,128)(2,1)S(1)} %get-tuple-element.82), channel_id=1, source_target_pairs={{0,4},{1,5},{2,6},{3,7},{4,8},{5,9},{6,10},{7,11},{8,12},{9,13},{1... | collective-permute-start | bytes 786440 | tf_op jit(solution)/shard_map/ppermute | solution.py:38
  122.8 25.0 %collective-permute-start.15 = (bf16[4,128,256]{2,1,0:T(8,128)(2,1)}, bf16[4,128,256]{2,1,0:T(8,128)(2,1)S(1)}, u32[]{:S(2)}, u32[]{:S(2)}) collective-permute-start(bf16[4,128,256]{2,1,0:T(8,128)(2,1)} %get-tuple-element.77), channel_id=1, source_target_pairs={{0,1},{1,2},{2,3},{3,0},{4,5},{5,6},{6,7},{7,4},{8,9},{9,10},{10,1... | collective-permute-start | bytes 786440 | tf_op jit(solution)/shard_map/ppermute | solution.py:38
  122.8 25.0 %collective-permute-start.16 = (bf16[4,128,256]{2,1,0:T(8,128)(2,1)}, bf16[4,128,256]{2,1,0:T(8,128)(2,1)S(1)}, u32[]{:S(2)}, u32[]{:S(2)}) collective-permute-start(bf16[4,128,256]{2,1,0:T(8,128)(2,1)} %get-tuple-element.78), channel_id=1, source_target_pairs={{0,2},{1,3},{2,0},{3,1},{4,6},{5,7},{6,4},{7,5},{8,10},{9,11},{10,... | collective-permute-start | bytes 786440 | tf_op jit(solution)/shard_map/ppermute | solution.py:38
  124.3 23.5 %collective-permute-start.17 = (bf16[4,128,256]{2,1,0:T(8,128)(2,1)}, bf16[4,128,256]{2,1,0:T(8,128)(2,1)S(1)}, u32[]{:S(2)}, u32[]{:S(2)}) collective-permute-start(bf16[4,128,256]{2,1,0:T(8,128)(2,1)} %get-tuple-element.79), channel_id=1, source_target_pairs={{0,3},{1,0},{2,1},{3,2},{4,7},{5,4},{6,5},{7,6},{8,11},{9,8},{10,9... | collective-permute-start | bytes 786440 | tf_op jit(solution)/shard_map/ppermute | solution.py:38
  125.5 22.3 %collective-permute-start.20 = (bf16[4,128,256]{2,1,0:T(8,128)(2,1)}, bf16[4,128,256]{2,1,0:T(8,128)(2,1)S(1)}, u32[]{:S(2)}, u32[]{:S(2)}) collective-permute-start(bf16[4,128,256]{2,1,0:T(8,128)(2,1)} %get-tuple-element.85), channel_id=1, source_target_pairs={{0,12},{1,13},{2,14},{3,15},{4,0},{5,1},{6,2},{7,3},{8,4},{9,5},{1... | collective-permute-start | bytes 786440 | tf_op jit(solution)/shard_map/ppermute | solution.py:38
  130.4 17.4 %collective-permute-start.19 = (bf16[4,128,256]{2,1,0:T(8,128)(2,1)S(1)}, bf16[4,128,256]{2,1,0:T(8,128)(2,1)S(1)}, u32[]{:S(2)}, u32[]{:S(2)}) collective-permute-start(bf16[4,128,256]{2,1,0:T(8,128)(2,1)S(1)} %get-tuple-element.84), channel_id=1, source_target_pairs={{0,8},{1,9},{2,10},{3,11},{4,12},{5,13},{6,14},{7,15},{8,0},{9,1},... | collective-permute-start | bytes 786440 | tf_op jit(solution)/shard_map/ppermute | solution.py:38
  (2 other events, 10.8 us)

commit v7 on v6

--- a/solution.py
+++ b/solution.py
@@ -16,7 +16,8 @@
 VMEM = pl.BlockSpec(memory_space=pltpu.VMEM)
 SMEM = pl.BlockSpec(memory_space=pltpu.SMEM)
 SELECT_VMEM = 10 * 1024 * 1024
-SPREAD_VMEM = 8 * 1024 * 1024
+SPREAD_VMEM = 12 * 1024 * 1024
+SPREAD_FLOPS = 200_000_000_000
 ATTEND_VMEM = 20 * 1024 * 1024
 COLLECT_VMEM = 8 * 1024 * 1024
 
@@ -155,7 +156,7 @@
                     distance = lax.rem(where[1 - across] - mine[1 - across] + SIDE, SIDE)
                     row = distance * owned + where[2]
                     take_ref[across, k * most + count] = row
-                    add_ref[across, row * SIDE + k] = count + (other if across == 0 else k) * most
+                    add_ref[across, row * SIDE + k] = count
 
                 return count + found.astype(jnp.int32)
 
@@ -216,28 +217,27 @@
     return (out[:4], out[4:])
 
 
-def spread_body(add_ref, key_ref, *refs):
-    value_refs, key_outs, value_outs, (pool, sems) = refs[:4], refs[4:8], refs[8:12], refs[12:]
-    most = value_refs[0].shape[0]
+def spread_body(add_ref, *refs):
+    outs, (pool, sems) = (refs[8:12], refs[12:16]), refs[16:]
+    most = refs[0].shape[0]
     copies = [
-        pltpu.make_async_copy(ref, pool.at[pl.ds(k * most, most)], sems.at[k])
-        for k, ref in enumerate(value_refs)
+        pltpu.make_async_copy(ref, pool.at[pl.ds(n * most, most)], sems.at[n])
+        for n, ref in enumerate(refs[:8])
     ]
     for copy in copies:
         copy.start()
-    for across, terms, outs in ((0, key_ref, key_outs), (1, pool, value_outs)):
-        owned = outs[0].shape[0]
-        if across == 1:
-            for copy in copies:
-                copy.wait()
+    for across in range(2):
+        owned = outs[across][0].shape[0]
+        for copy in copies[SIDE * across : SIDE * (across + 1)]:
+            copy.wait()
 
         def add(n, carry):
-            for distance, out in enumerate(outs):
+            for distance, out in enumerate(outs[across]):
                 value = jnp.zeros(out.shape[1:], F32)
                 for k in range(SIDE):
                     index = add_ref[across, (distance * owned + n) * SIDE + k]
-                    term = terms[jnp.maximum(index, 0)].astype(F32)
-                    value += jnp.where(index >= 0, term, 0.0)
+                    slot = (SIDE * across + k) * most + jnp.maximum(index, 0)
+                    value += jnp.where(index >= 0, pool[slot].astype(F32), 0.0)
                 out[n] = value.astype(out.dtype)
             return carry
 
@@ -249,15 +249,22 @@
 
 
 def spread(add, keys, values, owned):
-    rows, nbr, width = keys.shape
+    most, nbr, width = keys[0].shape
+    return_shapes = chunk_shapes(owned, nbr, width, F32) * 2
     out = pl.pallas_call(
         spread_body,
-        out_shape=chunk_shapes(owned, nbr, width, F32) * 2,
-        in_specs=[SMEM, VMEM] + [HBM] * 4,
+        out_shape=return_shapes,
+        in_specs=[SMEM] + [HBM] * 8,
         out_specs=(VMEM,) * 8,
-        scratch_shapes=[pltpu.VMEM((rows, nbr, width), BF16), pltpu.SemaphoreType.DMA((SIDE,))],
+        scratch_shapes=[
+            pltpu.VMEM((2 * SIDE * most, nbr, width), BF16),
+            pltpu.SemaphoreType.DMA((2 * SIDE,)),
+        ],
         compiler_params=pltpu.CompilerParams(vmem_limit_bytes=SPREAD_VMEM),
-    )(add, keys, *in_hbm(values))
+        cost_estimate=pl.CostEstimate(
+            flops=SPREAD_FLOPS, bytes_accessed=4 * 1024 * 1024, transcendentals=0
+        ),
+    )(add, *in_hbm(keys), *in_hbm(values))
     return (out[:4], out[4:])
 
 
@@ -265,10 +272,9 @@
     groups, distinct, owned, most, unroll, ids_ref, refs_ref, tokens_ref, *refs
 ):
     key_parts, value_parts = refs[:4], refs[4:8]
-    gq_out, key_all, value_out = refs[8], refs[9], refs[10:14]
-    key_out = [key_all.at[pl.ds(k * most, most)] for k in range(SIDE)]
+    gq_out, key_out, value_out = refs[8], refs[9:13], refs[13:17]
     (keys, values, key_sum, value_sum, gq_ref, key_send, value_send, query_last, grad_last, held,
-     key_rows, value_rows, key_back, value_back, counts, in_sems, out_sems, gq_sem) = refs[14:]
+     key_rows, value_rows, key_back, value_back, counts, in_sems, out_sems, gq_sem) = refs[17:]
     scale = 1.0 / math.sqrt(DH)
     copies = [
         pltpu.make_async_copy(part, pool.at[pl.ds(k * most, most)], in_sems.at[i, k])
@@ -302,7 +308,7 @@
             distance = (mine[i] - where[i] + SIDE) % SIDE
             count = counts[i * SIDE + distance]
             table[j] = distance * most + count
-            back_rows[(where[0] if i == 0 else distance) * most + count] = j
+            back_rows[distance * most + count] = j
             counts[i * SIDE + distance] = count + 1
         return carry
 
@@ -400,15 +406,14 @@
     rows = pltpu.VMEM((GROUP, width), F32)
     table = pltpu.SMEM((distinct,), jnp.int32)
     reverse = pltpu.SMEM((SIDE * most,), jnp.int32)
-    shapes = (
-        jax.ShapeDtypeStruct((parts, part_tokens, width), BF16),
-        jax.ShapeDtypeStruct((SIDE * most, nbr, width), BF16),
-    ) + chunk_shapes(most, nbr, width)
+    shapes = (jax.ShapeDtypeStruct((parts, part_tokens, width), BF16),) + chunk_shapes(
+        most, nbr, width
+    ) * 2
     out = pl.pallas_call(
         functools.partial(attend_body, groups, distinct, owned, most, 8),
         out_shape=tuple(pltpu.HBM(shape.shape, shape.dtype) for shape in shapes),
         in_specs=[SMEM, SMEM, VMEM] + [HBM] * 8,
-        out_specs=(HBM,) * 6,
+        out_specs=(HBM,) * 9,
         scratch_shapes=[pool, pool, total, total, pltpu.VMEM((parts, part_tokens, width), BF16),
                         pool, pool, rows, rows, rows, table, table, reverse, reverse,
                         pltpu.SMEM((2 * SIDE,), jnp.int32),
@@ -416,7 +421,7 @@
                         pltpu.SemaphoreType.DMA],
         compiler_params=pltpu.CompilerParams(vmem_limit_bytes=ATTEND_VMEM),
     )(ids, flat, tokens, *in_hbm(keys), *in_hbm(values))
-    return (out[0], out[1], out[2:])
+    return (out[0], out[1:5], out[5:])
 
 
 def collect_body(*refs):
@@ -451,12 +456,7 @@
     keys, values = select(take, *lines, most)
     keys, values = exchange_lines(((keys, "y", 1), (values, "x", 1)))
     back, keys, values = attend(distinct_ids, group_refs, tokens, keys, values, owned, most)
-    keys = lax.all_to_all(
-        keys, "dp", split_axis=0, concat_axis=0, tiled=True,
-        axis_index_groups=[[y * SIDE + x for y in range(SIDE)] for x in range(SIDE)],
-    )
-    values = (values[0],) + tuple(shift(values[k], "x", -k) for k in range(1, SIDE))
-    back, keys, values = lax.optimization_barrier((back, keys, values))
+    keys, values = exchange_lines(((keys, "y", -1), (values, "x", -1)))
     back = lax.all_to_all(back, "ctx", split_axis=0, concat_axis=0, tiled=True)
     keys, values = spread(add, keys, values, owned)
     keys, values = exchange_lines(((keys, "x", 1), (values, "y", 1)))

time: 149 us -> 138 us (0.926)
  the two profiles are of different devices: /device:TPU:1 before, /device:TPU:3 now
where the time goes in v7:
time: 138 us; the launch traced here: 137 us
  starting transfers between devices  57.7 us (42%)
  waiting for transfers between devices  46.3 us (34%)
  Pallas kernels  30.4 us (22%)
  local copies, waits for them, and re-layouts  2.22 us (2%)
    ppermute x24, waiting for transfers between devices, shift(): return lax.ppermute(value, 'dp', pairs)  33.3 us
    ppermute x24, starting transfers between devices, shift(): return lax.ppermute(value, 'dp', pairs)  31.5 us
    all_to_all x1, starting transfers between devices, on_device(): back = lax.all_to_all(back, 'ctx', split_axis=0, concat_axis=0, tiled=True)  16.9 us
    all_to_all x1, waiting for transfers between devices, on_device(): back = lax.all_to_all(back, 'ctx', split_axis=0, concat_axis=0, tiled=True)  13 us
    pallas_call x1, Pallas kernels, attend(): pl.pallas_call(functools.partial(attend_body, groups, distinct, owned, mo...  12 us
    all_to_all x1, starting transfers between devices, on_device(): lax.all_to_all(packed, 'ctx', split_axis=0, concat_axis=0, tiled=True)  9.3 us
    pallas_call x1, Pallas kernels, spread(): pl.pallas_call(spread_body, out_shape=return_shapes, in_specs=[SMEM] + [H...  4.49 us
    pallas_call x1, Pallas kernels, tables(): pl.pallas_call(functools.partial(tables_body, owned, most), out_shape=(ja...  3.94 us
  transfers between devices with their start and end apart: 26, of which 12 were waited for; matrix products, arithmetic and copies ran while one was open for 0% of the time, Pallas kernels for 11%

profile of v7, /device:TPU:3, one launch (start us, length us, event | category | flops | bytes accessed | tf_op | source)
XLA Modules:
  0.0 137.5 jit_solution(7822898703282716543)
XLA Ops:
  0.6 2.7 %shard_map.85 = bf16[16,2,128,256]{3,2,1,0:T(8,128)(2,1)} custom-call(bf16[128,4096]{1,0:T(8,128)(2,1)} %bitcast.5, bf16[128,4096]{1,0:T(8,128)(2,1)} %bitcast.6), custom_call_target="tpu_custom_call" | custom-call | tf_op jit(solution)/shard_map/pallas_call | solution.py:87
  3.4 9.3 %all-to-all-start = ((bf16[16,2,128,256]{3,2,1,0:T(8,128)(2,1)}), bf16[16,2,128,256]{3,2,1,0:T(8,128)(2,1)S(1)}, u32[]{:S(2)}, u32[]{:S(2)}) async-start(bf16[16,2,128,256]{3,2,1,0:T(8,128)(2,1)} %shard_map.85), calls=%async_computation | async-start | bytes 4194304 | tf_op jit(solution)/shard_map/all_to_all | solution.py:455
  12.7 2.8 %collective-permute-start.3 = (bf16[4,128,256]{2,1,0:T(8,128)(2,1)S(1)}, bf16[4,128,256]{2,1,0:T(8,128)(2,1)S(1)}, u32[]{:S(2)}, u32[]{:S(2)}) collective-permute-start(bf16[4,128,256]{2,1,0:T(8,128)(2,1)S(1)} %copy-done.1), channel_id=1, source_target_pairs={{0,12},{1,13},{2,14},{3,15},{4,0},{5,1},{6,2},{7,3},{8,4},{9,5},{1... | collective-permute-start | bytes 786440 | tf_op jit(solution)/shard_map/ppermute | solution.py:39
  15.5 1.8 %collective-permute-start.1 = (bf16[4,128,256]{2,1,0:T(8,128)(2,1)S(1)}, bf16[4,128,256]{2,1,0:T(8,128)(2,1)S(1)}, u32[]{:S(2)}, u32[]{:S(2)}) collective-permute-start(bf16[4,128,256]{2,1,0:T(8,128)(2,1)S(1)} %copy-done), channel_id=1, source_target_pairs={{0,2},{1,3},{2,0},{3,1},{4,6},{5,7},{6,4},{7,5},{8,10},{9,11},{10,... | collective-permute-start | bytes 786440 | tf_op jit(solution)/shard_map/ppermute | solution.py:39
  17.4 1.2 collective-permute-start
  18.9 2.3 %collective-permute-done.3.refs_5_ = bf16[4,128,256]{2,1,0:T(8,128)(2,1)S(1)} collective-permute-done((bf16[4,128,256]{2,1,0:T(8,128)(2,1)S(1)}, bf16[4,128,256]{2,1,0:T(8,128)(2,1)S(1)}, u32[]{:S(2)}, u32[]{:S(2)}) %collective-permute-start.3) | collective-permute-done | bytes 262176 | tf_op jit(solution)/shard_map/ppermute | solution.py:39
  21.2 2.4 %collective-permute-start.4 = (bf16[4,128,256]{2,1,0:T(8,128)(2,1)S(1)}, bf16[4,128,256]{2,1,0:T(8,128)(2,1)}, u32[]{:S(2)}, u32[]{:S(2)}) collective-permute-start(bf16[4,128,256]{2,1,0:T(8,128)(2,1)S(1)} %copy-done.1), channel_id=1, source_target_pairs={{0,8},{1,9},{2,10},{3,11},{4,12},{5,13},{6,14},{7,15},{8,0},{9,1},... | collective-permute-start | bytes 786440 | tf_op jit(solution)/shard_map/ppermute | solution.py:39
  23.6 3.9 %shard_map.86 = (s32[2,32]{1,0:T(2,128)}, s32[2,64]{1,0:T(2,128)}) custom-call(s32[16,16]{1,0:T(8,128)} %ids_ref.3), custom_call_target="tpu_custom_call" | custom-call | tf_op jit(solution)/shard_map/pallas_call | solution.py:167
  27.5 3.5 %collective-permute-done.refs_1_ = bf16[4,128,256]{2,1,0:T(8,128)(2,1)S(1)} collective-permute-done((bf16[4,128,256]{2,1,0:T(8,128)(2,1)S(1)}, bf16[4,128,256]{2,1,0:T(8,128)(2,1)S(1)}, u32[]{:S(2)}, u32[]{:S(2)}) %collective-permute-start) | collective-permute-done | bytes 262176 | tf_op jit(solution)/shard_map/ppermute | solution.py:39
  32.1 3.9 %shard_map.87 = (bf16[8,128,256]{2,1,0:T(8,128)(2,1)}, bf16[8,128,256]{2,1,0:T(8,128)(2,1)}, bf16[8,128,256]{2,1,0:T(8,128)(2,1)}, bf16[8,128,256]{2,1,0:T(8,128...) custom-call(s32[2,32]{1,0:T(2,128)S(1)} %copy-done.3, ...), custom_call_target="tpu_custom_call" | custom-call | tf_op jit(solution)/shard_map/pallas_call | solution.py:209
  36.0 1.1 collective-permute-start.9
  37.1 3.1 %collective-permute-start.7 = (bf16[8,128,256]{2,1,0:T(8,128)(2,1)}, bf16[8,128,256]{2,1,0:T(8,128)(2,1)}, u32[]{:S(2)}, u32[]{:S(2)}) collective-permute-start(bf16[8,128,256]{2,1,0:T(8,128)(2,1)} %get-tuple-element.54), channel_id=1, source_target_pairs={{0,8},{1,9},{2,10},{3,11},{4,12},{5,13},{6,14},{7,15},{8,0},{9,1},... | collective-permute-start | bytes 1572872 | tf_op jit(solution)/shard_map/ppermute | solution.py:39
  40.4 1.4 %collective-permute-start.11 = (bf16[8,128,256]{2,1,0:T(8,128)(2,1)}, bf16[8,128,256]{2,1,0:T(8,128)(2,1)}, u32[]{:S(2)}, u32[]{:S(2)}) collective-permute-start(bf16[8,128,256]{2,1,0:T(8,128)(2,1)} %get-tuple-element.61), channel_id=1, source_target_pairs={{0,3},{1,0},{2,1},{3,2},{4,7},{5,4},{6,5},{7,6},{8,11},{9,8},{10,9... | collective-permute-start | bytes 1572872 | tf_op jit(solution)/shard_map/ppermute | solution.py:39
  41.8 4.6 %collective-permute-done.9.refs_5_ = bf16[8,128,256]{2,1,0:T(8,128)(2,1)S(1)} collective-permute-done((bf16[8,128,256]{2,1,0:T(8,128)(2,1)S(1)}, bf16[8,128,256]{2,1,0:T(8,128)(2,1)S(1)}, u32[]{:S(2)}, u32[]{:S(2)}) %collective-permute-start.9) | collective-permute-done | bytes 524320 | tf_op jit(solution)/shard_map/ppermute | solution.py:39
  46.4 2.3 %collective-permute-start.10 = (bf16[8,128,256]{2,1,0:T(8,128)(2,1)}, bf16[8,128,256]{2,1,0:T(8,128)(2,1)}, u32[]{:S(2)}, u32[]{:S(2)}) collective-permute-start(bf16[8,128,256]{2,1,0:T(8,128)(2,1)} %get-tuple-element.60), channel_id=1, source_target_pairs={{0,2},{1,3},{2,0},{3,1},{4,6},{5,7},{6,4},{7,5},{8,10},{9,11},{10,... | collective-permute-start | bytes 1572872 | tf_op jit(solution)/shard_map/ppermute | solution.py:39
  49.6 12.1 %collective-permute-done.7.refs_2_ = bf16[8,128,256]{2,1,0:T(8,128)(2,1)} collective-permute-done((bf16[8,128,256]{2,1,0:T(8,128)(2,1)}, bf16[8,128,256]{2,1,0:T(8,128)(2,1)}, u32[]{:S(2)}, u32[]{:S(2)}) %collective-permute-start.7) | collective-permute-done | bytes 524320 | tf_op jit(solution)/shard_map/ppermute | solution.py:39
  61.7 1.6 %collective-permute-done.8.refs_3_ = bf16[8,128,256]{2,1,0:T(8,128)(2,1)} collective-permute-done((bf16[8,128,256]{2,1,0:T(8,128)(2,1)}, bf16[8,128,256]{2,1,0:T(8,128)(2,1)}, u32[]{:S(2)}, u32[]{:S(2)}) %collective-permute-start.8) | collective-permute-done | bytes 524320 | tf_op jit(solution)/shard_map/ppermute | solution.py:39
  63.3 0.9 collective-permute-done.10.refs_6_
  64.3 12.0 %shard_map.88 = (bf16[16,128,256]{2,1,0:T(8,128)(2,1)}, bf16[8,128,256]{2,1,0:T(8,128)(2,1)}, bf16[8,128,256]{2,1,0:T(8,128)(2,1)}, bf16[8,128,256]{2,1,0:T(8,12...) custom-call(s32[16,16]{1,0:T(8,128)S(1)} %copy-done.2, ...), custom_call_target="tpu_custom_call" | custom-call | tf_op jit(solution)/shard_map/pallas_call | solution.py:412
  76.6 2.9 %collective-permute-start.12 = (bf16[8,128,256]{2,1,0:T(8,128)(2,1)}, bf16[8,128,256]{2,1,0:T(8,128)(2,1)S(1)}, u32[]{:S(2)}, u32[]{:S(2)}) collective-permute-start(bf16[8,128,256]{2,1,0:T(8,128)(2,1)} %get-tuple-element.65), channel_id=1, source_target_pairs={{0,12},{1,13},{2,14},{3,15},{4,0},{5,1},{6,2},{7,3},{8,4},{9,5},{1... | collective-permute-start | bytes 1572872 | tf_op jit(solution)/shard_map/ppermute | solution.py:39
  80.3 1.1 collective-permute-start.17
  81.4 5.0 %collective-permute-done.15.refs_5_ = bf16[8,128,256]{2,1,0:T(8,128)(2,1)S(1)} collective-permute-done((bf16[8,128,256]{2,1,0:T(8,128)(2,1)}, bf16[8,128,256]{2,1,0:T(8,128)(2,1)S(1)}, u32[]{:S(2)}, u32[]{:S(2)}) %collective-permute-start.15) | collective-permute-done | bytes 524320 | tf_op jit(solution)/shard_map/ppermute | solution.py:39
  86.4 2.8 %collective-permute-start.16 = (bf16[8,128,256]{2,1,0:T(8,128)(2,1)}, bf16[8,128,256]{2,1,0:T(8,128)(2,1)S(1)}, u32[]{:S(2)}, u32[]{:S(2)}) collective-permute-start(bf16[8,128,256]{2,1,0:T(8,128)(2,1)} %get-tuple-element.72), channel_id=1, source_target_pairs={{0,2},{1,3},{2,0},{3,1},{4,6},{5,7},{6,4},{7,5},{8,10},{9,11},{10,... | collective-permute-start | bytes 1572872 | tf_op jit(solution)/shard_map/ppermute | solution.py:39
  89.2 16.9 %all-to-all-start.1 = ((bf16[16,128,256]{2,1,0:T(8,128)(2,1)}), bf16[16,128,256]{2,1,0:T(8,128)(2,1)}, u32[]{:S(2)}, u32[]{:S(2)}) async-start(bf16[16,128,256]{2,1,0:T(8,128)(2,1)} %get-tuple-element.62), calls=%async_computation.1 | async-start | bytes 2097152 | tf_op jit(solution)/shard_map/all_to_all | solution.py:460
  107.7 4.5 %shard_map.90 = (f32[4,128,256]{2,1,0:T(8,128)S(1)}, bf16[4,128,256]{2,1,0:T(8,128)(2,1)}, bf16[4,128,256]{2,1,0:T(8,128)(2,1)}, bf16[4,128,256]{2,1,0:T(8,128)(...) custom-call(s32[2,64]{1,0:T(2,128)S(1)} %copy-done.4, ...), custom_call_target="tpu_custom_call" | custom-call | flops 199999995904 | bytes 4194304 | tf_op jit(solution)/shard_map/pallas_call | solution.py:254
  112.3 1.2 collective-permute-start.18
  113.4 2.9 %collective-permute-start.19 = (bf16[4,128,256]{2,1,0:T(8,128)(2,1)}, bf16[4,128,256]{2,1,0:T(8,128)(2,1)S(1)}, u32[]{:S(2)}, u32[]{:S(2)}) collective-permute-start(bf16[4,128,256]{2,1,0:T(8,128)(2,1)} %get-tuple-element.76), channel_id=1, source_target_pairs={{0,2},{1,3},{2,0},{3,1},{4,6},{5,7},{6,4},{7,5},{8,10},{9,11},{10,... | collective-permute-start | bytes 786440 | tf_op jit(solution)/shard_map/ppermute | solution.py:39
  116.6 2.6 %collective-permute-start.23 = (bf16[4,128,256]{2,1,0:T(8,128)(2,1)S(1)}, bf16[4,128,256]{2,1,0:T(8,128)(2,1)S(1)}, u32[]{:S(2)}, u32[]{:S(2)}) collective-permute-start(bf16[4,128,256]{2,1,0:T(8,128)(2,1)S(1)} %get-tuple-element.83), channel_id=1, source_target_pairs={{0,12},{1,13},{2,14},{3,15},{4,0},{5,1},{6,2},{7,3},{8,4},{9,5},{1... | collective-permute-start | bytes 786440 | tf_op jit(solution)/shard_map/ppermute | solution.py:39
  119.2 1.9 %collective-permute-done.21.refs_5_ = bf16[4,128,256]{2,1,0:T(8,128)(2,1)S(1)} collective-permute-done((bf16[4,128,256]{2,1,0:T(8,128)(2,1)S(1)}, bf16[4,128,256]{2,1,0:T(8,128)(2,1)S(1)}, u32[]{:S(2)}, u32[]{:S(2)}) %collective-permute-start.21) | collective-permute-done | bytes 262176 | tf_op jit(solution)/shard_map/ppermute | solution.py:39
  121.1 13.0 %all-to-all-done.1.in_ref = bf16[16,128,256]{2,1,0:T(8,128)(2,1)} async-done(((bf16[16,128,256]{2,1,0:T(8,128)(2,1)}), bf16[16,128,256]{2,1,0:T(8,128)(2,1)}, u32[]{:S(2)}, u32[]{:S(2)}) %all-to-all-start.1) | async-done | bytes 1048608 | tf_op jit(solution)/shard_map/all_to_all | solution.py:460
  134.2 2.3 %shard_map.89 = bf16[128,4096]{1,0:T(8,128)(2,1)} custom-call(bf16[16,128,256]{2,1,0:T(8,128)(2,1)} %all-to-all-done.1.in_ref), custom_call_target="tpu_custom_call" | custom-call | tf_op jit(solution)/shard_map/pallas_call | solution.py:113
  136.5 0.9 shard_map.91
  (57 shorter events, 5.4 us)
Async XLA Ops:
  3.4 45.4 %copy-start.7 = (s32[16,32,2]{1,2,0:T(2,128)S(1)}, s32[16,32,2]{1,2,0:T(2,128)}, u32[]{:S(2)}) copy-start(s32[16,32,2]{1,2,0:T(2,128)} %param.11) | copy-start | bytes 12292
  3.4 60.9 %all-to-all-start = ((bf16[16,2,128,256]{3,2,1,0:T(8,128)(2,1)}), bf16[16,2,128,256]{3,2,1,0:T(8,128)(2,1)S(1)}, u32[]{:S(2)}, u32[]{:S(2)}) async-start(bf16[16,2,128,256]{3,2,1,0:T(8,128)(2,1)} %shard_map.85), calls=%async_computation | async-start | bytes 4194304 | tf_op jit(solution)/shard_map/all_to_all | solution.py:455
  12.7 51.6 %copy-start.2 = (s32[16,16]{1,0:T(8,128)S(1)}, s32[16,16]{1,0:T(8,128)}, u32[]{:S(2)}) copy-start(s32[16,16]{1,0:T(8,128)} %ids_ref.3) | copy-start | bytes 3076
  12.7 8.5 %collective-permute-start.3 = (bf16[4,128,256]{2,1,0:T(8,128)(2,1)S(1)}, bf16[4,128,256]{2,1,0:T(8,128)(2,1)S(1)}, u32[]{:S(2)}, u32[]{:S(2)}) collective-permute-start(bf16[4,128,256]{2,1,0:T(8,128)(2,1)S(1)} %copy-done.1), channel_id=1, source_target_pairs={{0,12},{1,13},{2,14},{3,15},{4,0},{5,1},{6,2},{7,3},{8,4},{9,5},{1... | collective-permute-start | bytes 786440 | tf_op jit(solution)/shard_map/ppermute | solution.py:39
  15.5 12.0 %collective-permute-start.1 = (bf16[4,128,256]{2,1,0:T(8,128)(2,1)S(1)}, bf16[4,128,256]{2,1,0:T(8,128)(2,1)S(1)}, u32[]{:S(2)}, u32[]{:S(2)}) collective-permute-start(bf16[4,128,256]{2,1,0:T(8,128)(2,1)S(1)} %copy-done), channel_id=1, source_target_pairs={{0,2},{1,3},{2,0},{3,1},{4,6},{5,7},{6,4},{7,5},{8,10},{9,11},{10,... | collective-permute-start | bytes 786440 | tf_op jit(solution)/shard_map/ppermute | solution.py:39
  17.4 13.6 %collective-permute-start = (bf16[4,128,256]{2,1,0:T(8,128)(2,1)S(1)}, bf16[4,128,256]{2,1,0:T(8,128)(2,1)S(1)}, u32[]{:S(2)}, u32[]{:S(2)}) collective-permute-start(bf16[4,128,256]{2,1,0:T(8,128)(2,1)S(1)} %copy-done), channel_id=1, source_target_pairs={{0,3},{1,0},{2,1},{3,2},{4,7},{5,4},{6,5},{7,6},{8,11},{9,8},{10,9... | collective-permute-start | bytes 786440 | tf_op jit(solution)/shard_map/ppermute | solution.py:39
  18.5 12.5 %collective-permute-start.2 = (bf16[4,128,256]{2,1,0:T(8,128)(2,1)S(1)}, bf16[4,128,256]{2,1,0:T(8,128)(2,1)}, u32[]{:S(2)}, u32[]{:S(2)}) collective-permute-start(bf16[4,128,256]{2,1,0:T(8,128)(2,1)S(1)} %copy-done), channel_id=1, source_target_pairs={{0,1},{1,2},{2,3},{3,0},{4,5},{5,6},{6,7},{7,4},{8,9},{9,10},{10,1... | collective-permute-start | bytes 786440 | tf_op jit(solution)/shard_map/ppermute | solution.py:39
  18.9 12.1 %collective-permute-start.5 = (bf16[4,128,256]{2,1,0:T(8,128)(2,1)S(1)}, bf16[4,128,256]{2,1,0:T(8,128)(2,1)}, u32[]{:S(2)}, u32[]{:S(2)}) collective-permute-start(bf16[4,128,256]{2,1,0:T(8,128)(2,1)S(1)} %copy-done.1), channel_id=1, source_target_pairs={{0,4},{1,5},{2,6},{3,7},{4,8},{5,9},{6,10},{7,11},{8,12},{9,13},{1... | collective-permute-start | bytes 786440 | tf_op jit(solution)/shard_map/ppermute | solution.py:39
  21.2 10.2 %collective-permute-start.4 = (bf16[4,128,256]{2,1,0:T(8,128)(2,1)S(1)}, bf16[4,128,256]{2,1,0:T(8,128)(2,1)}, u32[]{:S(2)}, u32[]{:S(2)}) collective-permute-start(bf16[4,128,256]{2,1,0:T(8,128)(2,1)S(1)} %copy-done.1), channel_id=1, source_target_pairs={{0,8},{1,9},{2,10},{3,11},{4,12},{5,13},{6,14},{7,15},{8,0},{9,1},... | collective-permute-start | bytes 786440 | tf_op jit(solution)/shard_map/ppermute | solution.py:39
  36.0 10.4 %collective-permute-start.9 = (bf16[8,128,256]{2,1,0:T(8,128)(2,1)S(1)}, bf16[8,128,256]{2,1,0:T(8,128)(2,1)S(1)}, u32[]{:S(2)}, u32[]{:S(2)}) collective-permute-start(bf16[8,128,256]{2,1,0:T(8,128)(2,1)S(1)} %get-tuple-element.58), channel_id=1, source_target_pairs={{0,1},{1,2},{2,3},{3,0},{4,5},{5,6},{6,7},{7,4},{8,9},{9,10},{10,1... | collective-permute-start | bytes 1572872 | tf_op jit(solution)/shard_map/ppermute | solution.py:39
  37.1 12.5 %collective-permute-start.6 = (bf16[8,128,256]{2,1,0:T(8,128)(2,1)}, bf16[8,128,256]{2,1,0:T(8,128)(2,1)S(1)}, u32[]{:S(2)}, u32[]{:S(2)}) collective-permute-start(bf16[8,128,256]{2,1,0:T(8,128)(2,1)} %get-tuple-element.53), channel_id=1, source_target_pairs={{0,4},{1,5},{2,6},{3,7},{4,8},{5,9},{6,10},{7,11},{8,12},{9,13},{1... | collective-permute-start | bytes 1572872 | tf_op jit(solution)/shard_map/ppermute | solution.py:39
  37.1 24.6 %collective-permute-start.7 = (bf16[8,128,256]{2,1,0:T(8,128)(2,1)}, bf16[8,128,256]{2,1,0:T(8,128)(2,1)}, u32[]{:S(2)}, u32[]{:S(2)}) collective-permute-start(bf16[8,128,256]{2,1,0:T(8,128)(2,1)} %get-tuple-element.54), channel_id=1, source_target_pairs={{0,8},{1,9},{2,10},{3,11},{4,12},{5,13},{6,14},{7,15},{8,0},{9,1},... | collective-permute-start | bytes 1572872 | tf_op jit(solution)/shard_map/ppermute | solution.py:39
  40.2 23.1 %collective-permute-start.8 = (bf16[8,128,256]{2,1,0:T(8,128)(2,1)}, bf16[8,128,256]{2,1,0:T(8,128)(2,1)}, u32[]{:S(2)}, u32[]{:S(2)}) collective-permute-start(bf16[8,128,256]{2,1,0:T(8,128)(2,1)} %get-tuple-element.55), channel_id=1, source_target_pairs={{0,12},{1,13},{2,14},{3,15},{4,0},{5,1},{6,2},{7,3},{8,4},{9,5},{1... | collective-permute-start | bytes 1572872 | tf_op jit(solution)/shard_map/ppermute | solution.py:39
  40.4 22.9 %collective-permute-start.11 = (bf16[8,128,256]{2,1,0:T(8,128)(2,1)}, bf16[8,128,256]{2,1,0:T(8,128)(2,1)}, u32[]{:S(2)}, u32[]{:S(2)}) collective-permute-start(bf16[8,128,256]{2,1,0:T(8,128)(2,1)} %get-tuple-element.61), channel_id=1, source_target_pairs={{0,3},{1,0},{2,1},{3,2},{4,7},{5,4},{6,5},{7,6},{8,11},{9,8},{10,9... | collective-permute-start | bytes 1572872 | tf_op jit(solution)/shard_map/ppermute | solution.py:39
  46.4 17.9 %copy-start.5 = (bf16[8,128,256]{2,1,0:T(8,128)(2,1)}, bf16[8,128,256]{2,1,0:T(8,128)(2,1)S(1)}, u32[]{:S(2)}) copy-start(bf16[8,128,256]{2,1,0:T(8,128)(2,1)S(1)} %collective-permute-done.9.refs_5_) | copy-start | bytes 1572868
  46.4 17.9 %collective-permute-start.10 = (bf16[8,128,256]{2,1,0:T(8,128)(2,1)}, bf16[8,128,256]{2,1,0:T(8,128)(2,1)}, u32[]{:S(2)}, u32[]{:S(2)}) collective-permute-start(bf16[8,128,256]{2,1,0:T(8,128)(2,1)} %get-tuple-element.60), channel_id=1, source_target_pairs={{0,2},{1,3},{2,0},{3,1},{4,6},{5,7},{6,4},{7,5},{8,10},{9,11},{10,... | collective-permute-start | bytes 1572872 | tf_op jit(solution)/shard_map/ppermute | solution.py:39
  49.6 14.6 %copy-start.6 = (bf16[8,128,256]{2,1,0:T(8,128)(2,1)}, bf16[8,128,256]{2,1,0:T(8,128)(2,1)S(1)}, u32[]{:S(2)}) copy-start(bf16[8,128,256]{2,1,0:T(8,128)(2,1)S(1)} %collective-permute-done.6.refs_1_) | copy-start | bytes 1572868
  76.3 31.4 %copy-start.4 = (s32[2,64]{1,0:T(2,128)S(1)}, s32[2,64]{1,0:T(2,128)}, u32[]{:S(2)}) copy-start(s32[2,64]{1,0:T(2,128)} %get-tuple-element.63.add_ref) | copy-start | bytes 1540
  76.3 10.1 %collective-permute-start.15 = (bf16[8,128,256]{2,1,0:T(8,128)(2,1)}, bf16[8,128,256]{2,1,0:T(8,128)(2,1)S(1)}, u32[]{:S(2)}, u32[]{:S(2)}) collective-permute-start(bf16[8,128,256]{2,1,0:T(8,128)(2,1)} %get-tuple-element.70), channel_id=1, source_target_pairs={{0,3},{1,0},{2,1},{3,2},{4,7},{5,4},{6,5},{7,6},{8,11},{9,8},{10,9... | collective-permute-start | bytes 1572872 | tf_op jit(solution)/shard_map/ppermute | solution.py:39
  76.6 29.5 %collective-permute-start.12 = (bf16[8,128,256]{2,1,0:T(8,128)(2,1)}, bf16[8,128,256]{2,1,0:T(8,128)(2,1)S(1)}, u32[]{:S(2)}, u32[]{:S(2)}) collective-permute-start(bf16[8,128,256]{2,1,0:T(8,128)(2,1)} %get-tuple-element.65), channel_id=1, source_target_pairs={{0,12},{1,13},{2,14},{3,15},{4,0},{5,1},{6,2},{7,3},{8,4},{9,5},{1... | collective-permute-start | bytes 1572872 | tf_op jit(solution)/shard_map/ppermute | solution.py:39
  79.5 26.6 %collective-permute-start.13 = (bf16[8,128,256]{2,1,0:T(8,128)(2,1)}, bf16[8,128,256]{2,1,0:T(8,128)(2,1)S(1)}, u32[]{:S(2)}, u32[]{:S(2)}) collective-permute-start(bf16[8,128,256]{2,1,0:T(8,128)(2,1)} %get-tuple-element.66), channel_id=1, source_target_pairs={{0,8},{1,9},{2,10},{3,11},{4,12},{5,13},{6,14},{7,15},{8,0},{9,1},... | collective-permute-start | bytes 1572872 | tf_op jit(solution)/shard_map/ppermute | solution.py:39
  80.3 26.0 %collective-permute-start.14 = (bf16[8,128,256]{2,1,0:T(8,128)(2,1)}, bf16[8,128,256]{2,1,0:T(8,128)(2,1)S(1)}, u32[]{:S(2)}, u32[]{:S(2)}) collective-permute-start(bf16[8,128,256]{2,1,0:T(8,128)(2,1)} %get-tuple-element.67), channel_id=1, source_target_pairs={{0,4},{1,5},{2,6},{3,7},{4,8},{5,9},{6,10},{7,11},{8,12},{9,13},{1... | collective-permute-start | bytes 1572872 | tf_op jit(solution)/shard_map/ppermute | solution.py:39
  80.3 26.0 %collective-permute-start.17 = (bf16[8,128,256]{2,1,0:T(8,128)(2,1)}, bf16[8,128,256]{2,1,0:T(8,128)(2,1)S(1)}, u32[]{:S(2)}, u32[]{:S(2)}) collective-permute-start(bf16[8,128,256]{2,1,0:T(8,128)(2,1)} %get-tuple-element.73), channel_id=1, source_target_pairs={{0,1},{1,2},{2,3},{3,0},{4,5},{5,6},{6,7},{7,4},{8,9},{9,10},{10,1... | collective-permute-start | bytes 1572872 | tf_op jit(solution)/shard_map/ppermute | solution.py:39
  86.4 21.3 %copy-start.8 = (bf16[8,128,256]{2,1,0:T(8,128)(2,1)}, bf16[8,128,256]{2,1,0:T(8,128)(2,1)S(1)}, u32[]{:S(2)}) copy-start(bf16[8,128,256]{2,1,0:T(8,128)(2,1)S(1)} %collective-permute-done.15.refs_5_) | copy-start | bytes 1572868
  86.4 19.9 %collective-permute-start.16 = (bf16[8,128,256]{2,1,0:T(8,128)(2,1)}, bf16[8,128,256]{2,1,0:T(8,128)(2,1)S(1)}, u32[]{:S(2)}, u32[]{:S(2)}) collective-permute-start(bf16[8,128,256]{2,1,0:T(8,128)(2,1)} %get-tuple-element.72), channel_id=1, source_target_pairs={{0,2},{1,3},{2,0},{3,1},{4,6},{5,7},{6,4},{7,5},{8,10},{9,11},{10,... | collective-permute-start | bytes 1572872 | tf_op jit(solution)/shard_map/ppermute | solution.py:39
  89.2 45.0 %all-to-all-start.1 = ((bf16[16,128,256]{2,1,0:T(8,128)(2,1)}), bf16[16,128,256]{2,1,0:T(8,128)(2,1)}, u32[]{:S(2)}, u32[]{:S(2)}) async-start(bf16[16,128,256]{2,1,0:T(8,128)(2,1)} %get-tuple-element.62), calls=%async_computation.1 | async-start | bytes 2097152 | tf_op jit(solution)/shard_map/all_to_all | solution.py:460
  112.2 8.9 %collective-permute-start.21 = (bf16[4,128,256]{2,1,0:T(8,128)(2,1)S(1)}, bf16[4,128,256]{2,1,0:T(8,128)(2,1)S(1)}, u32[]{:S(2)}, u32[]{:S(2)}) collective-permute-start(bf16[4,128,256]{2,1,0:T(8,128)(2,1)S(1)} %get-tuple-element.80), channel_id=1, source_target_pairs={{0,4},{1,5},{2,6},{3,7},{4,8},{5,9},{6,10},{7,11},{8,12},{9,13},{1... | collective-permute-start | bytes 786440 | tf_op jit(solution)/shard_map/ppermute | solution.py:39
  112.3 24.2 %collective-permute-start.18 = (bf16[4,128,256]{2,1,0:T(8,128)(2,1)}, bf16[4,128,256]{2,1,0:T(8,128)(2,1)S(1)}, u32[]{:S(2)}, u32[]{:S(2)}) collective-permute-start(bf16[4,128,256]{2,1,0:T(8,128)(2,1)} %get-tuple-element.75), channel_id=1, source_target_pairs={{0,1},{1,2},{2,3},{3,0},{4,5},{5,6},{6,7},{7,4},{8,9},{9,10},{10,1... | collective-permute-start | bytes 786440 | tf_op jit(solution)/shard_map/ppermute | solution.py:39
  113.4 23.1 %collective-permute-start.19 = (bf16[4,128,256]{2,1,0:T(8,128)(2,1)}, bf16[4,128,256]{2,1,0:T(8,128)(2,1)S(1)}, u32[]{:S(2)}, u32[]{:S(2)}) collective-permute-start(bf16[4,128,256]{2,1,0:T(8,128)(2,1)} %get-tuple-element.76), channel_id=1, source_target_pairs={{0,2},{1,3},{2,0},{3,1},{4,6},{5,7},{6,4},{7,5},{8,10},{9,11},{10,... | collective-permute-start | bytes 786440 | tf_op jit(solution)/shard_map/ppermute | solution.py:39
  116.3 20.2 %collective-permute-start.20 = (bf16[4,128,256]{2,1,0:T(8,128)(2,1)S(1)}, bf16[4,128,256]{2,1,0:T(8,128)(2,1)S(1)}, u32[]{:S(2)}, u32[]{:S(2)}) collective-permute-start(bf16[4,128,256]{2,1,0:T(8,128)(2,1)S(1)} %get-tuple-element.77), channel_id=1, source_target_pairs={{0,3},{1,0},{2,1},{3,2},{4,7},{5,4},{6,5},{7,6},{8,11},{9,8},{10,9... | collective-permute-start | bytes 786440 | tf_op jit(solution)/shard_map/ppermute | solution.py:39
  116.6 19.9 %collective-permute-start.23 = (bf16[4,128,256]{2,1,0:T(8,128)(2,1)S(1)}, bf16[4,128,256]{2,1,0:T(8,128)(2,1)S(1)}, u32[]{:S(2)}, u32[]{:S(2)}) collective-permute-start(bf16[4,128,256]{2,1,0:T(8,128)(2,1)S(1)} %get-tuple-element.83), channel_id=1, source_target_pairs={{0,12},{1,13},{2,14},{3,15},{4,0},{5,1},{6,2},{7,3},{8,4},{9,5},{1... | collective-permute-start | bytes 786440 | tf_op jit(solution)/shard_map/ppermute | solution.py:39
  121.1 15.4 %collective-permute-start.22 = (bf16[4,128,256]{2,1,0:T(8,128)(2,1)S(1)}, bf16[4,128,256]{2,1,0:T(8,128)(2,1)S(1)}, u32[]{:S(2)}, u32[]{:S(2)}) collective-permute-start(bf16[4,128,256]{2,1,0:T(8,128)(2,1)S(1)} %get-tuple-element.82), channel_id=1, source_target_pairs={{0,8},{1,9},{2,10},{3,11},{4,12},{5,13},{6,14},{7,15},{8,0},{9,1},... | collective-permute-start | bytes 786440 | tf_op jit(solution)/shard_map/ppermute | solution.py:39
  (8 other events, 27.5 us)

commit v8 on v7

--- a/solution.py
+++ b/solution.py
@@ -52,7 +52,13 @@
 
 
 def gather_lines(keys, values):
-    return exchange_lines((((keys,) * SIDE, "x", -1), ((values,) * SIDE, "y", -1)))
+    lines = [[keys, None, None, None], [values, None, None, None]]
+    for distance in (1, 3):
+        for line, axis in zip(lines, "xy"):
+            line[distance] = shift(line[0], axis, -distance)
+    for line, axis in zip(lines, "xy"):
+        line[2] = shift(line[1], axis, -1)
+    return lines
 
 
 def chunk_shapes(most, nbr, width, own_type=BF16):
@@ -176,42 +182,52 @@
 
 
 def select_body(take_ref, *refs):
-    lines, kept, sems = refs[16:18], refs[18:20], refs[20]
-    copies = []
+    outs = (refs[8:12], refs[12:16])
+    line, picked, in_sems, out_sems = refs[16:]
+    owned = refs[0].shape[0]
+    most = outs[0][0].shape[0]
+    arrivals = [
+        pltpu.make_async_copy(ref, line.at[pl.ds(n * owned, owned)], in_sems.at[n])
+        for n, ref in enumerate(refs[:8])
+    ]
+    for copy in arrivals:
+        copy.start()
+    departures = []
     for across in range(2):
-        parts = refs[4 * across : 4 * across + 4]
-        line = lines[across]
-        owned = parts[0].shape[0]
-        for k, part in enumerate(parts):
-            for n in range(owned):
-                line[k * owned + n] = part[n]
-        own, *sent = refs[8 + 4 * across : 12 + 4 * across]
-        most = own.shape[0]
-
-        def pick(n, carry):
-            kept[across][n] = line[take_ref[across, n]]
-            for k, out in enumerate(sent):
-                out[n] = line[take_ref[across, (k + 1) * most + n]]
-            return carry
-
-        lax.fori_loop(0, most, pick, 0, unroll=2)
-        copies.append(pltpu.make_async_copy(kept[across], own, sems.at[across]))
-        copies[-1].start()
-    for copy in copies:
+        for copy in arrivals[SIDE * across : SIDE * (across + 1)]:
+            copy.wait()
+        for k in (2, 1, 3, 0) if across == 0 else (1, 3, 2, 0):
+            base = (SIDE * across + k) * most
+
+            def pick(n, carry):
+                picked[base + n] = line[SIDE * owned * across + take_ref[across, k * most + n]]
+                return carry
+
+            lax.fori_loop(0, most, pick, 0, unroll=4)
+            copy = pltpu.make_async_copy(
+                picked.at[pl.ds(base, most)], outs[across][k], out_sems.at[SIDE * across + k]
+            )
+            copy.start()
+            departures.append(copy)
+    for copy in departures:
         copy.wait()
 
 
 def select(take, keys, values, most):
     owned, nbr, width = keys[0].shape
-    line = pltpu.VMEM((SIDE * owned, nbr, width), BF16)
-    kept = pltpu.VMEM((most, nbr, width), BF16)
-    shapes = chunk_shapes(most, nbr, width)
     out = pl.pallas_call(
         select_body,
-        out_shape=((pltpu.HBM(shapes[0].shape, BF16),) + shapes[1:]) * 2,
-        in_specs=[SMEM] + [VMEM] * 8,
-        out_specs=((HBM,) + (VMEM,) * 3) * 2,
-        scratch_shapes=[line, line, kept, kept, pltpu.SemaphoreType.DMA((2,))],
+        out_shape=tuple(
+            pltpu.HBM(shape.shape, shape.dtype) for shape in chunk_shapes(most, nbr, width) * 2
+        ),
+        in_specs=[SMEM] + [HBM] * 8,
+        out_specs=(HBM,) * 8,
+        scratch_shapes=[
+            pltpu.VMEM((2 * SIDE * owned, nbr, width), BF16),
+            pltpu.VMEM((2 * SIDE * most, nbr, width), BF16),
+            pltpu.SemaphoreType.DMA((2 * SIDE,)),
+            pltpu.SemaphoreType.DMA((2 * SIDE,)),
+        ],
         compiler_params=pltpu.CompilerParams(vmem_limit_bytes=SELECT_VMEM),
     )(take, *keys, *values)
     return (out[:4], out[4:])

time: 138 us -> 138 us (level)
  the two profiles are of different devices: /device:TPU:3 before, /device:TPU:11 now
where the time goes in v8:
time: 138 us; the launch traced here: 137 us
  starting transfers between devices  53.6 us (39%)
  waiting for transfers between devices  50.4 us (37%)
  Pallas kernels  30.2 us (22%)
  local copies, waits for them, and re-layouts  2.31 us (2%)
    ppermute x24, waiting for transfers between devices, shift(): return lax.ppermute(value, 'dp', pairs)  36.1 us
    ppermute x24, starting transfers between devices, shift(): return lax.ppermute(value, 'dp', pairs)  27.1 us
    all_to_all x1, starting transfers between devices, on_device(): back = lax.all_to_all(back, 'ctx', split_axis=0, concat_axis=0, tiled=True)  17.2 us
    all_to_all x1, waiting for transfers between devices, on_device(): back = lax.all_to_all(back, 'ctx', split_axis=0, concat_axis=0, tiled=True)  14.4 us
    pallas_call x1, Pallas kernels, attend(): pl.pallas_call(functools.partial(attend_body, groups, distinct, owned, mo...  12.1 us
    all_to_all x1, starting transfers between devices, on_device(): lax.all_to_all(packed, 'ctx', split_axis=0, concat_axis=0, tiled=True)  9.3 us
    pallas_call x1, Pallas kernels, spread(): pl.pallas_call(spread_body, out_shape=return_shapes, in_specs=[SMEM] + [H...  4.49 us
    pallas_call x1, Pallas kernels, tables(): pl.pallas_call(functools.partial(tables_body, owned, most), out_shape=(ja...  3.94 us
  transfers between devices with their start and end apart: 26, of which 9 were waited for; matrix products, arithmetic and copies ran while one was open for 0% of the time, Pallas kernels for 11%

profile of v8, /device:TPU:11, one launch (start us, length us, event | category | flops | bytes accessed | tf_op | source)
XLA Modules:
  0.0 137.4 jit_solution(16988041527536662329)
XLA Ops:
  0.6 2.7 %shard_map.85 = bf16[16,2,128,256]{3,2,1,0:T(8,128)(2,1)} custom-call(bf16[128,4096]{1,0:T(8,128)(2,1)} %bitcast.5, bf16[128,4096]{1,0:T(8,128)(2,1)} %bitcast.6), custom_call_target="tpu_custom_call" | custom-call | tf_op jit(solution)/shard_map/pallas_call | solution.py:93
  3.4 9.3 %all-to-all-start = ((bf16[16,2,128,256]{3,2,1,0:T(8,128)(2,1)}), bf16[16,2,128,256]{3,2,1,0:T(8,128)(2,1)S(1)}, u32[]{:S(2)}, u32[]{:S(2)}) async-start(bf16[16,2,128,256]{3,2,1,0:T(8,128)(2,1)} %shard_map.85), calls=%async_computation | async-start | bytes 4194304 | tf_op jit(solution)/shard_map/all_to_all | solution.py:471
  13.2 1.2 collective-permute-start.2
  14.4 1.3 collective-permute-start.5
  15.7 5.0 %collective-permute-done.refs_1_ = bf16[4,128,256]{2,1,0:T(8,128)(2,1)S(1)} collective-permute-done((bf16[4,128,256]{2,1,0:T(8,128)(2,1)S(1)}, bf16[4,128,256]{2,1,0:T(8,128)(2,1)S(1)}, u32[]{:S(2)}, u32[]{:S(2)}) %collective-permute-start) | collective-permute-done | bytes 262176 | tf_op jit(solution)/shard_map/ppermute | solution.py:39
  21.4 3.9 %shard_map.86 = (s32[2,32]{1,0:T(2,128)}, s32[2,64]{1,0:T(2,128)}) custom-call(s32[16,16]{1,0:T(8,128)} %ids_ref.3), custom_call_target="tpu_custom_call" | custom-call | tf_op jit(solution)/shard_map/pallas_call | solution.py:173
  25.3 2.6 %collective-permute-done.1.refs_2_ = bf16[4,128,256]{2,1,0:T(8,128)(2,1)} collective-permute-done((bf16[4,128,256]{2,1,0:T(8,128)(2,1)S(1)}, bf16[4,128,256]{2,1,0:T(8,128)(2,1)}, u32[]{:S(2)}, u32[]{:S(2)}) %collective-permute-start.1) | collective-permute-done | bytes 262176 | tf_op jit(solution)/shard_map/ppermute | solution.py:39
  28.6 3.7 %shard_map.87 = (bf16[8,128,256]{2,1,0:T(8,128)(2,1)}, bf16[8,128,256]{2,1,0:T(8,128)(2,1)}, bf16[8,128,256]{2,1,0:T(8,128)(2,1)}, bf16[8,128,256]{2,1,0:T(8,128...) custom-call(s32[2,32]{1,0:T(2,128)S(1)} %copy-done.3, ...), custom_call_target="tpu_custom_call" | custom-call | tf_op jit(solution)/shard_map/pallas_call | solution.py:218
  32.4 2.0 %collective-permute-start.9 = (bf16[8,128,256]{2,1,0:T(8,128)(2,1)}, bf16[8,128,256]{2,1,0:T(8,128)(2,1)S(1)}, u32[]{:S(2)}, u32[]{:S(2)}) collective-permute-start(bf16[8,128,256]{2,1,0:T(8,128)(2,1)} %get-tuple-element.54), channel_id=1, source_target_pairs={{0,1},{1,2},{2,3},{3,0},{4,5},{5,6},{6,7},{7,4},{8,9},{9,10},{10,1... | collective-permute-start | bytes 1572872 | tf_op jit(solution)/shard_map/ppermute | solution.py:39
  34.4 1.3 collective-permute-start.6
  35.7 1.8 %collective-permute-start.7 = (bf16[8,128,256]{2,1,0:T(8,128)(2,1)}, bf16[8,128,256]{2,1,0:T(8,128)(2,1)}, u32[]{:S(2)}, u32[]{:S(2)}) collective-permute-start(bf16[8,128,256]{2,1,0:T(8,128)(2,1)} %get-tuple-element.50), channel_id=1, source_target_pairs={{0,8},{1,9},{2,10},{3,11},{4,12},{5,13},{6,14},{7,15},{8,0},{9,1},... | collective-permute-start | bytes 1572872 | tf_op jit(solution)/shard_map/ppermute | solution.py:39
  37.4 2.1 %collective-permute-start.8 = (bf16[8,128,256]{2,1,0:T(8,128)(2,1)}, bf16[8,128,256]{2,1,0:T(8,128)(2,1)}, u32[]{:S(2)}, u32[]{:S(2)}) collective-permute-start(bf16[8,128,256]{2,1,0:T(8,128)(2,1)} %get-tuple-element.51), channel_id=1, source_target_pairs={{0,12},{1,13},{2,14},{3,15},{4,0},{5,1},{6,2},{7,3},{8,4},{9,5},{1... | collective-permute-start | bytes 1572872 | tf_op jit(solution)/shard_map/ppermute | solution.py:39
  39.5 1.7 %collective-permute-start.11 = (bf16[8,128,256]{2,1,0:T(8,128)(2,1)}, bf16[8,128,256]{2,1,0:T(8,128)(2,1)}, u32[]{:S(2)}, u32[]{:S(2)}) collective-permute-start(bf16[8,128,256]{2,1,0:T(8,128)(2,1)} %get-tuple-element.57), channel_id=1, source_target_pairs={{0,3},{1,0},{2,1},{3,2},{4,7},{5,4},{6,5},{7,6},{8,11},{9,8},{10,9... | collective-permute-start | bytes 1572872 | tf_op jit(solution)/shard_map/ppermute | solution.py:39
  41.2 5.1 %collective-permute-done.9.refs_5_ = bf16[8,128,256]{2,1,0:T(8,128)(2,1)S(1)} collective-permute-done((bf16[8,128,256]{2,1,0:T(8,128)(2,1)}, bf16[8,128,256]{2,1,0:T(8,128)(2,1)S(1)}, u32[]{:S(2)}, u32[]{:S(2)}) %collective-permute-start.9) | collective-permute-done | bytes 524320 | tf_op jit(solution)/shard_map/ppermute | solution.py:39
  46.3 2.1 %collective-permute-start.10 = (bf16[8,128,256]{2,1,0:T(8,128)(2,1)}, bf16[8,128,256]{2,1,0:T(8,128)(2,1)}, u32[]{:S(2)}, u32[]{:S(2)}) collective-permute-start(bf16[8,128,256]{2,1,0:T(8,128)(2,1)} %get-tuple-element.56), channel_id=1, source_target_pairs={{0,2},{1,3},{2,0},{3,1},{4,6},{5,7},{6,4},{7,5},{8,10},{9,11},{10,... | collective-permute-start | bytes 1572872 | tf_op jit(solution)/shard_map/ppermute | solution.py:39
  49.0 13.6 %collective-permute-done.8.refs_3_ = bf16[8,128,256]{2,1,0:T(8,128)(2,1)} collective-permute-done((bf16[8,128,256]{2,1,0:T(8,128)(2,1)}, bf16[8,128,256]{2,1,0:T(8,128)(2,1)}, u32[]{:S(2)}, u32[]{:S(2)}) %collective-permute-start.8) | collective-permute-done | bytes 524320 | tf_op jit(solution)/shard_map/ppermute | solution.py:39
  62.6 0.9 collective-permute-done.10.refs_6_
  63.5 12.1 %shard_map.88 = (bf16[16,128,256]{2,1,0:T(8,128)(2,1)}, bf16[8,128,256]{2,1,0:T(8,128)(2,1)}, bf16[8,128,256]{2,1,0:T(8,128)(2,1)}, bf16[8,128,256]{2,1,0:T(8,12...) custom-call(s32[16,16]{1,0:T(8,128)S(1)} %copy-done.2, ...), custom_call_target="tpu_custom_call" | custom-call | tf_op jit(solution)/shard_map/pallas_call | solution.py:428
  75.6 0.9 collective-permute-start.15
  76.5 2.0 %collective-permute-start.13 = (bf16[8,128,256]{2,1,0:T(8,128)(2,1)}, bf16[8,128,256]{2,1,0:T(8,128)(2,1)S(1)}, u32[]{:S(2)}, u32[]{:S(2)}) collective-permute-start(bf16[8,128,256]{2,1,0:T(8,128)(2,1)} %get-tuple-element.62), channel_id=1, source_target_pairs={{0,8},{1,9},{2,10},{3,11},{4,12},{5,13},{6,14},{7,15},{8,0},{9,1},... | collective-permute-start | bytes 1572872 | tf_op jit(solution)/shard_map/ppermute | solution.py:39
  78.5 2.1 %collective-permute-start.14 = (bf16[8,128,256]{2,1,0:T(8,128)(2,1)}, bf16[8,128,256]{2,1,0:T(8,128)(2,1)S(1)}, u32[]{:S(2)}, u32[]{:S(2)}) collective-permute-start(bf16[8,128,256]{2,1,0:T(8,128)(2,1)} %get-tuple-element.63), channel_id=1, source_target_pairs={{0,4},{1,5},{2,6},{3,7},{4,8},{5,9},{6,10},{7,11},{8,12},{9,13},{1... | collective-permute-start | bytes 1572872 | tf_op jit(solution)/shard_map/ppermute | solution.py:39
  80.6 5.1 %collective-permute-done.15.refs_5_ = bf16[8,128,256]{2,1,0:T(8,128)(2,1)S(1)} collective-permute-done((bf16[8,128,256]{2,1,0:T(8,128)(2,1)}, bf16[8,128,256]{2,1,0:T(8,128)(2,1)S(1)}, u32[]{:S(2)}, u32[]{:S(2)}) %collective-permute-start.15) | collective-permute-done | bytes 524320 | tf_op jit(solution)/shard_map/ppermute | solution.py:39
  85.7 3.2 %collective-permute-start.16 = (bf16[8,128,256]{2,1,0:T(8,128)(2,1)}, bf16[8,128,256]{2,1,0:T(8,128)(2,1)S(1)}, u32[]{:S(2)}, u32[]{:S(2)}) collective-permute-start(bf16[8,128,256]{2,1,0:T(8,128)(2,1)} %get-tuple-element.68), channel_id=1, source_target_pairs={{0,2},{1,3},{2,0},{3,1},{4,6},{5,7},{6,4},{7,5},{8,10},{9,11},{10,... | collective-permute-start | bytes 1572872 | tf_op jit(solution)/shard_map/ppermute | solution.py:39
  88.9 17.2 %all-to-all-start.1 = ((bf16[16,128,256]{2,1,0:T(8,128)(2,1)}), bf16[16,128,256]{2,1,0:T(8,128)(2,1)}, u32[]{:S(2)}, u32[]{:S(2)}) async-start(bf16[16,128,256]{2,1,0:T(8,128)(2,1)} %get-tuple-element.58), calls=%async_computation.1 | async-start | bytes 2097152 | tf_op jit(solution)/shard_map/all_to_all | solution.py:476
  106.2 0.7 copy-done.9
  107.6 4.5 %shard_map.90 = (f32[4,128,256]{2,1,0:T(8,128)S(1)}, bf16[4,128,256]{2,1,0:T(8,128)(2,1)}, bf16[4,128,256]{2,1,0:T(8,128)(2,1)}, bf16[4,128,256]{2,1,0:T(8,128)(...) custom-call(s32[2,64]{1,0:T(2,128)S(1)} %copy-done.4, ...), custom_call_target="tpu_custom_call" | custom-call | flops 199999995904 | bytes 4194304 | tf_op jit(solution)/shard_map/pallas_call | solution.py:270
  112.3 2.6 %collective-permute-start.19 = (bf16[4,128,256]{2,1,0:T(8,128)(2,1)}, bf16[4,128,256]{2,1,0:T(8,128)(2,1)S(1)}, u32[]{:S(2)}, u32[]{:S(2)}) collective-permute-start(bf16[4,128,256]{2,1,0:T(8,128)(2,1)} %get-tuple-element.72), channel_id=1, source_target_pairs={{0,2},{1,3},{2,0},{3,1},{4,6},{5,7},{6,4},{7,5},{8,10},{9,11},{10,... | collective-permute-start | bytes 786440 | tf_op jit(solution)/shard_map/ppermute | solution.py:39
  114.9 1.6 %collective-permute-start.23 = (bf16[4,128,256]{2,1,0:T(8,128)(2,1)S(1)}, bf16[4,128,256]{2,1,0:T(8,128)(2,1)S(1)}, u32[]{:S(2)}, u32[]{:S(2)}) collective-permute-start(bf16[4,128,256]{2,1,0:T(8,128)(2,1)S(1)} %get-tuple-element.79), channel_id=1, source_target_pairs={{0,12},{1,13},{2,14},{3,15},{4,0},{5,1},{6,2},{7,3},{8,4},{9,5},{1... | collective-permute-start | bytes 786440 | tf_op jit(solution)/shard_map/ppermute | solution.py:39
  116.4 3.3 %collective-permute-done.21.refs_5_ = bf16[4,128,256]{2,1,0:T(8,128)(2,1)S(1)} collective-permute-done((bf16[4,128,256]{2,1,0:T(8,128)(2,1)S(1)}, bf16[4,128,256]{2,1,0:T(8,128)(2,1)S(1)}, u32[]{:S(2)}, u32[]{:S(2)}) %collective-permute-start.21) | collective-permute-done | bytes 262176 | tf_op jit(solution)/shard_map/ppermute | solution.py:39
  119.8 14.4 %all-to-all-done.1.in_ref = bf16[16,128,256]{2,1,0:T(8,128)(2,1)} async-done(((bf16[16,128,256]{2,1,0:T(8,128)(2,1)}), bf16[16,128,256]{2,1,0:T(8,128)(2,1)}, u32[]{:S(2)}, u32[]{:S(2)}) %all-to-all-start.1) | async-done | bytes 1048608 | tf_op jit(solution)/shard_map/all_to_all | solution.py:476
  134.1 2.3 %shard_map.89 = bf16[128,4096]{1,0:T(8,128)(2,1)} custom-call(bf16[16,128,256]{2,1,0:T(8,128)(2,1)} %all-to-all-done.1.in_ref), custom_call_target="tpu_custom_call" | custom-call | tf_op jit(solution)/shard_map/pallas_call | solution.py:119
  136.5 0.9 shard_map.91
  (57 shorter events, 3.3 us)
Async XLA Ops:
  3.4 45.1 %copy-start.7 = (s32[16,32,2]{1,2,0:T(2,128)S(1)}, s32[16,32,2]{1,2,0:T(2,128)}, u32[]{:S(2)}) copy-start(s32[16,32,2]{1,2,0:T(2,128)} %param.11) | copy-start | bytes 12292
  3.4 60.1 %all-to-all-start = ((bf16[16,2,128,256]{3,2,1,0:T(8,128)(2,1)}), bf16[16,2,128,256]{3,2,1,0:T(8,128)(2,1)S(1)}, u32[]{:S(2)}, u32[]{:S(2)}) async-start(bf16[16,2,128,256]{3,2,1,0:T(8,128)(2,1)} %shard_map.85), calls=%async_computation | async-start | bytes 4194304 | tf_op jit(solution)/shard_map/all_to_all | solution.py:471
  12.7 50.8 %copy-start.2 = (s32[16,16]{1,0:T(8,128)S(1)}, s32[16,16]{1,0:T(8,128)}, u32[]{:S(2)}) copy-start(s32[16,16]{1,0:T(8,128)} %ids_ref.3) | copy-start | bytes 3076
  12.7 8.1 %collective-permute-start = (bf16[4,128,256]{2,1,0:T(8,128)(2,1)S(1)}, bf16[4,128,256]{2,1,0:T(8,128)(2,1)S(1)}, u32[]{:S(2)}, u32[]{:S(2)}) collective-permute-start(bf16[4,128,256]{2,1,0:T(8,128)(2,1)S(1)} %copy-done), channel_id=1, source_target_pairs={{0,3},{1,0},{2,1},{3,2},{4,7},{5,4},{6,5},{7,6},{8,11},{9,8},{10,9... | collective-permute-start | bytes 786440 | tf_op jit(solution)/shard_map/ppermute | solution.py:39
  13.1 8.1 %collective-permute-start.3 = (bf16[4,128,256]{2,1,0:T(8,128)(2,1)S(1)}, bf16[4,128,256]{2,1,0:T(8,128)(2,1)S(1)}, u32[]{:S(2)}, u32[]{:S(2)}) collective-permute-start(bf16[4,128,256]{2,1,0:T(8,128)(2,1)S(1)} %copy-done.1), channel_id=1, source_target_pairs={{0,12},{1,13},{2,14},{3,15},{4,0},{5,1},{6,2},{7,3},{8,4},{9,5},{1... | collective-permute-start | bytes 786440 | tf_op jit(solution)/shard_map/ppermute | solution.py:39
  13.2 12.1 %collective-permute-start.2 = (bf16[4,128,256]{2,1,0:T(8,128)(2,1)S(1)}, bf16[4,128,256]{2,1,0:T(8,128)(2,1)S(1)}, u32[]{:S(2)}, u32[]{:S(2)}) collective-permute-start(bf16[4,128,256]{2,1,0:T(8,128)(2,1)S(1)} %copy-done), channel_id=1, source_target_pairs={{0,1},{1,2},{2,3},{3,0},{4,5},{5,6},{6,7},{7,4},{8,9},{9,10},{10,1... | collective-permute-start | bytes 786440 | tf_op jit(solution)/shard_map/ppermute | solution.py:39
  14.4 10.9 %collective-permute-start.5 = (bf16[4,128,256]{2,1,0:T(8,128)(2,1)S(1)}, bf16[4,128,256]{2,1,0:T(8,128)(2,1)}, u32[]{:S(2)}, u32[]{:S(2)}) collective-permute-start(bf16[4,128,256]{2,1,0:T(8,128)(2,1)S(1)} %copy-done.1), channel_id=1, source_target_pairs={{0,4},{1,5},{2,6},{3,7},{4,8},{5,9},{6,10},{7,11},{8,12},{9,13},{1... | collective-permute-start | bytes 786440 | tf_op jit(solution)/shard_map/ppermute | solution.py:39
  20.8 7.2 %collective-permute-start.1 = (bf16[4,128,256]{2,1,0:T(8,128)(2,1)S(1)}, bf16[4,128,256]{2,1,0:T(8,128)(2,1)}, u32[]{:S(2)}, u32[]{:S(2)}) collective-permute-start(bf16[4,128,256]{2,1,0:T(8,128)(2,1)S(1)} %collective-permute-done.refs_1_), channel_id=1, source_target_pairs={{0,3},{1,0},{2,1},{3,2},{4,7},{5,4},{6,5},{7,6},{8,11},{9,8},{10,9... | collective-permute-start | bytes 786440 | tf_op jit(solution)/shard_map/ppermute | solution.py:39
  21.2 6.8 %collective-permute-start.4 = (bf16[4,128,256]{2,1,0:T(8,128)(2,1)S(1)}, bf16[4,128,256]{2,1,0:T(8,128)(2,1)}, u32[]{:S(2)}, u32[]{:S(2)}) collective-permute-start(bf16[4,128,256]{2,1,0:T(8,128)(2,1)S(1)} %collective-permute-done.3.refs_5_), channel_id=1, source_target_pairs={{0,12},{1,13},{2,14},{3,15},{4,0},{5,1},{6,2},{7,3},{8,4},{9,5},{1... | collective-permute-start | bytes 786440 | tf_op jit(solution)/shard_map/ppermute | solution.py:39
  32.4 14.0 %collective-permute-start.9 = (bf16[8,128,256]{2,1,0:T(8,128)(2,1)}, bf16[8,128,256]{2,1,0:T(8,128)(2,1)S(1)}, u32[]{:S(2)}, u32[]{:S(2)}) collective-permute-start(bf16[8,128,256]{2,1,0:T(8,128)(2,1)} %get-tuple-element.54), channel_id=1, source_target_pairs={{0,1},{1,2},{2,3},{3,0},{4,5},{5,6},{6,7},{7,4},{8,9},{9,10},{10,1... | collective-permute-start | bytes 1572872 | tf_op jit(solution)/shard_map/ppermute | solution.py:39
  34.4 14.2 %collective-permute-start.6 = (bf16[8,128,256]{2,1,0:T(8,128)(2,1)}, bf16[8,128,256]{2,1,0:T(8,128)(2,1)S(1)}, u32[]{:S(2)}, u32[]{:S(2)}) collective-permute-start(bf16[8,128,256]{2,1,0:T(8,128)(2,1)} %get-tuple-element.49), channel_id=1, source_target_pairs={{0,4},{1,5},{2,6},{3,7},{4,8},{5,9},{6,10},{7,11},{8,12},{9,13},{1... | collective-permute-start | bytes 1572872 | tf_op jit(solution)/shard_map/ppermute | solution.py:39
  35.7 13.3 %collective-permute-start.7 = (bf16[8,128,256]{2,1,0:T(8,128)(2,1)}, bf16[8,128,256]{2,1,0:T(8,128)(2,1)}, u32[]{:S(2)}, u32[]{:S(2)}) collective-permute-start(bf16[8,128,256]{2,1,0:T(8,128)(2,1)} %get-tuple-element.50), channel_id=1, source_target_pairs={{0,8},{1,9},{2,10},{3,11},{4,12},{5,13},{6,14},{7,15},{8,0},{9,1},... | collective-permute-start | bytes 1572872 | tf_op jit(solution)/shard_map/ppermute | solution.py:39
  37.4 25.1 %collective-permute-start.8 = (bf16[8,128,256]{2,1,0:T(8,128)(2,1)}, bf16[8,128,256]{2,1,0:T(8,128)(2,1)}, u32[]{:S(2)}, u32[]{:S(2)}) collective-permute-start(bf16[8,128,256]{2,1,0:T(8,128)(2,1)} %get-tuple-element.51), channel_id=1, source_target_pairs={{0,12},{1,13},{2,14},{3,15},{4,0},{5,1},{6,2},{7,3},{8,4},{9,5},{1... | collective-permute-start | bytes 1572872 | tf_op jit(solution)/shard_map/ppermute | solution.py:39
  39.5 23.1 %collective-permute-start.11 = (bf16[8,128,256]{2,1,0:T(8,128)(2,1)}, bf16[8,128,256]{2,1,0:T(8,128)(2,1)}, u32[]{:S(2)}, u32[]{:S(2)}) collective-permute-start(bf16[8,128,256]{2,1,0:T(8,128)(2,1)} %get-tuple-element.57), channel_id=1, source_target_pairs={{0,3},{1,0},{2,1},{3,2},{4,7},{5,4},{6,5},{7,6},{8,11},{9,8},{10,9... | collective-permute-start | bytes 1572872 | tf_op jit(solution)/shard_map/ppermute | solution.py:39
  46.3 17.2 %copy-start.5 = (bf16[8,128,256]{2,1,0:T(8,128)(2,1)}, bf16[8,128,256]{2,1,0:T(8,128)(2,1)S(1)}, u32[]{:S(2)}) copy-start(bf16[8,128,256]{2,1,0:T(8,128)(2,1)S(1)} %collective-permute-done.9.refs_5_) | copy-start | bytes 1572868
  46.3 17.2 %collective-permute-start.10 = (bf16[8,128,256]{2,1,0:T(8,128)(2,1)}, bf16[8,128,256]{2,1,0:T(8,128)(2,1)}, u32[]{:S(2)}, u32[]{:S(2)}) collective-permute-start(bf16[8,128,256]{2,1,0:T(8,128)(2,1)} %get-tuple-element.56), channel_id=1, source_target_pairs={{0,2},{1,3},{2,0},{3,1},{4,6},{5,7},{6,4},{7,5},{8,10},{9,11},{10,... | collective-permute-start | bytes 1572872 | tf_op jit(solution)/shard_map/ppermute | solution.py:39
  48.6 14.9 %copy-start.6 = (bf16[8,128,256]{2,1,0:T(8,128)(2,1)}, bf16[8,128,256]{2,1,0:T(8,128)(2,1)S(1)}, u32[]{:S(2)}) copy-start(bf16[8,128,256]{2,1,0:T(8,128)(2,1)S(1)} %collective-permute-done.6.refs_1_) | copy-start | bytes 1572868
  75.6 32.0 %copy-start.4 = (s32[2,64]{1,0:T(2,128)S(1)}, s32[2,64]{1,0:T(2,128)}, u32[]{:S(2)}) copy-start(s32[2,64]{1,0:T(2,128)} %get-tuple-element.59.add_ref) | copy-start | bytes 1540
  75.6 10.0 %collective-permute-start.15 = (bf16[8,128,256]{2,1,0:T(8,128)(2,1)}, bf16[8,128,256]{2,1,0:T(8,128)(2,1)S(1)}, u32[]{:S(2)}, u32[]{:S(2)}) collective-permute-start(bf16[8,128,256]{2,1,0:T(8,128)(2,1)} %get-tuple-element.66), channel_id=1, source_target_pairs={{0,3},{1,0},{2,1},{3,2},{4,7},{5,4},{6,5},{7,6},{8,11},{9,8},{10,9... | collective-permute-start | bytes 1572872 | tf_op jit(solution)/shard_map/ppermute | solution.py:39
  76.5 29.6 %collective-permute-start.12 = (bf16[8,128,256]{2,1,0:T(8,128)(2,1)}, bf16[8,128,256]{2,1,0:T(8,128)(2,1)S(1)}, u32[]{:S(2)}, u32[]{:S(2)}) collective-permute-start(bf16[8,128,256]{2,1,0:T(8,128)(2,1)} %get-tuple-element.61), channel_id=1, source_target_pairs={{0,12},{1,13},{2,14},{3,15},{4,0},{5,1},{6,2},{7,3},{8,4},{9,5},{1... | collective-permute-start | bytes 1572872 | tf_op jit(solution)/shard_map/ppermute | solution.py:39
  76.5 29.6 %collective-permute-start.13 = (bf16[8,128,256]{2,1,0:T(8,128)(2,1)}, bf16[8,128,256]{2,1,0:T(8,128)(2,1)S(1)}, u32[]{:S(2)}, u32[]{:S(2)}) collective-permute-start(bf16[8,128,256]{2,1,0:T(8,128)(2,1)} %get-tuple-element.62), channel_id=1, source_target_pairs={{0,8},{1,9},{2,10},{3,11},{4,12},{5,13},{6,14},{7,15},{8,0},{9,1},... | collective-permute-start | bytes 1572872 | tf_op jit(solution)/shard_map/ppermute | solution.py:39
  78.5 27.6 %collective-permute-start.14 = (bf16[8,128,256]{2,1,0:T(8,128)(2,1)}, bf16[8,128,256]{2,1,0:T(8,128)(2,1)S(1)}, u32[]{:S(2)}, u32[]{:S(2)}) collective-permute-start(bf16[8,128,256]{2,1,0:T(8,128)(2,1)} %get-tuple-element.63), channel_id=1, source_target_pairs={{0,4},{1,5},{2,6},{3,7},{4,8},{5,9},{6,10},{7,11},{8,12},{9,13},{1... | collective-permute-start | bytes 1572872 | tf_op jit(solution)/shard_map/ppermute | solution.py:39
  80.6 25.5 %collective-permute-start.17 = (bf16[8,128,256]{2,1,0:T(8,128)(2,1)}, bf16[8,128,256]{2,1,0:T(8,128)(2,1)S(1)}, u32[]{:S(2)}, u32[]{:S(2)}) collective-permute-start(bf16[8,128,256]{2,1,0:T(8,128)(2,1)} %get-tuple-element.69), channel_id=1, source_target_pairs={{0,1},{1,2},{2,3},{3,0},{4,5},{5,6},{6,7},{7,4},{8,9},{9,10},{10,1... | collective-permute-start | bytes 1572872 | tf_op jit(solution)/shard_map/ppermute | solution.py:39
  85.7 21.9 %copy-start.8 = (bf16[8,128,256]{2,1,0:T(8,128)(2,1)}, bf16[8,128,256]{2,1,0:T(8,128)(2,1)S(1)}, u32[]{:S(2)}) copy-start(bf16[8,128,256]{2,1,0:T(8,128)(2,1)S(1)} %collective-permute-done.15.refs_5_) | copy-start | bytes 1572868
  85.7 20.5 %collective-permute-start.16 = (bf16[8,128,256]{2,1,0:T(8,128)(2,1)}, bf16[8,128,256]{2,1,0:T(8,128)(2,1)S(1)}, u32[]{:S(2)}, u32[]{:S(2)}) collective-permute-start(bf16[8,128,256]{2,1,0:T(8,128)(2,1)} %get-tuple-element.68), channel_id=1, source_target_pairs={{0,2},{1,3},{2,0},{3,1},{4,6},{5,7},{6,4},{7,5},{8,10},{9,11},{10,... | collective-permute-start | bytes 1572872 | tf_op jit(solution)/shard_map/ppermute | solution.py:39
  88.9 45.3 %all-to-all-start.1 = ((bf16[16,128,256]{2,1,0:T(8,128)(2,1)}), bf16[16,128,256]{2,1,0:T(8,128)(2,1)}, u32[]{:S(2)}, u32[]{:S(2)}) async-start(bf16[16,128,256]{2,1,0:T(8,128)(2,1)} %get-tuple-element.58), calls=%async_computation.1 | async-start | bytes 2097152 | tf_op jit(solution)/shard_map/all_to_all | solution.py:476
  112.1 7.6 %collective-permute-start.21 = (bf16[4,128,256]{2,1,0:T(8,128)(2,1)S(1)}, bf16[4,128,256]{2,1,0:T(8,128)(2,1)S(1)}, u32[]{:S(2)}, u32[]{:S(2)}) collective-permute-start(bf16[4,128,256]{2,1,0:T(8,128)(2,1)S(1)} %get-tuple-element.76), channel_id=1, source_target_pairs={{0,4},{1,5},{2,6},{3,7},{4,8},{5,9},{6,10},{7,11},{8,12},{9,13},{1... | collective-permute-start | bytes 786440 | tf_op jit(solution)/shard_map/ppermute | solution.py:39
  112.2 24.2 %collective-permute-start.18 = (bf16[4,128,256]{2,1,0:T(8,128)(2,1)}, bf16[4,128,256]{2,1,0:T(8,128)(2,1)S(1)}, u32[]{:S(2)}, u32[]{:S(2)}) collective-permute-start(bf16[4,128,256]{2,1,0:T(8,128)(2,1)} %get-tuple-element.71), channel_id=1, source_target_pairs={{0,1},{1,2},{2,3},{3,0},{4,5},{5,6},{6,7},{7,4},{8,9},{9,10},{10,1... | collective-permute-start | bytes 786440 | tf_op jit(solution)/shard_map/ppermute | solution.py:39
  112.3 24.2 %collective-permute-start.19 = (bf16[4,128,256]{2,1,0:T(8,128)(2,1)}, bf16[4,128,256]{2,1,0:T(8,128)(2,1)S(1)}, u32[]{:S(2)}, u32[]{:S(2)}) collective-permute-start(bf16[4,128,256]{2,1,0:T(8,128)(2,1)} %get-tuple-element.72), channel_id=1, source_target_pairs={{0,2},{1,3},{2,0},{3,1},{4,6},{5,7},{6,4},{7,5},{8,10},{9,11},{10,... | collective-permute-start | bytes 786440 | tf_op jit(solution)/shard_map/ppermute | solution.py:39
  114.9 21.6 %collective-permute-start.20 = (bf16[4,128,256]{2,1,0:T(8,128)(2,1)S(1)}, bf16[4,128,256]{2,1,0:T(8,128)(2,1)S(1)}, u32[]{:S(2)}, u32[]{:S(2)}) collective-permute-start(bf16[4,128,256]{2,1,0:T(8,128)(2,1)S(1)} %get-tuple-element.73), channel_id=1, source_target_pairs={{0,3},{1,0},{2,1},{3,2},{4,7},{5,4},{6,5},{7,6},{8,11},{9,8},{10,9... | collective-permute-start | bytes 786440 | tf_op jit(solution)/shard_map/ppermute | solution.py:39
  114.9 21.6 %collective-permute-start.23 = (bf16[4,128,256]{2,1,0:T(8,128)(2,1)S(1)}, bf16[4,128,256]{2,1,0:T(8,128)(2,1)S(1)}, u32[]{:S(2)}, u32[]{:S(2)}) collective-permute-start(bf16[4,128,256]{2,1,0:T(8,128)(2,1)S(1)} %get-tuple-element.79), channel_id=1, source_target_pairs={{0,12},{1,13},{2,14},{3,15},{4,0},{5,1},{6,2},{7,3},{8,4},{9,5},{1... | collective-permute-start | bytes 786440 | tf_op jit(solution)/shard_map/ppermute | solution.py:39
  119.8 16.7 %collective-permute-start.22 = (bf16[4,128,256]{2,1,0:T(8,128)(2,1)S(1)}, bf16[4,128,256]{2,1,0:T(8,128)(2,1)S(1)}, u32[]{:S(2)}, u32[]{:S(2)}) collective-permute-start(bf16[4,128,256]{2,1,0:T(8,128)(2,1)S(1)} %get-tuple-element.78), channel_id=1, source_target_pairs={{0,8},{1,9},{2,10},{3,11},{4,12},{5,13},{6,14},{7,15},{8,0},{9,1},... | collective-permute-start | bytes 786440 | tf_op jit(solution)/shard_map/ppermute | solution.py:39
  (8 other events, 25.3 us)

commit v9 on v8

--- a/solution.py
+++ b/solution.py
@@ -52,13 +52,7 @@
 
 
 def gather_lines(keys, values):
-    lines = [[keys, None, None, None], [values, None, None, None]]
-    for distance in (1, 3):
-        for line, axis in zip(lines, "xy"):
-            line[distance] = shift(line[0], axis, -distance)
-    for line, axis in zip(lines, "xy"):
-        line[2] = shift(line[1], axis, -1)
-    return lines
+    return exchange_lines((((keys,) * SIDE, "x", -1), ((values,) * SIDE, "y", -1)))
 
 
 def chunk_shapes(most, nbr, width, own_type=BF16):
@@ -233,55 +227,51 @@
     return (out[:4], out[4:])
 
 
-def spread_body(add_ref, *refs):
-    outs, (pool, sems) = (refs[8:12], refs[12:16]), refs[16:]
-    most = refs[0].shape[0]
+def spread_body(across, add_ref, *refs):
+    outs, (pool, sems) = refs[4:8], refs[8:]
+    most, owned = refs[0].shape[0], outs[0].shape[0]
     copies = [
-        pltpu.make_async_copy(ref, pool.at[pl.ds(n * most, most)], sems.at[n])
-        for n, ref in enumerate(refs[:8])
+        pltpu.make_async_copy(ref, pool.at[pl.ds(k * most, most)], sems.at[k])
+        for k, ref in enumerate(refs[:4])
     ]
     for copy in copies:
         copy.start()
-    for across in range(2):
-        owned = outs[across][0].shape[0]
-        for copy in copies[SIDE * across : SIDE * (across + 1)]:
-            copy.wait()
-
-        def add(n, carry):
-            for distance, out in enumerate(outs[across]):
-                value = jnp.zeros(out.shape[1:], F32)
-                for k in range(SIDE):
-                    index = add_ref[across, (distance * owned + n) * SIDE + k]
-                    slot = (SIDE * across + k) * most + jnp.maximum(index, 0)
-                    value += jnp.where(index >= 0, pool[slot].astype(F32), 0.0)
-                out[n] = value.astype(out.dtype)
-            return carry
-
-        lax.fori_loop(0, owned, add, 0)
+    for copy in copies:
+        copy.wait()
+
+    def add(n, carry):
+        for distance, out in enumerate(outs):
+            value = jnp.zeros(out.shape[1:], F32)
+            for k in range(SIDE):
+                index = add_ref[across, (distance * owned + n) * SIDE + k]
+                term = pool[k * most + jnp.maximum(index, 0)].astype(F32)
+                value += jnp.where(index >= 0, term, 0.0)
+            out[n] = value.astype(out.dtype)
+        return carry
+
+    lax.fori_loop(0, owned, add, 0)
 
 
 def in_hbm(values):
     return [pltpu.with_memory_space_constraint(v, pltpu.MemorySpace.HBM) for v in values]
 
 
-def spread(add, keys, values, owned):
-    most, nbr, width = keys[0].shape
-    return_shapes = chunk_shapes(owned, nbr, width, F32) * 2
-    out = pl.pallas_call(
-        spread_body,
-        out_shape=return_shapes,
-        in_specs=[SMEM] + [HBM] * 8,
-        out_specs=(VMEM,) * 8,
+def spread(add, chunks, across, owned):
+    most, nbr, width = chunks[0].shape
+    return pl.pallas_call(
+        functools.partial(spread_body, across),
+        out_shape=chunk_shapes(owned, nbr, width, F32),
+        in_specs=[SMEM] + [HBM] * 4,
+        out_specs=(VMEM,) * 4,
         scratch_shapes=[
-            pltpu.VMEM((2 * SIDE * most, nbr, width), BF16),
-            pltpu.SemaphoreType.DMA((2 * SIDE,)),
+            pltpu.VMEM((SIDE * most, nbr, width), BF16),
+            pltpu.SemaphoreType.DMA((SIDE,)),
         ],
         compiler_params=pltpu.CompilerParams(vmem_limit_bytes=SPREAD_VMEM),
         cost_estimate=pl.CostEstimate(
-            flops=SPREAD_FLOPS, bytes_accessed=4 * 1024 * 1024, transcendentals=0
+            flops=SPREAD_FLOPS, bytes_accessed=2 * 1024 * 1024, transcendentals=0
         ),
-    )(add, *in_hbm(keys), *in_hbm(values))
-    return (out[:4], out[4:])
+    )(add, *in_hbm(chunks))
 
 
 def attend_body(
@@ -474,7 +464,9 @@
     back, keys, values = attend(distinct_ids, group_refs, tokens, keys, values, owned, most)
     keys, values = exchange_lines(((keys, "y", -1), (values, "x", -1)))
     back = lax.all_to_all(back, "ctx", split_axis=0, concat_axis=0, tiled=True)
-    keys, values = spread(add, keys, values, owned)
+    keys = list(spread(add, keys, 0, owned))
+    keys[0], values[0] = lax.optimization_barrier((keys[0], values[0]))
+    values = spread(add, values, 1, owned)
     keys, values = exchange_lines(((keys, "x", 1), (values, "y", 1)))
     grad_queries = join_heads(back)[None]
     grad_queries, keys, values = lax.optimization_barrier((grad_queries, keys, values))

time: 138 us -> 142 us (1.029)
  the two profiles are of different devices: /device:TPU:11 before, /device:TPU:8 now
where the time goes in v9:
time: 142 us; the launch traced here: 141 us
  starting transfers between devices  55.8 us (39%)
  waiting for transfers between devices  50.3 us (35%)
  Pallas kernels  32.3 us (23%)
  local copies, waits for them, and re-layouts  1.71 us (1%)
    ppermute x24, waiting for transfers between devices, shift(): return lax.ppermute(value, 'dp', pairs)  50.3 us
    ppermute x24, starting transfers between devices, shift(): return lax.ppermute(value, 'dp', pairs)  40.4 us
    pallas_call x1, Pallas kernels, attend(): pl.pallas_call(functools.partial(attend_body, groups, distinct, owned, mo...  12 us
    all_to_all x1, starting transfers between devices, on_device(): lax.all_to_all(packed, 'ctx', split_axis=0, concat_axis=0, tiled=True)  8.71 us
    all_to_all x1, starting transfers between devices, on_device(): back = lax.all_to_all(back, 'ctx', split_axis=0, concat_axis=0, tiled=True)  6.69 us
    pallas_call x2, Pallas kernels, spread(): pl.pallas_call(functools.partial(spread_body, across), out_shape=chunk_sh...  6.57 us
    pallas_call x1, Pallas kernels, tables(): pl.pallas_call(functools.partial(tables_body, owned, most), out_shape=(ja...  3.94 us
    pallas_call x1, Pallas kernels, select(): pl.pallas_call(select_body, out_shape=tuple((pltpu.HBM(shape.shape, shape...  3.75 us
  transfers between devices with their start and end apart: 26, of which 14 were waited for; matrix products, arithmetic and copies ran while one was open for 0% of the time, Pallas kernels for 12%

profile of v9, /device:TPU:8, one launch (start us, length us, event | category | flops | bytes accessed | tf_op | source)
XLA Modules:
  0.0 141.0 jit_solution(16655992111836287800)
XLA Ops:
  0.6 2.7 %shard_map.85 = bf16[16,2,128,256]{3,2,1,0:T(8,128)(2,1)} custom-call(bf16[128,4096]{1,0:T(8,128)(2,1)} %bitcast.5, bf16[128,4096]{1,0:T(8,128)(2,1)} %bitcast.6), custom_call_target="tpu_custom_call" | custom-call | tf_op jit(solution)/shard_map/pallas_call | solution.py:87
  3.4 8.7 %all-to-all-start = ((bf16[16,2,128,256]{3,2,1,0:T(8,128)(2,1)}), bf16[16,2,128,256]{3,2,1,0:T(8,128)(2,1)S(1)}, u32[]{:S(2)}, u32[]{:S(2)}) async-start(bf16[16,2,128,256]{3,2,1,0:T(8,128)(2,1)} %shard_map.85), calls=%async_computation | async-start | bytes 4194304 | tf_op jit(solution)/shard_map/all_to_all | solution.py:461
  12.7 3.0 %collective-permute-start.1 = (bf16[4,128,256]{2,1,0:T(8,128)(2,1)S(1)}, bf16[4,128,256]{2,1,0:T(8,128)(2,1)S(1)}, u32[]{:S(2)}, u32[]{:S(2)}) collective-permute-start(bf16[4,128,256]{2,1,0:T(8,128)(2,1)S(1)} %copy-done), channel_id=1, source_target_pairs={{0,2},{1,3},{2,0},{3,1},{4,6},{5,7},{6,4},{7,5},{8,10},{9,11},{10,... | collective-permute-start | bytes 786440 | tf_op jit(solution)/shard_map/ppermute | solution.py:39
  17.7 1.6 %collective-permute-start.5 = (bf16[4,128,256]{2,1,0:T(8,128)(2,1)S(1)}, bf16[4,128,256]{2,1,0:T(8,128)(2,1)}, u32[]{:S(2)}, u32[]{:S(2)}) collective-permute-start(bf16[4,128,256]{2,1,0:T(8,128)(2,1)S(1)} %copy-done.1), channel_id=1, source_target_pairs={{0,4},{1,5},{2,6},{3,7},{4,8},{5,9},{6,10},{7,11},{8,12},{9,13},{1... | collective-permute-start | bytes 786440 | tf_op jit(solution)/shard_map/ppermute | solution.py:39
  20.9 3.5 %collective-permute-start.4 = (bf16[4,128,256]{2,1,0:T(8,128)(2,1)S(1)}, bf16[4,128,256]{2,1,0:T(8,128)(2,1)}, u32[]{:S(2)}, u32[]{:S(2)}) collective-permute-start(bf16[4,128,256]{2,1,0:T(8,128)(2,1)S(1)} %copy-done.1), channel_id=1, source_target_pairs={{0,8},{1,9},{2,10},{3,11},{4,12},{5,13},{6,14},{7,15},{8,0},{9,1},... | collective-permute-start | bytes 786440 | tf_op jit(solution)/shard_map/ppermute | solution.py:39
  24.4 3.9 %shard_map.86 = (s32[2,32]{1,0:T(2,128)}, s32[2,64]{1,0:T(2,128)}) custom-call(s32[16,16]{1,0:T(8,128)} %ids_ref.3), custom_call_target="tpu_custom_call" | custom-call | tf_op jit(solution)/shard_map/pallas_call | solution.py:167
  28.4 2.2 %collective-permute-done.4.refs_6_ = bf16[4,128,256]{2,1,0:T(8,128)(2,1)} collective-permute-done((bf16[4,128,256]{2,1,0:T(8,128)(2,1)S(1)}, bf16[4,128,256]{2,1,0:T(8,128)(2,1)}, u32[]{:S(2)}, u32[]{:S(2)}) %collective-permute-start.4) | collective-permute-done | bytes 262176 | tf_op jit(solution)/shard_map/ppermute | solution.py:39
  31.3 3.7 %shard_map.87 = (bf16[8,128,256]{2,1,0:T(8,128)(2,1)}, bf16[8,128,256]{2,1,0:T(8,128)(2,1)}, bf16[8,128,256]{2,1,0:T(8,128)(2,1)}, bf16[8,128,256]{2,1,0:T(8,128...) custom-call(s32[2,32]{1,0:T(2,128)S(1)} %copy-done.3, ...), custom_call_target="tpu_custom_call" | custom-call | tf_op jit(solution)/shard_map/pallas_call | solution.py:212
  35.0 1.6 %collective-permute-start.9 = (bf16[8,128,256]{2,1,0:T(8,128)(2,1)}, bf16[8,128,256]{2,1,0:T(8,128)(2,1)S(1)}, u32[]{:S(2)}, u32[]{:S(2)}) collective-permute-start(bf16[8,128,256]{2,1,0:T(8,128)(2,1)} %get-tuple-element.60), channel_id=1, source_target_pairs={{0,1},{1,2},{2,3},{3,0},{4,5},{5,6},{6,7},{7,4},{8,9},{9,10},{10,1... | collective-permute-start | bytes 1572872 | tf_op jit(solution)/shard_map/ppermute | solution.py:39
  36.6 2.2 %collective-permute-start.6 = (bf16[8,128,256]{2,1,0:T(8,128)(2,1)}, bf16[8,128,256]{2,1,0:T(8,128)(2,1)S(1)}, u32[]{:S(2)}, u32[]{:S(2)}) collective-permute-start(bf16[8,128,256]{2,1,0:T(8,128)(2,1)} %get-tuple-element.55), channel_id=1, source_target_pairs={{0,4},{1,5},{2,6},{3,7},{4,8},{5,9},{6,10},{7,11},{8,12},{9,13},{1... | collective-permute-start | bytes 1572872 | tf_op jit(solution)/shard_map/ppermute | solution.py:39
  38.8 3.6 %collective-permute-start.7 = (bf16[8,128,256]{2,1,0:T(8,128)(2,1)}, bf16[8,128,256]{2,1,0:T(8,128)(2,1)}, u32[]{:S(2)}, u32[]{:S(2)}) collective-permute-start(bf16[8,128,256]{2,1,0:T(8,128)(2,1)} %get-tuple-element.56), channel_id=1, source_target_pairs={{0,8},{1,9},{2,10},{3,11},{4,12},{5,13},{6,14},{7,15},{8,0},{9,1},... | collective-permute-start | bytes 1572872 | tf_op jit(solution)/shard_map/ppermute | solution.py:39
  42.5 2.6 %collective-permute-start.11 = (bf16[8,128,256]{2,1,0:T(8,128)(2,1)}, bf16[8,128,256]{2,1,0:T(8,128)(2,1)}, u32[]{:S(2)}, u32[]{:S(2)}) collective-permute-start(bf16[8,128,256]{2,1,0:T(8,128)(2,1)} %get-tuple-element.63), channel_id=1, source_target_pairs={{0,3},{1,0},{2,1},{3,2},{4,7},{5,4},{6,5},{7,6},{8,11},{9,8},{10,9... | collective-permute-start | bytes 1572872 | tf_op jit(solution)/shard_map/ppermute | solution.py:39
  45.0 4.4 %collective-permute-done.9.refs_5_ = bf16[8,128,256]{2,1,0:T(8,128)(2,1)S(1)} collective-permute-done((bf16[8,128,256]{2,1,0:T(8,128)(2,1)}, bf16[8,128,256]{2,1,0:T(8,128)(2,1)S(1)}, u32[]{:S(2)}, u32[]{:S(2)}) %collective-permute-start.9) | collective-permute-done | bytes 524320 | tf_op jit(solution)/shard_map/ppermute | solution.py:39
  49.4 1.8 %collective-permute-start.10 = (bf16[8,128,256]{2,1,0:T(8,128)(2,1)}, bf16[8,128,256]{2,1,0:T(8,128)(2,1)}, u32[]{:S(2)}, u32[]{:S(2)}) collective-permute-start(bf16[8,128,256]{2,1,0:T(8,128)(2,1)} %get-tuple-element.62), channel_id=1, source_target_pairs={{0,2},{1,3},{2,0},{3,1},{4,6},{5,7},{6,4},{7,5},{8,10},{9,11},{10,... | collective-permute-start | bytes 1572872 | tf_op jit(solution)/shard_map/ppermute | solution.py:39
  51.3 9.4 %collective-permute-done.6.refs_1_ = bf16[8,128,256]{2,1,0:T(8,128)(2,1)S(1)} collective-permute-done((bf16[8,128,256]{2,1,0:T(8,128)(2,1)}, bf16[8,128,256]{2,1,0:T(8,128)(2,1)S(1)}, u32[]{:S(2)}, u32[]{:S(2)}) %collective-permute-start.6) | collective-permute-done | bytes 524320 | tf_op jit(solution)/shard_map/ppermute | solution.py:39
  60.7 3.6 %collective-permute-done.8.refs_3_ = bf16[8,128,256]{2,1,0:T(8,128)(2,1)} collective-permute-done((bf16[8,128,256]{2,1,0:T(8,128)(2,1)}, bf16[8,128,256]{2,1,0:T(8,128)(2,1)}, u32[]{:S(2)}, u32[]{:S(2)}) %collective-permute-start.8) | collective-permute-done | bytes 524320 | tf_op jit(solution)/shard_map/ppermute | solution.py:39
  64.8 12.0 %shard_map.88 = (bf16[16,128,256]{2,1,0:T(8,128)(2,1)}, bf16[8,128,256]{2,1,0:T(8,128)(2,1)}, bf16[8,128,256]{2,1,0:T(8,128)(2,1)}, bf16[8,128,256]{2,1,0:T(8,12...) custom-call(s32[16,16]{1,0:T(8,128)S(1)} %copy-done.2, ...), custom_call_target="tpu_custom_call" | custom-call | tf_op jit(solution)/shard_map/pallas_call | solution.py:418
  76.8 3.9 %collective-permute-start.18 = (bf16[8,128,256]{2,1,0:T(8,128)(2,1)}, bf16[8,128,256]{2,1,0:T(8,128)(2,1)S(1)}, u32[]{:S(2)}, u32[]{:S(2)}) collective-permute-start(bf16[8,128,256]{2,1,0:T(8,128)(2,1)} %get-tuple-element.78), channel_id=1, source_target_pairs={{0,3},{1,0},{2,1},{3,2},{4,7},{5,4},{6,5},{7,6},{8,11},{9,8},{10,9... | collective-permute-start | bytes 1572872 | tf_op jit(solution)/shard_map/ppermute | solution.py:39
  80.7 1.9 %collective-permute-start.12 = (bf16[8,128,256]{2,1,0:T(8,128)(2,1)}, bf16[8,128,256]{2,1,0:T(8,128)(2,1)S(1)}, u32[]{:S(2)}, u32[]{:S(2)}) collective-permute-start(bf16[8,128,256]{2,1,0:T(8,128)(2,1)} %get-tuple-element.67), channel_id=1, source_target_pairs={{0,12},{1,13},{2,14},{3,15},{4,0},{5,1},{6,2},{7,3},{8,4},{9,5},{1... | collective-permute-start | bytes 1572872 | tf_op jit(solution)/shard_map/ppermute | solution.py:39
  84.4 6.7 %all-to-all-start.1 = ((bf16[16,128,256]{2,1,0:T(8,128)(2,1)}), bf16[16,128,256]{2,1,0:T(8,128)(2,1)}, u32[]{:S(2)}, u32[]{:S(2)}) async-start(bf16[16,128,256]{2,1,0:T(8,128)(2,1)} %get-tuple-element.64), calls=%async_computation.1 | async-start | bytes 2097152 | tf_op jit(solution)/shard_map/all_to_all | solution.py:466
  91.2 2.3 %collective-permute-start.19 = (bf16[8,128,256]{2,1,0:T(8,128)(2,1)}, bf16[8,128,256]{2,1,0:T(8,128)(2,1)}, u32[]{:S(2)}, u32[]{:S(2)}) collective-permute-start(bf16[8,128,256]{2,1,0:T(8,128)(2,1)} %get-tuple-element.80), channel_id=1, source_target_pairs={{0,2},{1,3},{2,0},{3,1},{4,6},{5,7},{6,4},{7,5},{8,10},{9,11},{10,... | collective-permute-start | bytes 1572872 | tf_op jit(solution)/shard_map/ppermute | solution.py:39
  93.5 2.1 %collective-permute-done.12.refs_1_ = bf16[8,128,256]{2,1,0:T(8,128)(2,1)S(1)} collective-permute-done((bf16[8,128,256]{2,1,0:T(8,128)(2,1)}, bf16[8,128,256]{2,1,0:T(8,128)(2,1)S(1)}, u32[]{:S(2)}, u32[]{:S(2)}) %collective-permute-start.12) | collective-permute-done | bytes 524320 | tf_op jit(solution)/shard_map/ppermute | solution.py:39
  95.7 8.7 %collective-permute-done.13.refs_2_ = bf16[8,128,256]{2,1,0:T(8,128)(2,1)S(1)} collective-permute-done((bf16[8,128,256]{2,1,0:T(8,128)(2,1)}, bf16[8,128,256]{2,1,0:T(8,128)(2,1)S(1)}, u32[]{:S(2)}, u32[]{:S(2)}) %collective-permute-start.13) | collective-permute-done | bytes 524320 | tf_op jit(solution)/shard_map/ppermute | solution.py:39
  106.5 2.9 %shard_map.90 = (f32[4,128,256]{2,1,0:T(8,128)S(1)}, bf16[4,128,256]{2,1,0:T(8,128)(2,1)S(1)}, bf16[4,128,256]{2,1,0:T(8,128)(2,1)S(1)}, bf16[4,128,256]{2,1,0:T(8,128)(2,1)S(1)}) custom-call(s32[2,64]{1,0:T(2,128)S(1)} %copy-done.4, bf16[8,128,256]{2,1,0:T(8,128)(2,1)} %get-tuple-element.66.refs_0_, bf16[8,128,256]{2,1,0:T(8,128)(2,1)} %copy-done.9, ...), custom_call_target="tpu_custom_call" | custom-call | flops 199999995904 | bytes 2097152 | tf_op jit(solution)/shard_map/pallas_call | solution.py:261
  109.4 8.6 %collective-permute-done.20.refs_3_ = bf16[8,128,256]{2,1,0:T(8,128)(2,1)} collective-permute-done((bf16[8,128,256]{2,1,0:T(8,128)(2,1)}, bf16[8,128,256]{2,1,0:T(8,128)(2,1)}, u32[]{:S(2)}, u32[]{:S(2)}) %collective-permute-start.20) | collective-permute-done | bytes 524320 | tf_op jit(solution)/shard_map/ppermute | solution.py:39
  118.0 3.7 %shard_map.91 = (f32[4,128,256]{2,1,0:T(8,128)S(1)}, bf16[4,128,256]{2,1,0:T(8,128)(2,1)S(1)}, bf16[4,128,256]{2,1,0:T(8,128)(2,1)}, bf16[4,128,256]{2,1,0:T(8,128)(2,1)}) custom-call(s32[2,64]{1,0:T(2,128)S(1)} %copy-done.4, bf16[8,128,256]{2,1,0:T(8,128)(2,1)} %get-tuple-element.76.refs_0_, bf16[8,128,256]{2,1,0:T(8,128)(2,1)} %copy-done.8, ...), custom_call_target="tpu_custom_call" | custom-call | flops 199999995904 | bytes 2097152 | tf_op jit(solution)/shard_map/pallas_call | solution.py:261
  121.7 2.4 %collective-permute-start.21 = (bf16[4,128,256]{2,1,0:T(8,128)(2,1)S(1)}, bf16[4,128,256]{2,1,0:T(8,128)(2,1)S(1)}, u32[]{:S(2)}, u32[]{:S(2)}) collective-permute-start(bf16[4,128,256]{2,1,0:T(8,128)(2,1)S(1)} %get-tuple-element.84), channel_id=1, source_target_pairs={{0,4},{1,5},{2,6},{3,7},{4,8},{5,9},{6,10},{7,11},{8,12},{9,13},{1... | collective-permute-start | bytes 786440 | tf_op jit(solution)/shard_map/ppermute | solution.py:39
  125.1 2.2 %collective-permute-start.17 = (bf16[4,128,256]{2,1,0:T(8,128)(2,1)S(1)}, bf16[4,128,256]{2,1,0:T(8,128)(2,1)S(1)}, u32[]{:S(2)}, u32[]{:S(2)}) collective-permute-start(bf16[4,128,256]{2,1,0:T(8,128)(2,1)S(1)} %get-tuple-element.75), channel_id=1, source_target_pairs={{0,3},{1,0},{2,1},{3,2},{4,7},{5,4},{6,5},{7,6},{8,11},{9,8},{10,9... | collective-permute-start | bytes 786440 | tf_op jit(solution)/shard_map/ppermute | solution.py:39
  127.4 2.1 %collective-permute-done.21.refs_5_ = bf16[4,128,256]{2,1,0:T(8,128)(2,1)S(1)} collective-permute-done((bf16[4,128,256]{2,1,0:T(8,128)(2,1)S(1)}, bf16[4,128,256]{2,1,0:T(8,128)(2,1)S(1)}, u32[]{:S(2)}, u32[]{:S(2)}) %collective-permute-start.21) | collective-permute-done | bytes 262176 | tf_op jit(solution)/shard_map/ppermute | solution.py:39
  129.5 2.3 %collective-permute-start.22 = (bf16[4,128,256]{2,1,0:T(8,128)(2,1)}, bf16[4,128,256]{2,1,0:T(8,128)(2,1)S(1)}, u32[]{:S(2)}, u32[]{:S(2)}) collective-permute-start(bf16[4,128,256]{2,1,0:T(8,128)(2,1)} %get-tuple-element.86), channel_id=1, source_target_pairs={{0,8},{1,9},{2,10},{3,11},{4,12},{5,13},{6,14},{7,15},{8,0},{9,1},... | collective-permute-start | bytes 786440 | tf_op jit(solution)/shard_map/ppermute | solution.py:39
  131.8 2.3 %shard_map.89 = bf16[128,4096]{1,0:T(8,128)(2,1)} custom-call(bf16[16,128,256]{2,1,0:T(8,128)(2,1)} %all-to-all-done.1.in_ref), custom_call_target="tpu_custom_call" | custom-call | tf_op jit(solution)/shard_map/pallas_call | solution.py:113
  134.1 4.3 %collective-permute-done.15.refs_1_ = bf16[4,128,256]{2,1,0:T(8,128)(2,1)S(1)} collective-permute-done((bf16[4,128,256]{2,1,0:T(8,128)(2,1)S(1)}, bf16[4,128,256]{2,1,0:T(8,128)(2,1)S(1)}, u32[]{:S(2)}, u32[]{:S(2)}) %collective-permute-start.15) | collective-permute-done | bytes 262176 | tf_op jit(solution)/shard_map/ppermute | solution.py:39
  (54 shorter events, 13.2 us)
Async XLA Ops:
  3.4 47.8 %copy-start.7 = (s32[16,32,2]{1,2,0:T(2,128)S(1)}, s32[16,32,2]{1,2,0:T(2,128)}, u32[]{:S(2)}) copy-start(s32[16,32,2]{1,2,0:T(2,128)} %param.11) | copy-start | bytes 12292
  3.4 61.4 %all-to-all-start = ((bf16[16,2,128,256]{3,2,1,0:T(8,128)(2,1)}), bf16[16,2,128,256]{3,2,1,0:T(8,128)(2,1)S(1)}, u32[]{:S(2)}, u32[]{:S(2)}) async-start(bf16[16,2,128,256]{3,2,1,0:T(8,128)(2,1)} %shard_map.85), calls=%async_computation | async-start | bytes 4194304 | tf_op jit(solution)/shard_map/all_to_all | solution.py:461
  12.1 52.6 %copy-start.2 = (s32[16,16]{1,0:T(8,128)S(1)}, s32[16,16]{1,0:T(8,128)}, u32[]{:S(2)}) copy-start(s32[16,16]{1,0:T(8,128)} %ids_ref.3) | copy-start | bytes 3076
  12.1 8.7 %collective-permute-start.3 = (bf16[4,128,256]{2,1,0:T(8,128)(2,1)S(1)}, bf16[4,128,256]{2,1,0:T(8,128)(2,1)S(1)}, u32[]{:S(2)}, u32[]{:S(2)}) collective-permute-start(bf16[4,128,256]{2,1,0:T(8,128)(2,1)S(1)} %copy-done.1), channel_id=1, source_target_pairs={{0,12},{1,13},{2,14},{3,15},{4,0},{5,1},{6,2},{7,3},{8,4},{9,5},{1... | collective-permute-start | bytes 786440 | tf_op jit(solution)/shard_map/ppermute | solution.py:39
  12.7 15.6 %collective-permute-start.1 = (bf16[4,128,256]{2,1,0:T(8,128)(2,1)S(1)}, bf16[4,128,256]{2,1,0:T(8,128)(2,1)S(1)}, u32[]{:S(2)}, u32[]{:S(2)}) collective-permute-start(bf16[4,128,256]{2,1,0:T(8,128)(2,1)S(1)} %copy-done), channel_id=1, source_target_pairs={{0,2},{1,3},{2,0},{3,1},{4,6},{5,7},{6,4},{7,5},{8,10},{9,11},{10,... | collective-permute-start | bytes 786440 | tf_op jit(solution)/shard_map/ppermute | solution.py:39
  15.7 12.6 %collective-permute-start = (bf16[4,128,256]{2,1,0:T(8,128)(2,1)S(1)}, bf16[4,128,256]{2,1,0:T(8,128)(2,1)S(1)}, u32[]{:S(2)}, u32[]{:S(2)}) collective-permute-start(bf16[4,128,256]{2,1,0:T(8,128)(2,1)S(1)} %copy-done), channel_id=1, source_target_pairs={{0,3},{1,0},{2,1},{3,2},{4,7},{5,4},{6,5},{7,6},{8,11},{9,8},{10,9... | collective-permute-start | bytes 786440 | tf_op jit(solution)/shard_map/ppermute | solution.py:39
  16.8 11.5 %collective-permute-start.2 = (bf16[4,128,256]{2,1,0:T(8,128)(2,1)S(1)}, bf16[4,128,256]{2,1,0:T(8,128)(2,1)}, u32[]{:S(2)}, u32[]{:S(2)}) collective-permute-start(bf16[4,128,256]{2,1,0:T(8,128)(2,1)S(1)} %copy-done), channel_id=1, source_target_pairs={{0,1},{1,2},{2,3},{3,0},{4,5},{5,6},{6,7},{7,4},{8,9},{9,10},{10,1... | collective-permute-start | bytes 786440 | tf_op jit(solution)/shard_map/ppermute | solution.py:39
  17.7 10.6 %collective-permute-start.5 = (bf16[4,128,256]{2,1,0:T(8,128)(2,1)S(1)}, bf16[4,128,256]{2,1,0:T(8,128)(2,1)}, u32[]{:S(2)}, u32[]{:S(2)}) collective-permute-start(bf16[4,128,256]{2,1,0:T(8,128)(2,1)S(1)} %copy-done.1), channel_id=1, source_target_pairs={{0,4},{1,5},{2,6},{3,7},{4,8},{5,9},{6,10},{7,11},{8,12},{9,13},{1... | collective-permute-start | bytes 786440 | tf_op jit(solution)/shard_map/ppermute | solution.py:39
  20.9 9.7 %collective-permute-start.4 = (bf16[4,128,256]{2,1,0:T(8,128)(2,1)S(1)}, bf16[4,128,256]{2,1,0:T(8,128)(2,1)}, u32[]{:S(2)}, u32[]{:S(2)}) collective-permute-start(bf16[4,128,256]{2,1,0:T(8,128)(2,1)S(1)} %copy-done.1), channel_id=1, source_target_pairs={{0,8},{1,9},{2,10},{3,11},{4,12},{5,13},{6,14},{7,15},{8,0},{9,1},... | collective-permute-start | bytes 786440 | tf_op jit(solution)/shard_map/ppermute | solution.py:39
  35.0 14.4 %collective-permute-start.9 = (bf16[8,128,256]{2,1,0:T(8,128)(2,1)}, bf16[8,128,256]{2,1,0:T(8,128)(2,1)S(1)}, u32[]{:S(2)}, u32[]{:S(2)}) collective-permute-start(bf16[8,128,256]{2,1,0:T(8,128)(2,1)} %get-tuple-element.60), channel_id=1, source_target_pairs={{0,1},{1,2},{2,3},{3,0},{4,5},{5,6},{6,7},{7,4},{8,9},{9,10},{10,1... | collective-permute-start | bytes 1572872 | tf_op jit(solution)/shard_map/ppermute | solution.py:39
  36.6 24.1 %collective-permute-start.6 = (bf16[8,128,256]{2,1,0:T(8,128)(2,1)}, bf16[8,128,256]{2,1,0:T(8,128)(2,1)S(1)}, u32[]{:S(2)}, u32[]{:S(2)}) collective-permute-start(bf16[8,128,256]{2,1,0:T(8,128)(2,1)} %get-tuple-element.55), channel_id=1, source_target_pairs={{0,4},{1,5},{2,6},{3,7},{4,8},{5,9},{6,10},{7,11},{8,12},{9,13},{1... | collective-permute-start | bytes 1572872 | tf_op jit(solution)/shard_map/ppermute | solution.py:39
  38.8 21.9 %collective-permute-start.7 = (bf16[8,128,256]{2,1,0:T(8,128)(2,1)}, bf16[8,128,256]{2,1,0:T(8,128)(2,1)}, u32[]{:S(2)}, u32[]{:S(2)}) collective-permute-start(bf16[8,128,256]{2,1,0:T(8,128)(2,1)} %get-tuple-element.56), channel_id=1, source_target_pairs={{0,8},{1,9},{2,10},{3,11},{4,12},{5,13},{6,14},{7,15},{8,0},{9,1},... | collective-permute-start | bytes 1572872 | tf_op jit(solution)/shard_map/ppermute | solution.py:39
  42.4 21.9 %collective-permute-start.8 = (bf16[8,128,256]{2,1,0:T(8,128)(2,1)}, bf16[8,128,256]{2,1,0:T(8,128)(2,1)}, u32[]{:S(2)}, u32[]{:S(2)}) collective-permute-start(bf16[8,128,256]{2,1,0:T(8,128)(2,1)} %get-tuple-element.57), channel_id=1, source_target_pairs={{0,12},{1,13},{2,14},{3,15},{4,0},{5,1},{6,2},{7,3},{8,4},{9,5},{1... | collective-permute-start | bytes 1572872 | tf_op jit(solution)/shard_map/ppermute | solution.py:39
  42.5 22.3 %collective-permute-start.11 = (bf16[8,128,256]{2,1,0:T(8,128)(2,1)}, bf16[8,128,256]{2,1,0:T(8,128)(2,1)}, u32[]{:S(2)}, u32[]{:S(2)}) collective-permute-start(bf16[8,128,256]{2,1,0:T(8,128)(2,1)} %get-tuple-element.63), channel_id=1, source_target_pairs={{0,3},{1,0},{2,1},{3,2},{4,7},{5,4},{6,5},{7,6},{8,11},{9,8},{10,9... | collective-permute-start | bytes 1572872 | tf_op jit(solution)/shard_map/ppermute | solution.py:39
  49.4 15.4 %copy-start.5 = (bf16[8,128,256]{2,1,0:T(8,128)(2,1)}, bf16[8,128,256]{2,1,0:T(8,128)(2,1)S(1)}, u32[]{:S(2)}) copy-start(bf16[8,128,256]{2,1,0:T(8,128)(2,1)S(1)} %collective-permute-done.9.refs_5_) | copy-start | bytes 1572868
  49.4 15.4 %collective-permute-start.10 = (bf16[8,128,256]{2,1,0:T(8,128)(2,1)}, bf16[8,128,256]{2,1,0:T(8,128)(2,1)}, u32[]{:S(2)}, u32[]{:S(2)}) collective-permute-start(bf16[8,128,256]{2,1,0:T(8,128)(2,1)} %get-tuple-element.62), channel_id=1, source_target_pairs={{0,2},{1,3},{2,0},{3,1},{4,6},{5,7},{6,4},{7,5},{8,10},{9,11},{10,... | collective-permute-start | bytes 1572872 | tf_op jit(solution)/shard_map/ppermute | solution.py:39
  76.8 29.7 %copy-start.4 = (s32[2,64]{1,0:T(2,128)S(1)}, s32[2,64]{1,0:T(2,128)}, u32[]{:S(2)}) copy-start(s32[2,64]{1,0:T(2,128)} %get-tuple-element.65.add_ref) | copy-start | bytes 1540
  76.8 14.3 %collective-permute-start.18 = (bf16[8,128,256]{2,1,0:T(8,128)(2,1)}, bf16[8,128,256]{2,1,0:T(8,128)(2,1)S(1)}, u32[]{:S(2)}, u32[]{:S(2)}) collective-permute-start(bf16[8,128,256]{2,1,0:T(8,128)(2,1)} %get-tuple-element.78), channel_id=1, source_target_pairs={{0,3},{1,0},{2,1},{3,2},{4,7},{5,4},{6,5},{7,6},{8,11},{9,8},{10,9... | collective-permute-start | bytes 1572872 | tf_op jit(solution)/shard_map/ppermute | solution.py:39
  80.7 15.0 %collective-permute-start.12 = (bf16[8,128,256]{2,1,0:T(8,128)(2,1)}, bf16[8,128,256]{2,1,0:T(8,128)(2,1)S(1)}, u32[]{:S(2)}, u32[]{:S(2)}) collective-permute-start(bf16[8,128,256]{2,1,0:T(8,128)(2,1)} %get-tuple-element.67), channel_id=1, source_target_pairs={{0,12},{1,13},{2,14},{3,15},{4,0},{5,1},{6,2},{7,3},{8,4},{9,5},{1... | collective-permute-start | bytes 1572872 | tf_op jit(solution)/shard_map/ppermute | solution.py:39
  82.6 21.7 %collective-permute-start.13 = (bf16[8,128,256]{2,1,0:T(8,128)(2,1)}, bf16[8,128,256]{2,1,0:T(8,128)(2,1)S(1)}, u32[]{:S(2)}, u32[]{:S(2)}) collective-permute-start(bf16[8,128,256]{2,1,0:T(8,128)(2,1)} %get-tuple-element.68), channel_id=1, source_target_pairs={{0,8},{1,9},{2,10},{3,11},{4,12},{5,13},{6,14},{7,15},{8,0},{9,1},... | collective-permute-start | bytes 1572872 | tf_op jit(solution)/shard_map/ppermute | solution.py:39
  83.7 21.9 %collective-permute-start.14 = (bf16[8,128,256]{2,1,0:T(8,128)(2,1)}, bf16[8,128,256]{2,1,0:T(8,128)(2,1)S(1)}, u32[]{:S(2)}, u32[]{:S(2)}) collective-permute-start(bf16[8,128,256]{2,1,0:T(8,128)(2,1)} %get-tuple-element.69), channel_id=1, source_target_pairs={{0,4},{1,5},{2,6},{3,7},{4,8},{5,9},{6,10},{7,11},{8,12},{9,13},{1... | collective-permute-start | bytes 1572872 | tf_op jit(solution)/shard_map/ppermute | solution.py:39
  84.4 47.4 %all-to-all-start.1 = ((bf16[16,128,256]{2,1,0:T(8,128)(2,1)}), bf16[16,128,256]{2,1,0:T(8,128)(2,1)}, u32[]{:S(2)}, u32[]{:S(2)}) async-start(bf16[16,128,256]{2,1,0:T(8,128)(2,1)} %get-tuple-element.64), calls=%async_computation.1 | async-start | bytes 2097152 | tf_op jit(solution)/shard_map/all_to_all | solution.py:466
  91.1 26.9 %collective-permute-start.20 = (bf16[8,128,256]{2,1,0:T(8,128)(2,1)}, bf16[8,128,256]{2,1,0:T(8,128)(2,1)}, u32[]{:S(2)}, u32[]{:S(2)}) collective-permute-start(bf16[8,128,256]{2,1,0:T(8,128)(2,1)} %get-tuple-element.81), channel_id=1, source_target_pairs={{0,1},{1,2},{2,3},{3,0},{4,5},{5,6},{6,7},{7,4},{8,9},{9,10},{10,1... | collective-permute-start | bytes 1572872 | tf_op jit(solution)/shard_map/ppermute | solution.py:39
  91.2 14.5 %copy-start.8 = (bf16[8,128,256]{2,1,0:T(8,128)(2,1)}, bf16[8,128,256]{2,1,0:T(8,128)(2,1)S(1)}, u32[]{:S(2)}) copy-start(bf16[8,128,256]{2,1,0:T(8,128)(2,1)S(1)} %collective-permute-done.18.refs_1_) | copy-start | bytes 1572868
  91.2 26.8 %collective-permute-start.19 = (bf16[8,128,256]{2,1,0:T(8,128)(2,1)}, bf16[8,128,256]{2,1,0:T(8,128)(2,1)}, u32[]{:S(2)}, u32[]{:S(2)}) collective-permute-start(bf16[8,128,256]{2,1,0:T(8,128)(2,1)} %get-tuple-element.80), channel_id=1, source_target_pairs={{0,2},{1,3},{2,0},{3,1},{4,6},{5,7},{6,4},{7,5},{8,10},{9,11},{10,... | collective-permute-start | bytes 1572872 | tf_op jit(solution)/shard_map/ppermute | solution.py:39
  95.7 10.0 %copy-start.9 = (bf16[8,128,256]{2,1,0:T(8,128)(2,1)}, bf16[8,128,256]{2,1,0:T(8,128)(2,1)S(1)}, u32[]{:S(2)}) copy-start(bf16[8,128,256]{2,1,0:T(8,128)(2,1)S(1)} %collective-permute-done.12.refs_1_) | copy-start | bytes 1572868
  121.7 7.8 %collective-permute-start.21 = (bf16[4,128,256]{2,1,0:T(8,128)(2,1)S(1)}, bf16[4,128,256]{2,1,0:T(8,128)(2,1)S(1)}, u32[]{:S(2)}, u32[]{:S(2)}) collective-permute-start(bf16[4,128,256]{2,1,0:T(8,128)(2,1)S(1)} %get-tuple-element.84), channel_id=1, source_target_pairs={{0,4},{1,5},{2,6},{3,7},{4,8},{5,9},{6,10},{7,11},{8,12},{9,13},{1... | collective-permute-start | bytes 786440 | tf_op jit(solution)/shard_map/ppermute | solution.py:39
  124.1 14.2 %collective-permute-start.15 = (bf16[4,128,256]{2,1,0:T(8,128)(2,1)S(1)}, bf16[4,128,256]{2,1,0:T(8,128)(2,1)S(1)}, u32[]{:S(2)}, u32[]{:S(2)}) collective-permute-start(bf16[4,128,256]{2,1,0:T(8,128)(2,1)S(1)} %get-tuple-element.73), channel_id=1, source_target_pairs={{0,1},{1,2},{2,3},{3,0},{4,5},{5,6},{6,7},{7,4},{8,9},{9,10},{10,1... | collective-permute-start | bytes 786440 | tf_op jit(solution)/shard_map/ppermute | solution.py:39
  124.1 14.2 %collective-permute-start.16 = (bf16[4,128,256]{2,1,0:T(8,128)(2,1)S(1)}, bf16[4,128,256]{2,1,0:T(8,128)(2,1)S(1)}, u32[]{:S(2)}, u32[]{:S(2)}) collective-permute-start(bf16[4,128,256]{2,1,0:T(8,128)(2,1)S(1)} %get-tuple-element.74), channel_id=1, source_target_pairs={{0,2},{1,3},{2,0},{3,1},{4,6},{5,7},{6,4},{7,5},{8,10},{9,11},{10,... | collective-permute-start | bytes 786440 | tf_op jit(solution)/shard_map/ppermute | solution.py:39
  125.1 13.8 %collective-permute-start.17 = (bf16[4,128,256]{2,1,0:T(8,128)(2,1)S(1)}, bf16[4,128,256]{2,1,0:T(8,128)(2,1)S(1)}, u32[]{:S(2)}, u32[]{:S(2)}) collective-permute-start(bf16[4,128,256]{2,1,0:T(8,128)(2,1)S(1)} %get-tuple-element.75), channel_id=1, source_target_pairs={{0,3},{1,0},{2,1},{3,2},{4,7},{5,4},{6,5},{7,6},{8,11},{9,8},{10,9... | collective-permute-start | bytes 786440 | tf_op jit(solution)/shard_map/ppermute | solution.py:39
  127.4 11.6 %collective-permute-start.23 = (bf16[4,128,256]{2,1,0:T(8,128)(2,1)}, bf16[4,128,256]{2,1,0:T(8,128)(2,1)S(1)}, u32[]{:S(2)}, u32[]{:S(2)}) collective-permute-start(bf16[4,128,256]{2,1,0:T(8,128)(2,1)} %get-tuple-element.87), channel_id=1, source_target_pairs={{0,12},{1,13},{2,14},{3,15},{4,0},{5,1},{6,2},{7,3},{8,4},{9,5},{1... | collective-permute-start | bytes 786440 | tf_op jit(solution)/shard_map/ppermute | solution.py:39
  129.5 10.6 %collective-permute-start.22 = (bf16[4,128,256]{2,1,0:T(8,128)(2,1)}, bf16[4,128,256]{2,1,0:T(8,128)(2,1)S(1)}, u32[]{:S(2)}, u32[]{:S(2)}) collective-permute-start(bf16[4,128,256]{2,1,0:T(8,128)(2,1)} %get-tuple-element.86), channel_id=1, source_target_pairs={{0,8},{1,9},{2,10},{3,11},{4,12},{5,13},{6,14},{7,15},{8,0},{9,1},... | collective-permute-start | bytes 786440 | tf_op jit(solution)/shard_map/ppermute | solution.py:39
  (6 other events, 24.9 us)

commit v10 on v9

--- a/solution.py
+++ b/solution.py
@@ -464,6 +464,8 @@
     back, keys, values = attend(distinct_ids, group_refs, tokens, keys, values, owned, most)
     keys, values = exchange_lines(((keys, "y", -1), (values, "x", -1)))
     back = lax.all_to_all(back, "ctx", split_axis=0, concat_axis=0, tiled=True)
+    keys, values = list(keys), list(values)
+    keys[0], values[3] = lax.optimization_barrier((keys[0], values[3]))
     keys = list(spread(add, keys, 0, owned))
     keys[0], values[0] = lax.optimization_barrier((keys[0], values[0]))
     values = spread(add, values, 1, owned)

time: 142 us -> 137 us (0.965)
  waiting for transfers between devices: 50.3 us -> 44.2 us
    ppermute x24, waiting for transfers between devices: 50.3 us -> 44.2 us  [shift(): return lax.ppermute(value, 'dp', pairs)]
  transfers between devices with their start and end apart: 26 -> 26, of which waited for: 14 -> 14; matrix products, arithmetic and copies ran while one was open for 0% -> 0% of each run, Pallas kernels for 12% -> 13%
where the time goes in v10:
time: 137 us; the launch traced here: 136 us
  starting transfers between devices  56.3 us (41%)
  waiting for transfers between devices  44.2 us (32%)
  Pallas kernels  32.8 us (24%)
  local copies, waits for them, and re-layouts  1.67 us (1%)
    ppermute x24, waiting for transfers between devices, shift(): return lax.ppermute(value, 'dp', pairs)  44.2 us
    ppermute x24, starting transfers between devices, shift(): return lax.ppermute(value, 'dp', pairs)  40.9 us
    pallas_call x1, Pallas kernels, attend(): pl.pallas_call(functools.partial(attend_body, groups, distinct, owned, mo...  12 us
    all_to_all x1, starting transfers between devices, on_device(): lax.all_to_all(packed, 'ctx', split_axis=0, concat_axis=0, tiled=True)  8.71 us
    pallas_call x2, Pallas kernels, spread(): pl.pallas_call(functools.partial(spread_body, across), out_shape=chunk_sh...  7.14 us
    all_to_all x1, starting transfers between devices, on_device(): back = lax.all_to_all(back, 'ctx', split_axis=0, concat_axis=0, tiled=True)  6.68 us
    pallas_call x1, Pallas kernels, tables(): pl.pallas_call(functools.partial(tables_body, owned, most), out_shape=(ja...  3.94 us
    pallas_call x1, Pallas kernels, select(): pl.pallas_call(select_body, out_shape=tuple((pltpu.HBM(shape.shape, shape...  3.74 us
  transfers between devices with their start and end apart: 26, of which 14 were waited for; matrix products, arithmetic and copies ran while one was open for 0% of the time, Pallas kernels for 13%

profile of v10, /device:TPU:8, one launch (start us, length us, event | category | flops | bytes accessed | tf_op | source)
XLA Modules:
  0.0 135.8 jit_solution(17797894317373406566)
XLA Ops:
  0.6 2.7 %shard_map.85 = bf16[16,2,128,256]{3,2,1,0:T(8,128)(2,1)} custom-call(bf16[128,4096]{1,0:T(8,128)(2,1)} %bitcast.5, bf16[128,4096]{1,0:T(8,128)(2,1)} %bitcast.6), custom_call_target="tpu_custom_call" | custom-call | tf_op jit(solution)/shard_map/pallas_call | solution.py:87
  3.4 8.7 %all-to-all-start = ((bf16[16,2,128,256]{3,2,1,0:T(8,128)(2,1)}), bf16[16,2,128,256]{3,2,1,0:T(8,128)(2,1)S(1)}, u32[]{:S(2)}, u32[]{:S(2)}) async-start(bf16[16,2,128,256]{3,2,1,0:T(8,128)(2,1)} %shard_map.85), calls=%async_computation | async-start | bytes 4194304 | tf_op jit(solution)/shard_map/all_to_all | solution.py:461
  12.7 3.0 %collective-permute-start.1 = (bf16[4,128,256]{2,1,0:T(8,128)(2,1)S(1)}, bf16[4,128,256]{2,1,0:T(8,128)(2,1)S(1)}, u32[]{:S(2)}, u32[]{:S(2)}) collective-permute-start(bf16[4,128,256]{2,1,0:T(8,128)(2,1)S(1)} %copy-done), channel_id=1, source_target_pairs={{0,2},{1,3},{2,0},{3,1},{4,6},{5,7},{6,4},{7,5},{8,10},{9,11},{10,... | collective-permute-start | bytes 786440 | tf_op jit(solution)/shard_map/ppermute | solution.py:39
  17.7 1.6 %collective-permute-start.5 = (bf16[4,128,256]{2,1,0:T(8,128)(2,1)S(1)}, bf16[4,128,256]{2,1,0:T(8,128)(2,1)}, u32[]{:S(2)}, u32[]{:S(2)}) collective-permute-start(bf16[4,128,256]{2,1,0:T(8,128)(2,1)S(1)} %copy-done.1), channel_id=1, source_target_pairs={{0,4},{1,5},{2,6},{3,7},{4,8},{5,9},{6,10},{7,11},{8,12},{9,13},{1... | collective-permute-start | bytes 786440 | tf_op jit(solution)/shard_map/ppermute | solution.py:39
  20.8 3.5 %collective-permute-start.4 = (bf16[4,128,256]{2,1,0:T(8,128)(2,1)S(1)}, bf16[4,128,256]{2,1,0:T(8,128)(2,1)}, u32[]{:S(2)}, u32[]{:S(2)}) collective-permute-start(bf16[4,128,256]{2,1,0:T(8,128)(2,1)S(1)} %copy-done.1), channel_id=1, source_target_pairs={{0,8},{1,9},{2,10},{3,11},{4,12},{5,13},{6,14},{7,15},{8,0},{9,1},... | collective-permute-start | bytes 786440 | tf_op jit(solution)/shard_map/ppermute | solution.py:39
  24.4 3.9 %shard_map.86 = (s32[2,32]{1,0:T(2,128)}, s32[2,64]{1,0:T(2,128)}) custom-call(s32[16,16]{1,0:T(8,128)} %ids_ref.3), custom_call_target="tpu_custom_call" | custom-call | tf_op jit(solution)/shard_map/pallas_call | solution.py:167
  28.3 2.2 %collective-permute-done.4.refs_6_ = bf16[4,128,256]{2,1,0:T(8,128)(2,1)} collective-permute-done((bf16[4,128,256]{2,1,0:T(8,128)(2,1)S(1)}, bf16[4,128,256]{2,1,0:T(8,128)(2,1)}, u32[]{:S(2)}, u32[]{:S(2)}) %collective-permute-start.4) | collective-permute-done | bytes 262176 | tf_op jit(solution)/shard_map/ppermute | solution.py:39
  31.2 3.7 %shard_map.87 = (bf16[8,128,256]{2,1,0:T(8,128)(2,1)}, bf16[8,128,256]{2,1,0:T(8,128)(2,1)}, bf16[8,128,256]{2,1,0:T(8,128)(2,1)}, bf16[8,128,256]{2,1,0:T(8,128...) custom-call(s32[2,32]{1,0:T(2,128)S(1)} %copy-done.3, ...), custom_call_target="tpu_custom_call" | custom-call | tf_op jit(solution)/shard_map/pallas_call | solution.py:212
  35.0 1.6 %collective-permute-start.9 = (bf16[8,128,256]{2,1,0:T(8,128)(2,1)}, bf16[8,128,256]{2,1,0:T(8,128)(2,1)S(1)}, u32[]{:S(2)}, u32[]{:S(2)}) collective-permute-start(bf16[8,128,256]{2,1,0:T(8,128)(2,1)} %get-tuple-element.62), channel_id=1, source_target_pairs={{0,1},{1,2},{2,3},{3,0},{4,5},{5,6},{6,7},{7,4},{8,9},{9,10},{10,1... | collective-permute-start | bytes 1572872 | tf_op jit(solution)/shard_map/ppermute | solution.py:39
  36.6 2.2 %collective-permute-start.6 = (bf16[8,128,256]{2,1,0:T(8,128)(2,1)}, bf16[8,128,256]{2,1,0:T(8,128)(2,1)S(1)}, u32[]{:S(2)}, u32[]{:S(2)}) collective-permute-start(bf16[8,128,256]{2,1,0:T(8,128)(2,1)} %get-tuple-element.57), channel_id=1, source_target_pairs={{0,4},{1,5},{2,6},{3,7},{4,8},{5,9},{6,10},{7,11},{8,12},{9,13},{1... | collective-permute-start | bytes 1572872 | tf_op jit(solution)/shard_map/ppermute | solution.py:39
  38.8 3.6 %collective-permute-start.7 = (bf16[8,128,256]{2,1,0:T(8,128)(2,1)}, bf16[8,128,256]{2,1,0:T(8,128)(2,1)}, u32[]{:S(2)}, u32[]{:S(2)}) collective-permute-start(bf16[8,128,256]{2,1,0:T(8,128)(2,1)} %get-tuple-element.58), channel_id=1, source_target_pairs={{0,8},{1,9},{2,10},{3,11},{4,12},{5,13},{6,14},{7,15},{8,0},{9,1},... | collective-permute-start | bytes 1572872 | tf_op jit(solution)/shard_map/ppermute | solution.py:39
  42.4 2.6 %collective-permute-start.11 = (bf16[8,128,256]{2,1,0:T(8,128)(2,1)}, bf16[8,128,256]{2,1,0:T(8,128)(2,1)}, u32[]{:S(2)}, u32[]{:S(2)}) collective-permute-start(bf16[8,128,256]{2,1,0:T(8,128)(2,1)} %get-tuple-element.65), channel_id=1, source_target_pairs={{0,3},{1,0},{2,1},{3,2},{4,7},{5,4},{6,5},{7,6},{8,11},{9,8},{10,9... | collective-permute-start | bytes 1572872 | tf_op jit(solution)/shard_map/ppermute | solution.py:39
  45.0 4.4 %collective-permute-done.9.refs_5_ = bf16[8,128,256]{2,1,0:T(8,128)(2,1)S(1)} collective-permute-done((bf16[8,128,256]{2,1,0:T(8,128)(2,1)}, bf16[8,128,256]{2,1,0:T(8,128)(2,1)S(1)}, u32[]{:S(2)}, u32[]{:S(2)}) %collective-permute-start.9) | collective-permute-done | bytes 524320 | tf_op jit(solution)/shard_map/ppermute | solution.py:39
  49.4 1.8 %collective-permute-start.10 = (bf16[8,128,256]{2,1,0:T(8,128)(2,1)}, bf16[8,128,256]{2,1,0:T(8,128)(2,1)}, u32[]{:S(2)}, u32[]{:S(2)}) collective-permute-start(bf16[8,128,256]{2,1,0:T(8,128)(2,1)} %get-tuple-element.64), channel_id=1, source_target_pairs={{0,2},{1,3},{2,0},{3,1},{4,6},{5,7},{6,4},{7,5},{8,10},{9,11},{10,... | collective-permute-start | bytes 1572872 | tf_op jit(solution)/shard_map/ppermute | solution.py:39
  51.3 9.4 %collective-permute-done.6.refs_1_ = bf16[8,128,256]{2,1,0:T(8,128)(2,1)S(1)} collective-permute-done((bf16[8,128,256]{2,1,0:T(8,128)(2,1)}, bf16[8,128,256]{2,1,0:T(8,128)(2,1)S(1)}, u32[]{:S(2)}, u32[]{:S(2)}) %collective-permute-start.6) | collective-permute-done | bytes 524320 | tf_op jit(solution)/shard_map/ppermute | solution.py:39
  60.7 3.6 %collective-permute-done.8.refs_3_ = bf16[8,128,256]{2,1,0:T(8,128)(2,1)} collective-permute-done((bf16[8,128,256]{2,1,0:T(8,128)(2,1)}, bf16[8,128,256]{2,1,0:T(8,128)(2,1)}, u32[]{:S(2)}, u32[]{:S(2)}) %collective-permute-start.8) | collective-permute-done | bytes 524320 | tf_op jit(solution)/shard_map/ppermute | solution.py:39
  64.8 12.0 %shard_map.88 = (bf16[16,128,256]{2,1,0:T(8,128)(2,1)}, bf16[8,128,256]{2,1,0:T(8,128)(2,1)}, bf16[8,128,256]{2,1,0:T(8,128)(2,1)}, bf16[8,128,256]{2,1,0:T(8,12...) custom-call(s32[16,16]{1,0:T(8,128)S(1)} %copy-done.2, ...), custom_call_target="tpu_custom_call" | custom-call | tf_op jit(solution)/shard_map/pallas_call | solution.py:418
  76.8 3.1 %collective-permute-start.12 = (bf16[8,128,256]{2,1,0:T(8,128)(2,1)}, bf16[8,128,256]{2,1,0:T(8,128)(2,1)S(1)}, u32[]{:S(2)}, u32[]{:S(2)}) collective-permute-start(bf16[8,128,256]{2,1,0:T(8,128)(2,1)} %get-tuple-element.69), channel_id=1, source_target_pairs={{0,1},{1,2},{2,3},{3,0},{4,5},{5,6},{6,7},{7,4},{8,9},{9,10},{10,1... | collective-permute-start | bytes 1572872 | tf_op jit(solution)/shard_map/ppermute | solution.py:39
  80.8 1.9 %collective-permute-start.13 = (bf16[8,128,256]{2,1,0:T(8,128)(2,1)}, bf16[8,128,256]{2,1,0:T(8,128)(2,1)S(1)}, u32[]{:S(2)}, u32[]{:S(2)}) collective-permute-start(bf16[8,128,256]{2,1,0:T(8,128)(2,1)} %get-tuple-element.71), channel_id=1, source_target_pairs={{0,12},{1,13},{2,14},{3,15},{4,0},{5,1},{6,2},{7,3},{8,4},{9,5},{1... | collective-permute-start | bytes 1572872 | tf_op jit(solution)/shard_map/ppermute | solution.py:39
  84.5 6.7 %all-to-all-start.1 = ((bf16[16,128,256]{2,1,0:T(8,128)(2,1)}), bf16[16,128,256]{2,1,0:T(8,128)(2,1)}, u32[]{:S(2)}, u32[]{:S(2)}) async-start(bf16[16,128,256]{2,1,0:T(8,128)(2,1)} %get-tuple-element.66), calls=%async_computation.1 | async-start | bytes 2097152 | tf_op jit(solution)/shard_map/all_to_all | solution.py:466
  91.8 2.2 %collective-permute-start.20 = (bf16[8,128,256]{2,1,0:T(8,128)(2,1)}, bf16[8,128,256]{2,1,0:T(8,128)(2,1)}, u32[]{:S(2)}, u32[]{:S(2)}) collective-permute-start(bf16[8,128,256]{2,1,0:T(8,128)(2,1)} %get-tuple-element.84), channel_id=1, source_target_pairs={{0,2},{1,3},{2,0},{3,1},{4,6},{5,7},{6,4},{7,5},{8,10},{9,11},{10,... | collective-permute-start | bytes 1572872 | tf_op jit(solution)/shard_map/ppermute | solution.py:39
  94.0 2.5 %collective-permute-done.13.refs_1_ = bf16[8,128,256]{2,1,0:T(8,128)(2,1)S(1)} collective-permute-done((bf16[8,128,256]{2,1,0:T(8,128)(2,1)}, bf16[8,128,256]{2,1,0:T(8,128)(2,1)S(1)}, u32[]{:S(2)}, u32[]{:S(2)}) %collective-permute-start.13) | collective-permute-done | bytes 524320 | tf_op jit(solution)/shard_map/ppermute | solution.py:39
  96.6 8.1 %collective-permute-done.14.refs_2_ = bf16[8,128,256]{2,1,0:T(8,128)(2,1)S(1)} collective-permute-done((bf16[8,128,256]{2,1,0:T(8,128)(2,1)}, bf16[8,128,256]{2,1,0:T(8,128)(2,1)S(1)}, u32[]{:S(2)}, u32[]{:S(2)}) %collective-permute-start.14) | collective-permute-done | bytes 524320 | tf_op jit(solution)/shard_map/ppermute | solution.py:39
  104.7 1.7 %collective-permute-done.15.refs_3_ = bf16[8,128,256]{2,1,0:T(8,128)(2,1)S(1)} collective-permute-done((bf16[8,128,256]{2,1,0:T(8,128)(2,1)}, bf16[8,128,256]{2,1,0:T(8,128)(2,1)S(1)}, u32[]{:S(2)}, u32[]{:S(2)}) %collective-permute-start.15) | collective-permute-done | bytes 524320 | tf_op jit(solution)/shard_map/ppermute | solution.py:39
  107.2 3.5 %shard_map.90 = (f32[4,128,256]{2,1,0:T(8,128)S(1)}, bf16[4,128,256]{2,1,0:T(8,128)(2,1)}, bf16[4,128,256]{2,1,0:T(8,128)(2,1)S(1)}, bf16[4,128,256]{2,1,0:T(8,128)(2,1)S(1)}) custom-call(s32[2,64]{1,0:T(2,128)S(1)} %copy-done.4, bf16[8,128,256]{2,1,0:T(8,128)(2,1)} %get-tuple-element.70.refs_0_, bf16[8,128,256]{2,1,0:T(8,128)(2,1)} %copy-done.10, ...), custom_call_target="tpu_custom_call" | custom-call | flops 199999995904 | bytes 2097152 | tf_op jit(solution)/shard_map/pallas_call | solution.py:261
  110.7 3.6 %shard_map.91 = (f32[4,128,256]{2,1,0:T(8,128)S(1)}, bf16[4,128,256]{2,1,0:T(8,128)(2,1)S(1)}, bf16[4,128,256]{2,1,0:T(8,128)(2,1)S(1)}, bf16[4,128,256]{2,1,0:T(8,128)(2,1)}) custom-call(s32[2,64]{1,0:T(2,128)S(1)} %copy-done.4, bf16[8,128,256]{2,1,0:T(8,128)(2,1)} %get-tuple-element.80.refs_0_, bf16[8,128,256]{2,1,0:T(8,128)(2,1)} %copy-done.9, ...), custom_call_target="tpu_custom_call" | custom-call | flops 199999995904 | bytes 2097152 | tf_op jit(solution)/shard_map/pallas_call | solution.py:261
  115.8 2.5 %collective-permute-start.17 = (bf16[4,128,256]{2,1,0:T(8,128)(2,1)S(1)}, bf16[4,128,256]{2,1,0:T(8,128)(2,1)S(1)}, u32[]{:S(2)}, u32[]{:S(2)}) collective-permute-start(bf16[4,128,256]{2,1,0:T(8,128)(2,1)S(1)} %get-tuple-element.78), channel_id=1, source_target_pairs={{0,2},{1,3},{2,0},{3,1},{4,6},{5,7},{6,4},{7,5},{8,10},{9,11},{10,... | collective-permute-start | bytes 786440 | tf_op jit(solution)/shard_map/ppermute | solution.py:39
  118.3 1.9 %collective-permute-start.18 = (bf16[4,128,256]{2,1,0:T(8,128)(2,1)S(1)}, bf16[4,128,256]{2,1,0:T(8,128)(2,1)S(1)}, u32[]{:S(2)}, u32[]{:S(2)}) collective-permute-start(bf16[4,128,256]{2,1,0:T(8,128)(2,1)S(1)} %get-tuple-element.79), channel_id=1, source_target_pairs={{0,3},{1,0},{2,1},{3,2},{4,7},{5,4},{6,5},{7,6},{8,11},{9,8},{10,9... | collective-permute-start | bytes 786440 | tf_op jit(solution)/shard_map/ppermute | solution.py:39
  121.6 1.9 %collective-permute-done.21.refs_5_ = bf16[4,128,256]{2,1,0:T(8,128)(2,1)S(1)} collective-permute-done((bf16[4,128,256]{2,1,0:T(8,128)(2,1)S(1)}, bf16[4,128,256]{2,1,0:T(8,128)(2,1)S(1)}, u32[]{:S(2)}, u32[]{:S(2)}) %collective-permute-start.21) | collective-permute-done | bytes 262176 | tf_op jit(solution)/shard_map/ppermute | solution.py:39
  124.8 2.3 %shard_map.89 = bf16[128,4096]{1,0:T(8,128)(2,1)} custom-call(bf16[16,128,256]{2,1,0:T(8,128)(2,1)} %all-to-all-done.1.in_ref), custom_call_target="tpu_custom_call" | custom-call | tf_op jit(solution)/shard_map/pallas_call | solution.py:113
  127.1 3.8 %collective-permute-done.16.refs_1_ = bf16[4,128,256]{2,1,0:T(8,128)(2,1)S(1)} collective-permute-done((bf16[4,128,256]{2,1,0:T(8,128)(2,1)}, bf16[4,128,256]{2,1,0:T(8,128)(2,1)S(1)}, u32[]{:S(2)}, u32[]{:S(2)}) %collective-permute-start.16) | collective-permute-done | bytes 262176 | tf_op jit(solution)/shard_map/ppermute | solution.py:39
  131.3 3.5 %collective-permute-done.22.refs_6_ = bf16[4,128,256]{2,1,0:T(8,128)(2,1)S(1)} collective-permute-done((bf16[4,128,256]{2,1,0:T(8,128)(2,1)S(1)}, bf16[4,128,256]{2,1,0:T(8,128)(2,1)S(1)}, u32[]{:S(2)}, u32[]{:S(2)}) %collective-permute-start.22) | collective-permute-done | bytes 262176 | tf_op jit(solution)/shard_map/ppermute | solution.py:39
  (56 shorter events, 15.3 us)
Async XLA Ops:
  3.4 47.8 %copy-start.7 = (s32[16,32,2]{1,2,0:T(2,128)S(1)}, s32[16,32,2]{1,2,0:T(2,128)}, u32[]{:S(2)}) copy-start(s32[16,32,2]{1,2,0:T(2,128)} %param.11) | copy-start | bytes 12292
  3.4 61.4 %all-to-all-start = ((bf16[16,2,128,256]{3,2,1,0:T(8,128)(2,1)}), bf16[16,2,128,256]{3,2,1,0:T(8,128)(2,1)S(1)}, u32[]{:S(2)}, u32[]{:S(2)}) async-start(bf16[16,2,128,256]{3,2,1,0:T(8,128)(2,1)} %shard_map.85), calls=%async_computation | async-start | bytes 4194304 | tf_op jit(solution)/shard_map/all_to_all | solution.py:461
  12.1 52.6 %copy-start.2 = (s32[16,16]{1,0:T(8,128)S(1)}, s32[16,16]{1,0:T(8,128)}, u32[]{:S(2)}) copy-start(s32[16,16]{1,0:T(8,128)} %ids_ref.3) | copy-start | bytes 3076
  12.1 8.7 %collective-permute-start.3 = (bf16[4,128,256]{2,1,0:T(8,128)(2,1)S(1)}, bf16[4,128,256]{2,1,0:T(8,128)(2,1)S(1)}, u32[]{:S(2)}, u32[]{:S(2)}) collective-permute-start(bf16[4,128,256]{2,1,0:T(8,128)(2,1)S(1)} %copy-done.1), channel_id=1, source_target_pairs={{0,12},{1,13},{2,14},{3,15},{4,0},{5,1},{6,2},{7,3},{8,4},{9,5},{1... | collective-permute-start | bytes 786440 | tf_op jit(solution)/shard_map/ppermute | solution.py:39
  12.7 15.6 %collective-permute-start.1 = (bf16[4,128,256]{2,1,0:T(8,128)(2,1)S(1)}, bf16[4,128,256]{2,1,0:T(8,128)(2,1)S(1)}, u32[]{:S(2)}, u32[]{:S(2)}) collective-permute-start(bf16[4,128,256]{2,1,0:T(8,128)(2,1)S(1)} %copy-done), channel_id=1, source_target_pairs={{0,2},{1,3},{2,0},{3,1},{4,6},{5,7},{6,4},{7,5},{8,10},{9,11},{10,... | collective-permute-start | bytes 786440 | tf_op jit(solution)/shard_map/ppermute | solution.py:39
  15.7 12.6 %collective-permute-start = (bf16[4,128,256]{2,1,0:T(8,128)(2,1)S(1)}, bf16[4,128,256]{2,1,0:T(8,128)(2,1)S(1)}, u32[]{:S(2)}, u32[]{:S(2)}) collective-permute-start(bf16[4,128,256]{2,1,0:T(8,128)(2,1)S(1)} %copy-done), channel_id=1, source_target_pairs={{0,3},{1,0},{2,1},{3,2},{4,7},{5,4},{6,5},{7,6},{8,11},{9,8},{10,9... | collective-permute-start | bytes 786440 | tf_op jit(solution)/shard_map/ppermute | solution.py:39
  16.8 11.5 %collective-permute-start.2 = (bf16[4,128,256]{2,1,0:T(8,128)(2,1)S(1)}, bf16[4,128,256]{2,1,0:T(8,128)(2,1)}, u32[]{:S(2)}, u32[]{:S(2)}) collective-permute-start(bf16[4,128,256]{2,1,0:T(8,128)(2,1)S(1)} %copy-done), channel_id=1, source_target_pairs={{0,1},{1,2},{2,3},{3,0},{4,5},{5,6},{6,7},{7,4},{8,9},{9,10},{10,1... | collective-permute-start | bytes 786440 | tf_op jit(solution)/shard_map/ppermute | solution.py:39
  17.7 10.6 %collective-permute-start.5 = (bf16[4,128,256]{2,1,0:T(8,128)(2,1)S(1)}, bf16[4,128,256]{2,1,0:T(8,128)(2,1)}, u32[]{:S(2)}, u32[]{:S(2)}) collective-permute-start(bf16[4,128,256]{2,1,0:T(8,128)(2,1)S(1)} %copy-done.1), channel_id=1, source_target_pairs={{0,4},{1,5},{2,6},{3,7},{4,8},{5,9},{6,10},{7,11},{8,12},{9,13},{1... | collective-permute-start | bytes 786440 | tf_op jit(solution)/shard_map/ppermute | solution.py:39
  20.8 9.7 %collective-permute-start.4 = (bf16[4,128,256]{2,1,0:T(8,128)(2,1)S(1)}, bf16[4,128,256]{2,1,0:T(8,128)(2,1)}, u32[]{:S(2)}, u32[]{:S(2)}) collective-permute-start(bf16[4,128,256]{2,1,0:T(8,128)(2,1)S(1)} %copy-done.1), channel_id=1, source_target_pairs={{0,8},{1,9},{2,10},{3,11},{4,12},{5,13},{6,14},{7,15},{8,0},{9,1},... | collective-permute-start | bytes 786440 | tf_op jit(solution)/shard_map/ppermute | solution.py:39
  35.0 14.4 %collective-permute-start.9 = (bf16[8,128,256]{2,1,0:T(8,128)(2,1)}, bf16[8,128,256]{2,1,0:T(8,128)(2,1)S(1)}, u32[]{:S(2)}, u32[]{:S(2)}) collective-permute-start(bf16[8,128,256]{2,1,0:T(8,128)(2,1)} %get-tuple-element.62), channel_id=1, source_target_pairs={{0,1},{1,2},{2,3},{3,0},{4,5},{5,6},{6,7},{7,4},{8,9},{9,10},{10,1... | collective-permute-start | bytes 1572872 | tf_op jit(solution)/shard_map/ppermute | solution.py:39
  36.6 24.1 %collective-permute-start.6 = (bf16[8,128,256]{2,1,0:T(8,128)(2,1)}, bf16[8,128,256]{2,1,0:T(8,128)(2,1)S(1)}, u32[]{:S(2)}, u32[]{:S(2)}) collective-permute-start(bf16[8,128,256]{2,1,0:T(8,128)(2,1)} %get-tuple-element.57), channel_id=1, source_target_pairs={{0,4},{1,5},{2,6},{3,7},{4,8},{5,9},{6,10},{7,11},{8,12},{9,13},{1... | collective-permute-start | bytes 1572872 | tf_op jit(solution)/shard_map/ppermute | solution.py:39
  38.8 21.9 %collective-permute-start.7 = (bf16[8,128,256]{2,1,0:T(8,128)(2,1)}, bf16[8,128,256]{2,1,0:T(8,128)(2,1)}, u32[]{:S(2)}, u32[]{:S(2)}) collective-permute-start(bf16[8,128,256]{2,1,0:T(8,128)(2,1)} %get-tuple-element.58), channel_id=1, source_target_pairs={{0,8},{1,9},{2,10},{3,11},{4,12},{5,13},{6,14},{7,15},{8,0},{9,1},... | collective-permute-start | bytes 1572872 | tf_op jit(solution)/shard_map/ppermute | solution.py:39
  42.4 21.9 %collective-permute-start.8 = (bf16[8,128,256]{2,1,0:T(8,128)(2,1)}, bf16[8,128,256]{2,1,0:T(8,128)(2,1)}, u32[]{:S(2)}, u32[]{:S(2)}) collective-permute-start(bf16[8,128,256]{2,1,0:T(8,128)(2,1)} %get-tuple-element.59), channel_id=1, source_target_pairs={{0,12},{1,13},{2,14},{3,15},{4,0},{5,1},{6,2},{7,3},{8,4},{9,5},{1... | collective-permute-start | bytes 1572872 | tf_op jit(solution)/shard_map/ppermute | solution.py:39
  42.4 22.3 %collective-permute-start.11 = (bf16[8,128,256]{2,1,0:T(8,128)(2,1)}, bf16[8,128,256]{2,1,0:T(8,128)(2,1)}, u32[]{:S(2)}, u32[]{:S(2)}) collective-permute-start(bf16[8,128,256]{2,1,0:T(8,128)(2,1)} %get-tuple-element.65), channel_id=1, source_target_pairs={{0,3},{1,0},{2,1},{3,2},{4,7},{5,4},{6,5},{7,6},{8,11},{9,8},{10,9... | collective-permute-start | bytes 1572872 | tf_op jit(solution)/shard_map/ppermute | solution.py:39
  49.4 15.4 %copy-start.5 = (bf16[8,128,256]{2,1,0:T(8,128)(2,1)}, bf16[8,128,256]{2,1,0:T(8,128)(2,1)S(1)}, u32[]{:S(2)}) copy-start(bf16[8,128,256]{2,1,0:T(8,128)(2,1)S(1)} %collective-permute-done.9.refs_5_) | copy-start | bytes 1572868
  49.4 15.4 %collective-permute-start.10 = (bf16[8,128,256]{2,1,0:T(8,128)(2,1)}, bf16[8,128,256]{2,1,0:T(8,128)(2,1)}, u32[]{:S(2)}, u32[]{:S(2)}) collective-permute-start(bf16[8,128,256]{2,1,0:T(8,128)(2,1)} %get-tuple-element.64), channel_id=1, source_target_pairs={{0,2},{1,3},{2,0},{3,1},{4,6},{5,7},{6,4},{7,5},{8,10},{9,11},{10,... | collective-permute-start | bytes 1572872 | tf_op jit(solution)/shard_map/ppermute | solution.py:39
  76.8 30.4 %copy-start.4 = (s32[2,64]{1,0:T(2,128)S(1)}, s32[2,64]{1,0:T(2,128)}, u32[]{:S(2)}) copy-start(s32[2,64]{1,0:T(2,128)} %get-tuple-element.67.add_ref) | copy-start | bytes 1540
  76.8 15.0 %collective-permute-start.12 = (bf16[8,128,256]{2,1,0:T(8,128)(2,1)}, bf16[8,128,256]{2,1,0:T(8,128)(2,1)S(1)}, u32[]{:S(2)}, u32[]{:S(2)}) collective-permute-start(bf16[8,128,256]{2,1,0:T(8,128)(2,1)} %get-tuple-element.69), channel_id=1, source_target_pairs={{0,1},{1,2},{2,3},{3,0},{4,5},{5,6},{6,7},{7,4},{8,9},{9,10},{10,1... | collective-permute-start | bytes 1572872 | tf_op jit(solution)/shard_map/ppermute | solution.py:39
  79.9 11.9 %collective-permute-start.19 = (bf16[8,128,256]{2,1,0:T(8,128)(2,1)}, bf16[8,128,256]{2,1,0:T(8,128)(2,1)S(1)}, u32[]{:S(2)}, u32[]{:S(2)}) collective-permute-start(bf16[8,128,256]{2,1,0:T(8,128)(2,1)} %get-tuple-element.82), channel_id=1, source_target_pairs={{0,3},{1,0},{2,1},{3,2},{4,7},{5,4},{6,5},{7,6},{8,11},{9,8},{10,9... | collective-permute-start | bytes 1572872 | tf_op jit(solution)/shard_map/ppermute | solution.py:39
  80.8 15.7 %collective-permute-start.13 = (bf16[8,128,256]{2,1,0:T(8,128)(2,1)}, bf16[8,128,256]{2,1,0:T(8,128)(2,1)S(1)}, u32[]{:S(2)}, u32[]{:S(2)}) collective-permute-start(bf16[8,128,256]{2,1,0:T(8,128)(2,1)} %get-tuple-element.71), channel_id=1, source_target_pairs={{0,12},{1,13},{2,14},{3,15},{4,0},{5,1},{6,2},{7,3},{8,4},{9,5},{1... | collective-permute-start | bytes 1572872 | tf_op jit(solution)/shard_map/ppermute | solution.py:39
  82.7 21.9 %collective-permute-start.14 = (bf16[8,128,256]{2,1,0:T(8,128)(2,1)}, bf16[8,128,256]{2,1,0:T(8,128)(2,1)S(1)}, u32[]{:S(2)}, u32[]{:S(2)}) collective-permute-start(bf16[8,128,256]{2,1,0:T(8,128)(2,1)} %get-tuple-element.72), channel_id=1, source_target_pairs={{0,8},{1,9},{2,10},{3,11},{4,12},{5,13},{6,14},{7,15},{8,0},{9,1},... | collective-permute-start | bytes 1572872 | tf_op jit(solution)/shard_map/ppermute | solution.py:39
  83.8 22.6 %collective-permute-start.15 = (bf16[8,128,256]{2,1,0:T(8,128)(2,1)}, bf16[8,128,256]{2,1,0:T(8,128)(2,1)S(1)}, u32[]{:S(2)}, u32[]{:S(2)}) collective-permute-start(bf16[8,128,256]{2,1,0:T(8,128)(2,1)} %get-tuple-element.73), channel_id=1, source_target_pairs={{0,4},{1,5},{2,6},{3,7},{4,8},{5,9},{6,10},{7,11},{8,12},{9,13},{1... | collective-permute-start | bytes 1572872 | tf_op jit(solution)/shard_map/ppermute | solution.py:39
  84.5 40.3 %all-to-all-start.1 = ((bf16[16,128,256]{2,1,0:T(8,128)(2,1)}), bf16[16,128,256]{2,1,0:T(8,128)(2,1)}, u32[]{:S(2)}, u32[]{:S(2)}) async-start(bf16[16,128,256]{2,1,0:T(8,128)(2,1)} %get-tuple-element.66), calls=%async_computation.1 | async-start | bytes 2097152 | tf_op jit(solution)/shard_map/all_to_all | solution.py:466
  91.8 14.5 %copy-start.8 = (bf16[8,128,256]{2,1,0:T(8,128)(2,1)}, bf16[8,128,256]{2,1,0:T(8,128)(2,1)S(1)}, u32[]{:S(2)}) copy-start(bf16[8,128,256]{2,1,0:T(8,128)(2,1)S(1)} %collective-permute-done.12.refs_3_) | copy-start | bytes 1572868
  91.8 18.9 %copy-start.9 = (bf16[8,128,256]{2,1,0:T(8,128)(2,1)}, bf16[8,128,256]{2,1,0:T(8,128)(2,1)S(1)}, u32[]{:S(2)}) copy-start(bf16[8,128,256]{2,1,0:T(8,128)(2,1)S(1)} %collective-permute-done.19.refs_1_) | copy-start | bytes 1572868
  91.8 18.9 %collective-permute-start.20 = (bf16[8,128,256]{2,1,0:T(8,128)(2,1)}, bf16[8,128,256]{2,1,0:T(8,128)(2,1)}, u32[]{:S(2)}, u32[]{:S(2)}) collective-permute-start(bf16[8,128,256]{2,1,0:T(8,128)(2,1)} %get-tuple-element.84), channel_id=1, source_target_pairs={{0,2},{1,3},{2,0},{3,1},{4,6},{5,7},{6,4},{7,5},{8,10},{9,11},{10,... | collective-permute-start | bytes 1572872 | tf_op jit(solution)/shard_map/ppermute | solution.py:39
  114.3 9.1 %collective-permute-start.21 = (bf16[4,128,256]{2,1,0:T(8,128)(2,1)S(1)}, bf16[4,128,256]{2,1,0:T(8,128)(2,1)S(1)}, u32[]{:S(2)}, u32[]{:S(2)}) collective-permute-start(bf16[4,128,256]{2,1,0:T(8,128)(2,1)S(1)} %get-tuple-element.88), channel_id=1, source_target_pairs={{0,4},{1,5},{2,6},{3,7},{4,8},{5,9},{6,10},{7,11},{8,12},{9,13},{1... | collective-permute-start | bytes 786440 | tf_op jit(solution)/shard_map/ppermute | solution.py:39
  115.8 15.1 %collective-permute-start.16 = (bf16[4,128,256]{2,1,0:T(8,128)(2,1)}, bf16[4,128,256]{2,1,0:T(8,128)(2,1)S(1)}, u32[]{:S(2)}, u32[]{:S(2)}) collective-permute-start(bf16[4,128,256]{2,1,0:T(8,128)(2,1)} %get-tuple-element.77), channel_id=1, source_target_pairs={{0,1},{1,2},{2,3},{3,0},{4,5},{5,6},{6,7},{7,4},{8,9},{9,10},{10,1... | collective-permute-start | bytes 786440 | tf_op jit(solution)/shard_map/ppermute | solution.py:39
  115.8 15.1 %collective-permute-start.17 = (bf16[4,128,256]{2,1,0:T(8,128)(2,1)S(1)}, bf16[4,128,256]{2,1,0:T(8,128)(2,1)S(1)}, u32[]{:S(2)}, u32[]{:S(2)}) collective-permute-start(bf16[4,128,256]{2,1,0:T(8,128)(2,1)S(1)} %get-tuple-element.78), channel_id=1, source_target_pairs={{0,2},{1,3},{2,0},{3,1},{4,6},{5,7},{6,4},{7,5},{8,10},{9,11},{10,... | collective-permute-start | bytes 786440 | tf_op jit(solution)/shard_map/ppermute | solution.py:39
  118.3 13.0 %collective-permute-start.18 = (bf16[4,128,256]{2,1,0:T(8,128)(2,1)S(1)}, bf16[4,128,256]{2,1,0:T(8,128)(2,1)S(1)}, u32[]{:S(2)}, u32[]{:S(2)}) collective-permute-start(bf16[4,128,256]{2,1,0:T(8,128)(2,1)S(1)} %get-tuple-element.79), channel_id=1, source_target_pairs={{0,3},{1,0},{2,1},{3,2},{4,7},{5,4},{6,5},{7,6},{8,11},{9,8},{10,9... | collective-permute-start | bytes 786440 | tf_op jit(solution)/shard_map/ppermute | solution.py:39
  120.2 11.2 %collective-permute-start.23 = (bf16[4,128,256]{2,1,0:T(8,128)(2,1)}, bf16[4,128,256]{2,1,0:T(8,128)(2,1)S(1)}, u32[]{:S(2)}, u32[]{:S(2)}) collective-permute-start(bf16[4,128,256]{2,1,0:T(8,128)(2,1)} %get-tuple-element.91), channel_id=1, source_target_pairs={{0,12},{1,13},{2,14},{3,15},{4,0},{5,1},{6,2},{7,3},{8,4},{9,5},{1... | collective-permute-start | bytes 786440 | tf_op jit(solution)/shard_map/ppermute | solution.py:39
  123.5 11.4 %collective-permute-start.22 = (bf16[4,128,256]{2,1,0:T(8,128)(2,1)S(1)}, bf16[4,128,256]{2,1,0:T(8,128)(2,1)S(1)}, u32[]{:S(2)}, u32[]{:S(2)}) collective-permute-start(bf16[4,128,256]{2,1,0:T(8,128)(2,1)S(1)} %get-tuple-element.90), channel_id=1, source_target_pairs={{0,8},{1,9},{2,10},{3,11},{4,12},{5,13},{6,14},{7,15},{8,0},{9,1},... | collective-permute-start | bytes 786440 | tf_op jit(solution)/shard_map/ppermute | solution.py:39
  (7 other events, 35.1 us)

commit v11 on v10

--- a/solution.py
+++ b/solution.py
@@ -228,23 +228,15 @@
 
 
 def spread_body(across, add_ref, *refs):
-    outs, (pool, sems) = refs[4:8], refs[8:]
-    most, owned = refs[0].shape[0], outs[0].shape[0]
-    copies = [
-        pltpu.make_async_copy(ref, pool.at[pl.ds(k * most, most)], sems.at[k])
-        for k, ref in enumerate(refs[:4])
-    ]
-    for copy in copies:
-        copy.start()
-    for copy in copies:
-        copy.wait()
+    chunks, outs = refs[:4], refs[4:8]
+    owned = outs[0].shape[0]
 
     def add(n, carry):
         for distance, out in enumerate(outs):
             value = jnp.zeros(out.shape[1:], F32)
-            for k in range(SIDE):
+            for k, chunk in enumerate(chunks):
                 index = add_ref[across, (distance * owned + n) * SIDE + k]
-                term = pool[k * most + jnp.maximum(index, 0)].astype(F32)
+                term = chunk[jnp.maximum(index, 0)].astype(F32)
                 value += jnp.where(index >= 0, term, 0.0)
             out[n] = value.astype(out.dtype)
         return carry
@@ -261,17 +253,13 @@
     return pl.pallas_call(
         functools.partial(spread_body, across),
         out_shape=chunk_shapes(owned, nbr, width, F32),
-        in_specs=[SMEM] + [HBM] * 4,
+        in_specs=[SMEM] + [VMEM] * 4,
         out_specs=(VMEM,) * 4,
-        scratch_shapes=[
-            pltpu.VMEM((SIDE * most, nbr, width), BF16),
-            pltpu.SemaphoreType.DMA((SIDE,)),
-        ],
         compiler_params=pltpu.CompilerParams(vmem_limit_bytes=SPREAD_VMEM),
         cost_estimate=pl.CostEstimate(
             flops=SPREAD_FLOPS, bytes_accessed=2 * 1024 * 1024, transcendentals=0
         ),
-    )(add, *in_hbm(chunks))
+    )(add, *chunks)
 
 
 def attend_body(

time: 137 us -> 133 us (0.971)
  Pallas kernels: 32.8 us -> 29.7 us
    pallas_call x2, Pallas kernels: 7.14 us -> 4.01 us  [spread(): pl.pallas_call(functools.partial(spread_body, across), out_shape=chunk_sh...]
  transfers between devices with their start and end apart: 26 -> 26, of which waited for: 14 -> 14; matrix products, arithmetic and copies ran while one was open for 0% -> 0% of each run, Pallas kernels for 13% -> 11%
where the time goes in v11:
time: 133 us; the launch traced here: 132 us
  starting transfers between devices  55.8 us (42%)
  waiting for transfers between devices  43.7 us (33%)
  Pallas kernels  29.7 us (22%)
  local copies, waits for them, and re-layouts  1.67 us (1%)
    ppermute x24, waiting for transfers between devices, shift(): return lax.ppermute(value, 'dp', pairs)  43.7 us
    ppermute x24, starting transfers between devices, shift(): return lax.ppermute(value, 'dp', pairs)  40.4 us
    pallas_call x1, Pallas kernels, attend(): pl.pallas_call(functools.partial(attend_body, groups, distinct, owned, mo...  12 us
    all_to_all x1, starting transfers between devices, on_device(): lax.all_to_all(packed, 'ctx', split_axis=0, concat_axis=0, tiled=True)  8.71 us
    all_to_all x1, starting transfers between devices, on_device(): back = lax.all_to_all(back, 'ctx', split_axis=0, concat_axis=0, tiled=True)  6.69 us
    pallas_call x2, Pallas kernels, spread(): pl.pallas_call(functools.partial(spread_body, across), out_shape=chunk_sh...  4.01 us
    pallas_call x1, Pallas kernels, tables(): pl.pallas_call(functools.partial(tables_body, owned, most), out_shape=(ja...  3.94 us
    pallas_call x1, Pallas kernels, select(): pl.pallas_call(select_body, out_shape=tuple((pltpu.HBM(shape.shape, shape...  3.75 us
  transfers between devices with their start and end apart: 26, of which 14 were waited for; matrix products, arithmetic and copies ran while one was open for 0% of the time, Pallas kernels for 11%

profile of v11, /device:TPU:8, one launch (start us, length us, event | category | flops | bytes accessed | tf_op | source)
XLA Modules:
  0.0 131.7 jit_solution(11802968012394052049)
XLA Ops:
  0.6 2.7 %shard_map.85 = bf16[16,2,128,256]{3,2,1,0:T(8,128)(2,1)} custom-call(bf16[128,4096]{1,0:T(8,128)(2,1)} %bitcast.5, bf16[128,4096]{1,0:T(8,128)(2,1)} %bitcast.6), custom_call_target="tpu_custom_call" | custom-call | tf_op jit(solution)/shard_map/pallas_call | solution.py:87
  3.4 8.7 %all-to-all-start = ((bf16[16,2,128,256]{3,2,1,0:T(8,128)(2,1)}), bf16[16,2,128,256]{3,2,1,0:T(8,128)(2,1)S(1)}, u32[]{:S(2)}, u32[]{:S(2)}) async-start(bf16[16,2,128,256]{3,2,1,0:T(8,128)(2,1)} %shard_map.85), calls=%async_computation | async-start | bytes 4194304 | tf_op jit(solution)/shard_map/all_to_all | solution.py:449
  12.7 3.0 %collective-permute-start.1 = (bf16[4,128,256]{2,1,0:T(8,128)(2,1)S(1)}, bf16[4,128,256]{2,1,0:T(8,128)(2,1)S(1)}, u32[]{:S(2)}, u32[]{:S(2)}) collective-permute-start(bf16[4,128,256]{2,1,0:T(8,128)(2,1)S(1)} %copy-done), channel_id=1, source_target_pairs={{0,2},{1,3},{2,0},{3,1},{4,6},{5,7},{6,4},{7,5},{8,10},{9,11},{10,... | collective-permute-start | bytes 786440 | tf_op jit(solution)/shard_map/ppermute | solution.py:39
  17.7 1.6 %collective-permute-start.5 = (bf16[4,128,256]{2,1,0:T(8,128)(2,1)S(1)}, bf16[4,128,256]{2,1,0:T(8,128)(2,1)}, u32[]{:S(2)}, u32[]{:S(2)}) collective-permute-start(bf16[4,128,256]{2,1,0:T(8,128)(2,1)S(1)} %copy-done.1), channel_id=1, source_target_pairs={{0,4},{1,5},{2,6},{3,7},{4,8},{5,9},{6,10},{7,11},{8,12},{9,13},{1... | collective-permute-start | bytes 786440 | tf_op jit(solution)/shard_map/ppermute | solution.py:39
  20.9 3.5 %collective-permute-start.4 = (bf16[4,128,256]{2,1,0:T(8,128)(2,1)S(1)}, bf16[4,128,256]{2,1,0:T(8,128)(2,1)}, u32[]{:S(2)}, u32[]{:S(2)}) collective-permute-start(bf16[4,128,256]{2,1,0:T(8,128)(2,1)S(1)} %copy-done.1), channel_id=1, source_target_pairs={{0,8},{1,9},{2,10},{3,11},{4,12},{5,13},{6,14},{7,15},{8,0},{9,1},... | collective-permute-start | bytes 786440 | tf_op jit(solution)/shard_map/ppermute | solution.py:39
  24.4 3.9 %shard_map.86 = (s32[2,32]{1,0:T(2,128)}, s32[2,64]{1,0:T(2,128)}) custom-call(s32[16,16]{1,0:T(8,128)} %ids_ref.3), custom_call_target="tpu_custom_call" | custom-call | tf_op jit(solution)/shard_map/pallas_call | solution.py:167
  28.4 2.2 %collective-permute-done.4.refs_6_ = bf16[4,128,256]{2,1,0:T(8,128)(2,1)} collective-permute-done((bf16[4,128,256]{2,1,0:T(8,128)(2,1)S(1)}, bf16[4,128,256]{2,1,0:T(8,128)(2,1)}, u32[]{:S(2)}, u32[]{:S(2)}) %collective-permute-start.4) | collective-permute-done | bytes 262176 | tf_op jit(solution)/shard_map/ppermute | solution.py:39
  31.3 3.7 %shard_map.87 = (bf16[8,128,256]{2,1,0:T(8,128)(2,1)}, bf16[8,128,256]{2,1,0:T(8,128)(2,1)}, bf16[8,128,256]{2,1,0:T(8,128)(2,1)}, bf16[8,128,256]{2,1,0:T(8,128...) custom-call(s32[2,32]{1,0:T(2,128)S(1)} %copy-done.3, ...), custom_call_target="tpu_custom_call" | custom-call | tf_op jit(solution)/shard_map/pallas_call | solution.py:212
  35.0 1.6 %collective-permute-start.9 = (bf16[8,128,256]{2,1,0:T(8,128)(2,1)}, bf16[8,128,256]{2,1,0:T(8,128)(2,1)S(1)}, u32[]{:S(2)}, u32[]{:S(2)}) collective-permute-start(bf16[8,128,256]{2,1,0:T(8,128)(2,1)} %get-tuple-element.62), channel_id=1, source_target_pairs={{0,1},{1,2},{2,3},{3,0},{4,5},{5,6},{6,7},{7,4},{8,9},{9,10},{10,1... | collective-permute-start | bytes 1572872 | tf_op jit(solution)/shard_map/ppermute | solution.py:39
  36.6 2.2 %collective-permute-start.6 = (bf16[8,128,256]{2,1,0:T(8,128)(2,1)}, bf16[8,128,256]{2,1,0:T(8,128)(2,1)S(1)}, u32[]{:S(2)}, u32[]{:S(2)}) collective-permute-start(bf16[8,128,256]{2,1,0:T(8,128)(2,1)} %get-tuple-element.57), channel_id=1, source_target_pairs={{0,4},{1,5},{2,6},{3,7},{4,8},{5,9},{6,10},{7,11},{8,12},{9,13},{1... | collective-permute-start | bytes 1572872 | tf_op jit(solution)/shard_map/ppermute | solution.py:39
  38.8 3.6 %collective-permute-start.7 = (bf16[8,128,256]{2,1,0:T(8,128)(2,1)}, bf16[8,128,256]{2,1,0:T(8,128)(2,1)}, u32[]{:S(2)}, u32[]{:S(2)}) collective-permute-start(bf16[8,128,256]{2,1,0:T(8,128)(2,1)} %get-tuple-element.58), channel_id=1, source_target_pairs={{0,8},{1,9},{2,10},{3,11},{4,12},{5,13},{6,14},{7,15},{8,0},{9,1},... | collective-permute-start | bytes 1572872 | tf_op jit(solution)/shard_map/ppermute | solution.py:39
  42.5 2.6 %collective-permute-start.11 = (bf16[8,128,256]{2,1,0:T(8,128)(2,1)}, bf16[8,128,256]{2,1,0:T(8,128)(2,1)}, u32[]{:S(2)}, u32[]{:S(2)}) collective-permute-start(bf16[8,128,256]{2,1,0:T(8,128)(2,1)} %get-tuple-element.65), channel_id=1, source_target_pairs={{0,3},{1,0},{2,1},{3,2},{4,7},{5,4},{6,5},{7,6},{8,11},{9,8},{10,9... | collective-permute-start | bytes 1572872 | tf_op jit(solution)/shard_map/ppermute | solution.py:39
  45.0 4.4 %collective-permute-done.9.refs_5_ = bf16[8,128,256]{2,1,0:T(8,128)(2,1)S(1)} collective-permute-done((bf16[8,128,256]{2,1,0:T(8,128)(2,1)}, bf16[8,128,256]{2,1,0:T(8,128)(2,1)S(1)}, u32[]{:S(2)}, u32[]{:S(2)}) %collective-permute-start.9) | collective-permute-done | bytes 524320 | tf_op jit(solution)/shard_map/ppermute | solution.py:39
  49.4 1.8 %collective-permute-start.10 = (bf16[8,128,256]{2,1,0:T(8,128)(2,1)}, bf16[8,128,256]{2,1,0:T(8,128)(2,1)}, u32[]{:S(2)}, u32[]{:S(2)}) collective-permute-start(bf16[8,128,256]{2,1,0:T(8,128)(2,1)} %get-tuple-element.64), channel_id=1, source_target_pairs={{0,2},{1,3},{2,0},{3,1},{4,6},{5,7},{6,4},{7,5},{8,10},{9,11},{10,... | collective-permute-start | bytes 1572872 | tf_op jit(solution)/shard_map/ppermute | solution.py:39
  51.3 9.4 %collective-permute-done.6.refs_1_ = bf16[8,128,256]{2,1,0:T(8,128)(2,1)S(1)} collective-permute-done((bf16[8,128,256]{2,1,0:T(8,128)(2,1)}, bf16[8,128,256]{2,1,0:T(8,128)(2,1)S(1)}, u32[]{:S(2)}, u32[]{:S(2)}) %collective-permute-start.6) | collective-permute-done | bytes 524320 | tf_op jit(solution)/shard_map/ppermute | solution.py:39
  60.7 3.6 %collective-permute-done.8.refs_3_ = bf16[8,128,256]{2,1,0:T(8,128)(2,1)} collective-permute-done((bf16[8,128,256]{2,1,0:T(8,128)(2,1)}, bf16[8,128,256]{2,1,0:T(8,128)(2,1)}, u32[]{:S(2)}, u32[]{:S(2)}) %collective-permute-start.8) | collective-permute-done | bytes 524320 | tf_op jit(solution)/shard_map/ppermute | solution.py:39
  64.8 12.0 %shard_map.88 = (bf16[16,128,256]{2,1,0:T(8,128)(2,1)}, bf16[8,128,256]{2,1,0:T(8,128)(2,1)}, bf16[8,128,256]{2,1,0:T(8,128)(2,1)}, bf16[8,128,256]{2,1,0:T(8,12...) custom-call(s32[16,16]{1,0:T(8,128)S(1)} %copy-done.2, ...), custom_call_target="tpu_custom_call" | custom-call | tf_op jit(solution)/shard_map/pallas_call | solution.py:406
  76.8 3.1 %collective-permute-start.12 = (bf16[8,128,256]{2,1,0:T(8,128)(2,1)}, bf16[8,128,256]{2,1,0:T(8,128)(2,1)S(1)}, u32[]{:S(2)}, u32[]{:S(2)}) collective-permute-start(bf16[8,128,256]{2,1,0:T(8,128)(2,1)} %get-tuple-element.69), channel_id=1, source_target_pairs={{0,1},{1,2},{2,3},{3,0},{4,5},{5,6},{6,7},{7,4},{8,9},{9,10},{10,1... | collective-permute-start | bytes 1572872 | tf_op jit(solution)/shard_map/ppermute | solution.py:39
  80.8 1.9 %collective-permute-start.13 = (bf16[8,128,256]{2,1,0:T(8,128)(2,1)}, bf16[8,128,256]{2,1,0:T(8,128)(2,1)S(1)}, u32[]{:S(2)}, u32[]{:S(2)}) collective-permute-start(bf16[8,128,256]{2,1,0:T(8,128)(2,1)} %get-tuple-element.71), channel_id=1, source_target_pairs={{0,12},{1,13},{2,14},{3,15},{4,0},{5,1},{6,2},{7,3},{8,4},{9,5},{1... | collective-permute-start | bytes 1572872 | tf_op jit(solution)/shard_map/ppermute | solution.py:39
  84.5 6.7 %all-to-all-start.1 = ((bf16[16,128,256]{2,1,0:T(8,128)(2,1)}), bf16[16,128,256]{2,1,0:T(8,128)(2,1)}, u32[]{:S(2)}, u32[]{:S(2)}) async-start(bf16[16,128,256]{2,1,0:T(8,128)(2,1)} %get-tuple-element.66), calls=%async_computation.1 | async-start | bytes 2097152 | tf_op jit(solution)/shard_map/all_to_all | solution.py:454
  92.6 1.7 %collective-permute-start.20 = (bf16[8,128,256]{2,1,0:T(8,128)(2,1)}, bf16[8,128,256]{2,1,0:T(8,128)(2,1)}, u32[]{:S(2)}, u32[]{:S(2)}) collective-permute-start(bf16[8,128,256]{2,1,0:T(8,128)(2,1)} %get-tuple-element.84), channel_id=1, source_target_pairs={{0,2},{1,3},{2,0},{3,1},{4,6},{5,7},{6,4},{7,5},{8,10},{9,11},{10,... | collective-permute-start | bytes 1572872 | tf_op jit(solution)/shard_map/ppermute | solution.py:39
  94.3 2.3 %collective-permute-done.13.refs_1_ = bf16[8,128,256]{2,1,0:T(8,128)(2,1)S(1)} collective-permute-done((bf16[8,128,256]{2,1,0:T(8,128)(2,1)}, bf16[8,128,256]{2,1,0:T(8,128)(2,1)S(1)}, u32[]{:S(2)}, u32[]{:S(2)}) %collective-permute-start.13) | collective-permute-done | bytes 524320 | tf_op jit(solution)/shard_map/ppermute | solution.py:39
  96.6 8.1 %collective-permute-done.14.refs_2_ = bf16[8,128,256]{2,1,0:T(8,128)(2,1)S(1)} collective-permute-done((bf16[8,128,256]{2,1,0:T(8,128)(2,1)}, bf16[8,128,256]{2,1,0:T(8,128)(2,1)S(1)}, u32[]{:S(2)}, u32[]{:S(2)}) %collective-permute-start.14) | collective-permute-done | bytes 524320 | tf_op jit(solution)/shard_map/ppermute | solution.py:39
  104.7 1.7 %collective-permute-done.15.refs_3_ = bf16[8,128,256]{2,1,0:T(8,128)(2,1)S(1)} collective-permute-done((bf16[8,128,256]{2,1,0:T(8,128)(2,1)}, bf16[8,128,256]{2,1,0:T(8,128)(2,1)S(1)}, u32[]{:S(2)}, u32[]{:S(2)}) %collective-permute-start.15) | collective-permute-done | bytes 524320 | tf_op jit(solution)/shard_map/ppermute | solution.py:39
  106.4 2.1 %shard_map.90 = (f32[4,128,256]{2,1,0:T(8,128)S(1)}, bf16[4,128,256]{2,1,0:T(8,128)(2,1)}, bf16[4,128,256]{2,1,0:T(8,128)(2,1)}, bf16[4,128,256]{2,1,0:T(8,128)(2,1)S(1)}) custom-call(s32[2,64]{1,0:T(2,128)S(1)} %copy-done.8, bf16[8,128,256]{2,1,0:T(8,128)(2,1)S(1)} %copy-done.5, bf16[8,128,256]{2,1,0:T(8,128)(2,1)S(1)} %collective-permute-done.13.refs_1_, ...), custom_call_target="tpu_custom_call" | custom-call | flops 199999995904 | bytes 2097152 | tf_op jit(solution)/shard_map/pallas_call | solution.py:253
  108.5 1.9 %shard_map.91 = (f32[4,128,256]{2,1,0:T(8,128)S(1)}, bf16[4,128,256]{2,1,0:T(8,128)(2,1)S(1)}, bf16[4,128,256]{2,1,0:T(8,128)(2,1)S(1)}, bf16[4,128,256]{2,1,0:T(8,128)(2,1)S(1)}) custom-call(s32[2,64]{1,0:T(2,128)S(1)} %copy-done.8, bf16[8,128,256]{2,1,0:T(8,128)(2,1)S(1)} %copy-done.4, bf16[8,128,256]{2,1,0:T(8,128)(2,1)S(1)} %collective-permute-done.19.refs_1_, ...), custom_call_target="tpu_custom_call" | custom-call | flops 199999995904 | bytes 2097152 | tf_op jit(solution)/shard_map/pallas_call | solution.py:253
  110.4 1.9 %collective-permute-start.21 = (bf16[4,128,256]{2,1,0:T(8,128)(2,1)S(1)}, bf16[4,128,256]{2,1,0:T(8,128)(2,1)S(1)}, u32[]{:S(2)}, u32[]{:S(2)}) collective-permute-start(bf16[4,128,256]{2,1,0:T(8,128)(2,1)S(1)} %get-tuple-element.88), channel_id=1, source_target_pairs={{0,4},{1,5},{2,6},{3,7},{4,8},{5,9},{6,10},{7,11},{8,12},{9,13},{1... | collective-permute-start | bytes 786440 | tf_op jit(solution)/shard_map/ppermute | solution.py:39
  113.1 2.6 %collective-permute-start.17 = (bf16[4,128,256]{2,1,0:T(8,128)(2,1)}, bf16[4,128,256]{2,1,0:T(8,128)(2,1)S(1)}, u32[]{:S(2)}, u32[]{:S(2)}) collective-permute-start(bf16[4,128,256]{2,1,0:T(8,128)(2,1)} %get-tuple-element.78), channel_id=1, source_target_pairs={{0,2},{1,3},{2,0},{3,1},{4,6},{5,7},{6,4},{7,5},{8,10},{9,11},{10,... | collective-permute-start | bytes 786440 | tf_op jit(solution)/shard_map/ppermute | solution.py:39
  117.7 1.9 %collective-permute-done.21.refs_5_ = bf16[4,128,256]{2,1,0:T(8,128)(2,1)S(1)} collective-permute-done((bf16[4,128,256]{2,1,0:T(8,128)(2,1)S(1)}, bf16[4,128,256]{2,1,0:T(8,128)(2,1)S(1)}, u32[]{:S(2)}, u32[]{:S(2)}) %collective-permute-start.21) | collective-permute-done | bytes 262176 | tf_op jit(solution)/shard_map/ppermute | solution.py:39
  120.8 2.3 %shard_map.89 = bf16[128,4096]{1,0:T(8,128)(2,1)} custom-call(bf16[16,128,256]{2,1,0:T(8,128)(2,1)} %all-to-all-done.1.in_ref), custom_call_target="tpu_custom_call" | custom-call | tf_op jit(solution)/shard_map/pallas_call | solution.py:113
  123.2 3.8 %collective-permute-done.17.refs_2_ = bf16[4,128,256]{2,1,0:T(8,128)(2,1)S(1)} collective-permute-done((bf16[4,128,256]{2,1,0:T(8,128)(2,1)}, bf16[4,128,256]{2,1,0:T(8,128)(2,1)S(1)}, u32[]{:S(2)}, u32[]{:S(2)}) %collective-permute-start.17) | collective-permute-done | bytes 262176 | tf_op jit(solution)/shard_map/ppermute | solution.py:39
  127.6 3.1 %collective-permute-done.22.refs_6_ = bf16[4,128,256]{2,1,0:T(8,128)(2,1)S(1)} collective-permute-done((bf16[4,128,256]{2,1,0:T(8,128)(2,1)S(1)}, bf16[4,128,256]{2,1,0:T(8,128)(2,1)S(1)}, u32[]{:S(2)}, u32[]{:S(2)}) %collective-permute-start.22) | collective-permute-done | bytes 262176 | tf_op jit(solution)/shard_map/ppermute | solution.py:39
  (54 shorter events, 15.3 us)
Async XLA Ops:
  3.4 9.3 %copy-start = (bf16[4,128,256]{2,1,0:T(8,128)(2,1)S(1)}, bf16[4,128,256]{2,1,0:T(8,128)(2,1)}, u32[]{:S(2)}) copy-start(bf16[4,128,256]{2,1,0:T(8,128)(2,1)} %refs_0_.1) | copy-start | bytes 786436
  3.4 47.8 %copy-start.11 = (s32[16,32,2]{1,2,0:T(2,128)S(1)}, s32[16,32,2]{1,2,0:T(2,128)}, u32[]{:S(2)}) copy-start(s32[16,32,2]{1,2,0:T(2,128)} %param.11) | copy-start | bytes 12292
  3.4 61.4 %all-to-all-start = ((bf16[16,2,128,256]{3,2,1,0:T(8,128)(2,1)}), bf16[16,2,128,256]{3,2,1,0:T(8,128)(2,1)S(1)}, u32[]{:S(2)}, u32[]{:S(2)}) async-start(bf16[16,2,128,256]{3,2,1,0:T(8,128)(2,1)} %shard_map.85), calls=%async_computation | async-start | bytes 4194304 | tf_op jit(solution)/shard_map/all_to_all | solution.py:449
  12.1 52.6 %copy-start.2 = (s32[16,16]{1,0:T(8,128)S(1)}, s32[16,16]{1,0:T(8,128)}, u32[]{:S(2)}) copy-start(s32[16,16]{1,0:T(8,128)} %ids_ref.3) | copy-start | bytes 3076
  12.1 8.7 %collective-permute-start.3 = (bf16[4,128,256]{2,1,0:T(8,128)(2,1)S(1)}, bf16[4,128,256]{2,1,0:T(8,128)(2,1)S(1)}, u32[]{:S(2)}, u32[]{:S(2)}) collective-permute-start(bf16[4,128,256]{2,1,0:T(8,128)(2,1)S(1)} %copy-done.1), channel_id=1, source_target_pairs={{0,12},{1,13},{2,14},{3,15},{4,0},{5,1},{6,2},{7,3},{8,4},{9,5},{1... | collective-permute-start | bytes 786440 | tf_op jit(solution)/shard_map/ppermute | solution.py:39
  12.7 15.6 %collective-permute-start.1 = (bf16[4,128,256]{2,1,0:T(8,128)(2,1)S(1)}, bf16[4,128,256]{2,1,0:T(8,128)(2,1)S(1)}, u32[]{:S(2)}, u32[]{:S(2)}) collective-permute-start(bf16[4,128,256]{2,1,0:T(8,128)(2,1)S(1)} %copy-done), channel_id=1, source_target_pairs={{0,2},{1,3},{2,0},{3,1},{4,6},{5,7},{6,4},{7,5},{8,10},{9,11},{10,... | collective-permute-start | bytes 786440 | tf_op jit(solution)/shard_map/ppermute | solution.py:39
  15.7 12.6 %collective-permute-start = (bf16[4,128,256]{2,1,0:T(8,128)(2,1)S(1)}, bf16[4,128,256]{2,1,0:T(8,128)(2,1)S(1)}, u32[]{:S(2)}, u32[]{:S(2)}) collective-permute-start(bf16[4,128,256]{2,1,0:T(8,128)(2,1)S(1)} %copy-done), channel_id=1, source_target_pairs={{0,3},{1,0},{2,1},{3,2},{4,7},{5,4},{6,5},{7,6},{8,11},{9,8},{10,9... | collective-permute-start | bytes 786440 | tf_op jit(solution)/shard_map/ppermute | solution.py:39
  16.8 11.5 %collective-permute-start.2 = (bf16[4,128,256]{2,1,0:T(8,128)(2,1)S(1)}, bf16[4,128,256]{2,1,0:T(8,128)(2,1)}, u32[]{:S(2)}, u32[]{:S(2)}) collective-permute-start(bf16[4,128,256]{2,1,0:T(8,128)(2,1)S(1)} %copy-done), channel_id=1, source_target_pairs={{0,1},{1,2},{2,3},{3,0},{4,5},{5,6},{6,7},{7,4},{8,9},{9,10},{10,1... | collective-permute-start | bytes 786440 | tf_op jit(solution)/shard_map/ppermute | solution.py:39
  17.7 10.6 %collective-permute-start.5 = (bf16[4,128,256]{2,1,0:T(8,128)(2,1)S(1)}, bf16[4,128,256]{2,1,0:T(8,128)(2,1)}, u32[]{:S(2)}, u32[]{:S(2)}) collective-permute-start(bf16[4,128,256]{2,1,0:T(8,128)(2,1)S(1)} %copy-done.1), channel_id=1, source_target_pairs={{0,4},{1,5},{2,6},{3,7},{4,8},{5,9},{6,10},{7,11},{8,12},{9,13},{1... | collective-permute-start | bytes 786440 | tf_op jit(solution)/shard_map/ppermute | solution.py:39
  20.9 9.7 %collective-permute-start.4 = (bf16[4,128,256]{2,1,0:T(8,128)(2,1)S(1)}, bf16[4,128,256]{2,1,0:T(8,128)(2,1)}, u32[]{:S(2)}, u32[]{:S(2)}) collective-permute-start(bf16[4,128,256]{2,1,0:T(8,128)(2,1)S(1)} %copy-done.1), channel_id=1, source_target_pairs={{0,8},{1,9},{2,10},{3,11},{4,12},{5,13},{6,14},{7,15},{8,0},{9,1},... | collective-permute-start | bytes 786440 | tf_op jit(solution)/shard_map/ppermute | solution.py:39
  35.0 14.4 %collective-permute-start.9 = (bf16[8,128,256]{2,1,0:T(8,128)(2,1)}, bf16[8,128,256]{2,1,0:T(8,128)(2,1)S(1)}, u32[]{:S(2)}, u32[]{:S(2)}) collective-permute-start(bf16[8,128,256]{2,1,0:T(8,128)(2,1)} %get-tuple-element.62), channel_id=1, source_target_pairs={{0,1},{1,2},{2,3},{3,0},{4,5},{5,6},{6,7},{7,4},{8,9},{9,10},{10,1... | collective-permute-start | bytes 1572872 | tf_op jit(solution)/shard_map/ppermute | solution.py:39
  36.6 24.1 %collective-permute-start.6 = (bf16[8,128,256]{2,1,0:T(8,128)(2,1)}, bf16[8,128,256]{2,1,0:T(8,128)(2,1)S(1)}, u32[]{:S(2)}, u32[]{:S(2)}) collective-permute-start(bf16[8,128,256]{2,1,0:T(8,128)(2,1)} %get-tuple-element.57), channel_id=1, source_target_pairs={{0,4},{1,5},{2,6},{3,7},{4,8},{5,9},{6,10},{7,11},{8,12},{9,13},{1... | collective-permute-start | bytes 1572872 | tf_op jit(solution)/shard_map/ppermute | solution.py:39
  38.8 21.9 %collective-permute-start.7 = (bf16[8,128,256]{2,1,0:T(8,128)(2,1)}, bf16[8,128,256]{2,1,0:T(8,128)(2,1)}, u32[]{:S(2)}, u32[]{:S(2)}) collective-permute-start(bf16[8,128,256]{2,1,0:T(8,128)(2,1)} %get-tuple-element.58), channel_id=1, source_target_pairs={{0,8},{1,9},{2,10},{3,11},{4,12},{5,13},{6,14},{7,15},{8,0},{9,1},... | collective-permute-start | bytes 1572872 | tf_op jit(solution)/shard_map/ppermute | solution.py:39
  42.4 21.9 %collective-permute-start.8 = (bf16[8,128,256]{2,1,0:T(8,128)(2,1)}, bf16[8,128,256]{2,1,0:T(8,128)(2,1)}, u32[]{:S(2)}, u32[]{:S(2)}) collective-permute-start(bf16[8,128,256]{2,1,0:T(8,128)(2,1)} %get-tuple-element.59), channel_id=1, source_target_pairs={{0,12},{1,13},{2,14},{3,15},{4,0},{5,1},{6,2},{7,3},{8,4},{9,5},{1... | collective-permute-start | bytes 1572872 | tf_op jit(solution)/shard_map/ppermute | solution.py:39
  42.5 22.3 %collective-permute-start.11 = (bf16[8,128,256]{2,1,0:T(8,128)(2,1)}, bf16[8,128,256]{2,1,0:T(8,128)(2,1)}, u32[]{:S(2)}, u32[]{:S(2)}) collective-permute-start(bf16[8,128,256]{2,1,0:T(8,128)(2,1)} %get-tuple-element.65), channel_id=1, source_target_pairs={{0,3},{1,0},{2,1},{3,2},{4,7},{5,4},{6,5},{7,6},{8,11},{9,8},{10,9... | collective-permute-start | bytes 1572872 | tf_op jit(solution)/shard_map/ppermute | solution.py:39
  49.4 15.4 %copy-start.9 = (bf16[8,128,256]{2,1,0:T(8,128)(2,1)}, bf16[8,128,256]{2,1,0:T(8,128)(2,1)S(1)}, u32[]{:S(2)}) copy-start(bf16[8,128,256]{2,1,0:T(8,128)(2,1)S(1)} %collective-permute-done.9.refs_5_) | copy-start | bytes 1572868
  49.4 15.4 %collective-permute-start.10 = (bf16[8,128,256]{2,1,0:T(8,128)(2,1)}, bf16[8,128,256]{2,1,0:T(8,128)(2,1)}, u32[]{:S(2)}, u32[]{:S(2)}) collective-permute-start(bf16[8,128,256]{2,1,0:T(8,128)(2,1)} %get-tuple-element.64), channel_id=1, source_target_pairs={{0,2},{1,3},{2,0},{3,1},{4,6},{5,7},{6,4},{7,5},{8,10},{9,11},{10,... | collective-permute-start | bytes 1572872 | tf_op jit(solution)/shard_map/ppermute | solution.py:39
  76.8 29.6 %copy-start.5 = (bf16[8,128,256]{2,1,0:T(8,128)(2,1)S(1)}, bf16[8,128,256]{2,1,0:T(8,128)(2,1)}, u32[]{:S(2)}) copy-start(bf16[8,128,256]{2,1,0:T(8,128)(2,1)} %get-tuple-element.70.refs_0_) | copy-start | bytes 1572868
  76.8 29.5 %copy-start.8 = (s32[2,64]{1,0:T(2,128)S(1)}, s32[2,64]{1,0:T(2,128)}, u32[]{:S(2)}) copy-start(s32[2,64]{1,0:T(2,128)} %get-tuple-element.67.add_ref) | copy-start | bytes 1540
  76.8 15.0 %collective-permute-start.12 = (bf16[8,128,256]{2,1,0:T(8,128)(2,1)}, bf16[8,128,256]{2,1,0:T(8,128)(2,1)S(1)}, u32[]{:S(2)}, u32[]{:S(2)}) collective-permute-start(bf16[8,128,256]{2,1,0:T(8,128)(2,1)} %get-tuple-element.69), channel_id=1, source_target_pairs={{0,1},{1,2},{2,3},{3,0},{4,5},{5,6},{6,7},{7,4},{8,9},{9,10},{10,1... | collective-permute-start | bytes 1572872 | tf_op jit(solution)/shard_map/ppermute | solution.py:39
  79.9 12.7 %collective-permute-start.19 = (bf16[8,128,256]{2,1,0:T(8,128)(2,1)}, bf16[8,128,256]{2,1,0:T(8,128)(2,1)S(1)}, u32[]{:S(2)}, u32[]{:S(2)}) collective-permute-start(bf16[8,128,256]{2,1,0:T(8,128)(2,1)} %get-tuple-element.82), channel_id=1, source_target_pairs={{0,3},{1,0},{2,1},{3,2},{4,7},{5,4},{6,5},{7,6},{8,11},{9,8},{10,9... | collective-permute-start | bytes 1572872 | tf_op jit(solution)/shard_map/ppermute | solution.py:39
  80.8 15.8 %collective-permute-start.13 = (bf16[8,128,256]{2,1,0:T(8,128)(2,1)}, bf16[8,128,256]{2,1,0:T(8,128)(2,1)S(1)}, u32[]{:S(2)}, u32[]{:S(2)}) collective-permute-start(bf16[8,128,256]{2,1,0:T(8,128)(2,1)} %get-tuple-element.71), channel_id=1, source_target_pairs={{0,12},{1,13},{2,14},{3,15},{4,0},{5,1},{6,2},{7,3},{8,4},{9,5},{1... | collective-permute-start | bytes 1572872 | tf_op jit(solution)/shard_map/ppermute | solution.py:39
  82.7 21.9 %collective-permute-start.14 = (bf16[8,128,256]{2,1,0:T(8,128)(2,1)}, bf16[8,128,256]{2,1,0:T(8,128)(2,1)S(1)}, u32[]{:S(2)}, u32[]{:S(2)}) collective-permute-start(bf16[8,128,256]{2,1,0:T(8,128)(2,1)} %get-tuple-element.72), channel_id=1, source_target_pairs={{0,8},{1,9},{2,10},{3,11},{4,12},{5,13},{6,14},{7,15},{8,0},{9,1},... | collective-permute-start | bytes 1572872 | tf_op jit(solution)/shard_map/ppermute | solution.py:39
  83.8 22.6 %collective-permute-start.15 = (bf16[8,128,256]{2,1,0:T(8,128)(2,1)}, bf16[8,128,256]{2,1,0:T(8,128)(2,1)S(1)}, u32[]{:S(2)}, u32[]{:S(2)}) collective-permute-start(bf16[8,128,256]{2,1,0:T(8,128)(2,1)} %get-tuple-element.73), channel_id=1, source_target_pairs={{0,4},{1,5},{2,6},{3,7},{4,8},{5,9},{6,10},{7,11},{8,12},{9,13},{1... | collective-permute-start | bytes 1572872 | tf_op jit(solution)/shard_map/ppermute | solution.py:39
  84.5 36.4 %all-to-all-start.1 = ((bf16[16,128,256]{2,1,0:T(8,128)(2,1)}), bf16[16,128,256]{2,1,0:T(8,128)(2,1)}, u32[]{:S(2)}, u32[]{:S(2)}) async-start(bf16[16,128,256]{2,1,0:T(8,128)(2,1)} %get-tuple-element.66), calls=%async_computation.1 | async-start | bytes 2097152 | tf_op jit(solution)/shard_map/all_to_all | solution.py:454
  92.6 15.9 %collective-permute-start.20 = (bf16[8,128,256]{2,1,0:T(8,128)(2,1)}, bf16[8,128,256]{2,1,0:T(8,128)(2,1)}, u32[]{:S(2)}, u32[]{:S(2)}) collective-permute-start(bf16[8,128,256]{2,1,0:T(8,128)(2,1)} %get-tuple-element.84), channel_id=1, source_target_pairs={{0,2},{1,3},{2,0},{3,1},{4,6},{5,7},{6,4},{7,5},{8,10},{9,11},{10,... | collective-permute-start | bytes 1572872 | tf_op jit(solution)/shard_map/ppermute | solution.py:39
  110.4 9.1 %collective-permute-start.21 = (bf16[4,128,256]{2,1,0:T(8,128)(2,1)S(1)}, bf16[4,128,256]{2,1,0:T(8,128)(2,1)S(1)}, u32[]{:S(2)}, u32[]{:S(2)}) collective-permute-start(bf16[4,128,256]{2,1,0:T(8,128)(2,1)S(1)} %get-tuple-element.88), channel_id=1, source_target_pairs={{0,4},{1,5},{2,6},{3,7},{4,8},{5,9},{6,10},{7,11},{8,12},{9,13},{1... | collective-permute-start | bytes 786440 | tf_op jit(solution)/shard_map/ppermute | solution.py:39
  112.3 10.8 %collective-permute-start.16 = (bf16[4,128,256]{2,1,0:T(8,128)(2,1)}, bf16[4,128,256]{2,1,0:T(8,128)(2,1)S(1)}, u32[]{:S(2)}, u32[]{:S(2)}) collective-permute-start(bf16[4,128,256]{2,1,0:T(8,128)(2,1)} %get-tuple-element.77), channel_id=1, source_target_pairs={{0,1},{1,2},{2,3},{3,0},{4,5},{5,6},{6,7},{7,4},{8,9},{9,10},{10,1... | collective-permute-start | bytes 786440 | tf_op jit(solution)/shard_map/ppermute | solution.py:39
  113.1 13.9 %collective-permute-start.17 = (bf16[4,128,256]{2,1,0:T(8,128)(2,1)}, bf16[4,128,256]{2,1,0:T(8,128)(2,1)S(1)}, u32[]{:S(2)}, u32[]{:S(2)}) collective-permute-start(bf16[4,128,256]{2,1,0:T(8,128)(2,1)} %get-tuple-element.78), channel_id=1, source_target_pairs={{0,2},{1,3},{2,0},{3,1},{4,6},{5,7},{6,4},{7,5},{8,10},{9,11},{10,... | collective-permute-start | bytes 786440 | tf_op jit(solution)/shard_map/ppermute | solution.py:39
  115.7 11.9 %collective-permute-start.18 = (bf16[4,128,256]{2,1,0:T(8,128)(2,1)S(1)}, bf16[4,128,256]{2,1,0:T(8,128)(2,1)S(1)}, u32[]{:S(2)}, u32[]{:S(2)}) collective-permute-start(bf16[4,128,256]{2,1,0:T(8,128)(2,1)S(1)} %get-tuple-element.79), channel_id=1, source_target_pairs={{0,3},{1,0},{2,1},{3,2},{4,7},{5,4},{6,5},{7,6},{8,11},{9,8},{10,9... | collective-permute-start | bytes 786440 | tf_op jit(solution)/shard_map/ppermute | solution.py:39
  116.3 11.3 %collective-permute-start.23 = (bf16[4,128,256]{2,1,0:T(8,128)(2,1)S(1)}, bf16[4,128,256]{2,1,0:T(8,128)(2,1)S(1)}, u32[]{:S(2)}, u32[]{:S(2)}) collective-permute-start(bf16[4,128,256]{2,1,0:T(8,128)(2,1)S(1)} %get-tuple-element.91), channel_id=1, source_target_pairs={{0,12},{1,13},{2,14},{3,15},{4,0},{5,1},{6,2},{7,3},{8,4},{9,5},{1... | collective-permute-start | bytes 786440 | tf_op jit(solution)/shard_map/ppermute | solution.py:39
  119.5 11.2 %collective-permute-start.22 = (bf16[4,128,256]{2,1,0:T(8,128)(2,1)S(1)}, bf16[4,128,256]{2,1,0:T(8,128)(2,1)S(1)}, u32[]{:S(2)}, u32[]{:S(2)}) collective-permute-start(bf16[4,128,256]{2,1,0:T(8,128)(2,1)S(1)} %get-tuple-element.90), channel_id=1, source_target_pairs={{0,8},{1,9},{2,10},{3,11},{4,12},{5,13},{6,14},{7,15},{8,0},{9,1},... | collective-permute-start | bytes 786440 | tf_op jit(solution)/shard_map/ppermute | solution.py:39
  (6 other events, 18.5 us)

commit v12 on v11

--- a/solution.py
+++ b/solution.py
@@ -404,7 +404,7 @@
         most, nbr, width
     ) * 2
     out = pl.pallas_call(
-        functools.partial(attend_body, groups, distinct, owned, most, 8),
+        functools.partial(attend_body, groups, distinct, owned, most, 16),
         out_shape=tuple(pltpu.HBM(shape.shape, shape.dtype) for shape in shapes),
         in_specs=[SMEM, SMEM, VMEM] + [HBM] * 8,
         out_specs=(HBM,) * 9,

time: 133 us -> 132 us (level)
  no operation moved by 1% of the time
where the time goes in v12:
time: 132 us; the launch traced here: 131 us
  starting transfers between devices  55.6 us (42%)
  waiting for transfers between devices  43.7 us (33%)
  Pallas kernels  29.4 us (22%)
  local copies, waits for them, and re-layouts  1.67 us (1%)
    ppermute x24, waiting for transfers between devices, shift(): return lax.ppermute(value, 'dp', pairs)  43.7 us
    ppermute x24, starting transfers between devices, shift(): return lax.ppermute(value, 'dp', pairs)  40.2 us
    pallas_call x1, Pallas kernels, attend(): pl.pallas_call(functools.partial(attend_body, groups, distinct, owned, mo...  11.7 us
    all_to_all x1, starting transfers between devices, on_device(): lax.all_to_all(packed, 'ctx', split_axis=0, concat_axis=0, tiled=True)  8.71 us
    all_to_all x1, starting transfers between devices, on_device(): back = lax.all_to_all(back, 'ctx', split_axis=0, concat_axis=0, tiled=True)  6.69 us
    pallas_call x2, Pallas kernels, spread(): pl.pallas_call(functools.partial(spread_body, across), out_shape=chunk_sh...  4.01 us
    pallas_call x1, Pallas kernels, tables(): pl.pallas_call(functools.partial(tables_body, owned, most), out_shape=(ja...  3.94 us
    pallas_call x1, Pallas kernels, select(): pl.pallas_call(select_body, out_shape=tuple((pltpu.HBM(shape.shape, shape...  3.75 us
  transfers between devices with their start and end apart: 26, of which 14 were waited for; matrix products, arithmetic and copies ran while one was open for 0% of the time, Pallas kernels for 11%

profile of v12, /device:TPU:8, one launch (start us, length us, event | category | flops | bytes accessed | tf_op | source)
XLA Modules:
  0.0 131.2 jit_solution(10463297289343150110)
XLA Ops:
  0.6 2.7 %shard_map.85 = bf16[16,2,128,256]{3,2,1,0:T(8,128)(2,1)} custom-call(bf16[128,4096]{1,0:T(8,128)(2,1)} %bitcast.5, bf16[128,4096]{1,0:T(8,128)(2,1)} %bitcast.6), custom_call_target="tpu_custom_call" | custom-call | tf_op jit(solution)/shard_map/pallas_call | solution.py:87
  3.4 8.7 %all-to-all-start = ((bf16[16,2,128,256]{3,2,1,0:T(8,128)(2,1)}), bf16[16,2,128,256]{3,2,1,0:T(8,128)(2,1)S(1)}, u32[]{:S(2)}, u32[]{:S(2)}) async-start(bf16[16,2,128,256]{3,2,1,0:T(8,128)(2,1)} %shard_map.85), calls=%async_computation | async-start | bytes 4194304 | tf_op jit(solution)/shard_map/all_to_all | solution.py:449
  12.7 3.0 %collective-permute-start.1 = (bf16[4,128,256]{2,1,0:T(8,128)(2,1)S(1)}, bf16[4,128,256]{2,1,0:T(8,128)(2,1)S(1)}, u32[]{:S(2)}, u32[]{:S(2)}) collective-permute-start(bf16[4,128,256]{2,1,0:T(8,128)(2,1)S(1)} %copy-done), channel_id=1, source_target_pairs={{0,2},{1,3},{2,0},{3,1},{4,6},{5,7},{6,4},{7,5},{8,10},{9,11},{10,... | collective-permute-start | bytes 786440 | tf_op jit(solution)/shard_map/ppermute | solution.py:39
  17.7 1.6 %collective-permute-start.5 = (bf16[4,128,256]{2,1,0:T(8,128)(2,1)S(1)}, bf16[4,128,256]{2,1,0:T(8,128)(2,1)}, u32[]{:S(2)}, u32[]{:S(2)}) collective-permute-start(bf16[4,128,256]{2,1,0:T(8,128)(2,1)S(1)} %copy-done.1), channel_id=1, source_target_pairs={{0,4},{1,5},{2,6},{3,7},{4,8},{5,9},{6,10},{7,11},{8,12},{9,13},{1... | collective-permute-start | bytes 786440 | tf_op jit(solution)/shard_map/ppermute | solution.py:39
  20.9 3.5 %collective-permute-start.4 = (bf16[4,128,256]{2,1,0:T(8,128)(2,1)S(1)}, bf16[4,128,256]{2,1,0:T(8,128)(2,1)}, u32[]{:S(2)}, u32[]{:S(2)}) collective-permute-start(bf16[4,128,256]{2,1,0:T(8,128)(2,1)S(1)} %copy-done.1), channel_id=1, source_target_pairs={{0,8},{1,9},{2,10},{3,11},{4,12},{5,13},{6,14},{7,15},{8,0},{9,1},... | collective-permute-start | bytes 786440 | tf_op jit(solution)/shard_map/ppermute | solution.py:39
  24.4 3.9 %shard_map.86 = (s32[2,32]{1,0:T(2,128)}, s32[2,64]{1,0:T(2,128)}) custom-call(s32[16,16]{1,0:T(8,128)} %ids_ref.3), custom_call_target="tpu_custom_call" | custom-call | tf_op jit(solution)/shard_map/pallas_call | solution.py:167
  28.4 2.2 %collective-permute-done.4.refs_6_ = bf16[4,128,256]{2,1,0:T(8,128)(2,1)} collective-permute-done((bf16[4,128,256]{2,1,0:T(8,128)(2,1)S(1)}, bf16[4,128,256]{2,1,0:T(8,128)(2,1)}, u32[]{:S(2)}, u32[]{:S(2)}) %collective-permute-start.4) | collective-permute-done | bytes 262176 | tf_op jit(solution)/shard_map/ppermute | solution.py:39
  31.3 3.7 %shard_map.87 = (bf16[8,128,256]{2,1,0:T(8,128)(2,1)}, bf16[8,128,256]{2,1,0:T(8,128)(2,1)}, bf16[8,128,256]{2,1,0:T(8,128)(2,1)}, bf16[8,128,256]{2,1,0:T(8,128...) custom-call(s32[2,32]{1,0:T(2,128)S(1)} %copy-done.3, ...), custom_call_target="tpu_custom_call" | custom-call | tf_op jit(solution)/shard_map/pallas_call | solution.py:212
  35.0 1.6 %collective-permute-start.9 = (bf16[8,128,256]{2,1,0:T(8,128)(2,1)}, bf16[8,128,256]{2,1,0:T(8,128)(2,1)S(1)}, u32[]{:S(2)}, u32[]{:S(2)}) collective-permute-start(bf16[8,128,256]{2,1,0:T(8,128)(2,1)} %get-tuple-element.62), channel_id=1, source_target_pairs={{0,1},{1,2},{2,3},{3,0},{4,5},{5,6},{6,7},{7,4},{8,9},{9,10},{10,1... | collective-permute-start | bytes 1572872 | tf_op jit(solution)/shard_map/ppermute | solution.py:39
  36.6 2.2 %collective-permute-start.6 = (bf16[8,128,256]{2,1,0:T(8,128)(2,1)}, bf16[8,128,256]{2,1,0:T(8,128)(2,1)S(1)}, u32[]{:S(2)}, u32[]{:S(2)}) collective-permute-start(bf16[8,128,256]{2,1,0:T(8,128)(2,1)} %get-tuple-element.57), channel_id=1, source_target_pairs={{0,4},{1,5},{2,6},{3,7},{4,8},{5,9},{6,10},{7,11},{8,12},{9,13},{1... | collective-permute-start | bytes 1572872 | tf_op jit(solution)/shard_map/ppermute | solution.py:39
  38.8 3.6 %collective-permute-start.7 = (bf16[8,128,256]{2,1,0:T(8,128)(2,1)}, bf16[8,128,256]{2,1,0:T(8,128)(2,1)}, u32[]{:S(2)}, u32[]{:S(2)}) collective-permute-start(bf16[8,128,256]{2,1,0:T(8,128)(2,1)} %get-tuple-element.58), channel_id=1, source_target_pairs={{0,8},{1,9},{2,10},{3,11},{4,12},{5,13},{6,14},{7,15},{8,0},{9,1},... | collective-permute-start | bytes 1572872 | tf_op jit(solution)/shard_map/ppermute | solution.py:39
  42.5 2.6 %collective-permute-start.11 = (bf16[8,128,256]{2,1,0:T(8,128)(2,1)}, bf16[8,128,256]{2,1,0:T(8,128)(2,1)}, u32[]{:S(2)}, u32[]{:S(2)}) collective-permute-start(bf16[8,128,256]{2,1,0:T(8,128)(2,1)} %get-tuple-element.65), channel_id=1, source_target_pairs={{0,3},{1,0},{2,1},{3,2},{4,7},{5,4},{6,5},{7,6},{8,11},{9,8},{10,9... | collective-permute-start | bytes 1572872 | tf_op jit(solution)/shard_map/ppermute | solution.py:39
  45.0 4.4 %collective-permute-done.9.refs_5_ = bf16[8,128,256]{2,1,0:T(8,128)(2,1)S(1)} collective-permute-done((bf16[8,128,256]{2,1,0:T(8,128)(2,1)}, bf16[8,128,256]{2,1,0:T(8,128)(2,1)S(1)}, u32[]{:S(2)}, u32[]{:S(2)}) %collective-permute-start.9) | collective-permute-done | bytes 524320 | tf_op jit(solution)/shard_map/ppermute | solution.py:39
  49.4 1.8 %collective-permute-start.10 = (bf16[8,128,256]{2,1,0:T(8,128)(2,1)}, bf16[8,128,256]{2,1,0:T(8,128)(2,1)}, u32[]{:S(2)}, u32[]{:S(2)}) collective-permute-start(bf16[8,128,256]{2,1,0:T(8,128)(2,1)} %get-tuple-element.64), channel_id=1, source_target_pairs={{0,2},{1,3},{2,0},{3,1},{4,6},{5,7},{6,4},{7,5},{8,10},{9,11},{10,... | collective-permute-start | bytes 1572872 | tf_op jit(solution)/shard_map/ppermute | solution.py:39
  51.3 9.4 %collective-permute-done.6.refs_1_ = bf16[8,128,256]{2,1,0:T(8,128)(2,1)S(1)} collective-permute-done((bf16[8,128,256]{2,1,0:T(8,128)(2,1)}, bf16[8,128,256]{2,1,0:T(8,128)(2,1)S(1)}, u32[]{:S(2)}, u32[]{:S(2)}) %collective-permute-start.6) | collective-permute-done | bytes 524320 | tf_op jit(solution)/shard_map/ppermute | solution.py:39
  60.7 3.6 %collective-permute-done.8.refs_3_ = bf16[8,128,256]{2,1,0:T(8,128)(2,1)} collective-permute-done((bf16[8,128,256]{2,1,0:T(8,128)(2,1)}, bf16[8,128,256]{2,1,0:T(8,128)(2,1)}, u32[]{:S(2)}, u32[]{:S(2)}) %collective-permute-start.8) | collective-permute-done | bytes 524320 | tf_op jit(solution)/shard_map/ppermute | solution.py:39
  64.8 11.7 %shard_map.88 = (bf16[16,128,256]{2,1,0:T(8,128)(2,1)}, bf16[8,128,256]{2,1,0:T(8,128)(2,1)}, bf16[8,128,256]{2,1,0:T(8,128)(2,1)}, bf16[8,128,256]{2,1,0:T(8,12...) custom-call(s32[16,16]{1,0:T(8,128)S(1)} %copy-done.2, ...), custom_call_target="tpu_custom_call" | custom-call | tf_op jit(solution)/shard_map/pallas_call | solution.py:406
  76.5 2.9 %collective-permute-start.12 = (bf16[8,128,256]{2,1,0:T(8,128)(2,1)}, bf16[8,128,256]{2,1,0:T(8,128)(2,1)S(1)}, u32[]{:S(2)}, u32[]{:S(2)}) collective-permute-start(bf16[8,128,256]{2,1,0:T(8,128)(2,1)} %get-tuple-element.69), channel_id=1, source_target_pairs={{0,1},{1,2},{2,3},{3,0},{4,5},{5,6},{6,7},{7,4},{8,9},{9,10},{10,1... | collective-permute-start | bytes 1572872 | tf_op jit(solution)/shard_map/ppermute | solution.py:39
  80.3 1.9 %collective-permute-start.13 = (bf16[8,128,256]{2,1,0:T(8,128)(2,1)}, bf16[8,128,256]{2,1,0:T(8,128)(2,1)S(1)}, u32[]{:S(2)}, u32[]{:S(2)}) collective-permute-start(bf16[8,128,256]{2,1,0:T(8,128)(2,1)} %get-tuple-element.71), channel_id=1, source_target_pairs={{0,12},{1,13},{2,14},{3,15},{4,0},{5,1},{6,2},{7,3},{8,4},{9,5},{1... | collective-permute-start | bytes 1572872 | tf_op jit(solution)/shard_map/ppermute | solution.py:39
  84.0 6.7 %all-to-all-start.1 = ((bf16[16,128,256]{2,1,0:T(8,128)(2,1)}), bf16[16,128,256]{2,1,0:T(8,128)(2,1)}, u32[]{:S(2)}, u32[]{:S(2)}) async-start(bf16[16,128,256]{2,1,0:T(8,128)(2,1)} %get-tuple-element.66), calls=%async_computation.1 | async-start | bytes 2097152 | tf_op jit(solution)/shard_map/all_to_all | solution.py:454
  92.1 1.7 %collective-permute-start.20 = (bf16[8,128,256]{2,1,0:T(8,128)(2,1)}, bf16[8,128,256]{2,1,0:T(8,128)(2,1)}, u32[]{:S(2)}, u32[]{:S(2)}) collective-permute-start(bf16[8,128,256]{2,1,0:T(8,128)(2,1)} %get-tuple-element.84), channel_id=1, source_target_pairs={{0,2},{1,3},{2,0},{3,1},{4,6},{5,7},{6,4},{7,5},{8,10},{9,11},{10,... | collective-permute-start | bytes 1572872 | tf_op jit(solution)/shard_map/ppermute | solution.py:39
  93.8 2.3 %collective-permute-done.13.refs_1_ = bf16[8,128,256]{2,1,0:T(8,128)(2,1)S(1)} collective-permute-done((bf16[8,128,256]{2,1,0:T(8,128)(2,1)}, bf16[8,128,256]{2,1,0:T(8,128)(2,1)S(1)}, u32[]{:S(2)}, u32[]{:S(2)}) %collective-permute-start.13) | collective-permute-done | bytes 524320 | tf_op jit(solution)/shard_map/ppermute | solution.py:39
  96.1 8.1 %collective-permute-done.14.refs_2_ = bf16[8,128,256]{2,1,0:T(8,128)(2,1)S(1)} collective-permute-done((bf16[8,128,256]{2,1,0:T(8,128)(2,1)}, bf16[8,128,256]{2,1,0:T(8,128)(2,1)S(1)}, u32[]{:S(2)}, u32[]{:S(2)}) %collective-permute-start.14) | collective-permute-done | bytes 524320 | tf_op jit(solution)/shard_map/ppermute | solution.py:39
  104.2 1.7 %collective-permute-done.15.refs_3_ = bf16[8,128,256]{2,1,0:T(8,128)(2,1)S(1)} collective-permute-done((bf16[8,128,256]{2,1,0:T(8,128)(2,1)}, bf16[8,128,256]{2,1,0:T(8,128)(2,1)S(1)}, u32[]{:S(2)}, u32[]{:S(2)}) %collective-permute-start.15) | collective-permute-done | bytes 524320 | tf_op jit(solution)/shard_map/ppermute | solution.py:39
  105.9 2.1 %shard_map.90 = (f32[4,128,256]{2,1,0:T(8,128)S(1)}, bf16[4,128,256]{2,1,0:T(8,128)(2,1)}, bf16[4,128,256]{2,1,0:T(8,128)(2,1)}, bf16[4,128,256]{2,1,0:T(8,128)(2,1)S(1)}) custom-call(s32[2,64]{1,0:T(2,128)S(1)} %copy-done.8, bf16[8,128,256]{2,1,0:T(8,128)(2,1)S(1)} %copy-done.5, bf16[8,128,256]{2,1,0:T(8,128)(2,1)S(1)} %collective-permute-done.13.refs_1_, ...), custom_call_target="tpu_custom_call" | custom-call | flops 199999995904 | bytes 2097152 | tf_op jit(solution)/shard_map/pallas_call | solution.py:253
  108.0 1.9 %shard_map.91 = (f32[4,128,256]{2,1,0:T(8,128)S(1)}, bf16[4,128,256]{2,1,0:T(8,128)(2,1)S(1)}, bf16[4,128,256]{2,1,0:T(8,128)(2,1)S(1)}, bf16[4,128,256]{2,1,0:T(8,128)(2,1)S(1)}) custom-call(s32[2,64]{1,0:T(2,128)S(1)} %copy-done.8, bf16[8,128,256]{2,1,0:T(8,128)(2,1)S(1)} %copy-done.4, bf16[8,128,256]{2,1,0:T(8,128)(2,1)S(1)} %collective-permute-done.19.refs_1_, ...), custom_call_target="tpu_custom_call" | custom-call | flops 199999995904 | bytes 2097152 | tf_op jit(solution)/shard_map/pallas_call | solution.py:253
  109.9 1.9 %collective-permute-start.21 = (bf16[4,128,256]{2,1,0:T(8,128)(2,1)S(1)}, bf16[4,128,256]{2,1,0:T(8,128)(2,1)S(1)}, u32[]{:S(2)}, u32[]{:S(2)}) collective-permute-start(bf16[4,128,256]{2,1,0:T(8,128)(2,1)S(1)} %get-tuple-element.88), channel_id=1, source_target_pairs={{0,4},{1,5},{2,6},{3,7},{4,8},{5,9},{6,10},{7,11},{8,12},{9,13},{1... | collective-permute-start | bytes 786440 | tf_op jit(solution)/shard_map/ppermute | solution.py:39
  112.6 2.6 %collective-permute-start.17 = (bf16[4,128,256]{2,1,0:T(8,128)(2,1)}, bf16[4,128,256]{2,1,0:T(8,128)(2,1)S(1)}, u32[]{:S(2)}, u32[]{:S(2)}) collective-permute-start(bf16[4,128,256]{2,1,0:T(8,128)(2,1)} %get-tuple-element.78), channel_id=1, source_target_pairs={{0,2},{1,3},{2,0},{3,1},{4,6},{5,7},{6,4},{7,5},{8,10},{9,11},{10,... | collective-permute-start | bytes 786440 | tf_op jit(solution)/shard_map/ppermute | solution.py:39
  117.2 1.9 %collective-permute-done.21.refs_5_ = bf16[4,128,256]{2,1,0:T(8,128)(2,1)S(1)} collective-permute-done((bf16[4,128,256]{2,1,0:T(8,128)(2,1)S(1)}, bf16[4,128,256]{2,1,0:T(8,128)(2,1)S(1)}, u32[]{:S(2)}, u32[]{:S(2)}) %collective-permute-start.21) | collective-permute-done | bytes 262176 | tf_op jit(solution)/shard_map/ppermute | solution.py:39
  120.3 2.3 %shard_map.89 = bf16[128,4096]{1,0:T(8,128)(2,1)} custom-call(bf16[16,128,256]{2,1,0:T(8,128)(2,1)} %all-to-all-done.1.in_ref), custom_call_target="tpu_custom_call" | custom-call | tf_op jit(solution)/shard_map/pallas_call | solution.py:113
  122.7 3.8 %collective-permute-done.17.refs_2_ = bf16[4,128,256]{2,1,0:T(8,128)(2,1)S(1)} collective-permute-done((bf16[4,128,256]{2,1,0:T(8,128)(2,1)}, bf16[4,128,256]{2,1,0:T(8,128)(2,1)S(1)}, u32[]{:S(2)}, u32[]{:S(2)}) %collective-permute-start.17) | collective-permute-done | bytes 262176 | tf_op jit(solution)/shard_map/ppermute | solution.py:39
  127.1 3.1 %collective-permute-done.22.refs_6_ = bf16[4,128,256]{2,1,0:T(8,128)(2,1)S(1)} collective-permute-done((bf16[4,128,256]{2,1,0:T(8,128)(2,1)S(1)}, bf16[4,128,256]{2,1,0:T(8,128)(2,1)S(1)}, u32[]{:S(2)}, u32[]{:S(2)}) %collective-permute-start.22) | collective-permute-done | bytes 262176 | tf_op jit(solution)/shard_map/ppermute | solution.py:39
  (54 shorter events, 15.3 us)
Async XLA Ops:
  3.4 9.3 %copy-start = (bf16[4,128,256]{2,1,0:T(8,128)(2,1)S(1)}, bf16[4,128,256]{2,1,0:T(8,128)(2,1)}, u32[]{:S(2)}) copy-start(bf16[4,128,256]{2,1,0:T(8,128)(2,1)} %refs_0_.1) | copy-start | bytes 786436
  3.4 47.8 %copy-start.11 = (s32[16,32,2]{1,2,0:T(2,128)S(1)}, s32[16,32,2]{1,2,0:T(2,128)}, u32[]{:S(2)}) copy-start(s32[16,32,2]{1,2,0:T(2,128)} %param.11) | copy-start | bytes 12292
  3.4 61.4 %all-to-all-start = ((bf16[16,2,128,256]{3,2,1,0:T(8,128)(2,1)}), bf16[16,2,128,256]{3,2,1,0:T(8,128)(2,1)S(1)}, u32[]{:S(2)}, u32[]{:S(2)}) async-start(bf16[16,2,128,256]{3,2,1,0:T(8,128)(2,1)} %shard_map.85), calls=%async_computation | async-start | bytes 4194304 | tf_op jit(solution)/shard_map/all_to_all | solution.py:449
  12.1 52.6 %copy-start.2 = (s32[16,16]{1,0:T(8,128)S(1)}, s32[16,16]{1,0:T(8,128)}, u32[]{:S(2)}) copy-start(s32[16,16]{1,0:T(8,128)} %ids_ref.3) | copy-start | bytes 3076
  12.1 8.7 %collective-permute-start.3 = (bf16[4,128,256]{2,1,0:T(8,128)(2,1)S(1)}, bf16[4,128,256]{2,1,0:T(8,128)(2,1)S(1)}, u32[]{:S(2)}, u32[]{:S(2)}) collective-permute-start(bf16[4,128,256]{2,1,0:T(8,128)(2,1)S(1)} %copy-done.1), channel_id=1, source_target_pairs={{0,12},{1,13},{2,14},{3,15},{4,0},{5,1},{6,2},{7,3},{8,4},{9,5},{1... | collective-permute-start | bytes 786440 | tf_op jit(solution)/shard_map/ppermute | solution.py:39
  12.7 15.6 %collective-permute-start.1 = (bf16[4,128,256]{2,1,0:T(8,128)(2,1)S(1)}, bf16[4,128,256]{2,1,0:T(8,128)(2,1)S(1)}, u32[]{:S(2)}, u32[]{:S(2)}) collective-permute-start(bf16[4,128,256]{2,1,0:T(8,128)(2,1)S(1)} %copy-done), channel_id=1, source_target_pairs={{0,2},{1,3},{2,0},{3,1},{4,6},{5,7},{6,4},{7,5},{8,10},{9,11},{10,... | collective-permute-start | bytes 786440 | tf_op jit(solution)/shard_map/ppermute | solution.py:39
  15.7 12.6 %collective-permute-start = (bf16[4,128,256]{2,1,0:T(8,128)(2,1)S(1)}, bf16[4,128,256]{2,1,0:T(8,128)(2,1)S(1)}, u32[]{:S(2)}, u32[]{:S(2)}) collective-permute-start(bf16[4,128,256]{2,1,0:T(8,128)(2,1)S(1)} %copy-done), channel_id=1, source_target_pairs={{0,3},{1,0},{2,1},{3,2},{4,7},{5,4},{6,5},{7,6},{8,11},{9,8},{10,9... | collective-permute-start | bytes 786440 | tf_op jit(solution)/shard_map/ppermute | solution.py:39
  16.8 11.5 %collective-permute-start.2 = (bf16[4,128,256]{2,1,0:T(8,128)(2,1)S(1)}, bf16[4,128,256]{2,1,0:T(8,128)(2,1)}, u32[]{:S(2)}, u32[]{:S(2)}) collective-permute-start(bf16[4,128,256]{2,1,0:T(8,128)(2,1)S(1)} %copy-done), channel_id=1, source_target_pairs={{0,1},{1,2},{2,3},{3,0},{4,5},{5,6},{6,7},{7,4},{8,9},{9,10},{10,1... | collective-permute-start | bytes 786440 | tf_op jit(solution)/shard_map/ppermute | solution.py:39
  17.7 10.6 %collective-permute-start.5 = (bf16[4,128,256]{2,1,0:T(8,128)(2,1)S(1)}, bf16[4,128,256]{2,1,0:T(8,128)(2,1)}, u32[]{:S(2)}, u32[]{:S(2)}) collective-permute-start(bf16[4,128,256]{2,1,0:T(8,128)(2,1)S(1)} %copy-done.1), channel_id=1, source_target_pairs={{0,4},{1,5},{2,6},{3,7},{4,8},{5,9},{6,10},{7,11},{8,12},{9,13},{1... | collective-permute-start | bytes 786440 | tf_op jit(solution)/shard_map/ppermute | solution.py:39
  20.9 9.7 %collective-permute-start.4 = (bf16[4,128,256]{2,1,0:T(8,128)(2,1)S(1)}, bf16[4,128,256]{2,1,0:T(8,128)(2,1)}, u32[]{:S(2)}, u32[]{:S(2)}) collective-permute-start(bf16[4,128,256]{2,1,0:T(8,128)(2,1)S(1)} %copy-done.1), channel_id=1, source_target_pairs={{0,8},{1,9},{2,10},{3,11},{4,12},{5,13},{6,14},{7,15},{8,0},{9,1},... | collective-permute-start | bytes 786440 | tf_op jit(solution)/shard_map/ppermute | solution.py:39
  35.0 14.4 %collective-permute-start.9 = (bf16[8,128,256]{2,1,0:T(8,128)(2,1)}, bf16[8,128,256]{2,1,0:T(8,128)(2,1)S(1)}, u32[]{:S(2)}, u32[]{:S(2)}) collective-permute-start(bf16[8,128,256]{2,1,0:T(8,128)(2,1)} %get-tuple-element.62), channel_id=1, source_target_pairs={{0,1},{1,2},{2,3},{3,0},{4,5},{5,6},{6,7},{7,4},{8,9},{9,10},{10,1... | collective-permute-start | bytes 1572872 | tf_op jit(solution)/shard_map/ppermute | solution.py:39
  36.6 24.1 %collective-permute-start.6 = (bf16[8,128,256]{2,1,0:T(8,128)(2,1)}, bf16[8,128,256]{2,1,0:T(8,128)(2,1)S(1)}, u32[]{:S(2)}, u32[]{:S(2)}) collective-permute-start(bf16[8,128,256]{2,1,0:T(8,128)(2,1)} %get-tuple-element.57), channel_id=1, source_target_pairs={{0,4},{1,5},{2,6},{3,7},{4,8},{5,9},{6,10},{7,11},{8,12},{9,13},{1... | collective-permute-start | bytes 1572872 | tf_op jit(solution)/shard_map/ppermute | solution.py:39
  38.8 21.9 %collective-permute-start.7 = (bf16[8,128,256]{2,1,0:T(8,128)(2,1)}, bf16[8,128,256]{2,1,0:T(8,128)(2,1)}, u32[]{:S(2)}, u32[]{:S(2)}) collective-permute-start(bf16[8,128,256]{2,1,0:T(8,128)(2,1)} %get-tuple-element.58), channel_id=1, source_target_pairs={{0,8},{1,9},{2,10},{3,11},{4,12},{5,13},{6,14},{7,15},{8,0},{9,1},... | collective-permute-start | bytes 1572872 | tf_op jit(solution)/shard_map/ppermute | solution.py:39
  42.4 21.9 %collective-permute-start.8 = (bf16[8,128,256]{2,1,0:T(8,128)(2,1)}, bf16[8,128,256]{2,1,0:T(8,128)(2,1)}, u32[]{:S(2)}, u32[]{:S(2)}) collective-permute-start(bf16[8,128,256]{2,1,0:T(8,128)(2,1)} %get-tuple-element.59), channel_id=1, source_target_pairs={{0,12},{1,13},{2,14},{3,15},{4,0},{5,1},{6,2},{7,3},{8,4},{9,5},{1... | collective-permute-start | bytes 1572872 | tf_op jit(solution)/shard_map/ppermute | solution.py:39
  42.5 22.3 %collective-permute-start.11 = (bf16[8,128,256]{2,1,0:T(8,128)(2,1)}, bf16[8,128,256]{2,1,0:T(8,128)(2,1)}, u32[]{:S(2)}, u32[]{:S(2)}) collective-permute-start(bf16[8,128,256]{2,1,0:T(8,128)(2,1)} %get-tuple-element.65), channel_id=1, source_target_pairs={{0,3},{1,0},{2,1},{3,2},{4,7},{5,4},{6,5},{7,6},{8,11},{9,8},{10,9... | collective-permute-start | bytes 1572872 | tf_op jit(solution)/shard_map/ppermute | solution.py:39
  49.4 15.4 %copy-start.9 = (bf16[8,128,256]{2,1,0:T(8,128)(2,1)}, bf16[8,128,256]{2,1,0:T(8,128)(2,1)S(1)}, u32[]{:S(2)}) copy-start(bf16[8,128,256]{2,1,0:T(8,128)(2,1)S(1)} %collective-permute-done.9.refs_5_) | copy-start | bytes 1572868
  49.4 15.4 %collective-permute-start.10 = (bf16[8,128,256]{2,1,0:T(8,128)(2,1)}, bf16[8,128,256]{2,1,0:T(8,128)(2,1)}, u32[]{:S(2)}, u32[]{:S(2)}) collective-permute-start(bf16[8,128,256]{2,1,0:T(8,128)(2,1)} %get-tuple-element.64), channel_id=1, source_target_pairs={{0,2},{1,3},{2,0},{3,1},{4,6},{5,7},{6,4},{7,5},{8,10},{9,11},{10,... | collective-permute-start | bytes 1572872 | tf_op jit(solution)/shard_map/ppermute | solution.py:39
  76.5 29.4 %copy-start.5 = (bf16[8,128,256]{2,1,0:T(8,128)(2,1)S(1)}, bf16[8,128,256]{2,1,0:T(8,128)(2,1)}, u32[]{:S(2)}) copy-start(bf16[8,128,256]{2,1,0:T(8,128)(2,1)} %get-tuple-element.70.refs_0_) | copy-start | bytes 1572868
  76.5 29.4 %copy-start.8 = (s32[2,64]{1,0:T(2,128)S(1)}, s32[2,64]{1,0:T(2,128)}, u32[]{:S(2)}) copy-start(s32[2,64]{1,0:T(2,128)} %get-tuple-element.67.add_ref) | copy-start | bytes 1540
  76.5 14.8 %collective-permute-start.12 = (bf16[8,128,256]{2,1,0:T(8,128)(2,1)}, bf16[8,128,256]{2,1,0:T(8,128)(2,1)S(1)}, u32[]{:S(2)}, u32[]{:S(2)}) collective-permute-start(bf16[8,128,256]{2,1,0:T(8,128)(2,1)} %get-tuple-element.69), channel_id=1, source_target_pairs={{0,1},{1,2},{2,3},{3,0},{4,5},{5,6},{6,7},{7,4},{8,9},{9,10},{10,1... | collective-permute-start | bytes 1572872 | tf_op jit(solution)/shard_map/ppermute | solution.py:39
  79.4 12.7 %collective-permute-start.19 = (bf16[8,128,256]{2,1,0:T(8,128)(2,1)}, bf16[8,128,256]{2,1,0:T(8,128)(2,1)S(1)}, u32[]{:S(2)}, u32[]{:S(2)}) collective-permute-start(bf16[8,128,256]{2,1,0:T(8,128)(2,1)} %get-tuple-element.82), channel_id=1, source_target_pairs={{0,3},{1,0},{2,1},{3,2},{4,7},{5,4},{6,5},{7,6},{8,11},{9,8},{10,9... | collective-permute-start | bytes 1572872 | tf_op jit(solution)/shard_map/ppermute | solution.py:39
  80.3 15.8 %collective-permute-start.13 = (bf16[8,128,256]{2,1,0:T(8,128)(2,1)}, bf16[8,128,256]{2,1,0:T(8,128)(2,1)S(1)}, u32[]{:S(2)}, u32[]{:S(2)}) collective-permute-start(bf16[8,128,256]{2,1,0:T(8,128)(2,1)} %get-tuple-element.71), channel_id=1, source_target_pairs={{0,12},{1,13},{2,14},{3,15},{4,0},{5,1},{6,2},{7,3},{8,4},{9,5},{1... | collective-permute-start | bytes 1572872 | tf_op jit(solution)/shard_map/ppermute | solution.py:39
  82.2 21.9 %collective-permute-start.14 = (bf16[8,128,256]{2,1,0:T(8,128)(2,1)}, bf16[8,128,256]{2,1,0:T(8,128)(2,1)S(1)}, u32[]{:S(2)}, u32[]{:S(2)}) collective-permute-start(bf16[8,128,256]{2,1,0:T(8,128)(2,1)} %get-tuple-element.72), channel_id=1, source_target_pairs={{0,8},{1,9},{2,10},{3,11},{4,12},{5,13},{6,14},{7,15},{8,0},{9,1},... | collective-permute-start | bytes 1572872 | tf_op jit(solution)/shard_map/ppermute | solution.py:39
  83.3 22.6 %collective-permute-start.15 = (bf16[8,128,256]{2,1,0:T(8,128)(2,1)}, bf16[8,128,256]{2,1,0:T(8,128)(2,1)S(1)}, u32[]{:S(2)}, u32[]{:S(2)}) collective-permute-start(bf16[8,128,256]{2,1,0:T(8,128)(2,1)} %get-tuple-element.73), channel_id=1, source_target_pairs={{0,4},{1,5},{2,6},{3,7},{4,8},{5,9},{6,10},{7,11},{8,12},{9,13},{1... | collective-permute-start | bytes 1572872 | tf_op jit(solution)/shard_map/ppermute | solution.py:39
  84.0 36.4 %all-to-all-start.1 = ((bf16[16,128,256]{2,1,0:T(8,128)(2,1)}), bf16[16,128,256]{2,1,0:T(8,128)(2,1)}, u32[]{:S(2)}, u32[]{:S(2)}) async-start(bf16[16,128,256]{2,1,0:T(8,128)(2,1)} %get-tuple-element.66), calls=%async_computation.1 | async-start | bytes 2097152 | tf_op jit(solution)/shard_map/all_to_all | solution.py:454
  92.1 15.9 %collective-permute-start.20 = (bf16[8,128,256]{2,1,0:T(8,128)(2,1)}, bf16[8,128,256]{2,1,0:T(8,128)(2,1)}, u32[]{:S(2)}, u32[]{:S(2)}) collective-permute-start(bf16[8,128,256]{2,1,0:T(8,128)(2,1)} %get-tuple-element.84), channel_id=1, source_target_pairs={{0,2},{1,3},{2,0},{3,1},{4,6},{5,7},{6,4},{7,5},{8,10},{9,11},{10,... | collective-permute-start | bytes 1572872 | tf_op jit(solution)/shard_map/ppermute | solution.py:39
  109.9 9.1 %collective-permute-start.21 = (bf16[4,128,256]{2,1,0:T(8,128)(2,1)S(1)}, bf16[4,128,256]{2,1,0:T(8,128)(2,1)S(1)}, u32[]{:S(2)}, u32[]{:S(2)}) collective-permute-start(bf16[4,128,256]{2,1,0:T(8,128)(2,1)S(1)} %get-tuple-element.88), channel_id=1, source_target_pairs={{0,4},{1,5},{2,6},{3,7},{4,8},{5,9},{6,10},{7,11},{8,12},{9,13},{1... | collective-permute-start | bytes 786440 | tf_op jit(solution)/shard_map/ppermute | solution.py:39
  111.8 10.9 %collective-permute-start.16 = (bf16[4,128,256]{2,1,0:T(8,128)(2,1)}, bf16[4,128,256]{2,1,0:T(8,128)(2,1)S(1)}, u32[]{:S(2)}, u32[]{:S(2)}) collective-permute-start(bf16[4,128,256]{2,1,0:T(8,128)(2,1)} %get-tuple-element.77), channel_id=1, source_target_pairs={{0,1},{1,2},{2,3},{3,0},{4,5},{5,6},{6,7},{7,4},{8,9},{9,10},{10,1... | collective-permute-start | bytes 786440 | tf_op jit(solution)/shard_map/ppermute | solution.py:39
  112.6 13.9 %collective-permute-start.17 = (bf16[4,128,256]{2,1,0:T(8,128)(2,1)}, bf16[4,128,256]{2,1,0:T(8,128)(2,1)S(1)}, u32[]{:S(2)}, u32[]{:S(2)}) collective-permute-start(bf16[4,128,256]{2,1,0:T(8,128)(2,1)} %get-tuple-element.78), channel_id=1, source_target_pairs={{0,2},{1,3},{2,0},{3,1},{4,6},{5,7},{6,4},{7,5},{8,10},{9,11},{10,... | collective-permute-start | bytes 786440 | tf_op jit(solution)/shard_map/ppermute | solution.py:39
  115.2 11.9 %collective-permute-start.18 = (bf16[4,128,256]{2,1,0:T(8,128)(2,1)S(1)}, bf16[4,128,256]{2,1,0:T(8,128)(2,1)S(1)}, u32[]{:S(2)}, u32[]{:S(2)}) collective-permute-start(bf16[4,128,256]{2,1,0:T(8,128)(2,1)S(1)} %get-tuple-element.79), channel_id=1, source_target_pairs={{0,3},{1,0},{2,1},{3,2},{4,7},{5,4},{6,5},{7,6},{8,11},{9,8},{10,9... | collective-permute-start | bytes 786440 | tf_op jit(solution)/shard_map/ppermute | solution.py:39
  115.8 11.3 %collective-permute-start.23 = (bf16[4,128,256]{2,1,0:T(8,128)(2,1)S(1)}, bf16[4,128,256]{2,1,0:T(8,128)(2,1)S(1)}, u32[]{:S(2)}, u32[]{:S(2)}) collective-permute-start(bf16[4,128,256]{2,1,0:T(8,128)(2,1)S(1)} %get-tuple-element.91), channel_id=1, source_target_pairs={{0,12},{1,13},{2,14},{3,15},{4,0},{5,1},{6,2},{7,3},{8,4},{9,5},{1... | collective-permute-start | bytes 786440 | tf_op jit(solution)/shard_map/ppermute | solution.py:39
  119.0 11.2 %collective-permute-start.22 = (bf16[4,128,256]{2,1,0:T(8,128)(2,1)S(1)}, bf16[4,128,256]{2,1,0:T(8,128)(2,1)S(1)}, u32[]{:S(2)}, u32[]{:S(2)}) collective-permute-start(bf16[4,128,256]{2,1,0:T(8,128)(2,1)S(1)} %get-tuple-element.90), channel_id=1, source_target_pairs={{0,8},{1,9},{2,10},{3,11},{4,12},{5,13},{6,14},{7,15},{8,0},{9,1},... | collective-permute-start | bytes 786440 | tf_op jit(solution)/shard_map/ppermute | solution.py:39
  (6 other events, 18.5 us)
